TPU v7x, 32 devices: a whole 2x2x4 slice. The times are simulated.
32 devices in a mesh: ulysses: 4 (over x, core), blk: 8 (over z, y).
Axes of the slice: x: 2, y: 2, z: 4, core: 2. Of those that a mesh axis runs over, the one named last changes fastest.
Arguments:
- inputs: bfloat16 [2, 2048, 768], P(None, ('ulysses', 'blk')), may hold values from -6 to 6
- conditioning: bfloat16 [2, 128], replicated, may hold values from -4 to 4
- w_ada: bfloat16 [128, 4608], P(None, ('ulysses', 'blk')), may hold values from -0.5 to 0.5
- w_qkv: bfloat16 [768, 2304], P(('ulysses', 'blk')), may hold values from -0.21875 to 0.21875
- w_out: bfloat16 [768, 768], P(('ulysses', 'blk')), may hold values from -6 to 6
- w_up: bfloat16 [768, 3072], P(('ulysses', 'blk')), may hold values from -0.21875 to 0.21875
- w_down: bfloat16 [3072, 768], P(('ulysses', 'blk')), may hold values from -0.109375 to 0.109375
- gain_one: bfloat16 [768], P(('ulysses', 'blk')), may hold values from 0.099609375 to 1.8984375
- gain_two: bfloat16 [768], P(('ulysses', 'blk')), may hold values from 0.099609375 to 1.8984375
- cotangent: bfloat16 [2, 2048, 768], P(None, ('ulysses', 'blk')), may hold values from -6 to 6
Outputs:
- output: float32 [2, 2048, 768], P(None, ('ulysses', 'blk'))
- inputs_grad: float32 [2, 2048, 768], P(None, ('ulysses', 'blk'))
- conditioning_grad: float32 [2, 128], replicated
- w_ada_grad: float32 [128, 4608], P(None, ('ulysses', 'blk'))
- w_qkv_grad: float32 [768, 2304], P(('ulysses', 'blk'))
- w_out_grad: float32 [768, 768], P(('ulysses', 'blk'))
- w_up_grad: float32 [768, 3072], P(('ulysses', 'blk'))
- w_down_grad: float32 [3072, 768], P(('ulysses', 'blk'))
- gain_one_grad: float32 [768], P(('ulysses', 'blk'))
- gain_two_grad: float32 [768], P(('ulysses', 'blk'))
All inputs are finite; a program needn't handle non-finite values.
Results may differ from a plain program's by a relative error of at most 0.0158.
The roundings to bfloat16 on the way count: a program that leaves them out, or rounds other values in their place, can miss the bound.
Values may be sent and summed in bfloat16 or wider, within the bound.
No kernel may reach another device: no remote copies, remote signals or barrier semaphores. Data moves between devices by JAX's collectives and lax.ppermute only.
A program may use at most 256 MiB of HBM per device.

v0:
```python
import math

import jax
import jax.numpy as jnp
from jax import lax
from jax.sharding import PartitionSpec as P

HEADS = 12
HEAD_DIM = 64
SEQ_MB = 1
MICRO = 2


eps_norm = 1e-06
shard_group = 4


def normalize(values):
    average = jnp.mean(values, axis=-1, keepdims=True)
    centered = values - average
    variance = jnp.mean(centered * centered, axis=-1, keepdims=True)
    inv_std = lax.rsqrt(variance + eps_norm)
    return (centered * inv_std, inv_std)


def norm_back(grad_out, normed, inv_std, gain, scale_mod):
    factor = 1.0 + scale_mod
    d_normed = grad_out * gain * factor
    gain_term = jnp.sum(grad_out * normed * factor, axis=(0, 1))
    scale_term = jnp.sum(grad_out * normed * gain, axis=1)
    shift_term = jnp.sum(grad_out, axis=1)
    centred = d_normed - jnp.mean(d_normed, axis=-1, keepdims=True)
    d_inputs = inv_std * (centred - normed * jnp.mean(d_normed * normed, axis=-1, keepdims=True))
    return (d_inputs, gain_term, scale_term, shift_term)


def rotary_tables(positions):
    half_dim = HEAD_DIM // 2
    frequency = jnp.exp(
        -jnp.log(10000.0) * jnp.arange(half_dim, dtype=jnp.float32) * 2.0 / HEAD_DIM
    )
    angles = positions[:, None] * frequency[None, :]
    return (jnp.cos(angles)[:, None, :], jnp.sin(angles)[:, None, :])


def rotate(values, cos_table, sin_table):
    half_dim = values.shape[-1] // 2
    first_half = values[..., :half_dim]
    second_half = values[..., half_dim:]
    return jnp.concatenate(
        [
            first_half * cos_table - second_half * sin_table,
            second_half * cos_table + first_half * sin_table,
        ],
        axis=-1,
    )


def unrotate(grads, cos_table, sin_table):
    half_dim = grads.shape[-1] // 2
    first_half = grads[..., :half_dim]
    second_half = grads[..., half_dim:]
    return jnp.concatenate(
        [
            first_half * cos_table + second_half * sin_table,
            second_half * cos_table - first_half * sin_table,
        ],
        axis=-1,
    )


def gelu_tanh(values):
    return jax.nn.gelu(values, approximate=True)


def split_pairs(block):
    batch_seqs = block.shape[0]
    key_rows = block.shape[1]
    heads_here = block.shape[3] // HEAD_DIM
    keys = block[:, :, 0].reshape(batch_seqs, key_rows, heads_here, HEAD_DIM)
    values = block[:, :, 1].reshape(batch_seqs, key_rows, heads_here, HEAD_DIM)
    return (keys, values)


def split_blocks(piece, shard_rows):
    count = piece.shape[1] // shard_rows
    group = math.gcd(count, shard_group)
    steps = count // group
    shaped = piece.reshape((piece.shape[0], steps, group * shard_rows) + piece.shape[2:])
    return jnp.moveaxis(shaped, 1, 0)


def forward_block(query_heads, carry, block):
    top, totals, accum = carry
    keys, values = split_pairs(block)
    scores = jnp.einsum(
        "shqd,skhd->shqk", query_heads, keys, preferred_element_type=jnp.float32
    ) * HEAD_DIM ** (-0.5)
    new_top = jnp.maximum(top, jnp.max(scores, axis=-1))
    probs = jnp.exp(scores - new_top[..., None])
    fade = jnp.exp(top - new_top)
    totals = totals * fade + jnp.sum(probs, axis=-1)
    accum = accum * fade[..., None] + jnp.einsum(
        "shqk,skhd->shqd", probs.astype(jnp.bfloat16), values, preferred_element_type=jnp.float32
    )
    return (new_top, totals, accum)


def shards(inputs, conditioning, w_ada, w_qkv, w_out, w_up, w_down, gain_one, gain_two, cotangent):
    gathered = (
        lax.all_gather(w_ada, ("ulysses", "blk"), axis=1, tiled=True),
        lax.all_gather(w_qkv, ("ulysses", "blk"), axis=0, tiled=True),
        lax.all_gather(w_out, ("ulysses", "blk"), axis=0, tiled=True),
        lax.all_gather(w_up, ("ulysses", "blk"), axis=0, tiled=True),
        lax.all_gather(w_down, ("ulysses", "blk"), axis=0, tiled=True),
        lax.all_gather(gain_one, ("ulysses", "blk"), axis=0, tiled=True),
        lax.all_gather(gain_two, ("ulysses", "blk"), axis=0, tiled=True),
    )
    ada_full, qkv_full, out_full, up_full, down_full = (
        gathered[0],
        gathered[1],
        gathered[2],
        gathered[3],
        gathered[4],
    )
    gain_first = gathered[5].astype(jnp.float32)
    gain_second = gathered[6].astype(jnp.float32)
    rows = inputs.shape[1]
    width = inputs.shape[2]
    device_index = lax.axis_index(("ulysses", "blk"))
    positions = (device_index * rows + jnp.arange(rows, dtype=jnp.int32)).astype(jnp.float32)
    cos_table, sin_table = rotary_tables(positions)
    score_scale = HEAD_DIM ** (-0.5)
    ada_cols = w_ada.shape[1]
    grad_shapes = (
        w_qkv.shape,
        w_out.shape,
        w_up.shape,
        w_down.shape,
        gain_one.shape,
        gain_two.shape,
    )
    grad_totals = tuple((jnp.zeros(shape, jnp.float32) for shape in grad_shapes))
    ada_grad = jnp.zeros(w_ada.shape, jnp.float32)
    outputs_list = []
    input_grads = []
    cond_grads = []
    for micro_step in range(MICRO):
        offset = micro_step * SEQ_MB
        seq_inputs = inputs[offset : offset + SEQ_MB].astype(jnp.float32)
        cond_rows = conditioning[offset : offset + SEQ_MB]
        modulation = jnp.dot(cond_rows, ada_full, preferred_element_type=jnp.float32)
        pieces = [p[:, None, :] for p in jnp.split(modulation, 6, axis=1)]
        shift_one, scale_one, gate_one, shift_two, scale_two, gate_two = pieces
        normed_one, inv_one = normalize(seq_inputs)
        first_in = (normed_one * gain_first * (1.0 + scale_one) + shift_one).astype(jnp.bfloat16)
        projected = jnp.dot(first_in, qkv_full, preferred_element_type=jnp.float32)
        projected = projected.reshape(SEQ_MB, rows, 3, HEADS, HEAD_DIM)
        rot_query = rotate(projected[:, :, 0], cos_table, sin_table)
        rot_key = rotate(projected[:, :, 1], cos_table, sin_table)
        packed = jnp.stack([rot_query, rot_key, projected[:, :, 2]], axis=2).reshape(
            SEQ_MB, rows, 3, width
        )
        regrouped = lax.all_to_all(
            packed.astype(jnp.bfloat16), "ulysses", split_axis=3, concat_axis=1, tiled=True
        )
        query_rows = regrouped.shape[1]
        head_width = regrouped.shape[3]
        local_heads = head_width // HEAD_DIM
        query_heads = (
            regrouped[:, :, 0]
            .reshape(SEQ_MB, query_rows, local_heads, HEAD_DIM)
            .transpose(0, 2, 1, 3)
        )
        kv_local = regrouped[:, :, 1:]
        start_carry = (
            jnp.full((SEQ_MB, local_heads, query_rows), -1e30, jnp.float32),
            jnp.zeros((SEQ_MB, local_heads, query_rows), jnp.float32),
            jnp.zeros((SEQ_MB, local_heads, query_rows, HEAD_DIM), jnp.float32),
        )

        def scan_forward(carry, block):
            return (forward_block(query_heads, carry, block), None)

        result, _ = lax.scan(
            scan_forward,
            start_carry,
            split_blocks(lax.all_gather(kv_local, "blk", axis=1, tiled=True), query_rows),
        )
        carry = result
        top, totals, accum = carry
        attn_heads = accum / totals[..., None]
        log_total = top + jnp.log(totals)
        attn_tokens = (
            attn_heads.astype(jnp.bfloat16)
            .transpose(0, 2, 1, 3)
            .reshape(SEQ_MB, query_rows, head_width)
        )
        attended = lax.all_to_all(attn_tokens, "ulysses", split_axis=1, concat_axis=2, tiled=True)
        branch = jnp.dot(attended, out_full, preferred_element_type=jnp.float32)
        middle = seq_inputs + gate_one * branch
        normed_two, inv_two = normalize(middle)
        second_in = (normed_two * gain_second * (1.0 + scale_two) + shift_two).astype(jnp.bfloat16)
        raised = jnp.dot(second_in, up_full, preferred_element_type=jnp.float32)
        hidden, gelu_pull = jax.vjp(gelu_tanh, raised)
        hidden_low = hidden.astype(jnp.bfloat16)
        lowered = jnp.dot(hidden_low, down_full, preferred_element_type=jnp.float32)
        outputs_list.append(middle + gate_two * lowered)
        grad_out = cotangent[offset : offset + SEQ_MB].astype(jnp.float32)
        d_lowered = (gate_two * grad_out).astype(jnp.bfloat16)
        d_gate_two = jnp.sum(grad_out * lowered, axis=1)
        down_term = jnp.einsum(
            "srf,srd->fd", hidden_low, d_lowered, preferred_element_type=jnp.float32
        )
        d_hidden = jnp.einsum(
            "srd,fd->srf", d_lowered, down_full, preferred_element_type=jnp.float32
        )
        (d_raised,) = gelu_pull(d_hidden)
        d_raised_low = d_raised.astype(jnp.bfloat16)
        up_term = jnp.einsum(
            "srd,srf->df", second_in, d_raised_low, preferred_element_type=jnp.float32
        )
        d_second = jnp.einsum(
            "srf,df->srd", d_raised_low, up_full, preferred_element_type=jnp.float32
        )
        d_norm_two, gain_two_term, d_scale_two, d_shift_two = norm_back(
            d_second, normed_two, inv_two, gain_second, scale_two
        )
        d_middle = grad_out + d_norm_two
        d_gate_one = jnp.sum(d_middle * branch, axis=1)
        d_branch = (gate_one * d_middle).astype(jnp.bfloat16)
        out_term = jnp.einsum("srd,sre->de", attended, d_branch, preferred_element_type=jnp.float32)
        d_attended = jnp.einsum(
            "sre,de->srd", d_branch, out_full, preferred_element_type=jnp.float32
        ).astype(jnp.bfloat16)
        d_attn_rows = lax.all_to_all(d_attended, "ulysses", split_axis=2, concat_axis=1, tiled=True)
        d_attn_heads = d_attn_rows.reshape(SEQ_MB, query_rows, local_heads, HEAD_DIM).transpose(
            0, 2, 1, 3
        )
        delta = jnp.sum(d_attn_heads.astype(jnp.float32) * attn_heads, axis=-1)
        all_pairs = lax.all_gather(kv_local, "blk", axis=1, tiled=True)

        def back_step(d_query, block):
            keys, values = split_pairs(block)
            scores = (
                jnp.einsum("shqd,skhd->shqk", query_heads, keys, preferred_element_type=jnp.float32)
                * score_scale
            )
            probs = jnp.exp(scores - log_total[..., None])
            d_probs = jnp.einsum(
                "shqd,skhd->shqk", d_attn_heads, values, preferred_element_type=jnp.float32
            )
            d_scores = (probs * (d_probs - delta[..., None])).astype(jnp.bfloat16)
            d_query = (
                d_query
                + jnp.einsum("shqk,skhd->shqd", d_scores, keys, preferred_element_type=jnp.float32)
                * score_scale
            )
            d_keys = (
                jnp.einsum(
                    "shqk,shqd->skhd", d_scores, query_heads, preferred_element_type=jnp.float32
                )
                * score_scale
            )
            d_values = jnp.einsum(
                "shqk,shqd->skhd",
                probs.astype(jnp.bfloat16),
                d_attn_heads,
                preferred_element_type=jnp.float32,
            )
            key_rows = block.shape[1]
            pair = jnp.stack(
                [
                    d_keys.reshape(SEQ_MB, key_rows, head_width),
                    d_values.reshape(SEQ_MB, key_rows, head_width),
                ],
                axis=2,
            )
            return (d_query, pair)

        query_zero = jnp.zeros((SEQ_MB, local_heads, query_rows, HEAD_DIM), jnp.float32)
        d_query, pair_terms = lax.scan(back_step, query_zero, split_blocks(all_pairs, query_rows))
        pair_terms = jnp.moveaxis(pair_terms, 0, 1)
        pair_terms = pair_terms.reshape(
            SEQ_MB, pair_terms.shape[1] * pair_terms.shape[2], 2, head_width
        )
        pair_sums = lax.psum_scatter(pair_terms, "blk", scatter_dimension=1, tiled=True)
        query_grad = d_query.transpose(0, 2, 1, 3).reshape(SEQ_MB, query_rows, 1, head_width)
        d_packed = jnp.concatenate([query_grad, pair_sums], axis=2).astype(jnp.bfloat16)
        d_local = lax.all_to_all(d_packed, "ulysses", split_axis=1, concat_axis=3, tiled=True)
        d_local = d_local.astype(jnp.float32).reshape(SEQ_MB, rows, 3, HEADS, HEAD_DIM)
        d_projected = (
            jnp.stack(
                [
                    unrotate(d_local[:, :, 0], cos_table, sin_table),
                    unrotate(d_local[:, :, 1], cos_table, sin_table),
                    d_local[:, :, 2],
                ],
                axis=2,
            )
            .reshape(SEQ_MB, rows, 3 * width)
            .astype(jnp.bfloat16)
        )
        qkv_term = jnp.einsum(
            "srd,sre->de", first_in, d_projected, preferred_element_type=jnp.float32
        )
        d_first = jnp.einsum(
            "sre,de->srd", d_projected, qkv_full, preferred_element_type=jnp.float32
        )
        d_norm_one, gain_one_term, d_scale_one, d_shift_one = norm_back(
            d_first, normed_one, inv_one, gain_first, scale_one
        )
        input_grads.append(d_middle + d_norm_one)
        mod_local = jnp.concatenate(
            [d_shift_one, d_scale_one, d_gate_one, d_shift_two, d_scale_two, d_gate_two], axis=1
        )
        mod_total = lax.psum(mod_local, ("ulysses", "blk"))
        mod_low = mod_total.astype(jnp.bfloat16)
        cond_grads.append(
            jnp.einsum("sm,cm->sc", mod_low, ada_full, preferred_element_type=jnp.float32)
        )
        mod_part = lax.dynamic_slice_in_dim(mod_low, device_index * ada_cols, ada_cols, 1)
        ada_grad = ada_grad + jnp.einsum(
            "sc,sm->cm", cond_rows, mod_part, preferred_element_type=jnp.float32
        )
        terms = (qkv_term, out_term, up_term, down_term, gain_one_term, gain_two_term)
        reduced = (
            lax.psum_scatter(terms[0], ("ulysses", "blk"), scatter_dimension=0, tiled=True),
            lax.psum_scatter(terms[1], ("ulysses", "blk"), scatter_dimension=0, tiled=True),
            lax.psum_scatter(terms[2], ("ulysses", "blk"), scatter_dimension=0, tiled=True),
            lax.psum_scatter(terms[3], ("ulysses", "blk"), scatter_dimension=0, tiled=True),
            lax.psum_scatter(terms[4], ("ulysses", "blk"), scatter_dimension=0, tiled=True),
            lax.psum_scatter(terms[5], ("ulysses", "blk"), scatter_dimension=0, tiled=True),
        )
        grad_totals = tuple((a + b for a, b in zip(grad_totals, reduced)))
    output = jnp.concatenate(outputs_list, axis=0)
    inputs_grad = jnp.concatenate(input_grads, axis=0)
    conditioning_grad = jnp.concatenate(cond_grads, axis=0)
    return (
        output,
        inputs_grad,
        conditioning_grad,
        ada_grad,
        grad_totals[0],
        grad_totals[1],
        grad_totals[2],
        grad_totals[3],
        grad_totals[4],
        grad_totals[5],
    )


def solution(mesh):
    in_specs = (
        P(None, ("ulysses", "blk"), None),
        P(),
        P(None, ("ulysses", "blk")),
        P(("ulysses", "blk"), None),
        P(("ulysses", "blk"), None),
        P(("ulysses", "blk"), None),
        P(("ulysses", "blk"), None),
        P(("ulysses", "blk")),
        P(("ulysses", "blk")),
        P(None, ("ulysses", "blk"), None),
    )
    out_specs = (
        P(None, ("ulysses", "blk"), None),
        P(None, ("ulysses", "blk"), None),
        P(),
        P(None, ("ulysses", "blk")),
        P(("ulysses", "blk"), None),
        P(("ulysses", "blk"), None),
        P(("ulysses", "blk"), None),
        P(("ulysses", "blk"), None),
        P(("ulysses", "blk")),
        P(("ulysses", "blk")),
    )
    return jax.shard_map(shards, mesh=mesh, in_specs=in_specs, out_specs=out_specs, check_vma=False)
```

profile of v0, /device:TPU:0, one launch (start us, length us, event | category | flops | bytes accessed | tf_op | source)
XLA Modules:
  0.0 1250.2 jit_solution(7714770111622004763)
XLA Ops:
  10.4 42.0 %all-reduce.5 = (bf16[768]{0:T(1024)(128)(2,1)S(1)}, bf16[768]{0:T(1024)(128)(2,1)}) all-reduce(bf16[768]{0:T(1024)(128)(2,1)S(1)} %dynamic-update-slice, bf16[768]{0:T(1024)(128)(2,1)S(1)} %dynamic-update-slice.1), channel_id=1, replica_groups=mesh['ulysses'=4,'blk'=8] {'ulysses','blk'}, use_global_device_ids=true, to_apply=%add | all-reduce | flops 1536 | bytes 6144
  57.1 10.7 all-gather.8.cloned.1.call-done
  71.9 57.9 %all-gather.10.cloned.1.call-done = bf16[768,2304]{1,0:T(8,128)(2,1)} async-done(((bf16[24,2304]{1,0:T(8,128)(2,1)}), bf16[768,2304]{1,0:T(8,128)(2,1)}) %all-gather.10.cloned.1.call-update) | async-done | bytes 3538960 | tf_op jit(solution)/shard_map/all_gather | solution.py:112
  129.8 4.5 copy.202
  134.4 2.1 convolution_bitcast_fusion
  142.5 8.9 all_to_all.114
  158.0 9.0 all_to_all.115
  172.8 29.0 %all-gather.20.cloned.1.call-done = bf16[1,2048,2,192]{3,1,2,0:T(8,128)(2,1)} async-done(((bf16[1,256,2,192]{3,1,2,0:T(8,128)(2,1)}), bf16[1,2048,2,192]{3,1,2,0:T(8,128)(2,1)}) %all-gather.20.cloned.1.call-update) | async-done | bytes 1572880 | tf_op jit(solution)/shard_map/all_gather | solution.py:188
  201.8 3.9 copy.220
  205.7 9.6 while.57
  219.2 3.9 all-to-all-start.3
  223.2 29.2 %all-gather.12.cloned.1.call-done = bf16[1,2048,2,192]{3,1,2,0:T(8,128)(2,1)} async-done(((bf16[1,256,2,192]{3,1,2,0:T(8,128)(2,1)}), bf16[1,2048,2,192]{3,1,2,0:T(8,128)(2,1)}) %all-gather.12.cloned.1.call-update) | async-done | bytes 1572880 | tf_op jit(solution)/shard_map/all_gather | solution.py:188
  252.4 3.9 copy.210
  256.3 9.5 while.56
  269.3 3.7 all-to-all-start.1
  275.1 2.2 all-to-all-done.1
  277.8 30.1 %all-gather.14.cloned.1.call-done = bf16[768,768]{1,0:T(8,128)(2,1)} async-done(((bf16[24,768]{1,0:T(8,128)(2,1)}), bf16[768,768]{1,0:T(8,128)(2,1)}) %all-gather.14.cloned.1.call-update) | async-done | bytes 1179664 | tf_op jit(solution)/shard_map/all_gather | solution.py:113
  309.5 1.7 fusion.184
  311.7 61.5 %all-gather.16.cloned.1.call-done = bf16[768,3072]{1,0:T(8,128)(2,1)} async-done(((bf16[24,3072]{1,0:T(8,128)(2,1)}), bf16[768,3072]{1,0:T(8,128)(2,1)}) %all-gather.16.cloned.1.call-update) | async-done | bytes 4718608 | tf_op jit(solution)/shard_map/all_gather | solution.py:114
  373.2 3.3 fusion.172
  376.6 62.1 %all-gather.18.cloned.1.call-done = bf16[3072,768]{1,0:T(8,128)(2,1)} async-done(((bf16[96,768]{1,0:T(8,128)(2,1)}), bf16[3072,768]{1,0:T(8,128)(2,1)}) %all-gather.18.cloned.1.call-update) | async-done | bytes 4718608 | tf_op jit(solution)/shard_map/all_gather | solution.py:115
  438.6 3.5 fusion.179
  448.9 2.2 fusion.180
  451.1 2.4 fusion.105
  456.7 1.9 reduce.72
  459.4 3.3 all-to-all-start.6
  462.9 4.0 all-to-all-done.6
  469.5 2.5 broadcast.382.clone2
  472.0 77.9 %while.59 = (s32[]{:T(128)}, f32[1,3,256,64]{2,3,1,0:T(8,128)}, f32[2,1,1024,2,192]{2,0,4,3,1:T(2,128)}, bf16[2,1,1024,2,192]{2,4,3,1,0:T(8,128)(2,1)}, bf16[1,3...) while((s32[]{:T(128)}, f32[1,3,256,64]{2,3,1,0:T(8,128)}, ...), condition=%wide.region_28.29_spmd.clone, body=%wide.region_27.28_spmd.clone.sunk | while | flops 510345216 | bytes 37364948 | solution.py:282
  473.9 3.0 multiply_convert_fusion.13
  476.9 2.6 fusion.323
  483.4 27.6 %dynamic_update_slice.12 = f32[2,1,1024,2,192]{2,0,4,3,1:T(2,128)} dynamic-update-slice(f32[2,1,1024,2,192]{2,0,4,3,1:T(2,128)} %get-tuple-element.898, f32[1,1,1024,2,192]{2,0,4,3,1:T(1,128)S(1)} %copy.294, s32[]{:T(128)S(6)} %copy.326, s32[]{:T(128)} %constant.96.clone.1..sunk.3, s32[]{:T(128)} %constant.96.clone.1..sunk.3, s32[]{:T(128)} %constant.96.clone.1..sunk.3, s32[]{:T(128)} %constant.96.clone.1..sunk.3) | dynamic-update-slice | bytes 3145732 | tf_op jit(solution)/shard_map/while/body/jit(dynamic_update_index_in_dim)/dynamic_update_slice | solution.py:282
  512.9 2.9 multiply_convert_fusion.13
  515.8 2.6 fusion.323
  522.4 27.6 %dynamic_update_slice.12 = f32[2,1,1024,2,192]{2,0,4,3,1:T(2,128)} dynamic-update-slice(f32[2,1,1024,2,192]{2,0,4,3,1:T(2,128)} %get-tuple-element.898, f32[1,1,1024,2,192]{2,0,4,3,1:T(1,128)S(1)} %copy.294, s32[]{:T(128)S(6)} %copy.326, s32[]{:T(128)} %constant.96.clone.1..sunk.3, s32[]{:T(128)} %constant.96.clone.1..sunk.3, s32[]{:T(128)} %constant.96.clone.1..sunk.3, s32[]{:T(128)} %constant.96.clone.1..sunk.3) | dynamic-update-slice | bytes 3145732 | tf_op jit(solution)/shard_map/while/body/jit(dynamic_update_index_in_dim)/dynamic_update_slice | solution.py:282
  549.9 5.6 reshape_transpose.7
  557.7 1.9 reduce.73
  560.4 3.3 all-to-all-start.4
  564.0 4.0 all-to-all-done.4
  570.6 2.4 broadcast.382.clone2.1
  573.1 78.2 %while.58 = (s32[]{:T(128)}, f32[1,3,256,64]{2,3,1,0:T(8,128)}, f32[2,1,1024,2,192]{2,0,4,3,1:T(2,128)}, bf16[2,1,1024,2,192]{2,4,3,1,0:T(8,128)(2,1)}, bf16[1,3...) while((s32[]{:T(128)}, f32[1,3,256,64]{2,3,1,0:T(8,128)}, ...), condition=%wide.region_20.21_spmd.clone, body=%wide.region_19.20_spmd.clone.sunk | while | flops 510345216 | bytes 37364948 | solution.py:282
  575.0 3.0 multiply_convert_fusion.12
  578.0 2.7 fusion.309
  584.6 27.6 %dynamic_update_slice.11 = f32[2,1,1024,2,192]{2,0,4,3,1:T(2,128)} dynamic-update-slice(f32[2,1,1024,2,192]{2,0,4,3,1:T(2,128)} %get-tuple-element.928, f32[1,1,1024,2,192]{2,0,4,3,1:T(1,128)S(1)} %copy.293, s32[]{:T(128)S(6)} %copy.335, s32[]{:T(128)} %constant.96.clone.1..sunk.2, s32[]{:T(128)} %constant.96.clone.1..sunk.2, s32[]{:T(128)} %constant.96.clone.1..sunk.2, s32[]{:T(128)} %constant.96.clone.1..sunk.2) | dynamic-update-slice | bytes 3145732 | tf_op jit(solution)/shard_map/while/body/jit(dynamic_update_index_in_dim)/dynamic_update_slice | solution.py:282
  614.2 3.0 multiply_convert_fusion.12
  617.2 2.6 fusion.309
  623.8 27.6 %dynamic_update_slice.11 = f32[2,1,1024,2,192]{2,0,4,3,1:T(2,128)} dynamic-update-slice(f32[2,1,1024,2,192]{2,0,4,3,1:T(2,128)} %get-tuple-element.928, f32[1,1,1024,2,192]{2,0,4,3,1:T(1,128)S(1)} %copy.293, s32[]{:T(128)S(6)} %copy.335, s32[]{:T(128)} %constant.96.clone.1..sunk.2, s32[]{:T(128)} %constant.96.clone.1..sunk.2, s32[]{:T(128)} %constant.96.clone.1..sunk.2, s32[]{:T(128)} %constant.96.clone.1..sunk.2) | dynamic-update-slice | bytes 3145732 | tf_op jit(solution)/shard_map/while/body/jit(dynamic_update_index_in_dim)/dynamic_update_slice | solution.py:282
  651.3 5.6 reshape_transpose.6
  658.5 1.9 convolution_add_fusion.3
  662.2 5.1 convolution_add_fusion.2
  670.0 5.1 convolution_add_fusion.1
  678.2 3.5 all-to-all-start.7
  681.7 49.1 %reduce-scatter.7.cloned.1.call-done = f32[1,256,2,192]{1,3,2,0:T(8,128)} async-done(((f32[1,2048,2,192]{1,3,2,0:T(8,128)}), f32[1,256,2,192]{1,3,2,0:T(8,128)}) %reduce-scatter.7.cloned.1.call-update) | async-done | bytes 393232 | tf_op jit(solution)/shard_map/reduce_scatter | solution.py:287
  733.0 3.5 all-to-all-start.5
  737.1 8.2 all-to-all-done.5
  749.0 4.1 convolution_add_fusion
  755.9 1.8 pad_maximum_fusion.2
  757.7 2.3 fusion.194
  760.1 2.7 multiply_reduce_fusion.3
  763.7 43.9 %all-reduce.4 = (bf16[1,4608]{1,0:T(2,128)(2,1)S(1)}, bf16[1,4608]{1,0:T(2,128)(2,1)S(1)}, f32[768]{0:T(1024)S(1)}, f32[768]{0:T(1024)S(1)}) all-reduce(f32[1,4608]{1,0:T(1,128)S(1)} %constant_dynamic-update-slice_fusion.6, ...), channel_id=1, replica_groups=mesh['ulysses'=4,'blk'=8] {'ulysses','blk'}, use_global_device_ids=true, to_apply=%region_45.46 | all-reduce | flops 10752 | bytes 67584 | tf_op jit(solution)/shard_map/psum | solution.py:317
  816.7 18.1 %reduce-scatter.13.cloned.1.call-done = f32[24,768]{1,0:T(8,128)} async-done(((f32[768,768]{1,0:T(8,128)}), f32[24,768]{1,0:T(8,128)}) %reduce-scatter.13.cloned.1.call-update) | async-done | bytes 73744 | tf_op jit(solution)/shard_map/reduce_scatter | solution.py:329
  834.8 142.1 %reduce-scatter.15.cloned.1.call-done = f32[24,3072]{1,0:T(8,128)} async-done(((f32[768,3072]{1,0:T(8,128)}), f32[24,3072]{1,0:T(8,128)}) %reduce-scatter.15.cloned.1.call-update) | async-done | bytes 294928 | tf_op jit(solution)/shard_map/reduce_scatter | solution.py:330
  976.9 140.9 %reduce-scatter.17.cloned.1.call-done = f32[96,768]{1,0:T(8,128)} async-done(((f32[3072,768]{1,0:T(8,128)}), f32[96,768]{1,0:T(8,128)}) %reduce-scatter.17.cloned.1.call-update) | async-done | bytes 294928 | tf_op jit(solution)/shard_map/reduce_scatter | solution.py:331
  1117.9 125.3 %reduce-scatter.11.cloned.1.call-done = f32[24,2304]{1,0:T(8,128)} async-done(((f32[768,2304]{1,0:T(8,128)}), f32[24,2304]{1,0:T(8,128)}) %reduce-scatter.11.cloned.1.call-update) | async-done | bytes 221200 | tf_op jit(solution)/shard_map/reduce_scatter | solution.py:328
  (504 shorter events, 130.8 us)
Async XLA Ops:
  7.2 60.6 %all-gather.8.cloned.1.call-start = ((), (), s32[]{:S(2)}) async-start(), calls=%async_computation.14 | async-start | bytes 1216512 | tf_op jit(solution)/shard_map/all_gather | solution.py:111
  7.9 121.9 %all-gather.10.cloned.1.call-start = ((), (), s32[]{:S(2)}) async-start(), calls=%async_computation.15 | async-start | bytes 3649536 | tf_op jit(solution)/shard_map/all_gather | solution.py:112
  8.7 193.1 %all-gather.20.cloned.1.call-start = ((), (), s32[]{:S(2)}) async-start(), calls=%async_computation.20 | async-start | bytes 2359296 | tf_op jit(solution)/shard_map/all_gather | solution.py:188
  52.4 84.5 %copy-start.56 = (f32[768]{0:T(1024)}, f32[768]{0:T(1024)S(1)}, u32[]{:S(2)}) copy-start(f32[768]{0:T(1024)S(1)} %convert_element_type.242) | copy-start | bytes 9220
  71.9 62.4 %copy-start.66 = (f32[768]{0:T(1024)}, f32[768]{0:T(1024)S(1)}, u32[]{:S(2)}) copy-start(f32[768]{0:T(1024)S(1)} %get-tuple-element.476) | copy-start | bytes 9220
  71.9 65.0 %copy-start.58 = (f32[768]{0:T(1024)}, f32[768]{0:T(1024)S(1)}, u32[]{:S(2)}) copy-start(f32[768]{0:T(1024)S(1)} %get-tuple-element.630) | copy-start | bytes 9220
  71.9 65.0 %copy-start.68 = (f32[768]{0:T(1024)}, f32[768]{0:T(1024)S(1)}, u32[]{:S(2)}) copy-start(f32[768]{0:T(1024)S(1)} %get-tuple-element.631) | copy-start | bytes 9220
  153.7 98.7 %all-gather.12.cloned.1.call-start = ((), (), s32[]{:S(2)}) async-start(), calls=%async_computation.16 | async-start | bytes 2359296 | tf_op jit(solution)/shard_map/all_gather | solution.py:188
  169.3 138.6 %all-gather.14.cloned.1.call-start = ((), (), s32[]{:S(2)}) async-start(), calls=%async_computation.17 | async-start | bytes 1216512 | tf_op jit(solution)/shard_map/all_gather | solution.py:113
  169.9 203.3 %all-gather.16.cloned.1.call-start = ((), (), s32[]{:S(2)}) async-start(), calls=%async_computation.18 | async-start | bytes 4866048 | tf_op jit(solution)/shard_map/all_gather | solution.py:114
  170.5 268.2 %all-gather.18.cloned.1.call-start = ((), (), s32[]{:S(2)}) async-start(), calls=%async_computation.19 | async-start | bytes 4866048 | tf_op jit(solution)/shard_map/all_gather | solution.py:115
  219.2 50.1 %all-to-all-start.3 = ((bf16[4,2,6144]{2,1,0:T(2,128)(2,1)}), bf16[4,2,6144]{2,1,0:T(2,128)(2,1)}, u32[]{:S(2)}, u32[]{:S(2)}) async-start(bf16[4,2,6144]{2,1,0:T(2,128)(2,1)} %reshape.1089), calls=%async_computation.3 | async-start | bytes 196608 | tf_op jit(solution)/shard_map/all_to_all | solution.py:199
  265.9 43.6 %copy-start.24 = (bf16[2,64,768]{2,1,0:T(8,128)(2,1)S(1)}, bf16[2,64,768]{2,1,0:T(8,128)(2,1)}, u32[]{:S(2)}) copy-start(bf16[2,64,768]{2,1,0:T(8,128)(2,1)} %param.18) | copy-start | bytes 589828
  265.9 43.6 %copy-start.74 = (f32[768]{0:T(1024)S(1)}, f32[768]{0:T(1024)}, u32[]{:S(2)}) copy-start(f32[768]{0:T(1024)} %get-tuple-element.629) | copy-start | bytes 9220
  265.9 43.6 %copy-start.76 = (f32[768]{0:T(1024)S(1)}, f32[768]{0:T(1024)}, u32[]{:S(2)}) copy-start(f32[768]{0:T(1024)} %get-tuple-element.477) | copy-start | bytes 9220
  269.3 8.0 all-to-all-start.1
  274.8 98.4 %copy-start.64 = (f32[768]{0:T(1024)S(1)}, f32[768]{0:T(1024)}, u32[]{:S(2)}) copy-start(f32[768]{0:T(1024)} %get-tuple-element.474) | copy-start | bytes 9220
  274.8 98.4 %copy-start.80 = (f32[768]{0:T(1024)S(1)}, f32[768]{0:T(1024)}, u32[]{:S(2)}) copy-start(f32[768]{0:T(1024)} %get-tuple-element.478) | copy-start | bytes 9220
  275.1 34.3 %copy-start.52 = (bf16[64,768]{1,0:T(8,128)(2,1)}, bf16[64,768]{1,0:T(8,128)(2,1)S(1)}, u32[]{:S(2)}) copy-start(bf16[64,768]{1,0:T(8,128)(2,1)S(1)} %reshape.1021) | copy-start | bytes 294916
  277.8 95.4 %copy-start.54 = (bf16[64,768]{1,0:T(8,128)(2,1)}, bf16[64,768]{1,0:T(8,128)(2,1)S(1)}, u32[]{:S(2)}) copy-start(bf16[64,768]{1,0:T(8,128)(2,1)S(1)} %reshape.1016) | copy-start | bytes 294916
  311.2 142.3 %copy-start.21 = (f32[1,64,768]{2,1,0:T(8,128)}, f32[1,64,768]{2,1,0:T(8,128)S(1)}, u32[]{:S(2)}) copy-start(f32[1,64,768]{2,1,0:T(8,128)S(1)} %get-tuple-element.550) | copy-start | bytes 589828
  311.2 142.3 %copy-start.28 = (f32[1,64,768]{2,1,0:T(8,128)}, f32[1,64,768]{2,1,0:T(8,128)S(1)}, u32[]{:S(2)}) copy-start(f32[1,64,768]{2,1,0:T(8,128)S(1)} %get-tuple-element.602) | copy-start | bytes 589828
  311.3 142.3 %copy-start.100 = (f32[64]{0:T(128)}, f32[64]{0:T(128)S(1)}, u32[]{:S(2)}) copy-start(f32[64]{0:T(128)S(1)} %broadcast_multiply_fusion.8) | copy-start | bytes 772
  311.5 142.1 %copy-start.90 = (f32[64]{0:T(128)}, f32[64]{0:T(128)S(1)}, u32[]{:S(2)}) copy-start(f32[64]{0:T(128)S(1)} %broadcast_multiply_fusion.10) | copy-start | bytes 772
  311.7 141.9 %copy-start.106 = (f32[64]{0:T(128)}, f32[64]{0:T(128)S(1)}, u32[]{:S(2)}) copy-start(f32[64]{0:T(128)S(1)} %add_rsqrt_fusion) | copy-start | bytes 772
  311.7 141.9 %copy-start.102 = (f32[64]{0:T(128)}, f32[64]{0:T(128)S(1)}, u32[]{:S(2)}) copy-start(f32[64]{0:T(128)S(1)} %add_rsqrt_fusion.2) | copy-start | bytes 772
  376.5 67.5 %copy-start.30 = (f32[64,3072]{1,0:T(8,128)}, f32[64,3072]{1,0:T(8,128)S(1)}, u32[]{:S(2)}) copy-start(f32[64,3072]{1,0:T(8,128)S(1)} %fusion.172) | copy-start | bytes 2359300
  376.5 65.6 %copy-start.50 = (bf16[2,64,768]{2,1,0:T(8,128)(2,1)S(1)}, bf16[2,64,768]{2,1,0:T(8,128)(2,1)}, u32[]{:S(2)}) copy-start(bf16[2,64,768]{2,1,0:T(8,128)(2,1)} %param.27) | copy-start | bytes 589828
  376.5 65.6 %copy-start.82 = (f32[768]{0:T(1024)S(1)}, f32[768]{0:T(1024)}, u32[]{:S(2)}) copy-start(f32[768]{0:T(1024)} %get-tuple-element.473) | copy-start | bytes 9220
  438.6 3.8 copy-start.10
  447.3 3.8 copy-start.19
  448.9 4.6 copy-start.46
  451.1 4.7 copy-start.11
  453.5 9.4 copy-start.63
  453.6 15.0 %copy-start.18 = (f32[1,3,256,64]{2,3,1,0:T(8,128)S(1)}, f32[1,3,256,64]{2,3,1,0:T(8,128)}, u32[]{:S(2)}) copy-start(f32[1,3,256,64]{2,3,1,0:T(8,128)} %get-tuple-element.166) | copy-start | bytes 589828
  459.4 7.6 all-to-all-start.6
  462.7 213.4 %reduce-scatter.9.cloned.1.call-start = ((), (), s32[]{:S(2)}) async-start(), calls=%async_computation.22 | async-start | bytes 3538944 | tf_op jit(solution)/shard_map/reduce_scatter | solution.py:287
  476.9 4.2 copy-start
  476.9 4.2 copy-start.9
  515.8 4.2 copy-start
  515.8 4.2 copy-start.9
  555.5 8.5 copy-start.62
  555.6 14.1 %copy-start.15 = (f32[1,3,256,64]{2,3,1,0:T(8,128)S(1)}, f32[1,3,256,64]{2,3,1,0:T(8,128)}, u32[]{:S(2)}) copy-start(f32[1,3,256,64]{2,3,1,0:T(8,128)} %get-tuple-element.164) | copy-start | bytes 589828
  560.4 7.6 all-to-all-start.4
  563.8 167.1 %reduce-scatter.7.cloned.1.call-start = ((), (), s32[]{:S(2)}) async-start(), calls=%async_computation.21 | async-start | bytes 3538944 | tf_op jit(solution)/shard_map/reduce_scatter | solution.py:287
  578.0 4.2 copy-start.1
  578.0 4.2 copy-start.6
  617.2 4.2 copy-start.1
  617.2 4.2 copy-start.6
  657.0 177.8 %reduce-scatter.13.cloned.1.call-start = ((), (), s32[]{:S(2)}) async-start(), calls=%async_computation.24 | async-start | bytes 2433024 | tf_op jit(solution)/shard_map/reduce_scatter | solution.py:329
  660.5 316.4 %reduce-scatter.15.cloned.1.call-start = ((), (), s32[]{:S(2)}) async-start(), calls=%async_computation.25 | async-start | bytes 9732096 | tf_op jit(solution)/shard_map/reduce_scatter | solution.py:330
  667.4 450.5 %reduce-scatter.17.cloned.1.call-start = ((), (), s32[]{:S(2)}) async-start(), calls=%async_computation.26 | async-start | bytes 9732096 | tf_op jit(solution)/shard_map/reduce_scatter | solution.py:331
  675.1 6.6 copy-start.33
  678.2 54.8 %all-to-all-start.7 = ((bf16[1,256,3,192]{3,2,0,1:T(4,128)(2,1)}), bf16[1,256,3,192]{3,2,0,1:T(4,128)(2,1)S(1)}, u32[]{:S(2)}, u32[]{:S(2)}) async-start(bf16[1,256,3,192]{3,2,0,1:T(4,128)(2,1)} %copy.236), calls=%async_computation.9 | async-start | bytes 1048576 | tf_op jit(solution)/shard_map/all_to_all | solution.py:290
  733.0 12.3 all-to-all-start.5
  736.5 506.8 %reduce-scatter.11.cloned.1.call-start = ((), (), s32[]{:S(2)}) async-start(), calls=%async_computation.23 | async-start | bytes 7299072 | tf_op jit(solution)/shard_map/reduce_scatter | solution.py:328
  753.2 4.5 copy-start.3
  753.2 6.8 copy-start.26
  753.2 6.8 copy-start.36
  762.8 51.1 %copy-start.27 = (bf16[2,64,768]{2,1,0:T(8,128)(2,1)S(1)}, bf16[2,64,768]{2,1,0:T(8,128)(2,1)}, u32[]{:S(2)}) copy-start(bf16[2,64,768]{2,1,0:T(8,128)(2,1)} %param.18) | copy-start | bytes 589828
  762.8 51.1 %copy-start.41 = (f32[1,64,768]{2,1,0:T(8,128)S(1)}, f32[1,64,768]{2,1,0:T(8,128)}, u32[]{:S(2)}) copy-start(f32[1,64,768]{2,1,0:T(8,128)} %copy-done.39) | copy-start | bytes 589828
  762.8 51.1 %copy-start.44 = (f32[1,64,768]{2,1,0:T(8,128)S(1)}, f32[1,64,768]{2,1,0:T(8,128)}, u32[]{:S(2)}) copy-start(f32[1,64,768]{2,1,0:T(8,128)} %get-tuple-element.546) | copy-start | bytes 589828
  762.8 53.1 %copy-start.109 = (f32[128]{0:T(128)S(1)}, f32[128]{0:T(128)}, u32[]{:S(2)}) copy-start(f32[128]{0:T(128)} %get-tuple-element.621) | copy-start | bytes 1540
  762.8 53.1 %copy-start.110 = (f32[128]{0:T(128)S(1)}, f32[128]{0:T(128)}, u32[]{:S(2)}) copy-start(f32[128]{0:T(128)} %get-tuple-element.622) | copy-start | bytes 1540
  (78 other events, 135.6 us)
Sparse Core Ops, SparseCore 0:
  10.9 56.8 all-gather.7
  70.7 59.0 all-gather.9
  153.8 47.9 all-gather.19
  204.4 47.9 all-gather.11
  255.1 52.6 all-gather.13
  310.6 62.5 all-gather.15
  376.1 62.4 all-gather.17
  555.7 73.8 reduce-scatter.8
  657.1 73.6 reduce-scatter.6
  736.6 98.1 reduce-scatter.12
  842.3 134.5 reduce-scatter.14
  983.3 134.5 reduce-scatter.16
  1125.1 118.1 reduce-scatter.10
where the time goes:
time: 1270 us; the launch traced here: 1250 us
  waiting for transfers between devices  778 us (61%)
  local copies, waits for them, and re-layouts  193 us (15%)
  blocking collectives  104 us (8%)
  matrix products  95.7 us (8%)
  other arithmetic  41.2 us (3%)
  starting transfers between devices  22.3 us (2%)
  between operations  16.4 us (1%)
    reduce_scatter x1, waiting for transfers between devices, shards(): lax.psum_scatter(terms[2], ('ulysses', 'blk'), scatter_dimension=0, tiled...  142 us
    reduce_scatter x1, waiting for transfers between devices, shards(): lax.psum_scatter(terms[3], ('ulysses', 'blk'), scatter_dimension=0, tiled...  141 us
    reduce_scatter x1, waiting for transfers between devices, shards(): lax.psum_scatter(terms[0], ('ulysses', 'blk'), scatter_dimension=0, tiled...  125 us
    dynamic_update_slice x8, local copies, waits for them, and re-layouts, shards(): lax.scan(back_step, query_zero, split_blocks(all_pairs, query_rows))  117 us
    all_gather x1, waiting for transfers between devices, shards(): lax.all_gather(w_down, ('ulysses', 'blk'), axis=0, tiled=True)  62.1 us
    all_gather x1, waiting for transfers between devices, shards(): lax.all_gather(w_up, ('ulysses', 'blk'), axis=0, tiled=True)  61.5 us
    all_gather x2, waiting for transfers between devices, shards(): lax.all_gather(kv_local, 'blk', axis=1, tiled=True)  58.2 us
    all_gather x1, waiting for transfers between devices, shards(): lax.all_gather(w_qkv, ('ulysses', 'blk'), axis=0, tiled=True)  57.9 us
  transfers between devices with their start and end apart: 19, of which 16 were waited for; matrix products, arithmetic and copies ran while one was open for 16% of the time, Pallas kernels for 0%

commit v1 on v0

--- a/solution.py
+++ b/solution.py
@@ -1,9 +1,102 @@
+import functools
 import math
 
 import jax
 import jax.numpy as jnp
 from jax import lax
+from jax.experimental import pallas as pl
+from jax.experimental.pallas import tpu as pltpu
 from jax.sharding import PartitionSpec as P
+
+f32, bf16 = jnp.float32, jnp.bfloat16
+DOT = functools.partial(jnp.dot, preferred_element_type=f32)
+
+def attn_fwd_kernel(x_ref, o_ref, of_ref, lse_ref, kt_ref, v_ref):
+    nb, rows3, _ = x_ref.shape
+    half = rows3 // 3
+    rows = 2 * half
+    for j in range(nb):
+        kt_ref[:, j * rows : (j + 1) * rows] = x_ref[j, :rows, 64:].T
+        v_ref[j * rows : j * rows + half, :] = x_ref[j, rows:, :64]
+        v_ref[j * rows + half : (j + 1) * rows, :] = x_ref[j, rows:, 64:]
+
+    def step(j, _):
+        q = x_ref[j, :rows, :64] * jnp.asarray(0.125, bf16)
+        s = DOT(q, kt_ref[...])
+        top = jnp.max(s, axis=1, keepdims=True)
+        p = jnp.exp(s - top)
+        total = jnp.sum(p, axis=1, keepdims=True)
+        o = DOT(p.astype(bf16), v_ref[...]) / total
+        packed = jnp.concatenate([o[:half], o[half:]], axis=1)
+        of_ref[j] = packed
+        o_ref[j] = packed.astype(bf16)
+        lse = jnp.broadcast_to(top + jnp.log(total), (rows, 128)).T
+        lse_ref[j] = lse[:8]
+        return 0
+    lax.fori_loop(0, nb, step, 0, unroll=2)
+
+def attn_fwd(x):
+    nb, rows3, _ = x.shape
+    half = rows3 // 3
+    n = nb * half * 2
+    return pl.pallas_call(
+        attn_fwd_kernel,
+        out_shape=(jax.ShapeDtypeStruct((nb, half, 128), bf16), jax.ShapeDtypeStruct((nb, half, 128), f32),
+                   jax.ShapeDtypeStruct((nb, 8, 2 * half), f32)),
+        scratch_shapes=[pltpu.VMEM((64, n), bf16), pltpu.VMEM((n, 64), bf16)],
+        cost_estimate=pl.CostEstimate(flops=4 * n * n * 64, bytes_accessed=n * 64 * 2 * 8, transcendentals=n * n),
+        compiler_params=pltpu.CompilerParams(vmem_limit_bytes=32 << 20),
+        name="attn_fwd",
+    )(x)
+
+def attn_bwd_kernel(x_ref, d_ref, of_ref, lse_ref, g_ref, qt_ref, dt_ref, q_ref, dd_ref, lse_s, del_s, dqt_ref):
+    nb, rows3, _ = x_ref.shape
+    half = rows3 // 3
+    rows = 2 * half
+    for j in range(nb):
+        sl = slice(j * rows, (j + 1) * rows)
+        q = x_ref[j, :rows, :64] * jnp.asarray(0.125, bf16)
+        q_ref[sl, :] = q
+        qt_ref[:, sl] = q.T
+        d = jnp.concatenate([d_ref[j, :, :64], d_ref[j, :, 64:]], axis=0)
+        dd_ref[sl, :] = d
+        dt_ref[:, sl] = d.T
+        o = jnp.concatenate([of_ref[j, :, :64], of_ref[j, :, 64:]], axis=0)
+        delta = jnp.sum(d.astype(f32) * o, axis=1, keepdims=True)
+        del_s[:, sl] = jnp.broadcast_to(delta, (rows, 128)).T[:8]
+        lse_s[:, sl] = lse_ref[j]
+    dqt_ref[...] = jnp.zeros_like(dqt_ref)
+
+    def step(j, _):
+        k = x_ref[j, :rows, 64:]
+        v = jnp.concatenate([x_ref[j, rows:, :64], x_ref[j, rows:, 64:]], axis=0)
+        s = DOT(k, qt_ref[...])
+        p = jnp.exp(s - lse_s[0:1, :])
+        dp = DOT(v, dt_ref[...])
+        ds = (p * (dp - del_s[0:1, :])).astype(bf16)
+        dv = DOT(p.astype(bf16), dd_ref[...])
+        dk = DOT(ds, q_ref[...])
+        dqt_ref[...] += DOT(k.T, ds)
+        g_ref[j, :rows, 64:] = dk.astype(bf16)
+        g_ref[j, rows:, :] = jnp.concatenate([dv[:half], dv[half:]], axis=1).astype(bf16)
+        return 0
+    lax.fori_loop(0, nb, step, 0, unroll=2)
+    for j in range(nb):
+        g_ref[j, :rows, :64] = (dqt_ref[:, j * rows : (j + 1) * rows].T * 0.125).astype(bf16)
+
+def attn_bwd(x, d, of, lse):
+    nb, rows3, _ = x.shape
+    half = rows3 // 3
+    n = nb * half * 2
+    return pl.pallas_call(
+        attn_bwd_kernel,
+        out_shape=jax.ShapeDtypeStruct((nb, rows3, 128), bf16),
+        scratch_shapes=[pltpu.VMEM((64, n), bf16), pltpu.VMEM((64, n), bf16), pltpu.VMEM((n, 64), bf16), pltpu.VMEM((n, 64), bf16),
+                        pltpu.VMEM((8, n), f32), pltpu.VMEM((8, n), f32), pltpu.VMEM((64, n), f32)],
+        cost_estimate=pl.CostEstimate(flops=n * n * 64, bytes_accessed=n * 64 * 2, transcendentals=0),
+        compiler_params=pltpu.CompilerParams(vmem_limit_bytes=32 << 20),
+        name="attn_bwd",
+    )(x, d, of, lse)
 
 HEADS = 12
 HEAD_DIM = 64
@@ -350,7 +443,599 @@
     )
 
 
+def dot_nt(left, right):
+    return lax.dot_general(left, right, (((1,), (1,)), ((), ())), preferred_element_type=f32)
+
+
+def dot_tn(left, right):
+    return lax.dot_general(left, right, (((0,), (0,)), ((), ())), preferred_element_type=f32)
+
+
+def row_norm(values):
+    centered = values - jnp.mean(values, axis=1, keepdims=True)
+    inv_std = lax.rsqrt(jnp.mean(centered * centered, axis=1, keepdims=True) + eps_norm)
+    return centered * inv_std, inv_std
+
+
+def row_back(grads, normed, inv_std):
+    return inv_std * (
+        grads
+        - jnp.mean(grads, axis=1, keepdims=True)
+        - normed * jnp.mean(grads * normed, axis=1, keepdims=True)
+    )
+
+
+def turn(values, cos_ref, sin_ref, sign):
+    lane = lax.broadcasted_iota(jnp.int32, values.shape, 1) % HEAD_DIM
+    swapped = jnp.where(
+        lane < HEAD_DIM // 2, pltpu.roll(values, 128 - HEAD_DIM // 2, 1), pltpu.roll(values, HEAD_DIM // 2, 1)
+    )
+    return values * cos_ref[...] + sign * (swapped * sin_ref[...])
+
+
+def mod_row(table_ref, s, i):
+    width = table_ref.shape[1] // 7
+    return table_ref[s : s + 1, i * width : (i + 1) * width]
+
+
+EXTRA = 48
+
+
+def split_low(values):
+    high = values.astype(bf16).astype(f32)
+    return high, values - high
+
+
+def extra_rows(mods, gains, s_rows, store):
+    for s in range(s_rows):
+        for part, (mod, gain) in enumerate(zip(split_low(mods[s : s + 1]), split_low(gains[s : s + 1]))):
+            at = (part * s_rows + s) * 4
+            for i in range(3):
+                store(at + i, mod[:, EXTRA * i : EXTRA * (i + 1)])
+            store(at + 3, gain)
+
+
+def pack_kernel(
+    at_ref, x_ref, g_ref, qkv_ref, ada_ref, cond_ref, one_ref, two_ref, up_ref,
+    xc_ref, chunk_ref, p0, p1, p2, p3, ext_ref,
+):
+    u = at_ref[0]
+    n_all, block, cols = chunk_ref.shape
+    xc_ref[0] = x_ref[...]
+    xc_ref[1] = g_ref[...]
+    width = qkv_ref.shape[1] // 3
+    n_u = 4
+    heads = width // n_u // HEAD_DIM
+    ext_ref[...] = jnp.zeros_like(ext_ref)
+    mods = DOT(cond_ref[...], ada_ref[...])
+    gains = jnp.concatenate([one_ref[...], two_ref[...]], axis=0).astype(f32)
+
+    def store(row, value):
+        ext_ref[row : row + 1, : value.shape[1]] = value
+
+    extra_rows(mods, gains, mods.shape[0], store)
+    extra = ext_ref[...].astype(bf16)
+    for i in range(n_u):
+        pieces = []
+        for h in range(heads):
+            at = (i * heads + h) * HEAD_DIM
+            pieces += [qkv_ref[:, at : at + HEAD_DIM], qkv_ref[:, width + at : width + at + HEAD_DIM]]
+        at = 2 * width + i * heads * HEAD_DIM
+        pieces += [qkv_ref[:, at : at + heads * HEAD_DIM], extra]
+        whole = jnp.concatenate(pieces, axis=1)
+        for j in range(n_all // n_u):
+            chunk_ref[i * (n_all // n_u) + j] = whole
+    cols = up_ref.shape[1] // n_u
+    for i, out_ref in enumerate((p0, p1, p2, p3)):
+        out_ref[...] = up_ref[:, pl.ds(pl.multiple_of((u ^ i) * cols, 128), cols)]
+
+
+def first_kernel(at_ref, xg_ref, w_ref, cos_ref, sin_ref, chunk_ref, first_ref, table_ref):
+    u = at_ref[0]
+    n_u, _, seqs, rows, width = xg_ref.shape
+    span = n_u * rows
+    cols = w_ref.shape[1] - HEAD_DIM
+    heads = cols // 192
+    block = width // 32
+    for s in range(seqs):
+        mods, gains = [], []
+        for d in range(32):
+            at = d * block + s * 4
+            pair = w_ref[d * block : (d + 1) * block, cols:].astype(f32)
+            both = pair[s * 4 : s * 4 + 4] + pair[(seqs + s) * 4 : (seqs + s) * 4 + 4]
+            mods += [both[i : i + 1, :EXTRA] for i in range(3)]
+            gains.append(both[3:4, :block])
+        table_ref[s : s + 1, :] = jnp.concatenate(mods + gains, axis=1)
+    gain = mod_row(table_ref, 0, 6)
+    zero = jnp.zeros(chunk_ref.shape[1:], bf16)
+    chunk_ref[0] = zero
+    chunk_ref[chunk_ref.shape[0] - 1] = zero
+    for s in range(seqs):
+        factor = gain * (1.0 + mod_row(table_ref, s, 1))
+        for m in range(n_u):
+            normed, _ = row_norm(xg_ref[u ^ m, 0, s].astype(f32))
+            first = normed * factor + mod_row(table_ref, s, 0)
+            first_ref[s * span + m * rows : s * span + (m + 1) * rows, :] = first.astype(bf16)
+        projected = DOT(first_ref[s * span : (s + 1) * span, :], w_ref[:, :cols])
+        for h in range(heads):
+            pair = 1 + s * heads + h
+            both = turn(projected[:, 128 * h : 128 * (h + 1)], cos_ref, sin_ref, 1.0)
+            chunk_ref[pair, :span, :] = both.astype(bf16)
+            v = projected[:, 128 * heads + 64 * h : 128 * heads + 64 * (h + 1)].astype(bf16)
+            chunk_ref[pair, span:, :] = jnp.concatenate([v[: span // 2], v[span // 2 :]], axis=1)
+
+
+def unpack_tokens(t_ref, s, h, heads):
+    half = t_ref[1 + s * heads + h]
+    return jnp.concatenate([half[:, :HEAD_DIM], half[:, HEAD_DIM:]], axis=0)
+
+
+def store_parts(send_ref, keep_ref, part, s, rows):
+    for m in range(4):
+        block = part[m * rows : (m + 1) * rows]
+        if m % 2:
+            send_ref[m // 2, s] = block.astype(bf16)
+        else:
+            keep_ref[m // 2, s] = block
+
+
+def out_kernel(
+    at_ref, t_ref, a0, a1, a2, a3, a4, a5, a6, a7, att_ref, send_ref, keep_ref, w_ref, wide_ref,
+):
+    _, seqs, rows, _ = send_ref.shape
+    block = a0.shape[0]
+    for i, part_ref in enumerate((a0, a1, a2, a3, a4, a5, a6, a7)):
+        start = pl.multiple_of((at_ref[1] ^ i) * block, 8)
+        wide_ref[pl.ds(start, block), :] = part_ref[...].astype(f32)
+    w_ref[...] = wide_ref[...].astype(bf16)
+    heads = w_ref.shape[0] // HEAD_DIM
+    span = 4 * rows
+    for s in range(seqs):
+        att = jnp.concatenate([unpack_tokens(t_ref, s, h, heads) for h in range(heads)], axis=1)
+        att_ref[s * span : (s + 1) * span, :] = att
+        store_parts(send_ref, keep_ref, DOT(att, w_ref[...]), s, rows)
+
+
+def block_of(own_ref, got_ref, m, s):
+    return (got_ref if m % 2 else own_ref)[m // 2, s].astype(f32)
+
+
+def middle_of(xg_ref, own_ref, got_ref, table_ref, u, m, s):
+    return xg_ref[u ^ m, 0, s].astype(f32) + mod_row(table_ref, s, 2) * block_of(own_ref, got_ref, m, s)
+
+
+def ff_kernel(
+    at_ref, xg_ref, own_ref, got_ref, table_ref, a0, a1, a2, a3, a4, a5, a6, a7,
+    lsend_ref, lkeep_ref, dsend_ref, dkeep_ref, sums_ref, ukeep_ref, usend_ref, wkeep_ref, wsend_ref,
+    second_ref, hidden_ref, low_ref, raised_ref, normed_ref, wide_ref, up_ref, down_ref,
+):
+    u = at_ref[0]
+    n_u, _, seqs, rows, width = xg_ref.shape
+    span = n_u * rows
+    gain = mod_row(table_ref, 1, 6)
+    scale = math.sqrt(2.0 / math.pi)
+    block = width // 32
+    low = n_u * block
+    u, b = at_ref[0], at_ref[1]
+    for i, part_ref in enumerate((a0, a1, a2, a3, a4, a5, a6, a7)):
+        there = b ^ i
+        down_ref[pl.ds(pl.multiple_of(there * low, 32), low), :] = part_ref[low:, :]
+        for j in range(n_u):
+            start = pl.multiple_of(((u ^ j) * 8 + there) * block, 8)
+            wide_ref[pl.ds(start, block), :] = part_ref[j * block : (j + 1) * block, :].astype(f32)
+    up_ref[...] = wide_ref[...].astype(bf16)
+    for s in range(seqs):
+        at = slice(s * span, (s + 1) * span)
+        factor = gain * (1.0 + mod_row(table_ref, s, 4))
+        gate = mod_row(table_ref, s, 5)
+        for m in range(n_u):
+            here = slice(s * span + m * rows, s * span + (m + 1) * rows)
+            normed, _ = row_norm(middle_of(xg_ref, own_ref, got_ref, table_ref, u, m, s))
+            normed_ref[m * rows : (m + 1) * rows, :] = normed
+            second_ref[here, :] = (normed * factor + mod_row(table_ref, s, 3)).astype(bf16)
+            low_ref[here, :] = (gate * xg_ref[u ^ m, 1, s].astype(f32)).astype(bf16)
+        raised = DOT(second_ref[at, :], up_ref[...])
+        d_hidden = dot_nt(low_ref[at, :], down_ref[...])
+        square = raised * raised
+        t = jnp.tanh(scale * raised * (1.0 + 0.044715 * square))
+        hidden_ref[at, :] = (0.5 * raised * (1.0 + t)).astype(bf16)
+        slope = 0.5 * (1.0 + t) + 0.5 * raised * (1.0 - t * t) * (scale * (1.0 + 3.0 * 0.044715 * square))
+        raised_ref[at, :] = (d_hidden * slope).astype(bf16)
+        d_second = dot_nt(raised_ref[at, :], up_ref[...])
+        store_parts(dsend_ref, dkeep_ref, d_second, s, rows)
+        lowered = DOT(hidden_ref[at, :], down_ref[...])
+        store_parts(lsend_ref, lkeep_ref, lowered, s, rows)
+        sums_ref[s, 0:1, :] = jnp.sum(d_second, axis=0, keepdims=True)
+        sums_ref[s, 1:2, :] = jnp.sum(d_second * normed_ref[...], axis=0, keepdims=True)
+        gated = jnp.zeros((1, width), f32)
+        for m in range(n_u):
+            grad = xg_ref[u ^ m, 1, s].astype(f32)
+            gated = gated + jnp.sum(grad * lowered[m * rows : (m + 1) * rows], axis=0, keepdims=True)
+        sums_ref[s, 2:3, :] = gated
+    n_z = ukeep_ref.shape[0]
+    wide_ref[...] = dot_tn(second_ref[...], raised_ref[...])
+    for y, out_ref in enumerate((ukeep_ref, usend_ref)):
+        for z in range(n_z):
+            for i in range(n_u):
+                start = pl.multiple_of(((u ^ i) * 2 * n_z + (b ^ (2 * z + y))) * block, 8)
+                out_ref[z, i] = wide_ref[pl.ds(start, block), :].astype(bf16)
+    wide_ref[...] = dot_tn(hidden_ref[...], low_ref[...])
+    for y, out_ref in enumerate((wkeep_ref, wsend_ref)):
+        for z in range(n_z):
+            for i in range(n_u):
+                start = pl.multiple_of(((b ^ (2 * z + y)) * n_u + i) * block, 8)
+                out_ref[z, i] = wide_ref[pl.ds(start, block), :].astype(bf16)
+
+
+def middle_back_kernel(
+    at_ref, xg_ref, own_ref, got_ref, down_ref, dgot_ref, table_ref, w_ref, att_ref,
+    chunk_ref, dmid_ref, gate_ref, okeep_ref, osend_ref, branch_ref, outs_ref,
+):
+    u = at_ref[0]
+    n_u, _, seqs, rows, width = xg_ref.shape
+    span = n_u * rows
+    heads = w_ref.shape[0] // HEAD_DIM
+    gain = mod_row(table_ref, 1, 6)
+    zero = jnp.zeros(chunk_ref.shape[1:], bf16)
+    chunk_ref[0] = zero
+    chunk_ref[chunk_ref.shape[0] - 1] = zero
+    for s in range(seqs):
+        at = slice(s * span, (s + 1) * span)
+        factor = gain * (1.0 + mod_row(table_ref, s, 4))
+        gate = mod_row(table_ref, s, 2)
+        for m in range(n_u):
+            normed, inv_std = row_norm(middle_of(xg_ref, own_ref, got_ref, table_ref, u, m, s))
+            grads = block_of(down_ref, dgot_ref, m, s) * factor
+            d_middle = xg_ref[u ^ m, 1, s].astype(f32) + row_back(grads, normed, inv_std)
+            branch_ref[s * span + m * rows : s * span + (m + 1) * rows, :] = (gate * d_middle).astype(bf16)
+            if m == 0:
+                dmid_ref[s] = d_middle
+                gate_ref[s] = jnp.sum(d_middle * own_ref[0, s].astype(f32), axis=0, keepdims=True)
+        d_att = dot_nt(branch_ref[at, :], w_ref[...]).astype(bf16)
+        for h in range(heads):
+            d = d_att[:, HEAD_DIM * h : HEAD_DIM * (h + 1)]
+            chunk_ref[1 + s * heads + h] = jnp.concatenate([d[: span // 2], d[span // 2 :]], axis=1)
+    n_z, block, _ = okeep_ref.shape
+    outs_ref[...] = dot_tn(att_ref[...], branch_ref[...])
+    for y, out_ref in enumerate((okeep_ref, osend_ref)):
+        for z in range(n_z):
+            start = pl.multiple_of((at_ref[1] ^ (2 * z + y)) * block, 8)
+            out_ref[z] = outs_ref[pl.ds(start, block), :].astype(bf16)
+
+
+def first_back_kernel(
+    at_ref, t_ref, xg_ref, table_ref, cos_ref, sin_ref, w_ref, first_ref, gate_ref, two_ref,
+    send_ref, keep_ref, blocks_ref, proj_ref, normed_ref, sums_ref, ext_ref,
+):
+    u = at_ref[0]
+    n_u, _, seqs, rows, width = xg_ref.shape
+    span = n_u * rows
+    cols = w_ref.shape[1] - HEAD_DIM
+    heads = cols // 192
+    gain_grads = [jnp.zeros((1, width), f32)] * 2
+    total, block, _ = blocks_ref.shape
+    for s in range(seqs):
+        at = slice(s * span, (s + 1) * span)
+        for h in range(heads):
+            pair = t_ref[1 + s * heads + h]
+            both = turn(pair[:span].astype(f32), cos_ref, sin_ref, -1.0)
+            proj_ref[at, 128 * h : 128 * (h + 1)] = both.astype(bf16)
+            v = pair[span:]
+            proj_ref[at, 128 * heads + 64 * h : 128 * heads + 64 * (h + 1)] = jnp.concatenate(
+                [v[:, :HEAD_DIM], v[:, HEAD_DIM:]], axis=0
+            )
+        d_first = dot_nt(proj_ref[at, :], w_ref[:, :cols])
+        store_parts(send_ref, keep_ref, d_first, s, rows)
+        for m in range(n_u):
+            normed, _ = row_norm(xg_ref[u ^ m, 0, s].astype(f32))
+            normed_ref[m * rows : (m + 1) * rows, :] = normed
+        dots = [jnp.sum(d_first * normed_ref[...], axis=0, keepdims=True), two_ref[s, 1:2, :]]
+        for i in range(2):
+            gain_grads[i] = gain_grads[i] + dots[i] * (1.0 + mod_row(table_ref, s, 1 + 3 * i))
+        rows_out = [
+            jnp.sum(d_first, axis=0, keepdims=True),
+            dots[0] * mod_row(table_ref, 0, 6),
+            gate_ref[s],
+            two_ref[s, 0:1, :],
+            dots[1] * mod_row(table_ref, 1, 6),
+            two_ref[s, 2:3, :],
+        ]
+        for i, row in enumerate(rows_out):
+            sums_ref[s : s + 1, i * width : (i + 1) * width] = row
+    for i in range(2):
+        sums_ref[i : i + 1, 6 * width :] = gain_grads[i]
+    ext_ref[...] = jnp.zeros_like(ext_ref)
+    for d in range(total):
+
+        def store(row, value):
+            ext_ref[d * block + row : d * block + row + 1, : value.shape[1]] = value
+
+        mods = sums_ref[:, 3 * EXTRA * d : 3 * EXTRA * (d + 1)]
+        extra_rows(mods, sums_ref[:, 6 * width + block * d : 6 * width + block * (d + 1)], seqs, store)
+    grads = dot_tn(first_ref[...], proj_ref[...])
+    for i in range(total):
+        at = slice(i * block, (i + 1) * block)
+        blocks_ref[i, :, :cols] = grads[at].astype(bf16)
+        blocks_ref[i, :, cols:] = ext_ref[at].astype(bf16)
+
+
+def row_grad_kernel(at_ref, raw_ref, p0, p1, p2, p3, ada_ref, cond_ref, qkv_ref, up_ref, part_ref, adag_ref, gain_ref, mod_ref):
+    u = at_ref[0]
+    total, block, cols = raw_ref.shape
+    cols = cols - HEAD_DIM
+    n_u = 4
+    n_b = total // n_u
+    heads = cols // 192
+    width = qkv_ref.shape[1] // 3
+    seqs = mod_ref.shape[0]
+    extra = jnp.zeros((block, HEAD_DIM), f32)
+    for i in range(n_u):
+        part = raw_ref[i * n_b].astype(f32)
+        for j in range(1, n_b):
+            part = part + raw_ref[i * n_b + j].astype(f32)
+        extra = extra + part[:, cols:]
+        for h in range(heads):
+            to = (i * heads + h) * HEAD_DIM
+            qkv_ref[:, to : to + HEAD_DIM] = part[:, 128 * h : 128 * h + HEAD_DIM]
+            qkv_ref[:, width + to : width + to + HEAD_DIM] = part[:, 128 * h + HEAD_DIM : 128 * (h + 1)]
+        at = i * heads * HEAD_DIM
+        qkv_ref[:, 2 * width + at : 2 * width + at + heads * HEAD_DIM] = part[:, 128 * heads : cols]
+    for s in range(seqs):
+        both = extra[s * 4 : s * 4 + 4] + extra[(seqs + s) * 4 : (seqs + s) * 4 + 4]
+        mod_ref[s : s + 1, :] = jnp.concatenate([both[i : i + 1, :EXTRA] for i in range(3)], axis=1)
+        gain_ref[s : s + 1, :] = both[3:4, :block]
+    mods = mod_ref[...].astype(bf16)
+    grads = dot_nt(mods, ada_ref[...])
+    for i in range(total):
+        part_ref[i] = grads
+    adag_ref[...] = dot_tn(cond_ref[...], mods)
+    cols = up_ref.shape[1] // n_u
+    for i, piece_ref in enumerate((p0, p1, p2, p3)):
+        up_ref[:, pl.ds(pl.multiple_of((u ^ i) * cols, 128), cols)] = piece_ref[...]
+
+
+def input_grad_kernel(x_ref, near_ref, got_ref, dmid_ref, table_ref, out_ref):
+    seqs = x_ref.shape[0]
+    for s in range(seqs):
+        factor = mod_row(table_ref, 0, 6) * (1.0 + mod_row(table_ref, s, 1))
+        normed, inv_std = row_norm(x_ref[s].astype(f32))
+        grads = (near_ref[s] + got_ref[s].astype(f32)) * factor
+        out_ref[s] = dmid_ref[s] + row_back(grads, normed, inv_std)
+
+
+def call(kernel, name, outs, scratch, flops, *args, limit=16, staged=()):
+    count = len(args)
+    specs = [
+        pl.BlockSpec(
+            memory_space=pltpu.SMEM if a.dtype == jnp.int32 else pltpu.HBM if i in staged else pltpu.VMEM
+        )
+        for i, a in enumerate(args)
+    ]
+    size = sum(math.prod(a.shape) * a.dtype.itemsize for a in args)
+    size += sum(math.prod(shape) * jnp.dtype(dtype).itemsize for shape, dtype in outs)
+    shapes = [pltpu.VMEM(*s) for s in scratch]
+    body = kernel
+    if staged:
+        shapes = [pltpu.VMEM(args[i].shape, args[i].dtype) for i in staged] + [
+            pltpu.SemaphoreType.DMA((len(staged),))
+        ] + shapes
+
+        def body(*refs):
+            ins, rest = list(refs[:count]), refs[count:]
+            out_refs, held = rest[: len(outs)], rest[len(outs) :]
+            sems = held[len(staged)]
+            copies = []
+            for j, i in enumerate(staged):
+                copies.append(pltpu.make_async_copy(ins[i], held[j], sems.at[j]))
+                ins[i] = held[j]
+            for copy in copies:
+                copy.start()
+            for copy in copies:
+                copy.wait()
+            kernel(*ins, *out_refs, *held[len(staged) + 1 :])
+
+    return pl.pallas_call(
+        body,
+        out_shape=tuple(jax.ShapeDtypeStruct(shape, dtype) for shape, dtype in outs),
+        in_specs=specs,
+        out_specs=tuple(pl.BlockSpec(memory_space=pltpu.VMEM) for _ in outs),
+        scratch_shapes=shapes,
+        cost_estimate=pl.CostEstimate(flops=int(flops), bytes_accessed=int(size), transcendentals=0),
+        compiler_params=pltpu.CompilerParams(vmem_limit_bytes=limit << 20),
+        name=name,
+    )(*args)
+
+
+def fits_tp(mesh):
+    ulysses, blk = mesh.shape["ulysses"], mesh.shape["blk"]
+    return ulysses == 4 and blk == 8 and HEADS % ulysses == 0
+
+
+def swap_u(values, mask):
+    return lax.ppermute(values, "ulysses", [(i, i ^ mask) for i in range(4)])
+
+
+def swap_b(values, mask):
+    return lax.ppermute(values, "blk", [(i, i ^ mask) for i in range(8)])
+
+
+def exchange(blocks, axis):
+    return lax.all_to_all(blocks, axis, split_axis=0, concat_axis=0, tiled=True)
+
+
+def half_sum(send, keep):
+    return keep + swap_u(send, 1).astype(f32)
+
+
+def along_z(values):
+    return [values] + [swap_b(values, 2 * m) for m in (1, 2, 3)]
+
+
+def along_y(parts):
+    out = []
+    for part in parts:
+        out += [part, swap_b(part, 1)]
+    return out
+
+
+def sum_z(half):
+    total = half[0]
+    for m in (1, 2, 3):
+        total = total + swap_b(half[m].astype(bf16), 2 * m).astype(f32)
+    return total
+
+
+def tp_shards(inputs, conditioning, w_ada, w_qkv, w_out, w_up, w_down, gain_one, gain_two, cotangent):
+    n_u, n_b = 4, 8
+    n_all = n_u * n_b
+    everywhere = ("ulysses", "blk")
+    seqs, rows, width = inputs.shape
+    u = lax.axis_index("ulysses")
+    b = lax.axis_index("blk")
+    at = jnp.stack([u, b]).astype(jnp.int32)
+    heads = HEADS // n_u
+    head_width = heads * HEAD_DIM
+    cols = 3 * head_width
+    w_rows, down_rows = w_qkv.shape[0], w_down.shape[0]
+    ff_local = w_up.shape[1] // n_u
+    span = n_u * rows
+    tokens = seqs * span
+
+    packed = call(
+        pack_kernel, "pack",
+        [((2,) + inputs.shape, bf16), ((n_all, w_rows, cols + HEAD_DIM), bf16)] + [((w_rows, ff_local), bf16)] * n_u,
+        [((w_rows, HEAD_DIM), f32)], 0,
+        at, inputs, cotangent, w_qkv, w_ada, conditioning, gain_one[None], gain_two[None], w_up,
+        limit=60,
+    )
+    ff_near = jnp.concatenate([packed[2]] + [swap_u(packed[2 + m], m) for m in (1, 2, 3)] + [w_down], axis=0)
+    raw = exchange(packed[1], everywhere)
+    xg = lax.all_gather(packed[0], "ulysses", axis=0, tiled=False)
+    out_zy = along_y(along_z(w_out))
+    raw, xg, ff_near, out_zy = lax.optimization_barrier((raw, xg, ff_near, out_zy))
+    w_qkv_u = raw.reshape(width, cols + HEAD_DIM)
+
+    blocks = u ^ jnp.arange(n_u, dtype=jnp.int32)
+    positions = ((blocks * n_b + b) * rows)[:, None] + jnp.arange(rows, dtype=jnp.int32)[None, :]
+    cos_table, sin_table = rotary_tables(positions.reshape(-1).astype(f32))
+    cos_table, sin_table = cos_table[:, 0], sin_table[:, 0]
+    cos_table = jnp.concatenate([cos_table] * 4, axis=1)
+    sin_table = jnp.concatenate([-sin_table, sin_table] * 2, axis=1)
+
+    chunks, first_in, table = call(
+        first_kernel, "first",
+        [((n_b, 3 * span // 2, 128), bf16), ((tokens, width), bf16), ((seqs, 7 * width), f32)], [],
+        2 * tokens * width * cols,
+        at, xg, w_qkv_u, cos_table, sin_table,
+    )
+    owned = exchange(chunks, "blk")
+    owned, ff_near = lax.optimization_barrier((owned, ff_near))
+    ff_0y, ff_2 = swap_b(ff_near, 1), swap_b(ff_near, 4)
+    attn_low, attn_full, log_total = attn_fwd(owned)
+    part_shape = (2, seqs, rows, width)
+    attn_low, ff_0y, ff_2, ff_near = lax.optimization_barrier((attn_low, ff_0y, ff_2, ff_near))
+    attn_tokens = exchange(attn_low, "blk")
+    ff_1, ff_3, ff_2y = swap_b(ff_near, 2), swap_b(ff_near, 6), swap_b(ff_2, 1)
+    attn_tokens, ff_1, ff_3, ff_2y = lax.optimization_barrier((attn_tokens, ff_1, ff_3, ff_2y))
+    attended, send, keep, w_out_u = call(
+        out_kernel, "out",
+        [((tokens, head_width), bf16), (part_shape, bf16), (part_shape, f32), ((head_width, width), bf16)],
+        [((head_width, width), f32)],
+        2 * tokens * width * head_width,
+        at, attn_tokens, *out_zy,
+    )
+
+    half = half_sum(send, keep)
+    across = swap_u(half.astype(bf16), 2)
+    ff_zy = [ff_near, ff_0y, ff_1, swap_b(ff_1, 1), ff_2, ff_2y, ff_3, swap_b(ff_3, 1)]
+    across, ff_zy = lax.optimization_barrier((across, ff_zy))
+    own = (half + across[::-1].astype(f32)).astype(bf16)
+    got = swap_u(own, 1)
+    lsend, lkeep, dsend, dkeep, sums_two, up_keep, up_send, down_keep, down_send = call(
+        ff_kernel, "ff",
+        [(part_shape, bf16), (part_shape, f32), (part_shape, bf16), (part_shape, f32), ((seqs, 3, width), f32)]
+        + [((n_b // 2, n_u, w_rows, width), bf16)] * 4,
+        [((tokens, width), bf16), ((tokens, ff_local), bf16), ((tokens, width), bf16), ((tokens, ff_local), bf16),
+         ((span, width), f32), ((width, ff_local), f32), ((width, ff_local), bf16), ((ff_local, width), bf16)],
+        12 * tokens * width * ff_local,
+        at, xg, own, got, table, *ff_zy,
+        limit=28,
+    )
+    up_other, down_other = swap_b(up_send, 1), swap_b(down_send, 1)
+    half = half_sum(dsend, dkeep)
+    across = swap_u(half.astype(bf16), 2)
+    d_own = (half + across[::-1].astype(f32)).astype(bf16)
+    d_got = swap_u(d_own, 1)
+    d_chunks, d_middle, sum_gate, out_keep, out_send = call(
+        middle_back_kernel, "middle_back",
+        [((n_b, span // 2, 128), bf16), ((seqs, rows, width), f32), ((seqs, 1, width), f32)]
+        + [((n_b // 2, w_rows, width), bf16)] * 2,
+        [((tokens, width), bf16), ((head_width, width), f32)],
+        4 * tokens * width * head_width,
+        at, xg, own, got, d_own, d_got, table, w_out_u, attended,
+        limit=60,
+    )
+    d_chunks, up_other = lax.optimization_barrier((d_chunks, up_other))
+    d_attn = exchange(d_chunks, "blk")
+    up_sum = sum_z(up_keep.astype(f32) + up_other.astype(f32))
+    out_other = swap_b(out_send, 1)
+    d_attn, up_sum, down_other, out_other = lax.optimization_barrier((d_attn, up_sum, down_other, out_other))
+    down_sum = sum_z(
+        jnp.concatenate(
+            [down_keep.astype(f32) + down_other.astype(f32), (out_keep.astype(f32) + out_other.astype(f32))[:, None]],
+            axis=1,
+        )
+    )
+    d_owned = attn_bwd(owned, d_attn, attn_full, log_total)
+    lhalf = half_sum(lsend, lkeep)
+    lowered = lhalf[0] + swap_u(lhalf[1].astype(bf16), 2).astype(f32)
+    gates = table.reshape(2, 7, 1, width)
+    output = inputs.astype(f32) + gates[:, 2] * own[0].astype(f32) + gates[:, 5] * lowered
+    d_owned, output, down_sum = lax.optimization_barrier((d_owned, output, down_sum))
+    up_parts = [up_sum[0]] + [swap_u(up_sum[m], m) for m in (1, 2, 3)]
+    d_tokens = exchange(d_owned, "blk")
+    d_tokens, up_parts = lax.optimization_barrier((d_tokens, up_parts))
+
+    send, keep, qkv_blocks = call(
+        first_back_kernel, "first_back",
+        [(part_shape, bf16), (part_shape, f32), ((n_all, w_rows, cols + HEAD_DIM), bf16)],
+        [((tokens, cols), bf16), ((span, width), f32), ((seqs, 7 * width), f32), ((width, HEAD_DIM), f32)],
+        4 * tokens * width * cols,
+        at, d_tokens, xg, table, cos_table, sin_table, w_qkv_u, first_in, sum_gate, sums_two,
+        limit=60,
+    )
+    half = half_sum(send, keep)
+    far = swap_u(half[1].astype(bf16), 2)
+    inputs_grad, = call(
+        input_grad_kernel, "input_grad",
+        [((seqs, rows, width), f32)], [], 0,
+        inputs, half[0], far, d_middle, table,
+    )
+    qkv_grad, up_grad, cond_part, ada_grad, gain_grads, _ = call(
+        row_grad_kernel, "row_grad",
+        [(w_qkv.shape, f32), (w_up.shape, f32), ((n_all,) + conditioning.shape, f32), (w_ada.shape, f32),
+         ((2, w_rows), f32), ((seqs, w_ada.shape[1]), f32)],
+        [], 0,
+        at, exchange(qkv_blocks, everywhere), *up_parts, w_ada, conditioning,
+        limit=60,
+    )
+    conditioning_grad = jnp.sum(exchange(cond_part, everywhere), axis=0)
+    return (
+        output,
+        inputs_grad,
+        conditioning_grad,
+        ada_grad,
+        qkv_grad,
+        down_sum[n_u],
+        up_grad,
+        down_sum[:n_u].reshape(w_down.shape),
+        gain_grads[0],
+        gain_grads[1],
+    )
+
+
 def solution(mesh):
+    body = tp_shards if fits_tp(mesh) else shards
     in_specs = (
         P(None, ("ulysses", "blk"), None),
         P(),
@@ -375,4 +1060,4 @@
         P(("ulysses", "blk")),
         P(("ulysses", "blk")),
     )
-    return jax.shard_map(shards, mesh=mesh, in_specs=in_specs, out_specs=out_specs, check_vma=False)
+    return jax.shard_map(body, mesh=mesh, in_specs=in_specs, out_specs=out_specs, check_vma=False)

time: 1270 us -> 306 us (0.24); the launches traced: 1250 us -> 305 us
  waiting for transfers between devices: 778 us -> 120 us
  local copies, waits for them, and re-layouts: 193 us -> 22.9 us
  matrix products: 95.7 us -> 0 us
  blocking collectives: 104 us -> 21.2 us
  Pallas kernels: 0 us -> 48.3 us
  starting transfers between devices: 22.3 us -> 65.6 us
  other arithmetic: 41.2 us -> 12.1 us
    reduce_scatter x6 -> x0, waiting for transfers between devices: 476 us -> none  [the longest x1 142 us: shards(): lax.psum_scatter(terms[2], ('ulysses', 'blk'), scatter_dimension=0, tiled...]
    all_gather x7 -> x1, waiting for transfers between devices: 280 us -> 0.01 us  [tp_shards(): xg = lax.all_gather(packed[0], 'ulysses', axis=0, tiled=False)]
    dynamic_update_slice x8 -> x0, local copies, waits for them, and re-layouts: 117 us -> none  [shards(): lax.scan(back_step, query_zero, split_blocks(all_pairs, query_rows))]
    dot_general x56 -> x0, matrix products: 95.7 us -> none  [the longest x4 11.9 us: back_step(): jnp.einsum('shqd,skhd->shqk', d_attn_heads, values, preferred_element_typ...]
    ppermute x0 -> x39, waiting for transfers between devices: none -> 89.2 us  [the longest x23 55 us: swap_b(): return lax.ppermute(values, 'blk', [(i, i ^ mask) for i in range(8)])]
    pallas_call x0 -> x10, Pallas kernels: none -> 48.3 us  [the longest x8 26 us: call(): pl.pallas_call(body, out_shape=tuple((jax.ShapeDtypeStruct(shape, dtype)...]
    psum x1 -> x0, blocking collectives: 43.9 us -> none  [shards(): mod_total = lax.psum(mod_local, ('ulysses', 'blk'))]
    ppermute x0 -> x39, starting transfers between devices: none -> 42.1 us  [the longest x23 33.1 us: swap_b(): return lax.ppermute(values, 'blk', [(i, i ^ mask) for i in range(8)])]
  transfers between devices with their start and end apart: 19 -> 46, of which waited for: 16 -> 24; matrix products, arithmetic and copies ran while one was open for 16% -> 5% of each run, Pallas kernels for 0% -> 9%
where the time goes in v1:
time: 306 us; the launch traced here: 305 us
  waiting for transfers between devices  120 us (39%)
  starting transfers between devices  65.6 us (21%)
  Pallas kernels  48.3 us (16%)
  local copies, waits for them, and re-layouts  22.9 us (7%)
  blocking collectives  21.2 us (7%)
  between operations  14.7 us (5%)
  other arithmetic  12.1 us (4%)
    ppermute x23, waiting for transfers between devices, swap_b(): return lax.ppermute(values, 'blk', [(i, i ^ mask) for i in range(8)])  55 us
    ppermute x16, waiting for transfers between devices, swap_u(): return lax.ppermute(values, 'ulysses', [(i, i ^ mask) for i in range(4)])  34.1 us
    ppermute x23, starting transfers between devices, swap_b(): return lax.ppermute(values, 'blk', [(i, i ^ mask) for i in range(8)])  33.1 us
    all_to_all x6, waiting for transfers between devices, exchange(): return lax.all_to_all(blocks, axis, split_axis=0, concat_axis=0, tiled=True)  30.7 us
    pallas_call x8, Pallas kernels, call(): pl.pallas_call(body, out_shape=tuple((jax.ShapeDtypeStruct(shape, dtype)...  26 us
    all_to_all x6, starting transfers between devices, exchange(): return lax.all_to_all(blocks, axis, split_axis=0, concat_axis=0, tiled=True)  23.5 us
    all_to_all x1, blocking collectives, exchange(): return lax.all_to_all(blocks, axis, split_axis=0, concat_axis=0, tiled=True)  21.2 us
    unnamed x130, local copies, waits for them, and re-layouts  18.6 us
  transfers between devices with their start and end apart: 46, of which 24 were waited for; matrix products, arithmetic and copies ran while one was open for 5% of the time, Pallas kernels for 9%

profile of v1, /device:TPU:0, one launch (start us, length us, event | category | flops | bytes accessed | tf_op | source)
XLA Modules:
  0.0 304.7 jit_solution(4890183450394813745)
XLA Ops:
  7.2 1.5 copy.34.ada_ref
  9.3 2.6 pack.1
  12.1 7.3 %all-to-all-start = ((bf16[32,24,640]{2,1,0:T(8,128)(2,1)}), bf16[32,24,640]{2,1,0:T(8,128)(2,1)S(1)}, u32[]{:S(2)}, u32[]{:S(2)}) async-start(bf16[32,24,640]{2,1,0:T(8,128)(2,1)} %get-tuple-element.92), calls=%async_computation | async-start | bytes 1966080 | tf_op jit(solution)/shard_map/all_to_all | solution.py:863
  19.4 1.8 collective-permute-start.4
  21.2 2.4 collective-permute-start.6
  23.8 1.8 collective-permute-start.3
  26.8 1.5 collective-permute-start.1
  28.3 4.4 %collective-permute-done.1 = bf16[24,768]{1,0:T(8,128)(2,1)S(1)} collective-permute-done((bf16[24,768]{1,0:T(8,128)(2,1)S(1)}, bf16[24,768]{1,0:T(8,128)(2,1)S(1)}, u32[]{:S(2)}, u32[]{:S(2)}) %collective-permute-start.1) | collective-permute-done | bytes 36896 | tf_op jit(solution)/shard_map/ppermute | solution.py:855
  33.5 3.5 %collective-permute-done.4.a2 = bf16[24,768]{1,0:T(8,128)(2,1)S(1)} collective-permute-done((bf16[24,768]{1,0:T(8,128)(2,1)S(1)}, bf16[24,768]{1,0:T(8,128)(2,1)S(1)}, u32[]{:S(2)}, u32[]{:S(2)}) %collective-permute-start.4) | collective-permute-done | bytes 36896 | tf_op jit(solution)/shard_map/ppermute | solution.py:859
  37.0 1.9 collective-permute-start.5
  38.9 8.1 %collective-permute-done.6.a4 = bf16[24,768]{1,0:T(8,128)(2,1)S(1)} collective-permute-done((bf16[24,768]{1,0:T(8,128)(2,1)S(1)}, bf16[24,768]{1,0:T(8,128)(2,1)S(1)}, u32[]{:S(2)}, u32[]{:S(2)}) %collective-permute-start.6) | collective-permute-done | bytes 36896 | tf_op jit(solution)/shard_map/ppermute | solution.py:859
  47.0 1.5 collective-permute-start.7
  49.1 1.9 collective-permute-done.7.a5
  50.9 1.5 collective-permute-done.9.a7
  52.4 1.8 copy-done
  54.2 1.9 first.1
  57.1 21.2 %all_to_all.35.x_ref = bf16[8,384,128]{2,1,0:T(8,128)(2,1)S(1)} all-to-all(bf16[8,384,128]{2,1,0:T(8,128)(2,1)S(1)} %get-tuple-element.100), channel_id=1, replica_groups=mesh['ulysses'=4,'blk'=8] {'blk'}, dimensions={0} | all-to-all | bytes 1572864 | tf_op jit(solution)/shard_map/all_to_all | solution.py:863
  78.2 1.5 collective-permute-start.10
  79.7 8.5 %attn_fwd.1 = (bf16[8,128,128]{2,1,0:T(8,128)(2,1)}, f32[8,128,128]{2,1,0:T(8,128)S(1)}, f32[8,8,256]{2,1,0:T(8,128)S(1)}) custom-call(bf16[8,384,128]{2,1,0:T(8,128)(2,1)S(1)} %all_to_all.35.x_ref), custom_call_target="tpu_custom_call" | custom-call | flops 1073741824 | bytes 2097152 | tf_op jit(solution)/shard_map/attn_fwd/pallas_call | solution.py:42
  89.8 3.9 %collective-permute-done.11.a4 = bf16[192,768]{1,0:T(8,128)(2,1)S(1)} collective-permute-done((bf16[192,768]{1,0:T(8,128)(2,1)S(1)}, bf16[192,768]{1,0:T(8,128)(2,1)S(1)}, u32[]{:S(2)}, u32[]{:S(2)}) %collective-permute-start.11) | collective-permute-done | bytes 294944 | tf_op jit(solution)/shard_map/ppermute | solution.py:859
  93.7 3.6 %all-to-all-start.2 = ((bf16[8,128,128]{2,1,0:T(8,128)(2,1)}), bf16[8,128,128]{2,1,0:T(8,128)(2,1)S(1)}, u32[]{:S(2)}, u32[]{:S(2)}) async-start(bf16[8,128,128]{2,1,0:T(8,128)(2,1)} %get-tuple-element.105), calls=%async_computation.2 | async-start | bytes 524288 | tf_op jit(solution)/shard_map/all_to_all | solution.py:863
  97.3 2.0 collective-permute-start.12
  99.3 2.4 collective-permute-start.13
  101.7 1.5 collective-permute-start.14
  103.1 7.2 %collective-permute-done.12.a2 = bf16[192,768]{1,0:T(8,128)(2,1)S(1)} collective-permute-done((bf16[192,768]{1,0:T(8,128)(2,1)S(1)}, bf16[192,768]{1,0:T(8,128)(2,1)S(1)}, u32[]{:S(2)}, u32[]{:S(2)}) %collective-permute-start.12) | collective-permute-done | bytes 294944 | tf_op jit(solution)/shard_map/ppermute | solution.py:859
  110.3 8.2 %collective-permute-done.13.a6 = bf16[192,768]{1,0:T(8,128)(2,1)S(1)} collective-permute-done((bf16[192,768]{1,0:T(8,128)(2,1)S(1)}, bf16[192,768]{1,0:T(8,128)(2,1)S(1)}, u32[]{:S(2)}, u32[]{:S(2)}) %collective-permute-start.13) | collective-permute-done | bytes 294944 | tf_op jit(solution)/shard_map/ppermute | solution.py:859
  120.4 1.7 collective-permute-done.15
  122.3 2.0 collective-permute-start.16
  124.3 1.5 collective-permute-start.17
  126.3 7.9 %collective-permute-done.17.a3 = bf16[192,768]{1,0:T(8,128)(2,1)S(1)} collective-permute-done((bf16[192,768]{1,0:T(8,128)(2,1)S(1)}, bf16[192,768]{1,0:T(8,128)(2,1)S(1)}, u32[]{:S(2)}, u32[]{:S(2)}) %collective-permute-start.17) | collective-permute-done | bytes 294944 | tf_op jit(solution)/shard_map/ppermute | solution.py:859
  134.1 5.2 %collective-permute-done.18.a7 = bf16[192,768]{1,0:T(8,128)(2,1)S(1)} collective-permute-done((bf16[192,768]{1,0:T(8,128)(2,1)S(1)}, bf16[192,768]{1,0:T(8,128)(2,1)S(1)}, u32[]{:S(2)}, u32[]{:S(2)}) %collective-permute-start.18) | collective-permute-done | bytes 294944 | tf_op jit(solution)/shard_map/ppermute | solution.py:859
  139.6 1.7 collective-permute-done.19.got_ref
  144.4 6.7 %ff.1 = (bf16[2,2,64,768]{3,2,1,0:T(8,128)(2,1)S(1)}, f32[2,2,64,768]{3,2,1,0:T(8,128)S(1)}, bf16[2,2,64,768]{3,2,1,0:T(8,128)(2,1)S(1)}, f32[2,2,64,768]{3,2,1,...) custom-call(s32[2]{0:T(128)S(1)} %copy-done.28, ...), custom_call_target="tpu_custom_call" | custom-call | flops 3623878656 | bytes 9498632 | tf_op jit(solution)/shard_map/ff/pallas_call | solution.py:837
  155.9 1.7 collective-permute-done.20
  157.6 1.8 fusion.2
  159.8 1.5 collective-permute-start.23
  161.4 9.5 %collective-permute-done.21 = bf16[2,2,64,768]{3,2,1,0:T(8,128)(2,1)} collective-permute-done((bf16[2,2,64,768]{3,2,1,0:T(8,128)(2,1)}, bf16[2,2,64,768]{3,2,1,0:T(8,128)(2,1)}, u32[]{:S(2)}, u32[]{:S(2)}) %collective-permute-start.21) | collective-permute-done | bytes 393248 | tf_op jit(solution)/shard_map/ppermute | solution.py:855
  170.9 1.2 add_convert_fusion.down_ref
  172.3 1.5 collective-permute-start.27
  174.7 4.4 %middle_back.1 = (bf16[8,128,128]{2,1,0:T(8,128)(2,1)}, f32[2,64,768]{2,1,0:T(8,128)}, f32[2,1,768]{2,1,0:T(1,128)}, bf16[4,24,768]{2,1,0:T(8,128)(2,1)}, bf16[4,24,768]{2,1,0:T(8,128)(2,1)}) custom-call(s32[2]{0:T(128)} %pad_add_fusion.at_ref, bf16[4,2,2,64,768]{4,3,2,1,0:T(8,128)(2,1)} %bitcast.78, bf16[2,2,64,768]{3,2,1,0:T(8,128)(2,1)} %copy-done.3, ...), custom_call_target="tpu_custom_call" | custom-call | flops 301989888 | bytes 4636680 | tf_op jit(solution)/shard_map/middle_back/pallas_call | solution.py:837
  179.1 2.2 fusion.18
  183.1 3.3 %collective-permute-start.26 = (bf16[4,24,768]{2,1,0:T(8,128)(2,1)S(1)}, bf16[4,24,768]{2,1,0:T(8,128)(2,1)}, u32[]{:S(2)}, u32[]{:S(2)}) collective-permute-start(bf16[4,24,768]{2,1,0:T(8,128)(2,1)S(1)} %get-tuple-element.220), channel_id=1, source_target_pairs={{0,6},{1,7},{2,4},{3,5},{4,2},{5,3},{6,0},{7,1},{8,14},{9,15},{10,... | collective-permute-start | bytes 442376 | tf_op jit(solution)/shard_map/ppermute | solution.py:859
  186.5 3.6 %all-to-all-start.3 = ((bf16[8,128,128]{2,1,0:T(8,128)(2,1)}), bf16[8,128,128]{2,1,0:T(8,128)(2,1)S(1)}, u32[]{:S(2)}, u32[]{:S(2)}) async-start(bf16[8,128,128]{2,1,0:T(8,128)(2,1)} %get-tuple-element.139), calls=%async_computation.3 | async-start | bytes 524288 | tf_op jit(solution)/shard_map/all_to_all | solution.py:863
  190.6 1.7 collective-permute-start.28
  192.2 7.7 %collective-permute-done.25 = bf16[4,24,768]{2,1,0:T(8,128)(2,1)} collective-permute-done((bf16[4,24,768]{2,1,0:T(8,128)(2,1)S(1)}, bf16[4,24,768]{2,1,0:T(8,128)(2,1)}, u32[]{:S(2)}, u32[]{:S(2)}) %collective-permute-start.25) | collective-permute-done | bytes 147488 | tf_op jit(solution)/shard_map/ppermute | solution.py:859
  199.9 1.2 fusion.14
  201.2 3.6 %all-to-all-done.3.d_ref = bf16[8,128,128]{2,1,0:T(8,128)(2,1)S(1)} async-done(((bf16[8,128,128]{2,1,0:T(8,128)(2,1)}), bf16[8,128,128]{2,1,0:T(8,128)(2,1)S(1)}, u32[]{:S(2)}, u32[]{:S(2)}) %all-to-all-start.3) | async-done | bytes 262176 | tf_op jit(solution)/shard_map/all_to_all | solution.py:863
  205.7 1.2 convert_add_fusion
  209.2 2.4 collective-permute-start.33
  212.4 13.8 %attn_bwd.1 = bf16[8,384,128]{2,1,0:T(8,128)(2,1)} custom-call(bf16[8,384,128]{2,1,0:T(8,128)(2,1)S(1)} %all_to_all.35.x_ref, bf16[8,128,128]{2,1,0:T(8,128)(2,1)S(1)} %all-to-all-done.3.d_ref, f32[8,128,128]{2,1,0:T(8,128)S(1)} %copy-done.20, f32[8,8,256]{2,1,0:T(8,128)S(1)} %copy-done.26), custom_call_target="tpu_custom_call" | custom-call | flops 268435456 | bytes 262144 | tf_op jit(solution)/shard_map/attn_bwd/pallas_call | solution.py:91
  226.3 3.6 %all-to-all-start.4 = ((bf16[8,384,128]{2,1,0:T(8,128)(2,1)}), bf16[8,384,128]{2,1,0:T(8,128)(2,1)S(1)}, u32[]{:S(2)}, u32[]{:S(2)}) async-start(bf16[8,384,128]{2,1,0:T(8,128)(2,1)} %attn_bwd.1), calls=%async_computation.4 | async-start | bytes 1572864 | tf_op jit(solution)/shard_map/all_to_all | solution.py:863
  230.9 1.5 collective-permute-start.36
  232.4 3.2 %collective-permute-done.35.p2 = f32[24,768]{1,0:T(8,128)S(1)} collective-permute-done((f32[24,768]{1,0:T(8,128)S(1)}, f32[24,768]{1,0:T(8,128)S(1)}, u32[]{:S(2)}, u32[]{:S(2)}) %collective-permute-start.35) | collective-permute-done | bytes 73760 | tf_op jit(solution)/shard_map/ppermute | solution.py:855
  236.4 12.0 %all-to-all-done.4.t_ref = bf16[8,384,128]{2,1,0:T(8,128)(2,1)S(1)} async-done(((bf16[8,384,128]{2,1,0:T(8,128)(2,1)}), bf16[8,384,128]{2,1,0:T(8,128)(2,1)S(1)}, u32[]{:S(2)}, u32[]{:S(2)}) %all-to-all-start.4) | async-done | bytes 786464 | tf_op jit(solution)/shard_map/all_to_all | solution.py:863
  249.4 5.8 %first_back.1 = (bf16[2,2,64,768]{3,2,1,0:T(8,128)(2,1)}, f32[2,2,64,768]{3,2,1,0:T(8,128)}, bf16[32,24,640]{2,1,0:T(8,128)(2,1)}) custom-call(s32[2]{0:T(128)} %pad_add_fusion.at_ref, bf16[8,384,128]{2,1,0:T(8,128)(2,1)} %copy-done.47, bf16[4,2,2,64,768]{4,3,2,1,0:T(8,128)(2,1)} %bitcast.79, f32[2,5376]{1,0:T(2,128)} %copy-done.11, f32[256,128]{1,0:T(8,128)} %copy-done.6, ...), custom_call_target="tpu_custom_call" | custom-call | flops 905969664 | bytes 6621192 | tf_op jit(solution)/shard_map/first_back/pallas_call | solution.py:837
  255.2 2.8 all-to-all-start.5
  259.9 1.7 collective-permute-start.38
  261.7 10.6 %collective-permute-done.38.got_ref = bf16[2,64,768]{2,1,0:T(8,128)(2,1)S(1)} collective-permute-done((bf16[2,64,768]{2,1,0:T(8,128)(2,1)S(1)}, bf16[2,64,768]{2,1,0:T(8,128)(2,1)S(1)}, u32[]{:S(2)}, u32[]{:S(2)}) %collective-permute-start.38) | collective-permute-done | bytes 196640 | tf_op jit(solution)/shard_map/ppermute | solution.py:855
  273.4 10.8 %all-to-all-done.5.raw_ref = bf16[32,24,640]{2,1,0:T(8,128)(2,1)S(1)} async-done(((bf16[32,24,640]{2,1,0:T(8,128)(2,1)}), bf16[32,24,640]{2,1,0:T(8,128)(2,1)S(1)}, u32[]{:S(2)}, u32[]{:S(2)}) %all-to-all-start.5) | async-done | bytes 983072 | tf_op jit(solution)/shard_map/all_to_all | solution.py:863
  285.2 2.4 row_grad.1
  287.5 2.5 all-to-all-start.6
  290.1 1.3 slice_bitcast_fusion.15
  291.4 1.6 copy.38
  293.0 4.3 %all-to-all-done.6 = f32[32,2,128]{2,1,0:T(2,128)S(1)} async-done(((f32[32,2,128]{2,1,0:T(2,128)}), f32[32,2,128]{2,1,0:T(2,128)S(1)}, u32[]{:S(2)}, u32[]{:S(2)}) %all-to-all-start.6) | async-done | bytes 32800 | tf_op jit(solution)/shard_map/all_to_all | solution.py:863
  (203 shorter events, 31.5 us)
Async XLA Ops:
  7.2 45.2 %all-gather.3.cloned.1.call-start = ((), (), s32[]{:S(2)}) async-start(), calls=%async_computation.7 | async-start | bytes 1966080 | tf_op jit(solution)/shard_map/all_gather | solution.py:913
  12.0 20.7 %copy-start.58 = (bf16[24,768]{1,0:T(8,128)(2,1)S(1)}, bf16[24,768]{1,0:T(8,128)(2,1)}, u32[]{:S(2)}) copy-start(bf16[24,768]{1,0:T(8,128)(2,1)} %get-tuple-element.97) | copy-start | bytes 110596
  12.0 37.0 %copy-start.51 = (bf16[96,768]{1,0:T(8,128)(2,1)S(1)}, bf16[96,768]{1,0:T(8,128)(2,1)}, u32[]{:S(2)}) copy-start(bf16[96,768]{1,0:T(8,128)(2,1)} %param.16) | copy-start | bytes 442372
  12.1 40.3 %all-to-all-start = ((bf16[32,24,640]{2,1,0:T(8,128)(2,1)}), bf16[32,24,640]{2,1,0:T(8,128)(2,1)S(1)}, u32[]{:S(2)}, u32[]{:S(2)}) async-start(bf16[32,24,640]{2,1,0:T(8,128)(2,1)} %get-tuple-element.92), calls=%async_computation | async-start | bytes 1966080 | tf_op jit(solution)/shard_map/all_to_all | solution.py:863
  19.4 33.0 %copy-start.28 = (s32[2]{0:T(128)S(1)}, s32[2]{0:T(128)}, u32[]{:S(2)}) copy-start(s32[2]{0:T(128)} %pad_add_fusion.at_ref) | copy-start | bytes 28
  19.4 17.6 %collective-permute-start.4 = (bf16[24,768]{1,0:T(8,128)(2,1)S(1)}, bf16[24,768]{1,0:T(8,128)(2,1)S(1)}, u32[]{:S(2)}, u32[]{:S(2)}) collective-permute-start(bf16[24,768]{1,0:T(8,128)(2,1)S(1)} %copy-done.45), channel_id=1, source_target_pairs={{0,2},{1,3},{2,0},{3,1},{4,6},{5,7},{6,4},{7,5},{8,10},{9,11},{10,... | collective-permute-start | bytes 110600 | tf_op jit(solution)/shard_map/ppermute | solution.py:859
  21.2 25.7 %collective-permute-start.6 = (bf16[24,768]{1,0:T(8,128)(2,1)S(1)}, bf16[24,768]{1,0:T(8,128)(2,1)S(1)}, u32[]{:S(2)}, u32[]{:S(2)}) collective-permute-start(bf16[24,768]{1,0:T(8,128)(2,1)S(1)} %copy-done.45), channel_id=1, source_target_pairs={{0,4},{1,5},{2,6},{3,7},{4,0},{5,1},{6,2},{7,3},{8,12},{9,13},{10,... | collective-permute-start | bytes 110600 | tf_op jit(solution)/shard_map/ppermute | solution.py:859
  23.6 24.8 %collective-permute-start.8 = (bf16[24,768]{1,0:T(8,128)(2,1)S(1)}, bf16[24,768]{1,0:T(8,128)(2,1)S(1)}, u32[]{:S(2)}, u32[]{:S(2)}) collective-permute-start(bf16[24,768]{1,0:T(8,128)(2,1)S(1)} %copy-done.45), channel_id=1, source_target_pairs={{0,6},{1,7},{2,4},{3,5},{4,2},{5,3},{6,0},{7,1},{8,14},{9,15},{10,... | collective-permute-start | bytes 110600 | tf_op jit(solution)/shard_map/ppermute | solution.py:859
  23.8 25.2 %collective-permute-start.3 = (bf16[24,768]{1,0:T(8,128)(2,1)S(1)}, bf16[24,768]{1,0:T(8,128)(2,1)S(1)}, u32[]{:S(2)}, u32[]{:S(2)}) collective-permute-start(bf16[24,768]{1,0:T(8,128)(2,1)S(1)} %copy-done.45), channel_id=1, source_target_pairs={{0,1},{1,0},{2,3},{3,2},{4,5},{5,4},{6,7},{7,6},{8,9},{9,8},{10,11... | collective-permute-start | bytes 110600 | tf_op jit(solution)/shard_map/ppermute | solution.py:859
  25.6 1.2 collective-permute-start
  26.6 29.5 %copy-start.6 = (f32[256,128]{1,0:T(8,128)}, f32[256,128]{1,0:T(8,128)S(1)}, u32[]{:S(2)}) copy-start(f32[256,128]{1,0:T(8,128)S(1)} %get-tuple-element.233.cos_ref) | copy-start | bytes 393220
  26.6 29.5 %copy-start.7 = (f32[256,128]{1,0:T(8,128)}, f32[256,128]{1,0:T(8,128)S(1)}, u32[]{:S(2)}) copy-start(f32[256,128]{1,0:T(8,128)S(1)} %get-tuple-element.234.sin_ref) | copy-start | bytes 393220
  26.8 5.9 %collective-permute-start.1 = (bf16[24,768]{1,0:T(8,128)(2,1)S(1)}, bf16[24,768]{1,0:T(8,128)(2,1)S(1)}, u32[]{:S(2)}, u32[]{:S(2)}) collective-permute-start(bf16[24,768]{1,0:T(8,128)(2,1)S(1)} %copy-done.59), channel_id=1, source_target_pairs={{0,16},{8,24},{16,0},{24,8},{1,17},{9,25},{17,1},{25,9},{2,18},{10... | collective-permute-start | bytes 110600 | tf_op jit(solution)/shard_map/ppermute | solution.py:855
  32.7 16.3 %collective-permute-start.2 = (bf16[24,768]{1,0:T(8,128)(2,1)S(1)}, bf16[24,768]{1,0:T(8,128)(2,1)S(1)}, u32[]{:S(2)}, u32[]{:S(2)}) collective-permute-start(bf16[24,768]{1,0:T(8,128)(2,1)S(1)} %copy-done.58), channel_id=1, source_target_pairs={{0,24},{8,16},{16,8},{24,0},{1,25},{9,17},{17,9},{25,1},{2,26},{10... | collective-permute-start | bytes 110600 | tf_op jit(solution)/shard_map/ppermute | solution.py:855
  37.0 12.1 %collective-permute-start.5 = (bf16[24,768]{1,0:T(8,128)(2,1)S(1)}, bf16[24,768]{1,0:T(8,128)(2,1)S(1)}, u32[]{:S(2)}, u32[]{:S(2)}) collective-permute-start(bf16[24,768]{1,0:T(8,128)(2,1)S(1)} %collective-permute-done.4.a2), channel_id=1, source_target_pairs={{0,1},{1,0},{2,3},{3,2},{4,5},{5,4},{6,7},{7,6},{8,9},{9,8},{10,11... | collective-permute-start | bytes 110600 | tf_op jit(solution)/shard_map/ppermute | solution.py:859
  47.0 4.0 %collective-permute-start.7 = (bf16[24,768]{1,0:T(8,128)(2,1)S(1)}, bf16[24,768]{1,0:T(8,128)(2,1)S(1)}, u32[]{:S(2)}, u32[]{:S(2)}) collective-permute-start(bf16[24,768]{1,0:T(8,128)(2,1)S(1)} %collective-permute-done.6.a4), channel_id=1, source_target_pairs={{0,1},{1,0},{2,3},{3,2},{4,5},{5,4},{6,7},{7,6},{8,9},{9,8},{10,11... | collective-permute-start | bytes 110600 | tf_op jit(solution)/shard_map/ppermute | solution.py:859
  48.4 4.0 %collective-permute-start.9 = (bf16[24,768]{1,0:T(8,128)(2,1)S(1)}, bf16[24,768]{1,0:T(8,128)(2,1)S(1)}, u32[]{:S(2)}, u32[]{:S(2)}) collective-permute-start(bf16[24,768]{1,0:T(8,128)(2,1)S(1)} %collective-permute-done.8.a6), channel_id=1, source_target_pairs={{0,1},{1,0},{2,3},{3,2},{4,5},{5,4},{6,7},{7,6},{8,9},{9,8},{10,11... | collective-permute-start | bytes 110600 | tf_op jit(solution)/shard_map/ppermute | solution.py:859
  49.0 50.3 %copy-start.29 = (bf16[192,768]{1,0:T(8,128)(2,1)}, bf16[192,768]{1,0:T(8,128)(2,1)S(1)}, u32[]{:S(2)}) copy-start(bf16[192,768]{1,0:T(8,128)(2,1)S(1)} %constant_dynamic-update-slice_fusion.a0) | copy-start | bytes 884740
  57.0 31.2 %copy-start.11 = (f32[2,5376]{1,0:T(2,128)}, f32[2,5376]{1,0:T(2,128)S(1)}, u32[]{:S(2)}) copy-start(f32[2,5376]{1,0:T(2,128)S(1)} %get-tuple-element.124.table_ref) | copy-start | bytes 129028
  78.2 10.8 %collective-permute-start.10 = (bf16[192,768]{1,0:T(8,128)(2,1)S(1)}, bf16[192,768]{1,0:T(8,128)(2,1)S(1)}, u32[]{:S(2)}, u32[]{:S(2)}) collective-permute-start(bf16[192,768]{1,0:T(8,128)(2,1)S(1)} %constant_dynamic-update-slice_fusion.a0), channel_id=1, source_target_pairs={{0,1},{1,0},{2,3},{3,2},{4,5},{5,4},{6,7},{7,6},{8,9},{9,8},{10,11... | collective-permute-start | bytes 884744 | tf_op jit(solution)/shard_map/ppermute | solution.py:859
  79.7 14.0 %collective-permute-start.11 = (bf16[192,768]{1,0:T(8,128)(2,1)S(1)}, bf16[192,768]{1,0:T(8,128)(2,1)S(1)}, u32[]{:S(2)}, u32[]{:S(2)}) collective-permute-start(bf16[192,768]{1,0:T(8,128)(2,1)S(1)} %constant_dynamic-update-slice_fusion.a0), channel_id=1, source_target_pairs={{0,4},{1,5},{2,6},{3,7},{4,0},{5,1},{6,2},{7,3},{8,12},{9,13},{10,... | collective-permute-start | bytes 884744 | tf_op jit(solution)/shard_map/ppermute | solution.py:859
  89.0 33.1 %copy-start.25 = (f32[8,8,256]{2,1,0:T(8,128)}, f32[8,8,256]{2,1,0:T(8,128)S(1)}, u32[]{:S(2)}) copy-start(f32[8,8,256]{2,1,0:T(8,128)S(1)} %get-tuple-element.146.lse_ref) | copy-start | bytes 196612
  93.7 28.5 %copy-start.37 = (bf16[192,768]{1,0:T(8,128)(2,1)}, bf16[192,768]{1,0:T(8,128)(2,1)S(1)}, u32[]{:S(2)}) copy-start(bf16[192,768]{1,0:T(8,128)(2,1)S(1)} %collective-permute-done.11.a4) | copy-start | bytes 884740
  93.7 25.7 %all-to-all-start.2 = ((bf16[8,128,128]{2,1,0:T(8,128)(2,1)}), bf16[8,128,128]{2,1,0:T(8,128)(2,1)S(1)}, u32[]{:S(2)}, u32[]{:S(2)}) async-start(bf16[8,128,128]{2,1,0:T(8,128)(2,1)} %get-tuple-element.105), calls=%async_computation.2 | async-start | bytes 524288 | tf_op jit(solution)/shard_map/all_to_all | solution.py:863
  97.3 13.0 %collective-permute-start.12 = (bf16[192,768]{1,0:T(8,128)(2,1)S(1)}, bf16[192,768]{1,0:T(8,128)(2,1)S(1)}, u32[]{:S(2)}, u32[]{:S(2)}) collective-permute-start(bf16[192,768]{1,0:T(8,128)(2,1)S(1)} %constant_dynamic-update-slice_fusion.a0), channel_id=1, source_target_pairs={{0,2},{1,3},{2,0},{3,1},{4,6},{5,7},{6,4},{7,5},{8,10},{9,11},{10,... | collective-permute-start | bytes 884744 | tf_op jit(solution)/shard_map/ppermute | solution.py:859
  99.3 19.3 %collective-permute-start.13 = (bf16[192,768]{1,0:T(8,128)(2,1)S(1)}, bf16[192,768]{1,0:T(8,128)(2,1)S(1)}, u32[]{:S(2)}, u32[]{:S(2)}) collective-permute-start(bf16[192,768]{1,0:T(8,128)(2,1)S(1)} %constant_dynamic-update-slice_fusion.a0), channel_id=1, source_target_pairs={{0,6},{1,7},{2,4},{3,5},{4,2},{5,3},{6,0},{7,1},{8,14},{9,15},{10,... | collective-permute-start | bytes 884744 | tf_op jit(solution)/shard_map/ppermute | solution.py:859
  101.7 16.9 %collective-permute-start.14 = (bf16[192,768]{1,0:T(8,128)(2,1)S(1)}, bf16[192,768]{1,0:T(8,128)(2,1)S(1)}, u32[]{:S(2)}, u32[]{:S(2)}) collective-permute-start(bf16[192,768]{1,0:T(8,128)(2,1)S(1)} %collective-permute-done.11.a4), channel_id=1, source_target_pairs={{0,1},{1,0},{2,3},{3,2},{4,5},{5,4},{6,7},{7,6},{8,9},{9,8},{10,11... | collective-permute-start | bytes 884744 | tf_op jit(solution)/shard_map/ppermute | solution.py:859
  110.3 29.2 %copy-start.39 = (bf16[192,768]{1,0:T(8,128)(2,1)}, bf16[192,768]{1,0:T(8,128)(2,1)S(1)}, u32[]{:S(2)}) copy-start(bf16[192,768]{1,0:T(8,128)(2,1)S(1)} %collective-permute-done.12.a2) | copy-start | bytes 884740
  118.6 20.9 %copy-start.41 = (bf16[192,768]{1,0:T(8,128)(2,1)}, bf16[192,768]{1,0:T(8,128)(2,1)S(1)}, u32[]{:S(2)}) copy-start(bf16[192,768]{1,0:T(8,128)(2,1)S(1)} %collective-permute-done.13.a6) | copy-start | bytes 884740
  120.4 1.8 collective-permute-start.15
  122.2 19.2 %copy-start.36 = (bf16[192,768]{1,0:T(8,128)(2,1)S(1)}, bf16[192,768]{1,0:T(8,128)(2,1)}, u32[]{:S(2)}) copy-start(bf16[192,768]{1,0:T(8,128)(2,1)} %copy-done.35) | copy-start | bytes 884740
  122.2 19.2 %copy-start.44 = (bf16[192,768]{1,0:T(8,128)(2,1)S(1)}, bf16[192,768]{1,0:T(8,128)(2,1)}, u32[]{:S(2)}) copy-start(bf16[192,768]{1,0:T(8,128)(2,1)} %copy-done.43) | copy-start | bytes 884740
  122.3 17.0 %collective-permute-start.16 = (bf16[2,2,64,768]{3,2,1,0:T(8,128)(2,1)S(1)}, bf16[2,2,64,768]{3,2,1,0:T(8,128)(2,1)S(1)}, u32[]{:S(2)}, u32[]{:S(2)}) collective-permute-start(bf16[2,2,64,768]{3,2,1,0:T(8,128)(2,1)S(1)} %fusion.1), channel_id=1, source_target_pairs={{0,16},{8,24},{16,0},{24,8},{1,17},{9,25},{17,1},{25,9},{2,18},{10... | collective-permute-start | bytes 1179656 | tf_op jit(solution)/shard_map/ppermute | solution.py:855
  124.3 9.9 %collective-permute-start.17 = (bf16[192,768]{1,0:T(8,128)(2,1)S(1)}, bf16[192,768]{1,0:T(8,128)(2,1)S(1)}, u32[]{:S(2)}, u32[]{:S(2)}) collective-permute-start(bf16[192,768]{1,0:T(8,128)(2,1)S(1)} %collective-permute-done.12.a2), channel_id=1, source_target_pairs={{0,1},{1,0},{2,3},{3,2},{4,5},{5,4},{6,7},{7,6},{8,9},{9,8},{10,11... | collective-permute-start | bytes 884744 | tf_op jit(solution)/shard_map/ppermute | solution.py:859
  125.7 13.6 %collective-permute-start.18 = (bf16[192,768]{1,0:T(8,128)(2,1)S(1)}, bf16[192,768]{1,0:T(8,128)(2,1)S(1)}, u32[]{:S(2)}, u32[]{:S(2)}) collective-permute-start(bf16[192,768]{1,0:T(8,128)(2,1)S(1)} %collective-permute-done.13.a6), channel_id=1, source_target_pairs={{0,1},{1,0},{2,3},{3,2},{4,5},{5,4},{6,7},{7,6},{8,9},{9,8},{10,11... | collective-permute-start | bytes 884744 | tf_op jit(solution)/shard_map/ppermute | solution.py:859
  139.6 1.8 collective-permute-start.19
  155.8 1.9 collective-permute-start.20
  159.4 11.5 %collective-permute-start.21 = (bf16[2,2,64,768]{3,2,1,0:T(8,128)(2,1)}, bf16[2,2,64,768]{3,2,1,0:T(8,128)(2,1)}, u32[]{:S(2)}, u32[]{:S(2)}) collective-permute-start(bf16[2,2,64,768]{3,2,1,0:T(8,128)(2,1)} %fusion.2), channel_id=1, source_target_pairs={{0,16},{8,24},{16,0},{24,8},{1,17},{9,25},{17,1},{25,9},{2,18},{10... | collective-permute-start | bytes 1179656 | tf_op jit(solution)/shard_map/ppermute | solution.py:855
  159.8 19.3 %collective-permute-start.23 = (bf16[4,4,24,768]{3,2,1,0:T(8,128)(2,1)S(1)}, bf16[4,4,24,768]{3,2,1,0:T(8,128)(2,1)}, u32[]{:S(2)}, u32[]{:S(2)}) collective-permute-start(bf16[4,4,24,768]{3,2,1,0:T(8,128)(2,1)S(1)} %copy-done.32), channel_id=1, source_target_pairs={{0,1},{1,0},{2,3},{3,2},{4,5},{5,4},{6,7},{7,6},{8,9},{9,8},{10,11... | collective-permute-start | bytes 1769480 | tf_op jit(solution)/shard_map/ppermute | solution.py:859
  161.4 12.4 %collective-permute-start.29 = (bf16[2,2,64,768]{3,2,1,0:T(8,128)(2,1)S(1)}, bf16[2,2,64,768]{3,2,1,0:T(8,128)(2,1)S(1)}, u32[]{:S(2)}, u32[]{:S(2)}) collective-permute-start(bf16[2,2,64,768]{3,2,1,0:T(8,128)(2,1)S(1)} %copy-done.34), channel_id=1, source_target_pairs={{0,8},{8,0},{16,24},{24,16},{1,9},{9,1},{17,25},{25,17},{2,10},{10... | collective-permute-start | bytes 1179656 | tf_op jit(solution)/shard_map/ppermute | solution.py:855
  172.2 1.8 collective-permute-start.22
  172.3 28.9 %collective-permute-start.27 = (bf16[4,4,24,768]{3,2,1,0:T(8,128)(2,1)}, bf16[4,4,24,768]{3,2,1,0:T(8,128)(2,1)}, u32[]{:S(2)}, u32[]{:S(2)}) collective-permute-start(bf16[4,4,24,768]{3,2,1,0:T(8,128)(2,1)} %get-tuple-element.142), channel_id=1, source_target_pairs={{0,1},{1,0},{2,3},{3,2},{4,5},{5,4},{6,7},{7,6},{8,9},{9,8},{10,11... | collective-permute-start | bytes 1769480 | tf_op jit(solution)/shard_map/ppermute | solution.py:859
  182.1 22.7 %copy-start.52 = (bf16[4,24,768]{2,1,0:T(8,128)(2,1)S(1)}, bf16[4,24,768]{2,1,0:T(8,128)(2,1)}, u32[]{:S(2)}) copy-start(bf16[4,24,768]{2,1,0:T(8,128)(2,1)} %get-tuple-element.151) | copy-start | bytes 442372
  182.1 8.5 %collective-permute-start.24 = (bf16[4,24,768]{2,1,0:T(8,128)(2,1)}, bf16[4,24,768]{2,1,0:T(8,128)(2,1)}, u32[]{:S(2)}, u32[]{:S(2)}) collective-permute-start(bf16[4,24,768]{2,1,0:T(8,128)(2,1)} %get-tuple-element.219), channel_id=1, source_target_pairs={{0,2},{1,3},{2,0},{3,1},{4,6},{5,7},{6,4},{7,5},{8,10},{9,11},{10,... | collective-permute-start | bytes 442376 | tf_op jit(solution)/shard_map/ppermute | solution.py:859
  183.0 16.9 %collective-permute-start.25 = (bf16[4,24,768]{2,1,0:T(8,128)(2,1)S(1)}, bf16[4,24,768]{2,1,0:T(8,128)(2,1)}, u32[]{:S(2)}, u32[]{:S(2)}) collective-permute-start(bf16[4,24,768]{2,1,0:T(8,128)(2,1)S(1)} %get-tuple-element.221), channel_id=1, source_target_pairs={{0,4},{1,5},{2,6},{3,7},{4,0},{5,1},{6,2},{7,3},{8,12},{9,13},{10,... | collective-permute-start | bytes 442376 | tf_op jit(solution)/shard_map/ppermute | solution.py:859
  183.1 22.6 %copy-start.16 = (bf16[4,4,24,768]{3,2,1,0:T(8,128)(2,1)S(1)}, bf16[4,4,24,768]{3,2,1,0:T(8,128)(2,1)}, u32[]{:S(2)}) copy-start(bf16[4,4,24,768]{3,2,1,0:T(8,128)(2,1)} %copy-done.15) | copy-start | bytes 1769476
  183.1 16.8 %collective-permute-start.26 = (bf16[4,24,768]{2,1,0:T(8,128)(2,1)S(1)}, bf16[4,24,768]{2,1,0:T(8,128)(2,1)}, u32[]{:S(2)}, u32[]{:S(2)}) collective-permute-start(bf16[4,24,768]{2,1,0:T(8,128)(2,1)S(1)} %get-tuple-element.220), channel_id=1, source_target_pairs={{0,6},{1,7},{2,4},{3,5},{4,2},{5,3},{6,0},{7,1},{8,14},{9,15},{10,... | collective-permute-start | bytes 442376 | tf_op jit(solution)/shard_map/ppermute | solution.py:859
  186.5 18.3 %all-to-all-start.3 = ((bf16[8,128,128]{2,1,0:T(8,128)(2,1)}), bf16[8,128,128]{2,1,0:T(8,128)(2,1)S(1)}, u32[]{:S(2)}, u32[]{:S(2)}) async-start(bf16[8,128,128]{2,1,0:T(8,128)(2,1)} %get-tuple-element.139), calls=%async_computation.3 | async-start | bytes 524288 | tf_op jit(solution)/shard_map/all_to_all | solution.py:863
  190.1 21.4 %collective-permute-start.30 = (bf16[2,64,768]{2,1,0:T(8,128)(2,1)S(1)}, bf16[2,64,768]{2,1,0:T(8,128)(2,1)S(1)}, u32[]{:S(2)}, u32[]{:S(2)}) collective-permute-start(bf16[2,64,768]{2,1,0:T(8,128)(2,1)S(1)} %fusion.15), channel_id=1, source_target_pairs={{0,16},{8,24},{16,0},{24,8},{1,17},{9,25},{17,1},{25,9},{2,18},{10... | collective-permute-start | bytes 589832 | tf_op jit(solution)/shard_map/ppermute | solution.py:855
  190.6 10.6 %collective-permute-start.28 = (bf16[4,24,768]{2,1,0:T(8,128)(2,1)}, bf16[4,24,768]{2,1,0:T(8,128)(2,1)}, u32[]{:S(2)}, u32[]{:S(2)}) collective-permute-start(bf16[4,24,768]{2,1,0:T(8,128)(2,1)} %get-tuple-element.143), channel_id=1, source_target_pairs={{0,1},{1,0},{2,3},{3,2},{4,5},{5,4},{6,7},{7,6},{8,9},{9,8},{10,11... | collective-permute-start | bytes 442376 | tf_op jit(solution)/shard_map/ppermute | solution.py:859
  207.1 19.1 %collective-permute-start.31 = (bf16[5,24,768]{2,1,0:T(8,128)(2,1)S(1)}, bf16[5,24,768]{2,1,0:T(8,128)(2,1)S(1)}, u32[]{:S(2)}, u32[]{:S(2)}) collective-permute-start(bf16[5,24,768]{2,1,0:T(8,128)(2,1)S(1)} %get-tuple-element.216), channel_id=1, source_target_pairs={{0,2},{1,3},{2,0},{3,1},{4,6},{5,7},{6,4},{7,5},{8,10},{9,11},{10,... | collective-permute-start | bytes 552968 | tf_op jit(solution)/shard_map/ppermute | solution.py:859
  208.2 18.0 %collective-permute-start.32 = (bf16[5,24,768]{2,1,0:T(8,128)(2,1)S(1)}, bf16[5,24,768]{2,1,0:T(8,128)(2,1)S(1)}, u32[]{:S(2)}, u32[]{:S(2)}) collective-permute-start(bf16[5,24,768]{2,1,0:T(8,128)(2,1)S(1)} %get-tuple-element.218), channel_id=1, source_target_pairs={{0,4},{1,5},{2,6},{3,7},{4,0},{5,1},{6,2},{7,3},{8,12},{9,13},{10,... | collective-permute-start | bytes 552968 | tf_op jit(solution)/shard_map/ppermute | solution.py:859
  209.2 17.1 %collective-permute-start.33 = (bf16[5,24,768]{2,1,0:T(8,128)(2,1)S(1)}, bf16[5,24,768]{2,1,0:T(8,128)(2,1)S(1)}, u32[]{:S(2)}, u32[]{:S(2)}) collective-permute-start(bf16[5,24,768]{2,1,0:T(8,128)(2,1)S(1)} %get-tuple-element.217), channel_id=1, source_target_pairs={{0,6},{1,7},{2,4},{3,5},{4,2},{5,3},{6,0},{7,1},{8,14},{9,15},{10,... | collective-permute-start | bytes 552968 | tf_op jit(solution)/shard_map/ppermute | solution.py:859
  226.3 22.1 %all-to-all-start.4 = ((bf16[8,384,128]{2,1,0:T(8,128)(2,1)}), bf16[8,384,128]{2,1,0:T(8,128)(2,1)S(1)}, u32[]{:S(2)}, u32[]{:S(2)}) async-start(bf16[8,384,128]{2,1,0:T(8,128)(2,1)} %attn_bwd.1), calls=%async_computation.4 | async-start | bytes 1572864 | tf_op jit(solution)/shard_map/all_to_all | solution.py:863
  230.5 1.9 collective-permute-start.34
  230.5 5.1 %collective-permute-start.35 = (f32[24,768]{1,0:T(8,128)S(1)}, f32[24,768]{1,0:T(8,128)S(1)}, u32[]{:S(2)}, u32[]{:S(2)}) collective-permute-start(f32[24,768]{1,0:T(8,128)S(1)} %get-tuple-element.223), channel_id=1, source_target_pairs={{0,16},{8,24},{16,0},{24,8},{1,17},{9,25},{17,1},{25,9},{2,18},{10... | collective-permute-start | bytes 221192 | tf_op jit(solution)/shard_map/ppermute | solution.py:855
  230.9 5.5 %collective-permute-start.36 = (f32[24,768]{1,0:T(8,128)S(1)}, f32[24,768]{1,0:T(8,128)S(1)}, u32[]{:S(2)}, u32[]{:S(2)}) collective-permute-start(f32[24,768]{1,0:T(8,128)S(1)} %get-tuple-element.222), channel_id=1, source_target_pairs={{0,24},{8,16},{16,8},{24,0},{1,25},{9,17},{17,9},{25,1},{2,26},{10... | collective-permute-start | bytes 221192 | tf_op jit(solution)/shard_map/ppermute | solution.py:855
  232.4 27.2 %copy-start.53 = (f32[24,768]{1,0:T(8,128)}, f32[24,768]{1,0:T(8,128)S(1)}, u32[]{:S(2)}) copy-start(f32[24,768]{1,0:T(8,128)S(1)} %collective-permute-done.34.p1) | copy-start | bytes 221188
  235.6 24.0 %copy-start.54 = (f32[24,768]{1,0:T(8,128)}, f32[24,768]{1,0:T(8,128)S(1)}, u32[]{:S(2)}) copy-start(f32[24,768]{1,0:T(8,128)S(1)} %collective-permute-done.35.p2) | copy-start | bytes 221188
  236.4 23.2 %copy-start.55 = (f32[24,768]{1,0:T(8,128)}, f32[24,768]{1,0:T(8,128)S(1)}, u32[]{:S(2)}) copy-start(f32[24,768]{1,0:T(8,128)S(1)} %collective-permute-done.36.p3) | copy-start | bytes 221188
  255.2 29.0 %all-to-all-start.5 = ((bf16[32,24,640]{2,1,0:T(8,128)(2,1)}), bf16[32,24,640]{2,1,0:T(8,128)(2,1)S(1)}, u32[]{:S(2)}, u32[]{:S(2)}) async-start(bf16[32,24,640]{2,1,0:T(8,128)(2,1)} %get-tuple-element.163), calls=%async_computation.5 | async-start | bytes 1966080 | tf_op jit(solution)/shard_map/all_to_all | solution.py:863
  258.0 1.8 collective-permute-start.37
  259.9 12.3 %collective-permute-start.38 = (bf16[2,64,768]{2,1,0:T(8,128)(2,1)S(1)}, bf16[2,64,768]{2,1,0:T(8,128)(2,1)S(1)}, u32[]{:S(2)}, u32[]{:S(2)}) collective-permute-start(bf16[2,64,768]{2,1,0:T(8,128)(2,1)S(1)} %fusion.16), channel_id=1, source_target_pairs={{0,16},{8,24},{16,0},{24,8},{1,17},{9,25},{17,1},{25,9},{2,18},{10... | collective-permute-start | bytes 589832 | tf_op jit(solution)/shard_map/ppermute | solution.py:855
  287.5 9.7 %all-to-all-start.6 = ((f32[32,2,128]{2,1,0:T(2,128)}), f32[32,2,128]{2,1,0:T(2,128)S(1)}, u32[]{:S(2)}, u32[]{:S(2)}) async-start(f32[32,2,128]{2,1,0:T(2,128)} %get-tuple-element.168), calls=%async_computation.6 | async-start | bytes 65536 | tf_op jit(solution)/shard_map/all_to_all | solution.py:863
  (43 other events, 273.1 us)
Sparse Core Ops, SparseCore 0:
  12.1 30.7 all-gather.2

commit v2 on v1

--- a/solution.py
+++ b/solution.py
@@ -496,18 +496,16 @@
 
 
 def pack_kernel(
-    at_ref, x_ref, g_ref, qkv_ref, ada_ref, cond_ref, one_ref, two_ref, up_ref,
-    xc_ref, chunk_ref, p0, p1, p2, p3, ext_ref,
+    x_ref, g_ref, qkv_ref, ada_ref, cond_ref, one_ref, two_ref, up_ref, xc_ref, piece_ref, ext_ref,
 ):
-    u = at_ref[0]
-    n_all, block, cols = chunk_ref.shape
+    n_u, block, cols = piece_ref.shape
     xc_ref[0] = x_ref[...]
     xc_ref[1] = g_ref[...]
     width = qkv_ref.shape[1] // 3
-    n_u = 4
+    ff = up_ref.shape[1] // n_u
     heads = width // n_u // HEAD_DIM
     ext_ref[...] = jnp.zeros_like(ext_ref)
-    mods = DOT(cond_ref[...], ada_ref[...])
+    mods = dot_nt(cond_ref[...], ada_ref[...])
     gains = jnp.concatenate([one_ref[...], two_ref[...]], axis=0).astype(f32)
 
     def store(row, value):
@@ -522,26 +520,37 @@
             pieces += [qkv_ref[:, at : at + HEAD_DIM], qkv_ref[:, width + at : width + at + HEAD_DIM]]
         at = 2 * width + i * heads * HEAD_DIM
         pieces += [qkv_ref[:, at : at + heads * HEAD_DIM], extra]
-        whole = jnp.concatenate(pieces, axis=1)
-        for j in range(n_all // n_u):
-            chunk_ref[i * (n_all // n_u) + j] = whole
-    cols = up_ref.shape[1] // n_u
-    for i, out_ref in enumerate((p0, p1, p2, p3)):
-        out_ref[...] = up_ref[:, pl.ds(pl.multiple_of((u ^ i) * cols, 128), cols)]
-
-
-def first_kernel(at_ref, xg_ref, w_ref, cos_ref, sin_ref, chunk_ref, first_ref, table_ref):
-    u = at_ref[0]
+        piece_ref[i, :, : cols - ff] = jnp.concatenate(pieces, axis=1)
+        piece_ref[i, :, cols - ff :] = up_ref[:, i * ff : (i + 1) * ff]
+
+
+def first_kernel(
+    at_ref, xg_ref, cos_ref, sin_ref, a0, a1, a2, a3, a4, a5, a6, a7,
+    chunk_ref, first_ref, table_ref, w_ref, out_ref, wide_ref, wout_ref,
+):
+    u, b = at_ref[0], at_ref[1]
     n_u, _, seqs, rows, width = xg_ref.shape
     span = n_u * rows
-    cols = w_ref.shape[1] - HEAD_DIM
+    cols = w_ref.shape[1]
     heads = cols // 192
     block = width // 32
+    for i, part_ref in enumerate((a0, a1, a2, a3, a4, a5, a6, a7)):
+        there = b ^ i
+        part = part_ref[...].astype(f32)
+        quarter = part.shape[1] - cols - HEAD_DIM
+        for j in range(n_u):
+            start = pl.multiple_of((j * 8 + there) * block, 8)
+            wide_ref[pl.ds(start, block), :] = part[j * block : (j + 1) * block, : cols + HEAD_DIM]
+            start = pl.multiple_of(there * block, 8)
+            wout_ref[pl.ds(start, block), j * quarter : (j + 1) * quarter] = part[
+                j * block : (j + 1) * block, cols + HEAD_DIM :
+            ]
+    w_ref[...] = wide_ref[:, :cols].astype(bf16)
+    out_ref[...] = wout_ref[...].astype(bf16)
     for s in range(seqs):
         mods, gains = [], []
         for d in range(32):
-            at = d * block + s * 4
-            pair = w_ref[d * block : (d + 1) * block, cols:].astype(f32)
+            pair = wide_ref[d * block : (d + 1) * block, cols:]
             both = pair[s * 4 : s * 4 + 4] + pair[(seqs + s) * 4 : (seqs + s) * 4 + 4]
             mods += [both[i : i + 1, :EXTRA] for i in range(3)]
             gains.append(both[3:4, :block])
@@ -556,7 +565,7 @@
             normed, _ = row_norm(xg_ref[u ^ m, 0, s].astype(f32))
             first = normed * factor + mod_row(table_ref, s, 0)
             first_ref[s * span + m * rows : s * span + (m + 1) * rows, :] = first.astype(bf16)
-        projected = DOT(first_ref[s * span : (s + 1) * span, :], w_ref[:, :cols])
+        projected = DOT(first_ref[s * span : (s + 1) * span, :], w_ref[...])
         for h in range(heads):
             pair = 1 + s * heads + h
             both = turn(projected[:, 128 * h : 128 * (h + 1)], cos_ref, sin_ref, 1.0)
@@ -579,15 +588,8 @@
             keep_ref[m // 2, s] = block
 
 
-def out_kernel(
-    at_ref, t_ref, a0, a1, a2, a3, a4, a5, a6, a7, att_ref, send_ref, keep_ref, w_ref, wide_ref,
-):
+def out_kernel(t_ref, w_ref, att_ref, send_ref, keep_ref):
     _, seqs, rows, _ = send_ref.shape
-    block = a0.shape[0]
-    for i, part_ref in enumerate((a0, a1, a2, a3, a4, a5, a6, a7)):
-        start = pl.multiple_of((at_ref[1] ^ i) * block, 8)
-        wide_ref[pl.ds(start, block), :] = part_ref[...].astype(f32)
-    w_ref[...] = wide_ref[...].astype(bf16)
     heads = w_ref.shape[0] // HEAD_DIM
     span = 4 * rows
     for s in range(seqs):
@@ -605,8 +607,8 @@
 
 
 def ff_kernel(
-    at_ref, xg_ref, own_ref, got_ref, table_ref, a0, a1, a2, a3, a4, a5, a6, a7,
-    lsend_ref, lkeep_ref, dsend_ref, dkeep_ref, sums_ref, ukeep_ref, usend_ref, wkeep_ref, wsend_ref,
+    at_ref, xg_ref, own_ref, got_ref, table_ref, a0, a1, a2, a3, a4, a5, a6, a7, b0, b1, b2, b3, b4, b5, b6, b7,
+    lsend_ref, lkeep_ref, dsend_ref, dkeep_ref, sums_ref, ukeep_ref, usend_ref, dgrad_ref,
     second_ref, hidden_ref, low_ref, raised_ref, normed_ref, wide_ref, up_ref, down_ref,
 ):
     u = at_ref[0]
@@ -617,11 +619,12 @@
     block = width // 32
     low = n_u * block
     u, b = at_ref[0], at_ref[1]
-    for i, part_ref in enumerate((a0, a1, a2, a3, a4, a5, a6, a7)):
+    ups, downs = (a0, a1, a2, a3, a4, a5, a6, a7), (b0, b1, b2, b3, b4, b5, b6, b7)
+    for i, (part_ref, low_part_ref) in enumerate(zip(ups, downs)):
         there = b ^ i
-        down_ref[pl.ds(pl.multiple_of(there * low, 32), low), :] = part_ref[low:, :]
+        down_ref[pl.ds(pl.multiple_of(there * low, 32), low), :] = low_part_ref[...]
         for j in range(n_u):
-            start = pl.multiple_of(((u ^ j) * 8 + there) * block, 8)
+            start = pl.multiple_of((j * 8 + there) * block, 8)
             wide_ref[pl.ds(start, block), :] = part_ref[j * block : (j + 1) * block, :].astype(f32)
     up_ref[...] = wide_ref[...].astype(bf16)
     for s in range(seqs):
@@ -659,12 +662,7 @@
             for i in range(n_u):
                 start = pl.multiple_of(((u ^ i) * 2 * n_z + (b ^ (2 * z + y))) * block, 8)
                 out_ref[z, i] = wide_ref[pl.ds(start, block), :].astype(bf16)
-    wide_ref[...] = dot_tn(hidden_ref[...], low_ref[...])
-    for y, out_ref in enumerate((wkeep_ref, wsend_ref)):
-        for z in range(n_z):
-            for i in range(n_u):
-                start = pl.multiple_of(((b ^ (2 * z + y)) * n_u + i) * block, 8)
-                out_ref[z, i] = wide_ref[pl.ds(start, block), :].astype(bf16)
+    dgrad_ref[...] = dot_tn(hidden_ref[...], low_ref[...]).astype(bf16)
 
 
 def middle_back_kernel(
@@ -710,7 +708,7 @@
     u = at_ref[0]
     n_u, _, seqs, rows, width = xg_ref.shape
     span = n_u * rows
-    cols = w_ref.shape[1] - HEAD_DIM
+    cols = w_ref.shape[1]
     heads = cols // 192
     gain_grads = [jnp.zeros((1, width), f32)] * 2
     total, block, _ = blocks_ref.shape
@@ -724,7 +722,7 @@
             proj_ref[at, 128 * heads + 64 * h : 128 * heads + 64 * (h + 1)] = jnp.concatenate(
                 [v[:, :HEAD_DIM], v[:, HEAD_DIM:]], axis=0
             )
-        d_first = dot_nt(proj_ref[at, :], w_ref[:, :cols])
+        d_first = dot_nt(proj_ref[at, :], w_ref[...])
         store_parts(send_ref, keep_ref, d_first, s, rows)
         for m in range(n_u):
             normed, _ = row_norm(xg_ref[u ^ m, 0, s].astype(f32))
@@ -785,10 +783,10 @@
         mod_ref[s : s + 1, :] = jnp.concatenate([both[i : i + 1, :EXTRA] for i in range(3)], axis=1)
         gain_ref[s : s + 1, :] = both[3:4, :block]
     mods = mod_ref[...].astype(bf16)
-    grads = dot_nt(mods, ada_ref[...])
+    grads = DOT(mods, ada_ref[...])
     for i in range(total):
         part_ref[i] = grads
-    adag_ref[...] = dot_tn(cond_ref[...], mods)
+    adag_ref[...] = dot_tn(mods, cond_ref[...])
     cols = up_ref.shape[1] // n_u
     for i, piece_ref in enumerate((p0, p1, p2, p3)):
         up_ref[:, pl.ds(pl.multiple_of((u ^ i) * cols, 128), cols)] = piece_ref[...]
@@ -840,7 +838,7 @@
         in_specs=specs,
         out_specs=tuple(pl.BlockSpec(memory_space=pltpu.VMEM) for _ in outs),
         scratch_shapes=shapes,
-        cost_estimate=pl.CostEstimate(flops=int(flops), bytes_accessed=int(size), transcendentals=0),
+        cost_estimate=pl.CostEstimate(flops=int(flops) // 1000, bytes_accessed=int(size) // 1000, transcendentals=0),
         compiler_params=pltpu.CompilerParams(vmem_limit_bytes=limit << 20),
         name=name,
     )(*args)
@@ -901,20 +899,13 @@
     span = n_u * rows
     tokens = seqs * span
 
-    packed = call(
+    both, pieces = call(
         pack_kernel, "pack",
-        [((2,) + inputs.shape, bf16), ((n_all, w_rows, cols + HEAD_DIM), bf16)] + [((w_rows, ff_local), bf16)] * n_u,
+        [((2,) + inputs.shape, bf16), ((n_u, w_rows, cols + HEAD_DIM + ff_local), bf16)],
         [((w_rows, HEAD_DIM), f32)], 0,
-        at, inputs, cotangent, w_qkv, w_ada, conditioning, gain_one[None], gain_two[None], w_up,
+        inputs, cotangent, w_qkv, w_ada.T, conditioning, gain_one[None], gain_two[None], w_up,
         limit=60,
     )
-    ff_near = jnp.concatenate([packed[2]] + [swap_u(packed[2 + m], m) for m in (1, 2, 3)] + [w_down], axis=0)
-    raw = exchange(packed[1], everywhere)
-    xg = lax.all_gather(packed[0], "ulysses", axis=0, tiled=False)
-    out_zy = along_y(along_z(w_out))
-    raw, xg, ff_near, out_zy = lax.optimization_barrier((raw, xg, ff_near, out_zy))
-    w_qkv_u = raw.reshape(width, cols + HEAD_DIM)
-
     blocks = u ^ jnp.arange(n_u, dtype=jnp.int32)
     positions = ((blocks * n_b + b) * rows)[:, None] + jnp.arange(rows, dtype=jnp.int32)[None, :]
     cos_table, sin_table = rotary_tables(positions.reshape(-1).astype(f32))
@@ -922,46 +913,68 @@
     cos_table = jnp.concatenate([cos_table] * 4, axis=1)
     sin_table = jnp.concatenate([-sin_table, sin_table] * 2, axis=1)
 
-    chunks, first_in, table = call(
+    pieces, cos_table, sin_table, at = lax.optimization_barrier(
+        (exchange(pieces, "ulysses"), cos_table, sin_table, at)
+    )
+    pieces = pieces.reshape(n_u * w_rows, cols + HEAD_DIM + ff_local)
+    xg = lax.all_gather(both, "ulysses", axis=0, tiled=False)
+    up_near = pieces[:, cols + HEAD_DIM :]
+    down_z = along_z(w_down)
+    quarter = width // n_u
+    near = jnp.concatenate(
+        [
+            pieces[:, : cols + HEAD_DIM],
+            jnp.concatenate([w_out[:, i * quarter : (i + 1) * quarter] for i in range(n_u)], axis=0),
+        ],
+        axis=1,
+    )
+    near, down_z = lax.optimization_barrier((near, down_z))
+    rows_zy = along_y(along_z(near))
+
+    chunks, first_in, table, w_qkv_u, w_out_u = call(
         first_kernel, "first",
-        [((n_b, 3 * span // 2, 128), bf16), ((tokens, width), bf16), ((seqs, 7 * width), f32)], [],
+        [((n_b, 3 * span // 2, 128), bf16), ((tokens, width), bf16), ((seqs, 7 * width), f32),
+         ((width, cols), bf16), ((head_width, width), bf16)],
+        [((width, cols + HEAD_DIM), f32), ((head_width, width), f32)],
         2 * tokens * width * cols,
-        at, xg, w_qkv_u, cos_table, sin_table,
-    )
+        at, xg, cos_table, sin_table, *rows_zy,
+        limit=60,
+    )
+    chunks, down_z = lax.optimization_barrier((chunks, down_z))
     owned = exchange(chunks, "blk")
-    owned, ff_near = lax.optimization_barrier((owned, ff_near))
-    ff_0y, ff_2 = swap_b(ff_near, 1), swap_b(ff_near, 4)
+    down_zy = along_y(down_z)
+    owned, up_near, down_zy[1], down_zy[3] = lax.optimization_barrier((owned, up_near, down_zy[1], down_zy[3]))
+    up_z = along_z(up_near)
+    up_0y = swap_b(up_near, 1)
     attn_low, attn_full, log_total = attn_fwd(owned)
     part_shape = (2, seqs, rows, width)
-    attn_low, ff_0y, ff_2, ff_near = lax.optimization_barrier((attn_low, ff_0y, ff_2, ff_near))
+    attn_low, up_z, up_0y, down_zy = lax.optimization_barrier((attn_low, up_z, up_0y, down_zy))
     attn_tokens = exchange(attn_low, "blk")
-    ff_1, ff_3, ff_2y = swap_b(ff_near, 2), swap_b(ff_near, 6), swap_b(ff_2, 1)
-    attn_tokens, ff_1, ff_3, ff_2y = lax.optimization_barrier((attn_tokens, ff_1, ff_3, ff_2y))
-    attended, send, keep, w_out_u = call(
+    attended, send, keep = call(
         out_kernel, "out",
-        [((tokens, head_width), bf16), (part_shape, bf16), (part_shape, f32), ((head_width, width), bf16)],
-        [((head_width, width), f32)],
+        [((tokens, head_width), bf16), (part_shape, bf16), (part_shape, f32)], [],
         2 * tokens * width * head_width,
-        at, attn_tokens, *out_zy,
+        attn_tokens, w_out_u,
     )
 
     half = half_sum(send, keep)
     across = swap_u(half.astype(bf16), 2)
-    ff_zy = [ff_near, ff_0y, ff_1, swap_b(ff_1, 1), ff_2, ff_2y, ff_3, swap_b(ff_3, 1)]
-    across, ff_zy = lax.optimization_barrier((across, ff_zy))
+    up_zy = [up_near, up_0y] + along_y(up_z[1:])
+    across, up_zy = lax.optimization_barrier((across, up_zy))
     own = (half + across[::-1].astype(f32)).astype(bf16)
     got = swap_u(own, 1)
-    lsend, lkeep, dsend, dkeep, sums_two, up_keep, up_send, down_keep, down_send = call(
+    lsend, lkeep, dsend, dkeep, sums_two, up_keep, up_send, down_term = call(
         ff_kernel, "ff",
         [(part_shape, bf16), (part_shape, f32), (part_shape, bf16), (part_shape, f32), ((seqs, 3, width), f32)]
-        + [((n_b // 2, n_u, w_rows, width), bf16)] * 4,
+        + [((n_b // 2, n_u, w_rows, width), bf16)] * 2 + [((ff_local, width), bf16)],
         [((tokens, width), bf16), ((tokens, ff_local), bf16), ((tokens, width), bf16), ((tokens, ff_local), bf16),
          ((span, width), f32), ((width, ff_local), f32), ((width, ff_local), bf16), ((ff_local, width), bf16)],
         12 * tokens * width * ff_local,
-        at, xg, own, got, table, *ff_zy,
-        limit=28,
-    )
-    up_other, down_other = swap_b(up_send, 1), swap_b(down_send, 1)
+        at, xg, own, got, table, *up_zy, *down_zy,
+        limit=60,
+    )
+    up_other = swap_b(up_send, 1)
+    down_grad = lax.psum_scatter(down_term, "blk", scatter_dimension=0, tiled=True)
     half = half_sum(dsend, dkeep)
     across = swap_u(half.astype(bf16), 2)
     d_own = (half + across[::-1].astype(f32)).astype(bf16)
@@ -975,26 +988,24 @@
         at, xg, own, got, d_own, d_got, table, w_out_u, attended,
         limit=60,
     )
-    d_chunks, up_other = lax.optimization_barrier((d_chunks, up_other))
     d_attn = exchange(d_chunks, "blk")
-    up_sum = sum_z(up_keep.astype(f32) + up_other.astype(f32))
     out_other = swap_b(out_send, 1)
-    d_attn, up_sum, down_other, out_other = lax.optimization_barrier((d_attn, up_sum, down_other, out_other))
-    down_sum = sum_z(
-        jnp.concatenate(
-            [down_keep.astype(f32) + down_other.astype(f32), (out_keep.astype(f32) + out_other.astype(f32))[:, None]],
-            axis=1,
-        )
-    )
+    up_half = up_keep.astype(f32) + up_other.astype(f32)
+    up_1 = swap_b(up_half[1].astype(bf16), 2)
+    d_attn, up_1, out_other = lax.optimization_barrier((d_attn, up_1, out_other))
+    up_sum = up_half[0] + up_1.astype(f32)
+    for m in (2, 3):
+        up_sum = up_sum + swap_b(up_half[m].astype(bf16), 2 * m).astype(f32)
     d_owned = attn_bwd(owned, d_attn, attn_full, log_total)
     lhalf = half_sum(lsend, lkeep)
     lowered = lhalf[0] + swap_u(lhalf[1].astype(bf16), 2).astype(f32)
     gates = table.reshape(2, 7, 1, width)
     output = inputs.astype(f32) + gates[:, 2] * own[0].astype(f32) + gates[:, 5] * lowered
-    d_owned, output, down_sum = lax.optimization_barrier((d_owned, output, down_sum))
+    d_owned, output, up_sum, out_other = lax.optimization_barrier((d_owned, output, up_sum, out_other))
+    out_grad = sum_z(out_keep.astype(f32) + out_other.astype(f32))
     up_parts = [up_sum[0]] + [swap_u(up_sum[m], m) for m in (1, 2, 3)]
     d_tokens = exchange(d_owned, "blk")
-    d_tokens, up_parts = lax.optimization_barrier((d_tokens, up_parts))
+    d_tokens, up_parts, out_grad, down_grad = lax.optimization_barrier((d_tokens, up_parts, out_grad, down_grad))
 
     send, keep, qkv_blocks = call(
         first_back_kernel, "first_back",
@@ -1013,10 +1024,10 @@
     )
     qkv_grad, up_grad, cond_part, ada_grad, gain_grads, _ = call(
         row_grad_kernel, "row_grad",
-        [(w_qkv.shape, f32), (w_up.shape, f32), ((n_all,) + conditioning.shape, f32), (w_ada.shape, f32),
+        [(w_qkv.shape, f32), (w_up.shape, f32), ((n_all,) + conditioning.shape, f32), (w_ada.shape[::-1], f32),
          ((2, w_rows), f32), ((seqs, w_ada.shape[1]), f32)],
         [], 0,
-        at, exchange(qkv_blocks, everywhere), *up_parts, w_ada, conditioning,
+        at, exchange(qkv_blocks, everywhere), *up_parts, w_ada.T, conditioning,
         limit=60,
     )
     conditioning_grad = jnp.sum(exchange(cond_part, everywhere), axis=0)
@@ -1024,11 +1035,11 @@
         output,
         inputs_grad,
         conditioning_grad,
-        ada_grad,
+        ada_grad.T,
         qkv_grad,
-        down_sum[n_u],
+        out_grad,
         up_grad,
-        down_sum[:n_u].reshape(w_down.shape),
+        down_grad.astype(f32),
         gain_grads[0],
         gain_grads[1],
     )

time: 306 us -> 280 us (0.915)
  waiting for transfers between devices: 120 us -> 105 us
  local copies, waits for them, and re-layouts: 22.9 us -> 10.8 us
  blocking collectives: 21.2 us -> 11.8 us
  Pallas kernels: 48.3 us -> 52.6 us
  starting transfers between devices: 65.6 us -> 69.5 us
    unnamed x130 -> x104, local copies, waits for them, and re-layouts: 18.6 us -> 6.77 us
    ppermute x16 -> x13, waiting for transfers between devices: 34.1 us -> 22.5 us  [swap_u(): return lax.ppermute(values, 'ulysses', [(i, i ^ mask) for i in range(4)])]
    all_to_all x1, blocking collectives: 21.2 us -> 11.8 us  [exchange(): return lax.all_to_all(blocks, axis, split_axis=0, concat_axis=0, tiled=True)]
    all_to_all x6, waiting for transfers between devices: 30.7 us -> 24.3 us  [exchange(): return lax.all_to_all(blocks, axis, split_axis=0, concat_axis=0, tiled=True)]
    ppermute x23 -> x29, starting transfers between devices: 33.1 us -> 38.9 us  [swap_b(): return lax.ppermute(values, 'blk', [(i, i ^ mask) for i in range(8)])]
    pallas_call x8, Pallas kernels: 26 us -> 30.9 us  [call(): pl.pallas_call(body, out_shape=tuple((jax.ShapeDtypeStruct(shape, dtype)...]
    ppermute x23 -> x29, waiting for transfers between devices: 55 us -> 58.1 us  [swap_b(): return lax.ppermute(values, 'blk', [(i, i ^ mask) for i in range(8)])]
    ppermute x16 -> x13, starting transfers between devices: 9.04 us -> 7.24 us  [swap_u(): return lax.ppermute(values, 'ulysses', [(i, i ^ mask) for i in range(4)])]
  transfers between devices with their start and end apart: 46 -> 50, of which waited for: 24 -> 23; matrix products, arithmetic and copies ran while one was open for 5% -> 7% of each run, Pallas kernels for 9% -> 10%
where the time goes in v2:
time: 280 us; the launch traced here: 279 us
  waiting for transfers between devices  105 us (38%)
  starting transfers between devices  69.5 us (25%)
  Pallas kernels  52.6 us (19%)
  other arithmetic  14.9 us (5%)
  between operations  14.8 us (5%)
  blocking collectives  11.8 us (4%)
  local copies, waits for them, and re-layouts  10.8 us (4%)
    ppermute x29, waiting for transfers between devices, swap_b(): return lax.ppermute(values, 'blk', [(i, i ^ mask) for i in range(8)])  58.1 us
    ppermute x29, starting transfers between devices, swap_b(): return lax.ppermute(values, 'blk', [(i, i ^ mask) for i in range(8)])  38.9 us
    pallas_call x8, Pallas kernels, call(): pl.pallas_call(body, out_shape=tuple((jax.ShapeDtypeStruct(shape, dtype)...  30.9 us
    all_to_all x6, waiting for transfers between devices, exchange(): return lax.all_to_all(blocks, axis, split_axis=0, concat_axis=0, tiled=True)  24.3 us
    all_to_all x6, starting transfers between devices, exchange(): return lax.all_to_all(blocks, axis, split_axis=0, concat_axis=0, tiled=True)  23.2 us
    ppermute x13, waiting for transfers between devices, swap_u(): return lax.ppermute(values, 'ulysses', [(i, i ^ mask) for i in range(4)])  22.5 us
    pallas_call x1, Pallas kernels, attn_bwd(): pl.pallas_call(attn_bwd_kernel, out_shape=jax.ShapeDtypeStruct((nb, rows3...  13.8 us
    all_to_all x1, blocking collectives, exchange(): return lax.all_to_all(blocks, axis, split_axis=0, concat_axis=0, tiled=True)  11.8 us
  transfers between devices with their start and end apart: 50, of which 23 were waited for; matrix products, arithmetic and copies ran while one was open for 7% of the time, Pallas kernels for 10%

profile of v2, /device:TPU:0, one launch (start us, length us, event | category | flops | bytes accessed | tf_op | source)
XLA Modules:
  0.0 279.2 jit_solution(6529825866184688020)
XLA Ops:
  7.2 2.3 pack.1
  9.6 3.1 %collective-permute-start = (bf16[96,768]{1,0:T(8,128)(2,1)}, bf16[96,768]{1,0:T(8,128)(2,1)S(1)}, u32[]{:S(2)}, u32[]{:S(2)}) collective-permute-start(bf16[96,768]{1,0:T(8,128)(2,1)} %b0), channel_id=1, source_target_pairs={{0,2},{1,3},{2,0},{3,1},{4,6},{5,7},{6,4},{7,5},{8,10},{9,11},{10,... | collective-permute-start | bytes 442376 | tf_op jit(solution)/shard_map/ppermute | solution.py:857
  12.7 2.6 collective-permute-start.1
  15.3 3.5 %all-to-all-start = ((bf16[4,24,1408]{2,1,0:T(8,128)(2,1)}), bf16[4,24,1408]{2,1,0:T(8,128)(2,1)S(1)}, u32[]{:S(2)}, u32[]{:S(2)}) async-start(bf16[4,24,1408]{2,1,0:T(8,128)(2,1)} %get-tuple-element.98), calls=%async_computation | async-start | bytes 540672 | tf_op jit(solution)/shard_map/all_to_all | solution.py:861
  21.1 6.5 %all-to-all-done = bf16[4,24,1408]{2,1,0:T(8,128)(2,1)S(1)} async-done(((bf16[4,24,1408]{2,1,0:T(8,128)(2,1)}), bf16[4,24,1408]{2,1,0:T(8,128)(2,1)S(1)}, u32[]{:S(2)}, u32[]{:S(2)}) %all-to-all-start) | async-done | bytes 270368 | tf_op jit(solution)/shard_map/all_to_all | solution.py:861
  27.7 1.5 collective-permute-start.4
  29.2 3.1 %collective-permute-start.6 = (bf16[96,832]{1,0:T(8,128)(2,1)S(1)}, bf16[96,832]{1,0:T(8,128)(2,1)S(1)}, u32[]{:S(2)}, u32[]{:S(2)}) collective-permute-start(bf16[96,832]{1,0:T(8,128)(2,1)S(1)} %maximum_maximum_fusion.a0), channel_id=1, source_target_pairs={{0,4},{1,5},{2,6},{3,7},{4,0},{5,1},{6,2},{7,3},{8,12},{9,13},{10,... | collective-permute-start | bytes 479240 | tf_op jit(solution)/shard_map/ppermute | solution.py:857
  32.3 1.7 collective-permute-start.3
  34.0 1.7 collective-permute-done.4.a2
  35.7 2.1 collective-permute-start.5
  37.9 7.0 %collective-permute-done.6.a4 = bf16[96,832]{1,0:T(8,128)(2,1)S(1)} collective-permute-done((bf16[96,832]{1,0:T(8,128)(2,1)S(1)}, bf16[96,832]{1,0:T(8,128)(2,1)S(1)}, u32[]{:S(2)}, u32[]{:S(2)}) %collective-permute-start.6) | collective-permute-done | bytes 159776 | tf_op jit(solution)/shard_map/ppermute | solution.py:857
  44.9 1.5 collective-permute-start.7
  47.0 3.4 %collective-permute-done.7.a5 = bf16[96,832]{1,0:T(8,128)(2,1)S(1)} collective-permute-done((bf16[96,832]{1,0:T(8,128)(2,1)S(1)}, bf16[96,832]{1,0:T(8,128)(2,1)S(1)}, u32[]{:S(2)}, u32[]{:S(2)}) %collective-permute-start.7) | collective-permute-done | bytes 159776 | tf_op jit(solution)/shard_map/ppermute | solution.py:857
  50.3 1.8 collective-permute-done.9.a7
  52.8 4.9 %first.1 = (bf16[8,384,128]{2,1,0:T(8,128)(2,1)}, bf16[512,768]{1,0:T(8,128)(2,1)}, f32[2,5376]{1,0:T(2,128)}, bf16[768,576]{1,0:T(8,128)(2,1)}, bf16[192,768]{1,0:T(8,128)(2,1)}) custom-call(s32[2]{0:T(128)} %pad_add_fusion.at_ref, bf16[4,2,2,64,768]{4,3,2,1,0:T(8,128)(2,1)} %bitcast.73, f32[256,128]{1,0:T(8,128)} %get-tuple-element.101.cos_ref, ...), custom_call_target="tpu_custom_call" | custom-call | flops 452984 | bytes 5908 | tf_op jit(solution)/shard_map/first/pallas_call | solution.py:835
  57.7 5.2 %all-to-all-start.1 = ((bf16[8,384,128]{2,1,0:T(8,128)(2,1)}), bf16[8,384,128]{2,1,0:T(8,128)(2,1)S(1)}, u32[]{:S(2)}, u32[]{:S(2)}) async-start(bf16[8,384,128]{2,1,0:T(8,128)(2,1)} %get-tuple-element.110), calls=%async_computation.1 | async-start | bytes 1572864 | tf_op jit(solution)/shard_map/all_to_all | solution.py:861
  63.0 2.0 collective-permute-start.10
  65.1 1.9 collective-permute-start.16
  67.2 8.0 %collective-permute-done.10.b1 = bf16[96,768]{1,0:T(8,128)(2,1)S(1)} collective-permute-done((bf16[96,768]{1,0:T(8,128)(2,1)S(1)}, bf16[96,768]{1,0:T(8,128)(2,1)S(1)}, u32[]{:S(2)}, u32[]{:S(2)}) %collective-permute-start.10) | collective-permute-done | bytes 147488 | tf_op jit(solution)/shard_map/ppermute | solution.py:857
  75.2 4.2 %collective-permute-done.11.b3 = bf16[96,768]{1,0:T(8,128)(2,1)S(1)} collective-permute-done((bf16[96,768]{1,0:T(8,128)(2,1)S(1)}, bf16[96,768]{1,0:T(8,128)(2,1)S(1)}, u32[]{:S(2)}, u32[]{:S(2)}) %collective-permute-start.11) | collective-permute-done | bytes 147488 | tf_op jit(solution)/shard_map/ppermute | solution.py:857
  80.6 1.3 collective-permute-start.12
  81.9 1.5 collective-permute-start.13
  83.4 1.6 collective-permute-start.14
  84.9 1.2 collective-permute-start.15
  86.2 7.9 %attn_fwd.1 = (bf16[8,128,128]{2,1,0:T(8,128)(2,1)S(1)}, f32[8,128,128]{2,1,0:T(8,128)S(1)}, f32[8,8,256]{2,1,0:T(8,128)S(1)}) custom-call(bf16[8,384,128]{2,1,0:T(8,128)(2,1)S(1)} %all-to-all-done.1.x_ref), custom_call_target="tpu_custom_call" | custom-call | flops 1073741824 | bytes 2097152 | tf_op jit(solution)/shard_map/attn_fwd/pallas_call | solution.py:42
  94.2 11.8 %all_to_all.35.t_ref = bf16[8,128,128]{2,1,0:T(8,128)(2,1)S(1)} all-to-all(bf16[8,128,128]{2,1,0:T(8,128)(2,1)S(1)} %get-tuple-element.120), channel_id=1, replica_groups=mesh['ulysses'=4,'blk'=8] {'blk'}, dimensions={0} | all-to-all | bytes 524288 | tf_op jit(solution)/shard_map/all_to_all | solution.py:861
  106.6 1.7 collective-permute-done.18
  108.7 2.0 collective-permute-start.21
  110.8 4.6 %collective-permute-done.20.a3 = bf16[96,768]{1,0:T(8,128)(2,1)S(1)} collective-permute-done((bf16[96,768]{1,0:T(8,128)(2,1)S(1)}, bf16[96,768]{1,0:T(8,128)(2,1)S(1)}, u32[]{:S(2)}, u32[]{:S(2)}) %collective-permute-start.20) | collective-permute-done | bytes 147488 | tf_op jit(solution)/shard_map/ppermute | solution.py:857
  115.4 3.2 %collective-permute-done.21.a5 = bf16[96,768]{1,0:T(8,128)(2,1)S(1)} collective-permute-done((bf16[96,768]{1,0:T(8,128)(2,1)S(1)}, bf16[96,768]{1,0:T(8,128)(2,1)S(1)}, u32[]{:S(2)}, u32[]{:S(2)}) %collective-permute-start.21) | collective-permute-done | bytes 147488 | tf_op jit(solution)/shard_map/ppermute | solution.py:857
  118.5 2.2 collective-permute-done.22.a7
  121.0 1.7 collective-permute-done.23.got_ref
  123.5 9.6 %ff.1 = (bf16[2,2,64,768]{3,2,1,0:T(8,128)(2,1)}, f32[2,2,64,768]{3,2,1,0:T(8,128)}, bf16[2,2,64,768]{3,2,1,0:T(8,128)(2,1)}, f32[2,2,64,768]{3,2,1,0:T(8,128)},...) custom-call(s32[2]{0:T(128)} %pad_add_fusion.at_ref, ...), custom_call_target="tpu_custom_call" | custom-call | flops 3623878 | bytes 9498 | tf_op jit(solution)/shard_map/ff/pallas_call | solution.py:835
  133.7 1.3 collective-permute-done.24
  135.0 2.0 fusion.1
  137.1 1.7 collective-permute-start.25
  142.1 6.4 %collective-permute-done.25 = bf16[2,2,64,768]{3,2,1,0:T(8,128)(2,1)} collective-permute-done((bf16[2,2,64,768]{3,2,1,0:T(8,128)(2,1)}, bf16[2,2,64,768]{3,2,1,0:T(8,128)(2,1)}, u32[]{:S(2)}, u32[]{:S(2)}) %collective-permute-start.25) | collective-permute-done | bytes 393248 | tf_op jit(solution)/shard_map/ppermute | solution.py:853
  149.8 1.7 collective-permute-start.31
  151.5 5.4 %collective-permute-done.27 = bf16[4,4,24,768]{3,2,1,0:T(8,128)(2,1)} collective-permute-done((bf16[4,4,24,768]{3,2,1,0:T(8,128)(2,1)}, bf16[4,4,24,768]{3,2,1,0:T(8,128)(2,1)}, u32[]{:S(2)}, u32[]{:S(2)}) %collective-permute-start.27) | collective-permute-done | bytes 589856 | tf_op jit(solution)/shard_map/ppermute | solution.py:857
  156.9 2.5 convert_add_fusion
  160.2 4.4 %middle_back.1 = (bf16[8,128,128]{2,1,0:T(8,128)(2,1)}, f32[2,64,768]{2,1,0:T(8,128)}, f32[2,1,768]{2,1,0:T(1,128)}, bf16[4,24,768]{2,1,0:T(8,128)(2,1)}, bf16[4,24,768]{2,1,0:T(8,128)(2,1)}) custom-call(s32[2]{0:T(128)} %pad_add_fusion.at_ref, bf16[4,2,2,64,768]{4,3,2,1,0:T(8,128)(2,1)} %bitcast.75, bf16[2,2,64,768]{3,2,1,0:T(8,128)(2,1)} %copy-done.6, ...), custom_call_target="tpu_custom_call" | custom-call | flops 301989 | bytes 4636 | tf_op jit(solution)/shard_map/middle_back/pallas_call | solution.py:835
  164.6 3.8 %all-to-all-start.3 = ((bf16[8,128,128]{2,1,0:T(8,128)(2,1)}), bf16[8,128,128]{2,1,0:T(8,128)(2,1)S(1)}, u32[]{:S(2)}, u32[]{:S(2)}) async-start(bf16[8,128,128]{2,1,0:T(8,128)(2,1)} %get-tuple-element.149), calls=%async_computation.3 | async-start | bytes 524288 | tf_op jit(solution)/shard_map/all_to_all | solution.py:861
  168.4 1.8 slice_bitcast_fusion.5
  170.1 1.7 collective-permute-start.28
  171.8 2.4 collective-permute-start.32
  174.5 1.7 collective-permute-start.29
  176.2 1.6 fusion.4
  177.8 2.3 collective-permute-done.28
  180.8 13.8 %attn_bwd.1 = bf16[8,384,128]{2,1,0:T(8,128)(2,1)} custom-call(bf16[8,384,128]{2,1,0:T(8,128)(2,1)S(1)} %all-to-all-done.1.x_ref, bf16[8,128,128]{2,1,0:T(8,128)(2,1)S(1)} %all-to-all-done.3.d_ref, f32[8,128,128]{2,1,0:T(8,128)S(1)} %get-tuple-element.154.of_ref, f32[8,8,256]{2,1,0:T(8,128)S(1)} %get-tuple-element.155.lse_ref), custom_call_target="tpu_custom_call" | custom-call | flops 268435456 | bytes 262144 | tf_op jit(solution)/shard_map/attn_bwd/pallas_call | solution.py:91
  194.6 1.2 fusion.8
  195.8 5.1 %all-to-all-start.4 = ((bf16[8,384,128]{2,1,0:T(8,128)(2,1)}), bf16[8,384,128]{2,1,0:T(8,128)(2,1)S(1)}, u32[]{:S(2)}, u32[]{:S(2)}) async-start(bf16[8,384,128]{2,1,0:T(8,128)(2,1)} %attn_bwd.1), calls=%async_computation.4 | async-start | bytes 1572864 | tf_op jit(solution)/shard_map/all_to_all | solution.py:861
  201.9 2.1 collective-permute-start.37
  204.0 2.4 collective-permute-start.38
  207.6 6.3 %collective-permute-done.37 = bf16[24,768]{1,0:T(8,128)(2,1)S(1)} collective-permute-done((bf16[24,768]{1,0:T(8,128)(2,1)S(1)}, bf16[24,768]{1,0:T(8,128)(2,1)S(1)}, u32[]{:S(2)}, u32[]{:S(2)}) %collective-permute-start.37) | collective-permute-done | bytes 36896 | tf_op jit(solution)/shard_map/ppermute | solution.py:857
  214.0 7.9 %collective-permute-done.38 = bf16[24,768]{1,0:T(8,128)(2,1)S(1)} collective-permute-done((bf16[24,768]{1,0:T(8,128)(2,1)S(1)}, bf16[24,768]{1,0:T(8,128)(2,1)S(1)}, u32[]{:S(2)}, u32[]{:S(2)}) %collective-permute-start.38) | collective-permute-done | bytes 36896 | tf_op jit(solution)/shard_map/ppermute | solution.py:857
  223.6 5.8 %first_back.1 = (bf16[2,2,64,768]{3,2,1,0:T(8,128)(2,1)}, f32[2,2,64,768]{3,2,1,0:T(8,128)}, bf16[32,24,640]{2,1,0:T(8,128)(2,1)}) custom-call(s32[2]{0:T(128)} %pad_add_fusion.at_ref, bf16[8,384,128]{2,1,0:T(8,128)(2,1)} %copy-done.9, bf16[4,2,2,64,768]{4,3,2,1,0:T(8,128)(2,1)} %bitcast.76, f32[2,5376]{1,0:T(2,128)} %get-tuple-element.129.table_ref, ...), custom_call_target="tpu_custom_call" | custom-call | flops 905969 | bytes 6522 | tf_op jit(solution)/shard_map/first_back/pallas_call | solution.py:835
  229.4 3.1 %all-to-all-start.5 = ((bf16[32,24,640]{2,1,0:T(8,128)(2,1)}), bf16[32,24,640]{2,1,0:T(8,128)(2,1)S(1)}, u32[]{:S(2)}, u32[]{:S(2)}) async-start(bf16[32,24,640]{2,1,0:T(8,128)(2,1)} %get-tuple-element.174), calls=%async_computation.6 | async-start | bytes 1966080 | tf_op jit(solution)/shard_map/all_to_all | solution.py:861
  234.5 1.8 collective-permute-start.41
  236.3 10.6 %collective-permute-done.41.got_ref = bf16[2,64,768]{2,1,0:T(8,128)(2,1)S(1)} collective-permute-done((bf16[2,64,768]{2,1,0:T(8,128)(2,1)S(1)}, bf16[2,64,768]{2,1,0:T(8,128)(2,1)S(1)}, u32[]{:S(2)}, u32[]{:S(2)}) %collective-permute-start.41) | collective-permute-done | bytes 196640 | tf_op jit(solution)/shard_map/ppermute | solution.py:853
  248.0 10.7 %all-to-all-done.5.raw_ref = bf16[32,24,640]{2,1,0:T(8,128)(2,1)S(1)} async-done(((bf16[32,24,640]{2,1,0:T(8,128)(2,1)}), bf16[32,24,640]{2,1,0:T(8,128)(2,1)S(1)}, u32[]{:S(2)}, u32[]{:S(2)}) %all-to-all-start.5) | async-done | bytes 983072 | tf_op jit(solution)/shard_map/all_to_all | solution.py:861
  259.7 2.4 row_grad.1
  262.1 2.5 all-to-all-start.6
  264.6 1.3 slice_bitcast_fusion.15
  265.9 5.9 %all-to-all-done.6 = f32[32,2,128]{2,1,0:T(2,128)S(1)} async-done(((f32[32,2,128]{2,1,0:T(2,128)}), f32[32,2,128]{2,1,0:T(2,128)S(1)}, u32[]{:S(2)}, u32[]{:S(2)}) %all-to-all-start.6) | async-done | bytes 32800 | tf_op jit(solution)/shard_map/all_to_all | solution.py:861
  (186 shorter events, 22.5 us)
Async XLA Ops:
  7.2 45.0 %all-gather.3.cloned.1.call-start = ((), (), s32[]{:S(2)}) async-start(), calls=%async_computation.9 | async-start | bytes 1966080 | tf_op jit(solution)/shard_map/all_gather | solution.py:920
  9.6 18.1 %collective-permute-start = (bf16[96,768]{1,0:T(8,128)(2,1)}, bf16[96,768]{1,0:T(8,128)(2,1)S(1)}, u32[]{:S(2)}, u32[]{:S(2)}) collective-permute-start(bf16[96,768]{1,0:T(8,128)(2,1)} %b0), channel_id=1, source_target_pairs={{0,2},{1,3},{2,0},{3,1},{4,6},{5,7},{6,4},{7,5},{8,10},{9,11},{10,... | collective-permute-start | bytes 442376 | tf_op jit(solution)/shard_map/ppermute | solution.py:857
  12.7 15.0 %collective-permute-start.1 = (bf16[96,768]{1,0:T(8,128)(2,1)}, bf16[96,768]{1,0:T(8,128)(2,1)S(1)}, u32[]{:S(2)}, u32[]{:S(2)}) collective-permute-start(bf16[96,768]{1,0:T(8,128)(2,1)} %b0), channel_id=1, source_target_pairs={{0,4},{1,5},{2,6},{3,7},{4,0},{5,1},{6,2},{7,3},{8,12},{9,13},{10,... | collective-permute-start | bytes 442376 | tf_op jit(solution)/shard_map/ppermute | solution.py:857
  15.3 12.4 %collective-permute-start.2 = (bf16[96,768]{1,0:T(8,128)(2,1)}, bf16[96,768]{1,0:T(8,128)(2,1)S(1)}, u32[]{:S(2)}, u32[]{:S(2)}) collective-permute-start(bf16[96,768]{1,0:T(8,128)(2,1)} %b0), channel_id=1, source_target_pairs={{0,6},{1,7},{2,4},{3,5},{4,2},{5,3},{6,0},{7,1},{8,14},{9,15},{10,... | collective-permute-start | bytes 442376 | tf_op jit(solution)/shard_map/ppermute | solution.py:857
  15.3 12.3 %all-to-all-start = ((bf16[4,24,1408]{2,1,0:T(8,128)(2,1)}), bf16[4,24,1408]{2,1,0:T(8,128)(2,1)S(1)}, u32[]{:S(2)}, u32[]{:S(2)}) async-start(bf16[4,24,1408]{2,1,0:T(8,128)(2,1)} %get-tuple-element.98), calls=%async_computation | async-start | bytes 540672 | tf_op jit(solution)/shard_map/all_to_all | solution.py:861
  27.6 24.5 %copy-start.15 = (bf16[96,832]{1,0:T(8,128)(2,1)}, bf16[96,832]{1,0:T(8,128)(2,1)S(1)}, u32[]{:S(2)}) copy-start(bf16[96,832]{1,0:T(8,128)(2,1)S(1)} %maximum_maximum_fusion.a0) | copy-start | bytes 479236
  27.7 66.4 %copy-start.28 = (bf16[96,768]{1,0:T(8,128)(2,1)}, bf16[96,768]{1,0:T(8,128)(2,1)S(1)}, u32[]{:S(2)}) copy-start(bf16[96,768]{1,0:T(8,128)(2,1)S(1)} %collective-permute-done.b2) | copy-start | bytes 442372
  27.7 66.3 %copy-start.29 = (bf16[96,768]{1,0:T(8,128)(2,1)}, bf16[96,768]{1,0:T(8,128)(2,1)S(1)}, u32[]{:S(2)}) copy-start(bf16[96,768]{1,0:T(8,128)(2,1)S(1)} %collective-permute-done.1.b4) | copy-start | bytes 442372
  27.7 66.3 %copy-start.30 = (bf16[96,768]{1,0:T(8,128)(2,1)}, bf16[96,768]{1,0:T(8,128)(2,1)S(1)}, u32[]{:S(2)}) copy-start(bf16[96,768]{1,0:T(8,128)(2,1)S(1)} %collective-permute-done.2.b6) | copy-start | bytes 442372
  27.7 8.0 %collective-permute-start.4 = (bf16[96,832]{1,0:T(8,128)(2,1)S(1)}, bf16[96,832]{1,0:T(8,128)(2,1)S(1)}, u32[]{:S(2)}, u32[]{:S(2)}) collective-permute-start(bf16[96,832]{1,0:T(8,128)(2,1)S(1)} %maximum_maximum_fusion.a0), channel_id=1, source_target_pairs={{0,2},{1,3},{2,0},{3,1},{4,6},{5,7},{6,4},{7,5},{8,10},{9,11},{10,... | collective-permute-start | bytes 479240 | tf_op jit(solution)/shard_map/ppermute | solution.py:857
  29.2 15.7 %collective-permute-start.6 = (bf16[96,832]{1,0:T(8,128)(2,1)S(1)}, bf16[96,832]{1,0:T(8,128)(2,1)S(1)}, u32[]{:S(2)}, u32[]{:S(2)}) collective-permute-start(bf16[96,832]{1,0:T(8,128)(2,1)S(1)} %maximum_maximum_fusion.a0), channel_id=1, source_target_pairs={{0,4},{1,5},{2,6},{3,7},{4,0},{5,1},{6,2},{7,3},{8,12},{9,13},{10,... | collective-permute-start | bytes 479240 | tf_op jit(solution)/shard_map/ppermute | solution.py:857
  32.3 14.2 %collective-permute-start.8 = (bf16[96,832]{1,0:T(8,128)(2,1)S(1)}, bf16[96,832]{1,0:T(8,128)(2,1)S(1)}, u32[]{:S(2)}, u32[]{:S(2)}) collective-permute-start(bf16[96,832]{1,0:T(8,128)(2,1)S(1)} %maximum_maximum_fusion.a0), channel_id=1, source_target_pairs={{0,6},{1,7},{2,4},{3,5},{4,2},{5,3},{6,0},{7,1},{8,14},{9,15},{10,... | collective-permute-start | bytes 479240 | tf_op jit(solution)/shard_map/ppermute | solution.py:857
  32.3 14.7 %collective-permute-start.3 = (bf16[96,832]{1,0:T(8,128)(2,1)S(1)}, bf16[96,832]{1,0:T(8,128)(2,1)S(1)}, u32[]{:S(2)}, u32[]{:S(2)}) collective-permute-start(bf16[96,832]{1,0:T(8,128)(2,1)S(1)} %maximum_maximum_fusion.a0), channel_id=1, source_target_pairs={{0,1},{1,0},{2,3},{3,2},{4,5},{5,4},{6,7},{7,6},{8,9},{9,8},{10,11... | collective-permute-start | bytes 479240 | tf_op jit(solution)/shard_map/ppermute | solution.py:857
  35.7 16.4 %copy-start.20 = (bf16[96,832]{1,0:T(8,128)(2,1)}, bf16[96,832]{1,0:T(8,128)(2,1)S(1)}, u32[]{:S(2)}) copy-start(bf16[96,832]{1,0:T(8,128)(2,1)S(1)} %collective-permute-done.4.a2) | copy-start | bytes 479236
  35.7 11.2 %collective-permute-start.5 = (bf16[96,832]{1,0:T(8,128)(2,1)S(1)}, bf16[96,832]{1,0:T(8,128)(2,1)S(1)}, u32[]{:S(2)}, u32[]{:S(2)}) collective-permute-start(bf16[96,832]{1,0:T(8,128)(2,1)S(1)} %collective-permute-done.4.a2), channel_id=1, source_target_pairs={{0,1},{1,0},{2,3},{3,2},{4,5},{5,4},{6,7},{7,6},{8,9},{9,8},{10,11... | collective-permute-start | bytes 479240 | tf_op jit(solution)/shard_map/ppermute | solution.py:857
  44.9 5.4 %collective-permute-start.7 = (bf16[96,832]{1,0:T(8,128)(2,1)S(1)}, bf16[96,832]{1,0:T(8,128)(2,1)S(1)}, u32[]{:S(2)}, u32[]{:S(2)}) collective-permute-start(bf16[96,832]{1,0:T(8,128)(2,1)S(1)} %collective-permute-done.6.a4), channel_id=1, source_target_pairs={{0,1},{1,0},{2,3},{3,2},{4,5},{5,4},{6,7},{7,6},{8,9},{9,8},{10,11... | collective-permute-start | bytes 479240 | tf_op jit(solution)/shard_map/ppermute | solution.py:857
  46.4 5.7 %collective-permute-start.9 = (bf16[96,832]{1,0:T(8,128)(2,1)S(1)}, bf16[96,832]{1,0:T(8,128)(2,1)S(1)}, u32[]{:S(2)}, u32[]{:S(2)}) collective-permute-start(bf16[96,832]{1,0:T(8,128)(2,1)S(1)} %collective-permute-done.8.a6), channel_id=1, source_target_pairs={{0,1},{1,0},{2,3},{3,2},{4,5},{5,4},{6,7},{7,6},{8,9},{9,8},{10,11... | collective-permute-start | bytes 479240 | tf_op jit(solution)/shard_map/ppermute | solution.py:857
  57.7 22.9 %all-to-all-start.1 = ((bf16[8,384,128]{2,1,0:T(8,128)(2,1)}), bf16[8,384,128]{2,1,0:T(8,128)(2,1)S(1)}, u32[]{:S(2)}, u32[]{:S(2)}) async-start(bf16[8,384,128]{2,1,0:T(8,128)(2,1)} %get-tuple-element.110), calls=%async_computation.1 | async-start | bytes 1572864 | tf_op jit(solution)/shard_map/all_to_all | solution.py:861
  62.9 159.7 %reduce-scatter.2.cloned.1.call-start = ((), (), s32[]{:S(2)}) async-start(), calls=%async_computation.8 | async-start | bytes 1327104 | tf_op jit(solution)/shard_map/reduce_scatter | solution.py:977
  63.0 12.2 %collective-permute-start.10 = (bf16[96,768]{1,0:T(8,128)(2,1)S(1)}, bf16[96,768]{1,0:T(8,128)(2,1)S(1)}, u32[]{:S(2)}, u32[]{:S(2)}) collective-permute-start(bf16[96,768]{1,0:T(8,128)(2,1)S(1)} %copy-done.27), channel_id=1, source_target_pairs={{0,1},{1,0},{2,3},{3,2},{4,5},{5,4},{6,7},{7,6},{8,9},{9,8},{10,11... | collective-permute-start | bytes 442376 | tf_op jit(solution)/shard_map/ppermute | solution.py:857
  65.0 14.4 %collective-permute-start.11 = (bf16[96,768]{1,0:T(8,128)(2,1)S(1)}, bf16[96,768]{1,0:T(8,128)(2,1)S(1)}, u32[]{:S(2)}, u32[]{:S(2)}) collective-permute-start(bf16[96,768]{1,0:T(8,128)(2,1)S(1)} %collective-permute-done.b2), channel_id=1, source_target_pairs={{0,1},{1,0},{2,3},{3,2},{4,5},{5,4},{6,7},{7,6},{8,9},{9,8},{10,11... | collective-permute-start | bytes 442376 | tf_op jit(solution)/shard_map/ppermute | solution.py:857
  65.1 19.9 %collective-permute-start.16 = (bf16[96,768]{1,0:T(8,128)(2,1)S(1)}, bf16[96,768]{1,0:T(8,128)(2,1)S(1)}, u32[]{:S(2)}, u32[]{:S(2)}) collective-permute-start(bf16[96,768]{1,0:T(8,128)(2,1)S(1)} %collective-permute-done.1.b4), channel_id=1, source_target_pairs={{0,1},{1,0},{2,3},{3,2},{4,5},{5,4},{6,7},{7,6},{8,9},{9,8},{10,11... | collective-permute-start | bytes 442376 | tf_op jit(solution)/shard_map/ppermute | solution.py:857
  67.1 27.0 %copy-start.16 = (bf16[96,768]{1,0:T(8,128)(2,1)}, bf16[96,768]{1,0:T(8,128)(2,1)S(1)}, u32[]{:S(2)}) copy-start(bf16[96,768]{1,0:T(8,128)(2,1)S(1)} %slice.117.a0) | copy-start | bytes 442372
  67.1 39.0 %copy-start.1 = (bf16[192,768]{1,0:T(8,128)(2,1)S(1)}, bf16[192,768]{1,0:T(8,128)(2,1)}, u32[]{:S(2)}) copy-start(bf16[192,768]{1,0:T(8,128)(2,1)} %get-tuple-element.121.w_ref) | copy-start | bytes 884740
  67.1 27.0 %collective-permute-start.17 = (bf16[96,768]{1,0:T(8,128)(2,1)S(1)}, bf16[96,768]{1,0:T(8,128)(2,1)S(1)}, u32[]{:S(2)}, u32[]{:S(2)}) collective-permute-start(bf16[96,768]{1,0:T(8,128)(2,1)S(1)} %collective-permute-done.2.b6), channel_id=1, source_target_pairs={{0,1},{1,0},{2,3},{3,2},{4,5},{5,4},{6,7},{7,6},{8,9},{9,8},{10,11... | collective-permute-start | bytes 442376 | tf_op jit(solution)/shard_map/ppermute | solution.py:857
  75.2 18.9 %copy-start.31 = (bf16[96,768]{1,0:T(8,128)(2,1)}, bf16[96,768]{1,0:T(8,128)(2,1)S(1)}, u32[]{:S(2)}) copy-start(bf16[96,768]{1,0:T(8,128)(2,1)S(1)} %collective-permute-done.10.b1) | copy-start | bytes 442372
  79.4 14.7 %copy-start.32 = (bf16[96,768]{1,0:T(8,128)(2,1)}, bf16[96,768]{1,0:T(8,128)(2,1)S(1)}, u32[]{:S(2)}) copy-start(bf16[96,768]{1,0:T(8,128)(2,1)S(1)} %collective-permute-done.11.b3) | copy-start | bytes 442372
  80.6 13.6 %collective-permute-start.12 = (bf16[96,768]{1,0:T(8,128)(2,1)S(1)}, bf16[96,768]{1,0:T(8,128)(2,1)S(1)}, u32[]{:S(2)}, u32[]{:S(2)}) collective-permute-start(bf16[96,768]{1,0:T(8,128)(2,1)S(1)} %slice.117.a0), channel_id=1, source_target_pairs={{0,2},{1,3},{2,0},{3,1},{4,6},{5,7},{6,4},{7,5},{8,10},{9,11},{10,... | collective-permute-start | bytes 442376 | tf_op jit(solution)/shard_map/ppermute | solution.py:857
  81.9 12.2 %collective-permute-start.13 = (bf16[96,768]{1,0:T(8,128)(2,1)S(1)}, bf16[96,768]{1,0:T(8,128)(2,1)S(1)}, u32[]{:S(2)}, u32[]{:S(2)}) collective-permute-start(bf16[96,768]{1,0:T(8,128)(2,1)S(1)} %slice.117.a0), channel_id=1, source_target_pairs={{0,4},{1,5},{2,6},{3,7},{4,0},{5,1},{6,2},{7,3},{8,12},{9,13},{10,... | collective-permute-start | bytes 442376 | tf_op jit(solution)/shard_map/ppermute | solution.py:857
  83.4 10.8 %collective-permute-start.14 = (bf16[96,768]{1,0:T(8,128)(2,1)S(1)}, bf16[96,768]{1,0:T(8,128)(2,1)S(1)}, u32[]{:S(2)}, u32[]{:S(2)}) collective-permute-start(bf16[96,768]{1,0:T(8,128)(2,1)S(1)} %slice.117.a0), channel_id=1, source_target_pairs={{0,6},{1,7},{2,4},{3,5},{4,2},{5,3},{6,0},{7,1},{8,14},{9,15},{10,... | collective-permute-start | bytes 442376 | tf_op jit(solution)/shard_map/ppermute | solution.py:857
  84.9 9.2 %collective-permute-start.15 = (bf16[96,768]{1,0:T(8,128)(2,1)S(1)}, bf16[96,768]{1,0:T(8,128)(2,1)S(1)}, u32[]{:S(2)}, u32[]{:S(2)}) collective-permute-start(bf16[96,768]{1,0:T(8,128)(2,1)S(1)} %slice.117.a0), channel_id=1, source_target_pairs={{0,1},{1,0},{2,3},{3,2},{4,5},{5,4},{6,7},{7,6},{8,9},{9,8},{10,11... | collective-permute-start | bytes 442376 | tf_op jit(solution)/shard_map/ppermute | solution.py:857
  94.1 14.5 %copy-start.35 = (bf16[96,768]{1,0:T(8,128)(2,1)}, bf16[96,768]{1,0:T(8,128)(2,1)S(1)}, u32[]{:S(2)}) copy-start(bf16[96,768]{1,0:T(8,128)(2,1)S(1)} %collective-permute-done.12.a2) | copy-start | bytes 442372
  94.1 14.5 %copy-start.36 = (bf16[96,768]{1,0:T(8,128)(2,1)}, bf16[96,768]{1,0:T(8,128)(2,1)S(1)}, u32[]{:S(2)}) copy-start(bf16[96,768]{1,0:T(8,128)(2,1)S(1)} %collective-permute-done.13.a4) | copy-start | bytes 442372
  94.2 16.5 %copy-start.37 = (bf16[96,768]{1,0:T(8,128)(2,1)}, bf16[96,768]{1,0:T(8,128)(2,1)S(1)}, u32[]{:S(2)}) copy-start(bf16[96,768]{1,0:T(8,128)(2,1)S(1)} %collective-permute-done.14.a6) | copy-start | bytes 442372
  106.5 14.4 %copy-start.5 = (bf16[512,192]{1,0:T(8,128)(2,1)}, bf16[512,192]{1,0:T(8,128)(2,1)S(1)}, u32[]{:S(2)}) copy-start(bf16[512,192]{1,0:T(8,128)(2,1)S(1)} %get-tuple-element.148.att_ref) | copy-start | bytes 589828
  106.5 1.8 collective-permute-start.18
  108.4 12.4 %collective-permute-start.19 = (bf16[2,2,64,768]{3,2,1,0:T(8,128)(2,1)S(1)}, bf16[2,2,64,768]{3,2,1,0:T(8,128)(2,1)S(1)}, u32[]{:S(2)}, u32[]{:S(2)}) collective-permute-start(bf16[2,2,64,768]{3,2,1,0:T(8,128)(2,1)S(1)} %fusion), channel_id=1, source_target_pairs={{0,16},{8,24},{16,0},{24,8},{1,17},{9,25},{17,1},{25,9},{2,18},{10... | collective-permute-start | bytes 1179656 | tf_op jit(solution)/shard_map/ppermute | solution.py:853
  108.7 6.7 %collective-permute-start.20 = (bf16[96,768]{1,0:T(8,128)(2,1)S(1)}, bf16[96,768]{1,0:T(8,128)(2,1)S(1)}, u32[]{:S(2)}, u32[]{:S(2)}) collective-permute-start(bf16[96,768]{1,0:T(8,128)(2,1)S(1)} %collective-permute-done.12.a2), channel_id=1, source_target_pairs={{0,1},{1,0},{2,3},{3,2},{4,5},{5,4},{6,7},{7,6},{8,9},{9,8},{10,11... | collective-permute-start | bytes 442376 | tf_op jit(solution)/shard_map/ppermute | solution.py:857
  108.7 9.9 %collective-permute-start.21 = (bf16[96,768]{1,0:T(8,128)(2,1)S(1)}, bf16[96,768]{1,0:T(8,128)(2,1)S(1)}, u32[]{:S(2)}, u32[]{:S(2)}) collective-permute-start(bf16[96,768]{1,0:T(8,128)(2,1)S(1)} %collective-permute-done.13.a4), channel_id=1, source_target_pairs={{0,1},{1,0},{2,3},{3,2},{4,5},{5,4},{6,7},{7,6},{8,9},{9,8},{10,11... | collective-permute-start | bytes 442376 | tf_op jit(solution)/shard_map/ppermute | solution.py:857
  110.7 10.1 %collective-permute-start.22 = (bf16[96,768]{1,0:T(8,128)(2,1)S(1)}, bf16[96,768]{1,0:T(8,128)(2,1)S(1)}, u32[]{:S(2)}, u32[]{:S(2)}) collective-permute-start(bf16[96,768]{1,0:T(8,128)(2,1)S(1)} %collective-permute-done.14.a6), channel_id=1, source_target_pairs={{0,1},{1,0},{2,3},{3,2},{4,5},{5,4},{6,7},{7,6},{8,9},{9,8},{10,11... | collective-permute-start | bytes 442376 | tf_op jit(solution)/shard_map/ppermute | solution.py:857
  120.9 1.8 collective-permute-start.23
  133.0 2.0 collective-permute-start.24
  133.3 7.0 %collective-permute-start.30 = (bf16[2,2,64,768]{3,2,1,0:T(8,128)(2,1)}, bf16[2,2,64,768]{3,2,1,0:T(8,128)(2,1)S(1)}, u32[]{:S(2)}, u32[]{:S(2)}) collective-permute-start(bf16[2,2,64,768]{3,2,1,0:T(8,128)(2,1)} %get-tuple-element.157), channel_id=1, source_target_pairs={{0,8},{8,0},{16,24},{24,16},{1,9},{9,1},{17,25},{25,17},{2,10},{10... | collective-permute-start | bytes 1179656 | tf_op jit(solution)/shard_map/ppermute | solution.py:853
  137.1 11.5 %collective-permute-start.25 = (bf16[2,2,64,768]{3,2,1,0:T(8,128)(2,1)}, bf16[2,2,64,768]{3,2,1,0:T(8,128)(2,1)}, u32[]{:S(2)}, u32[]{:S(2)}) collective-permute-start(bf16[2,2,64,768]{3,2,1,0:T(8,128)(2,1)} %fusion.1), channel_id=1, source_target_pairs={{0,16},{8,24},{16,0},{24,8},{1,17},{9,25},{17,1},{25,9},{2,18},{10... | collective-permute-start | bytes 1179656 | tf_op jit(solution)/shard_map/ppermute | solution.py:853
  139.9 17.0 %collective-permute-start.27 = (bf16[4,4,24,768]{3,2,1,0:T(8,128)(2,1)}, bf16[4,4,24,768]{3,2,1,0:T(8,128)(2,1)}, u32[]{:S(2)}, u32[]{:S(2)}) collective-permute-start(bf16[4,4,24,768]{3,2,1,0:T(8,128)(2,1)} %get-tuple-element.151), channel_id=1, source_target_pairs={{0,1},{1,0},{2,3},{3,2},{4,5},{5,4},{6,7},{7,6},{8,9},{9,8},{10,11... | collective-permute-start | bytes 1769480 | tf_op jit(solution)/shard_map/ppermute | solution.py:857
  142.1 14.8 %copy-start.17 = (bf16[4,4,24,768]{3,2,1,0:T(8,128)(2,1)S(1)}, bf16[4,4,24,768]{3,2,1,0:T(8,128)(2,1)}, u32[]{:S(2)}) copy-start(bf16[4,4,24,768]{3,2,1,0:T(8,128)(2,1)} %get-tuple-element.150) | copy-start | bytes 1769476
  149.7 9.7 %collective-permute-start.26 = (bf16[2,2,64,768]{3,2,1,0:T(8,128)(2,1)S(1)}, bf16[2,2,64,768]{3,2,1,0:T(8,128)(2,1)S(1)}, u32[]{:S(2)}, u32[]{:S(2)}) collective-permute-start(bf16[2,2,64,768]{3,2,1,0:T(8,128)(2,1)S(1)} %add_convert_fusion.down_ref), channel_id=1, source_target_pairs={{0,8},{8,0},{16,24},{24,16},{1,9},{9,1},{17,25},{25,17},{2,10},{10... | collective-permute-start | bytes 1179656 | tf_op jit(solution)/shard_map/ppermute | solution.py:853
  149.8 26.4 %collective-permute-start.31 = (bf16[2,64,768]{2,1,0:T(8,128)(2,1)S(1)}, bf16[2,64,768]{2,1,0:T(8,128)(2,1)S(1)}, u32[]{:S(2)}, u32[]{:S(2)}) collective-permute-start(bf16[2,64,768]{2,1,0:T(8,128)(2,1)S(1)} %fusion.9), channel_id=1, source_target_pairs={{0,16},{8,24},{16,0},{24,8},{1,17},{9,25},{17,1},{25,9},{2,18},{10... | collective-permute-start | bytes 589832 | tf_op jit(solution)/shard_map/ppermute | solution.py:853
  164.6 16.2 %all-to-all-start.3 = ((bf16[8,128,128]{2,1,0:T(8,128)(2,1)}), bf16[8,128,128]{2,1,0:T(8,128)(2,1)S(1)}, u32[]{:S(2)}, u32[]{:S(2)}) async-start(bf16[8,128,128]{2,1,0:T(8,128)(2,1)} %get-tuple-element.149), calls=%async_computation.3 | async-start | bytes 524288 | tf_op jit(solution)/shard_map/all_to_all | solution.py:861
  170.1 9.9 %collective-permute-start.28 = (bf16[4,24,768]{2,1,0:T(8,128)(2,1)S(1)}, bf16[4,24,768]{2,1,0:T(8,128)(2,1)S(1)}, u32[]{:S(2)}, u32[]{:S(2)}) collective-permute-start(bf16[4,24,768]{2,1,0:T(8,128)(2,1)S(1)} %get-tuple-element.190), channel_id=1, source_target_pairs={{0,2},{1,3},{2,0},{3,1},{4,6},{5,7},{6,4},{7,5},{8,10},{9,11},{10,... | collective-permute-start | bytes 442376 | tf_op jit(solution)/shard_map/ppermute | solution.py:857
  171.8 22.7 %collective-permute-start.32 = (bf16[4,24,768]{2,1,0:T(8,128)(2,1)}, bf16[4,24,768]{2,1,0:T(8,128)(2,1)}, u32[]{:S(2)}, u32[]{:S(2)}) collective-permute-start(bf16[4,24,768]{2,1,0:T(8,128)(2,1)} %get-tuple-element.188), channel_id=1, source_target_pairs={{0,4},{1,5},{2,6},{3,7},{4,0},{5,1},{6,2},{7,3},{8,12},{9,13},{10,... | collective-permute-start | bytes 442376 | tf_op jit(solution)/shard_map/ppermute | solution.py:857
  174.2 20.4 %collective-permute-start.33 = (bf16[4,24,768]{2,1,0:T(8,128)(2,1)S(1)}, bf16[4,24,768]{2,1,0:T(8,128)(2,1)}, u32[]{:S(2)}, u32[]{:S(2)}) collective-permute-start(bf16[4,24,768]{2,1,0:T(8,128)(2,1)S(1)} %get-tuple-element.189), channel_id=1, source_target_pairs={{0,6},{1,7},{2,4},{3,5},{4,2},{5,3},{6,0},{7,1},{8,14},{9,15},{10,... | collective-permute-start | bytes 442376 | tf_op jit(solution)/shard_map/ppermute | solution.py:857
  174.5 6.2 %collective-permute-start.29 = (bf16[4,24,768]{2,1,0:T(8,128)(2,1)}, bf16[4,24,768]{2,1,0:T(8,128)(2,1)}, u32[]{:S(2)}, u32[]{:S(2)}) collective-permute-start(bf16[4,24,768]{2,1,0:T(8,128)(2,1)} %get-tuple-element.152), channel_id=1, source_target_pairs={{0,1},{1,0},{2,3},{3,2},{4,5},{5,4},{6,7},{7,6},{8,9},{9,8},{10,11... | collective-permute-start | bytes 442376 | tf_op jit(solution)/shard_map/ppermute | solution.py:857
  195.8 26.8 %all-to-all-start.4 = ((bf16[8,384,128]{2,1,0:T(8,128)(2,1)}), bf16[8,384,128]{2,1,0:T(8,128)(2,1)S(1)}, u32[]{:S(2)}, u32[]{:S(2)}) async-start(bf16[8,384,128]{2,1,0:T(8,128)(2,1)} %attn_bwd.1), calls=%async_computation.4 | async-start | bytes 1572864 | tf_op jit(solution)/shard_map/all_to_all | solution.py:861
  201.9 12.1 %collective-permute-start.37 = (bf16[24,768]{1,0:T(8,128)(2,1)S(1)}, bf16[24,768]{1,0:T(8,128)(2,1)S(1)}, u32[]{:S(2)}, u32[]{:S(2)}) collective-permute-start(bf16[24,768]{1,0:T(8,128)(2,1)S(1)} %get-tuple-element.197), channel_id=1, source_target_pairs={{0,2},{1,3},{2,0},{3,1},{4,6},{5,7},{6,4},{7,5},{8,10},{9,11},{10,... | collective-permute-start | bytes 110600 | tf_op jit(solution)/shard_map/ppermute | solution.py:857
  204.0 17.9 %collective-permute-start.38 = (bf16[24,768]{1,0:T(8,128)(2,1)S(1)}, bf16[24,768]{1,0:T(8,128)(2,1)S(1)}, u32[]{:S(2)}, u32[]{:S(2)}) collective-permute-start(bf16[24,768]{1,0:T(8,128)(2,1)S(1)} %get-tuple-element.199), channel_id=1, source_target_pairs={{0,4},{1,5},{2,6},{3,7},{4,0},{5,1},{6,2},{7,3},{8,12},{9,13},{10,... | collective-permute-start | bytes 110600 | tf_op jit(solution)/shard_map/ppermute | solution.py:857
  206.3 15.6 %collective-permute-start.39 = (bf16[24,768]{1,0:T(8,128)(2,1)S(1)}, bf16[24,768]{1,0:T(8,128)(2,1)S(1)}, u32[]{:S(2)}, u32[]{:S(2)}) collective-permute-start(bf16[24,768]{1,0:T(8,128)(2,1)S(1)} %get-tuple-element.198), channel_id=1, source_target_pairs={{0,6},{1,7},{2,4},{3,5},{4,2},{5,3},{6,0},{7,1},{8,14},{9,15},{10,... | collective-permute-start | bytes 110600 | tf_op jit(solution)/shard_map/ppermute | solution.py:857
  207.1 15.5 %collective-permute-start.34 = (f32[24,768]{1,0:T(8,128)S(1)}, f32[24,768]{1,0:T(8,128)S(1)}, u32[]{:S(2)}, u32[]{:S(2)}) collective-permute-start(f32[24,768]{1,0:T(8,128)S(1)} %get-tuple-element.195), channel_id=1, source_target_pairs={{0,8},{8,0},{16,24},{24,16},{1,9},{9,1},{17,25},{25,17},{2,10},{10... | collective-permute-start | bytes 221192 | tf_op jit(solution)/shard_map/ppermute | solution.py:853
  207.1 15.5 %collective-permute-start.35 = (f32[24,768]{1,0:T(8,128)S(1)}, f32[24,768]{1,0:T(8,128)S(1)}, u32[]{:S(2)}, u32[]{:S(2)}) collective-permute-start(f32[24,768]{1,0:T(8,128)S(1)} %get-tuple-element.194), channel_id=1, source_target_pairs={{0,16},{8,24},{16,0},{24,8},{1,17},{9,25},{17,1},{25,9},{2,18},{10... | collective-permute-start | bytes 221192 | tf_op jit(solution)/shard_map/ppermute | solution.py:853
  213.9 8.6 %collective-permute-start.36 = (f32[24,768]{1,0:T(8,128)S(1)}, f32[24,768]{1,0:T(8,128)S(1)}, u32[]{:S(2)}, u32[]{:S(2)}) collective-permute-start(f32[24,768]{1,0:T(8,128)S(1)} %get-tuple-element.193), channel_id=1, source_target_pairs={{0,24},{8,16},{16,8},{24,0},{1,25},{9,17},{17,9},{25,1},{2,26},{10... | collective-permute-start | bytes 221192 | tf_op jit(solution)/shard_map/ppermute | solution.py:853
  229.4 29.3 %all-to-all-start.5 = ((bf16[32,24,640]{2,1,0:T(8,128)(2,1)}), bf16[32,24,640]{2,1,0:T(8,128)(2,1)S(1)}, u32[]{:S(2)}, u32[]{:S(2)}) async-start(bf16[32,24,640]{2,1,0:T(8,128)(2,1)} %get-tuple-element.174), calls=%async_computation.6 | async-start | bytes 1966080 | tf_op jit(solution)/shard_map/all_to_all | solution.py:861
  232.6 1.8 collective-permute-start.40
  234.5 12.5 %collective-permute-start.41 = (bf16[2,64,768]{2,1,0:T(8,128)(2,1)S(1)}, bf16[2,64,768]{2,1,0:T(8,128)(2,1)S(1)}, u32[]{:S(2)}, u32[]{:S(2)}) collective-permute-start(bf16[2,64,768]{2,1,0:T(8,128)(2,1)S(1)} %fusion.10), channel_id=1, source_target_pairs={{0,16},{8,24},{16,0},{24,8},{1,17},{9,25},{17,1},{25,9},{2,18},{10... | collective-permute-start | bytes 589832 | tf_op jit(solution)/shard_map/ppermute | solution.py:853
  262.1 9.7 %all-to-all-start.6 = ((f32[32,2,128]{2,1,0:T(2,128)}), f32[32,2,128]{2,1,0:T(2,128)S(1)}, u32[]{:S(2)}, u32[]{:S(2)}) async-start(f32[32,2,128]{2,1,0:T(2,128)} %get-tuple-element.179), calls=%async_computation.7 | async-start | bytes 65536 | tf_op jit(solution)/shard_map/all_to_all | solution.py:861
  (37 other events, 250.4 us)
Sparse Core Ops, SparseCore 0:
  10.2 24.5 all-gather.2
  140.4 62.4 reduce-scatter.1

commit v3 on v2

--- a/solution.py
+++ b/solution.py
@@ -20,20 +20,21 @@
         v_ref[j * rows : j * rows + half, :] = x_ref[j, rows:, :64]
         v_ref[j * rows + half : (j + 1) * rows, :] = x_ref[j, rows:, 64:]
 
-    def step(j, _):
-        q = x_ref[j, :rows, :64] * jnp.asarray(0.125, bf16)
+    for j in range(0, nb, 2):
+        q = x_ref[j : j + 2, :rows, :64].reshape(2 * rows, 64) * jnp.asarray(0.125, bf16)
         s = DOT(q, kt_ref[...])
         top = jnp.max(s, axis=1, keepdims=True)
         p = jnp.exp(s - top)
         total = jnp.sum(p, axis=1, keepdims=True)
         o = DOT(p.astype(bf16), v_ref[...]) / total
-        packed = jnp.concatenate([o[:half], o[half:]], axis=1)
-        of_ref[j] = packed
-        o_ref[j] = packed.astype(bf16)
-        lse = jnp.broadcast_to(top + jnp.log(total), (rows, 128)).T
-        lse_ref[j] = lse[:8]
-        return 0
-    lax.fori_loop(0, nb, step, 0, unroll=2)
+        lse = jnp.broadcast_to(top + jnp.log(total), (2 * rows, 128)).T
+        for i in range(2):
+            packed = jnp.concatenate(
+                [o[i * rows : i * rows + half], o[i * rows + half : (i + 1) * rows]], axis=1
+            )
+            of_ref[j + i] = packed
+            o_ref[j + i] = packed.astype(bf16)
+            lse_ref[j + i] = lse[:8, i * rows : (i + 1) * rows]
 
 def attn_fwd(x):
     nb, rows3, _ = x.shape
@@ -67,20 +68,23 @@
         lse_s[:, sl] = lse_ref[j]
     dqt_ref[...] = jnp.zeros_like(dqt_ref)
 
-    def step(j, _):
-        k = x_ref[j, :rows, 64:]
-        v = jnp.concatenate([x_ref[j, rows:, :64], x_ref[j, rows:, 64:]], axis=0)
+    for j in range(0, nb, 2):
+        k = x_ref[j : j + 2, :rows, 64:].reshape(2 * rows, 64)
+        v = jnp.concatenate(
+            [x_ref[j + i, rows:, lanes] for i in range(2) for lanes in (slice(0, 64), slice(64, 128))], axis=0
+        )
         s = DOT(k, qt_ref[...])
         p = jnp.exp(s - lse_s[0:1, :])
         dp = DOT(v, dt_ref[...])
         ds = (p * (dp - del_s[0:1, :])).astype(bf16)
-        dv = DOT(p.astype(bf16), dd_ref[...])
+        dv = DOT(p.astype(bf16), dd_ref[...]).astype(bf16)
         dk = DOT(ds, q_ref[...])
         dqt_ref[...] += DOT(k.T, ds)
-        g_ref[j, :rows, 64:] = dk.astype(bf16)
-        g_ref[j, rows:, :] = jnp.concatenate([dv[:half], dv[half:]], axis=1).astype(bf16)
-        return 0
-    lax.fori_loop(0, nb, step, 0, unroll=2)
+        g_ref[j : j + 2, :rows, 64:] = dk.astype(bf16).reshape(2, rows, 64)
+        for i in range(2):
+            g_ref[j + i, rows:, :] = jnp.concatenate(
+                [dv[i * rows : i * rows + half], dv[i * rows + half : (i + 1) * rows]], axis=1
+            )
     for j in range(nb):
         g_ref[j, :rows, :64] = (dqt_ref[:, j * rows : (j + 1) * rows].T * 0.125).astype(bf16)
 
@@ -486,13 +490,15 @@
     return high, values - high
 
 
-def extra_rows(mods, gains, s_rows, store):
-    for s in range(s_rows):
-        for part, (mod, gain) in enumerate(zip(split_low(mods[s : s + 1]), split_low(gains[s : s + 1]))):
-            at = (part * s_rows + s) * 4
-            for i in range(3):
-                store(at + i, mod[:, EXTRA * i : EXTRA * (i + 1)])
-            store(at + 3, gain)
+def extra_rows(mods, gains, store):
+    mods = jnp.concatenate(split_low(mods), axis=0)
+    for i in range(3):
+        store(i * mods.shape[0], mods[:, EXTRA * i : EXTRA * (i + 1)])
+    store(3 * mods.shape[0], jnp.concatenate(split_low(gains), axis=0))
+
+
+def join_rows(rows, i, seqs):
+    return rows[2 * seqs * i : 2 * seqs * i + seqs] + rows[2 * seqs * i + seqs : 2 * seqs * (i + 1)]
 
 
 def pack_kernel(
@@ -509,9 +515,9 @@
     gains = jnp.concatenate([one_ref[...], two_ref[...]], axis=0).astype(f32)
 
     def store(row, value):
-        ext_ref[row : row + 1, : value.shape[1]] = value
-
-    extra_rows(mods, gains, mods.shape[0], store)
+        ext_ref[row : row + value.shape[0], : value.shape[1]] = value
+
+    extra_rows(mods, gains, store)
     extra = ext_ref[...].astype(bf16)
     for i in range(n_u):
         pieces = []
@@ -526,7 +532,7 @@
 
 def first_kernel(
     at_ref, xg_ref, cos_ref, sin_ref, a0, a1, a2, a3, a4, a5, a6, a7,
-    chunk_ref, first_ref, table_ref, w_ref, out_ref, wide_ref, wout_ref,
+    chunk_ref, first_ref, table_ref, w_ref, wide_ref,
 ):
     u, b = at_ref[0], at_ref[1]
     n_u, _, seqs, rows, width = xg_ref.shape
@@ -536,25 +542,16 @@
     block = width // 32
     for i, part_ref in enumerate((a0, a1, a2, a3, a4, a5, a6, a7)):
         there = b ^ i
-        part = part_ref[...].astype(f32)
-        quarter = part.shape[1] - cols - HEAD_DIM
         for j in range(n_u):
             start = pl.multiple_of((j * 8 + there) * block, 8)
-            wide_ref[pl.ds(start, block), :] = part[j * block : (j + 1) * block, : cols + HEAD_DIM]
-            start = pl.multiple_of(there * block, 8)
-            wout_ref[pl.ds(start, block), j * quarter : (j + 1) * quarter] = part[
-                j * block : (j + 1) * block, cols + HEAD_DIM :
-            ]
+            wide_ref[pl.ds(start, block), :] = part_ref[j * block : (j + 1) * block, :].astype(f32)
     w_ref[...] = wide_ref[:, :cols].astype(bf16)
-    out_ref[...] = wout_ref[...].astype(bf16)
-    for s in range(seqs):
-        mods, gains = [], []
-        for d in range(32):
-            pair = wide_ref[d * block : (d + 1) * block, cols:]
-            both = pair[s * 4 : s * 4 + 4] + pair[(seqs + s) * 4 : (seqs + s) * 4 + 4]
-            mods += [both[i : i + 1, :EXTRA] for i in range(3)]
-            gains.append(both[3:4, :block])
-        table_ref[s : s + 1, :] = jnp.concatenate(mods + gains, axis=1)
+    pieces, gains = [], []
+    for d in range(32):
+        part = wide_ref[d * block : (d + 1) * block, cols:]
+        pieces += [join_rows(part, i, seqs)[:, :EXTRA] for i in range(3)]
+        gains.append(join_rows(part, 3, seqs)[:, :block])
+    table_ref[...] = jnp.concatenate(pieces + gains, axis=1)
     gain = mod_row(table_ref, 0, 6)
     zero = jnp.zeros(chunk_ref.shape[1:], bf16)
     chunk_ref[0] = zero
@@ -585,11 +582,19 @@
         if m % 2:
             send_ref[m // 2, s] = block.astype(bf16)
         else:
-            keep_ref[m // 2, s] = block
-
-
-def out_kernel(t_ref, w_ref, att_ref, send_ref, keep_ref):
+            keep_ref[m // 2, s] = block.astype(bf16)
+
+
+def out_kernel(
+    at_ref, t_ref, a0, a1, a2, a3, a4, a5, a6, a7, att_ref, send_ref, keep_ref, w_ref, wide_ref,
+):
     _, seqs, rows, _ = send_ref.shape
+    block = w_ref.shape[0] // 8
+    low = a0.shape[0] - block
+    for i, part_ref in enumerate((a0, a1, a2, a3, a4, a5, a6, a7)):
+        start = pl.multiple_of((at_ref[1] ^ i) * block, 8)
+        wide_ref[pl.ds(start, block), :] = part_ref[low:, :].astype(f32)
+    w_ref[...] = wide_ref[...].astype(bf16)
     heads = w_ref.shape[0] // HEAD_DIM
     span = 4 * rows
     for s in range(seqs):
@@ -608,7 +613,7 @@
 
 def ff_kernel(
     at_ref, xg_ref, own_ref, got_ref, table_ref, a0, a1, a2, a3, a4, a5, a6, a7, b0, b1, b2, b3, b4, b5, b6, b7,
-    lsend_ref, lkeep_ref, dsend_ref, dkeep_ref, sums_ref, ukeep_ref, usend_ref, dgrad_ref,
+    lsend_ref, lkeep_ref, dsend_ref, dkeep_ref, sums_ref, ukeep_ref, usend_ref, wkeep_ref, wsend_ref,
     second_ref, hidden_ref, low_ref, raised_ref, normed_ref, wide_ref, up_ref, down_ref,
 ):
     u = at_ref[0]
@@ -622,7 +627,7 @@
     ups, downs = (a0, a1, a2, a3, a4, a5, a6, a7), (b0, b1, b2, b3, b4, b5, b6, b7)
     for i, (part_ref, low_part_ref) in enumerate(zip(ups, downs)):
         there = b ^ i
-        down_ref[pl.ds(pl.multiple_of(there * low, 32), low), :] = low_part_ref[...]
+        down_ref[pl.ds(pl.multiple_of(there * low, 32), low), :] = low_part_ref[:low, :]
         for j in range(n_u):
             start = pl.multiple_of((j * 8 + there) * block, 8)
             wide_ref[pl.ds(start, block), :] = part_ref[j * block : (j + 1) * block, :].astype(f32)
@@ -655,14 +660,18 @@
             grad = xg_ref[u ^ m, 1, s].astype(f32)
             gated = gated + jnp.sum(grad * lowered[m * rows : (m + 1) * rows], axis=0, keepdims=True)
         sums_ref[s, 2:3, :] = gated
-    n_z = ukeep_ref.shape[0]
+    n_z, side = ukeep_ref.shape[0], b % 2
+    wide_ref[...] = dot_tn(hidden_ref[...], low_ref[...])
+    for y, out_ref in enumerate((wkeep_ref, wsend_ref)):
+        for z in range(n_z):
+            start = pl.multiple_of((2 * z + (side ^ y)) * low, 32)
+            out_ref[z] = wide_ref[pl.ds(start, low), :].astype(bf16)
     wide_ref[...] = dot_tn(second_ref[...], raised_ref[...])
     for y, out_ref in enumerate((ukeep_ref, usend_ref)):
         for z in range(n_z):
             for i in range(n_u):
-                start = pl.multiple_of(((u ^ i) * 2 * n_z + (b ^ (2 * z + y))) * block, 8)
+                start = pl.multiple_of(((u ^ i) * 2 * n_z + 2 * z + (side ^ y)) * block, 8)
                 out_ref[z, i] = wide_ref[pl.ds(start, block), :].astype(bf16)
-    dgrad_ref[...] = dot_tn(hidden_ref[...], low_ref[...]).astype(bf16)
 
 
 def middle_back_kernel(
@@ -703,7 +712,7 @@
 
 def first_back_kernel(
     at_ref, t_ref, xg_ref, table_ref, cos_ref, sin_ref, w_ref, first_ref, gate_ref, two_ref,
-    send_ref, keep_ref, blocks_ref, proj_ref, normed_ref, sums_ref, ext_ref,
+    send_ref, keep_ref, blocks_ref, proj_ref, normed_ref, sums_ref, ext_ref, both_ref,
 ):
     u = at_ref[0]
     n_u, _, seqs, rows, width = xg_ref.shape
@@ -743,13 +752,15 @@
     for i in range(2):
         sums_ref[i : i + 1, 6 * width :] = gain_grads[i]
     ext_ref[...] = jnp.zeros_like(ext_ref)
+    high = sums_ref[...].astype(bf16).astype(f32)
+    both_ref[...] = jnp.concatenate([high, sums_ref[...] - high], axis=0)
+    lines = 2 * seqs
     for d in range(total):
-
-        def store(row, value):
-            ext_ref[d * block + row : d * block + row + 1, : value.shape[1]] = value
-
-        mods = sums_ref[:, 3 * EXTRA * d : 3 * EXTRA * (d + 1)]
-        extra_rows(mods, sums_ref[:, 6 * width + block * d : 6 * width + block * (d + 1)], seqs, store)
+        for i in range(3):
+            at = 3 * EXTRA * d + EXTRA * i
+            ext_ref[d * block + lines * i : d * block + lines * (i + 1), :EXTRA] = both_ref[:, at : at + EXTRA]
+        at = 6 * width + block * d
+        ext_ref[d * block + 3 * lines : d * block + 4 * lines, :block] = both_ref[:, at : at + block]
     grads = dot_tn(first_ref[...], proj_ref[...])
     for i in range(total):
         at = slice(i * block, (i + 1) * block)
@@ -778,10 +789,8 @@
             qkv_ref[:, width + to : width + to + HEAD_DIM] = part[:, 128 * h + HEAD_DIM : 128 * (h + 1)]
         at = i * heads * HEAD_DIM
         qkv_ref[:, 2 * width + at : 2 * width + at + heads * HEAD_DIM] = part[:, 128 * heads : cols]
-    for s in range(seqs):
-        both = extra[s * 4 : s * 4 + 4] + extra[(seqs + s) * 4 : (seqs + s) * 4 + 4]
-        mod_ref[s : s + 1, :] = jnp.concatenate([both[i : i + 1, :EXTRA] for i in range(3)], axis=1)
-        gain_ref[s : s + 1, :] = both[3:4, :block]
+    mod_ref[...] = jnp.concatenate([join_rows(extra, i, seqs)[:, :EXTRA] for i in range(3)], axis=1)
+    gain_ref[...] = join_rows(extra, 3, seqs)[:, :block]
     mods = mod_ref[...].astype(bf16)
     grads = DOT(mods, ada_ref[...])
     for i in range(total):
@@ -797,7 +806,7 @@
     for s in range(seqs):
         factor = mod_row(table_ref, 0, 6) * (1.0 + mod_row(table_ref, s, 1))
         normed, inv_std = row_norm(x_ref[s].astype(f32))
-        grads = (near_ref[s] + got_ref[s].astype(f32)) * factor
+        grads = (near_ref[s].astype(f32) + got_ref[s].astype(f32)) * factor
         out_ref[s] = dmid_ref[s] + row_back(grads, normed, inv_std)
 
 
@@ -857,12 +866,21 @@
     return lax.ppermute(values, "blk", [(i, i ^ mask) for i in range(8)])
 
 
+def scatter_z(blocks):
+    groups = [[2 * z + y for z in range(4)] for y in range(2)]
+    return lax.psum_scatter(blocks, "blk", scatter_dimension=0, axis_index_groups=groups, tiled=True)[0]
+
+
 def exchange(blocks, axis):
     return lax.all_to_all(blocks, axis, split_axis=0, concat_axis=0, tiled=True)
 
 
 def half_sum(send, keep):
-    return keep + swap_u(send, 1).astype(f32)
+    return (keep.astype(f32) + swap_u(send, 1).astype(f32)).astype(bf16)
+
+
+def pair_sum(left, right):
+    return (left.astype(f32) + right.astype(f32)).astype(bf16)
 
 
 def along_z(values):
@@ -919,23 +937,16 @@
     pieces = pieces.reshape(n_u * w_rows, cols + HEAD_DIM + ff_local)
     xg = lax.all_gather(both, "ulysses", axis=0, tiled=False)
     up_near = pieces[:, cols + HEAD_DIM :]
-    down_z = along_z(w_down)
-    quarter = width // n_u
-    near = jnp.concatenate(
-        [
-            pieces[:, : cols + HEAD_DIM],
-            jnp.concatenate([w_out[:, i * quarter : (i + 1) * quarter] for i in range(n_u)], axis=0),
-        ],
-        axis=1,
-    )
-    near, down_z = lax.optimization_barrier((near, down_z))
+    down_z = along_z(jnp.concatenate([w_down, w_out], axis=0))
+    pieces, down_z[1], down_z[2] = lax.optimization_barrier((pieces, down_z[1], down_z[2]))
+    near = pieces[:, : cols + HEAD_DIM]
     rows_zy = along_y(along_z(near))
 
-    chunks, first_in, table, w_qkv_u, w_out_u = call(
+    chunks, first_in, table, w_qkv_u = call(
         first_kernel, "first",
         [((n_b, 3 * span // 2, 128), bf16), ((tokens, width), bf16), ((seqs, 7 * width), f32),
-         ((width, cols), bf16), ((head_width, width), bf16)],
-        [((width, cols + HEAD_DIM), f32), ((head_width, width), f32)],
+         ((width, cols), bf16)],
+        [((width, cols + HEAD_DIM), f32)],
         2 * tokens * width * cols,
         at, xg, cos_table, sin_table, *rows_zy,
         limit=60,
@@ -945,39 +956,42 @@
     down_zy = along_y(down_z)
     owned, up_near, down_zy[1], down_zy[3] = lax.optimization_barrier((owned, up_near, down_zy[1], down_zy[3]))
     up_z = along_z(up_near)
-    up_0y = swap_b(up_near, 1)
     attn_low, attn_full, log_total = attn_fwd(owned)
     part_shape = (2, seqs, rows, width)
-    attn_low, up_z, up_0y, down_zy = lax.optimization_barrier((attn_low, up_z, up_0y, down_zy))
+    attn_low, up_z, down_zy = lax.optimization_barrier((attn_low, up_z, down_zy))
     attn_tokens = exchange(attn_low, "blk")
-    attended, send, keep = call(
+    up_zy = along_y(up_z[:1])
+    attn_tokens, up_zy = lax.optimization_barrier((attn_tokens, up_zy))
+    attended, send, keep, w_out_u = call(
         out_kernel, "out",
-        [((tokens, head_width), bf16), (part_shape, bf16), (part_shape, f32)], [],
+        [((tokens, head_width), bf16), (part_shape, bf16), (part_shape, bf16), ((head_width, width), bf16)],
+        [((head_width, width), f32)],
         2 * tokens * width * head_width,
-        attn_tokens, w_out_u,
+        at, attn_tokens, *down_zy,
     )
 
     half = half_sum(send, keep)
-    across = swap_u(half.astype(bf16), 2)
-    up_zy = [up_near, up_0y] + along_y(up_z[1:])
+    across = swap_u(half, 2)
+    up_zy = up_zy + along_y(up_z[1:])
     across, up_zy = lax.optimization_barrier((across, up_zy))
-    own = (half + across[::-1].astype(f32)).astype(bf16)
+    own = pair_sum(half, across[::-1])
     got = swap_u(own, 1)
-    lsend, lkeep, dsend, dkeep, sums_two, up_keep, up_send, down_term = call(
+    lsend, lkeep, dsend, dkeep, sums_two, up_keep, up_send, down_keep, down_send = call(
         ff_kernel, "ff",
-        [(part_shape, bf16), (part_shape, f32), (part_shape, bf16), (part_shape, f32), ((seqs, 3, width), f32)]
-        + [((n_b // 2, n_u, w_rows, width), bf16)] * 2 + [((ff_local, width), bf16)],
+        [(part_shape, bf16), (part_shape, bf16), (part_shape, bf16), (part_shape, bf16), ((seqs, 3, width), f32)]
+        + [((n_b // 2, n_u, w_rows, width), bf16)] * 2 + [((n_b // 2, down_rows, width), bf16)] * 2,
         [((tokens, width), bf16), ((tokens, ff_local), bf16), ((tokens, width), bf16), ((tokens, ff_local), bf16),
          ((span, width), f32), ((width, ff_local), f32), ((width, ff_local), bf16), ((ff_local, width), bf16)],
         12 * tokens * width * ff_local,
         at, xg, own, got, table, *up_zy, *down_zy,
         limit=60,
     )
-    up_other = swap_b(up_send, 1)
-    down_grad = lax.psum_scatter(down_term, "blk", scatter_dimension=0, tiled=True)
+    down_other, up_other = swap_b(down_send, 1), swap_b(up_send, 1)
     half = half_sum(dsend, dkeep)
-    across = swap_u(half.astype(bf16), 2)
-    d_own = (half + across[::-1].astype(f32)).astype(bf16)
+    across = swap_u(half, 2)
+    across, down_other = lax.optimization_barrier((across, down_other))
+    down_grad = scatter_z(pair_sum(down_keep, down_other))
+    d_own = pair_sum(half, across[::-1])
     d_got = swap_u(d_own, 1)
     d_chunks, d_middle, sum_gate, out_keep, out_send = call(
         middle_back_kernel, "middle_back",
@@ -990,33 +1004,33 @@
     )
     d_attn = exchange(d_chunks, "blk")
     out_other = swap_b(out_send, 1)
-    up_half = up_keep.astype(f32) + up_other.astype(f32)
-    up_1 = swap_b(up_half[1].astype(bf16), 2)
-    d_attn, up_1, out_other = lax.optimization_barrier((d_attn, up_1, out_other))
-    up_sum = up_half[0] + up_1.astype(f32)
-    for m in (2, 3):
-        up_sum = up_sum + swap_b(up_half[m].astype(bf16), 2 * m).astype(f32)
+    up_low = pair_sum(up_keep, up_other)
+    d_attn, up_low, out_other, down_grad = lax.optimization_barrier((d_attn, up_low, out_other, down_grad))
+    up_sum = scatter_z(up_low)
     d_owned = attn_bwd(owned, d_attn, attn_full, log_total)
+    d_owned, lsend, lkeep = lax.optimization_barrier((d_owned, lsend, lkeep))
     lhalf = half_sum(lsend, lkeep)
-    lowered = lhalf[0] + swap_u(lhalf[1].astype(bf16), 2).astype(f32)
+    lowered = lhalf[0].astype(f32) + swap_u(lhalf[1], 2).astype(f32)
     gates = table.reshape(2, 7, 1, width)
     output = inputs.astype(f32) + gates[:, 2] * own[0].astype(f32) + gates[:, 5] * lowered
-    d_owned, output, up_sum, out_other = lax.optimization_barrier((d_owned, output, up_sum, out_other))
-    out_grad = sum_z(out_keep.astype(f32) + out_other.astype(f32))
+    up_sum = up_sum.astype(f32)
     up_parts = [up_sum[0]] + [swap_u(up_sum[m], m) for m in (1, 2, 3)]
     d_tokens = exchange(d_owned, "blk")
-    d_tokens, up_parts, out_grad, down_grad = lax.optimization_barrier((d_tokens, up_parts, out_grad, down_grad))
+    d_tokens, up_parts, down_grad, output = lax.optimization_barrier((d_tokens, up_parts, down_grad, output))
 
     send, keep, qkv_blocks = call(
         first_back_kernel, "first_back",
-        [(part_shape, bf16), (part_shape, f32), ((n_all, w_rows, cols + HEAD_DIM), bf16)],
-        [((tokens, cols), bf16), ((span, width), f32), ((seqs, 7 * width), f32), ((width, HEAD_DIM), f32)],
+        [(part_shape, bf16), (part_shape, bf16), ((n_all, w_rows, cols + HEAD_DIM), bf16)],
+        [((tokens, cols), bf16), ((span, width), f32), ((seqs, 7 * width), f32), ((width, HEAD_DIM), f32),
+         ((2 * seqs, 7 * width), f32)],
         4 * tokens * width * cols,
         at, d_tokens, xg, table, cos_table, sin_table, w_qkv_u, first_in, sum_gate, sums_two,
         limit=60,
     )
     half = half_sum(send, keep)
-    far = swap_u(half[1].astype(bf16), 2)
+    far = swap_u(half[1], 2)
+    far, out_other = lax.optimization_barrier((far, out_other))
+    out_grad = sum_z(out_keep.astype(f32) + out_other.astype(f32))
     inputs_grad, = call(
         input_grad_kernel, "input_grad",
         [((seqs, rows, width), f32)], [], 0,
@@ -1028,7 +1042,7 @@
          ((2, w_rows), f32), ((seqs, w_ada.shape[1]), f32)],
         [], 0,
         at, exchange(qkv_blocks, everywhere), *up_parts, w_ada.T, conditioning,
-        limit=60,
+        limit=6,
     )
     conditioning_grad = jnp.sum(exchange(cond_part, everywhere), axis=0)
     return (

time: 280 us -> 267 us (0.954)
  waiting for transfers between devices: 105 us -> 118 us
  blocking collectives: 11.8 us -> 0 us
  local copies, waits for them, and re-layouts: 10.8 us -> 4.72 us
  other arithmetic: 14.9 us -> 9.52 us
  Pallas kernels: 52.6 us -> 47.7 us
  starting transfers between devices: 69.5 us -> 72.5 us
    all_to_all x1 -> x0, blocking collectives: 11.8 us -> none  [exchange(): return lax.all_to_all(blocks, axis, split_axis=0, concat_axis=0, tiled=True)]
    ppermute x29 -> x27, waiting for transfers between devices: 58.1 us -> 64.9 us  [swap_b(): return lax.ppermute(values, 'blk', [(i, i ^ mask) for i in range(8)])]
    reduce_scatter x1 -> x2, waiting for transfers between devices: 0.02 us -> 5.53 us  [scatter_z(): lax.psum_scatter(blocks, 'blk', scatter_dimension=0, axis_index_groups=gr...]
    all_to_all x6 -> x7, starting transfers between devices: 23.2 us -> 28.7 us  [exchange(): return lax.all_to_all(blocks, axis, split_axis=0, concat_axis=0, tiled=True)]
    add x4 -> x0, other arithmetic: 4.77 us -> none  [the longest x1 2.47 us: tp_shards(): up_half = up_keep.astype(f32) + up_other.astype(f32)]
    ppermute x29 -> x27, starting transfers between devices: 38.9 us -> 35.2 us  [swap_b(): return lax.ppermute(values, 'blk', [(i, i ^ mask) for i in range(8)])]
    unnamed x104 -> x105, local copies, waits for them, and re-layouts: 6.77 us -> 3.96 us
    all_to_all x6 -> x7, waiting for transfers between devices: 24.3 us -> 23.9 us  [exchange(): return lax.all_to_all(blocks, axis, split_axis=0, concat_axis=0, tiled=True)]
  transfers between devices with their start and end apart: 50 -> 50, of which waited for: 23 -> 29; matrix products, arithmetic and copies ran while one was open for 7% -> 3% of each run, Pallas kernels for 10% -> 11%
where the time goes in v3:
time: 267 us
  waiting for transfers between devices  118 us (44%)
  starting transfers between devices  72.5 us (27%)
  Pallas kernels  47.7 us (18%)
  between operations  14.5 us (5%)
  other arithmetic  9.52 us (4%)
  local copies, waits for them, and re-layouts  4.72 us (2%)
    ppermute x27, waiting for transfers between devices, swap_b(): return lax.ppermute(values, 'blk', [(i, i ^ mask) for i in range(8)])  64.9 us
    ppermute x27, starting transfers between devices, swap_b(): return lax.ppermute(values, 'blk', [(i, i ^ mask) for i in range(8)])  35.2 us
    pallas_call x8, Pallas kernels, call(): pl.pallas_call(body, out_shape=tuple((jax.ShapeDtypeStruct(shape, dtype)...  29.1 us
    all_to_all x7, starting transfers between devices, exchange(): return lax.all_to_all(blocks, axis, split_axis=0, concat_axis=0, tiled=True)  28.7 us
    all_to_all x7, waiting for transfers between devices, exchange(): return lax.all_to_all(blocks, axis, split_axis=0, concat_axis=0, tiled=True)  23.9 us
    ppermute x13, waiting for transfers between devices, swap_u(): return lax.ppermute(values, 'ulysses', [(i, i ^ mask) for i in range(4)])  23.5 us
    pallas_call x1, Pallas kernels, attn_bwd(): pl.pallas_call(attn_bwd_kernel, out_shape=jax.ShapeDtypeStruct((nb, rows3...  11.6 us
    ppermute x13, starting transfers between devices, swap_u(): return lax.ppermute(values, 'ulysses', [(i, i ^ mask) for i in range(4)])  8.06 us
  transfers between devices with their start and end apart: 50, of which 29 were waited for; matrix products, arithmetic and copies ran while one was open for 3% of the time, Pallas kernels for 11%

profile of v3, /device:TPU:0, one launch (start us, length us, event | category | flops | bytes accessed | tf_op | source)
XLA Modules:
  0.0 266.7 jit_solution(2318536986440916496)
XLA Ops:
  7.2 2.3 pack.1
  9.7 3.1 %collective-permute-start = (bf16[120,768]{1,0:T(8,128)(2,1)S(1)}, bf16[120,768]{1,0:T(8,128)(2,1)S(1)}, u32[]{:S(2)}, u32[]{:S(2)}) collective-permute-start(bf16[120,768]{1,0:T(8,128)(2,1)S(1)} %constant_dynamic-update-slice_fusion.a0.b0), channel_id=1, source_target_pairs={{0,2},{1,3},{2,0},{3,1},{4,6},{5,7},{6,4},{7,5},{8,10},{9,11},{10,... | collective-permute-start | bytes 552968 | tf_op jit(solution)/shard_map/ppermute | solution.py:866
  12.8 2.6 collective-permute-start.1
  15.4 3.4 %all-to-all-start = ((bf16[4,24,1408]{2,1,0:T(8,128)(2,1)}), bf16[4,24,1408]{2,1,0:T(8,128)(2,1)S(1)}, u32[]{:S(2)}, u32[]{:S(2)}) async-start(bf16[4,24,1408]{2,1,0:T(8,128)(2,1)} %get-tuple-element.104), calls=%async_computation | async-start | bytes 540672 | tf_op jit(solution)/shard_map/all_to_all | solution.py:875
  21.1 6.7 %all-to-all-done = bf16[4,24,1408]{2,1,0:T(8,128)(2,1)S(1)} async-done(((bf16[4,24,1408]{2,1,0:T(8,128)(2,1)}), bf16[4,24,1408]{2,1,0:T(8,128)(2,1)S(1)}, u32[]{:S(2)}, u32[]{:S(2)}) %all-to-all-start) | async-done | bytes 270368 | tf_op jit(solution)/shard_map/all_to_all | solution.py:875
  28.0 4.3 %collective-permute-start.7 = (bf16[96,640]{1,0:T(8,128)(2,1)S(1)}, bf16[96,640]{1,0:T(8,128)(2,1)S(1)}, u32[]{:S(2)}, u32[]{:S(2)}) collective-permute-start(bf16[96,640]{1,0:T(8,128)(2,1)S(1)} %slice.64.a0), channel_id=1, source_target_pairs={{0,6},{1,7},{2,4},{3,5},{4,2},{5,3},{6,0},{7,1},{8,14},{9,15},{10,... | collective-permute-start | bytes 368648 | tf_op jit(solution)/shard_map/ppermute | solution.py:866
  32.3 1.5 collective-permute-start.2
  34.4 1.5 collective-permute-start.4
  35.9 7.5 %collective-permute-done.5.a4 = bf16[96,640]{1,0:T(8,128)(2,1)S(1)} collective-permute-done((bf16[96,640]{1,0:T(8,128)(2,1)S(1)}, bf16[96,640]{1,0:T(8,128)(2,1)S(1)}, u32[]{:S(2)}, u32[]{:S(2)}) %collective-permute-start.5) | collective-permute-done | bytes 122912 | tf_op jit(solution)/shard_map/ppermute | solution.py:866
  43.4 1.5 collective-permute-start.6
  45.5 2.8 %collective-permute-done.6.a5 = bf16[96,640]{1,0:T(8,128)(2,1)S(1)} collective-permute-done((bf16[96,640]{1,0:T(8,128)(2,1)S(1)}, bf16[96,640]{1,0:T(8,128)(2,1)S(1)}, u32[]{:S(2)}, u32[]{:S(2)}) %collective-permute-start.6) | collective-permute-done | bytes 122912 | tf_op jit(solution)/shard_map/ppermute | solution.py:866
  48.3 1.5 collective-permute-done.8.a7
  50.5 4.4 %first.1 = (bf16[8,384,128]{2,1,0:T(8,128)(2,1)}, bf16[512,768]{1,0:T(8,128)(2,1)}, f32[2,5376]{1,0:T(2,128)}, bf16[768,576]{1,0:T(8,128)(2,1)}) custom-call(s32[2]{0:T(128)} %pad_add_fusion.at_ref, bf16[4,2,2,64,768]{4,3,2,1,0:T(8,128)(2,1)} %bitcast.59, f32[256,128]{1,0:T(8,128)} %get-tuple-element.107.cos_ref, f32[256,128]{1,0:T(8,128)} %get-tuple-element.108.sin_ref, ...), custom_call_target="tpu_custom_call" | custom-call | flops 452984 | bytes 5318 | tf_op jit(solution)/shard_map/first/pallas_call | solution.py:844
  54.9 3.9 %all-to-all-start.1 = ((bf16[8,384,128]{2,1,0:T(8,128)(2,1)}), bf16[8,384,128]{2,1,0:T(8,128)(2,1)S(1)}, u32[]{:S(2)}, u32[]{:S(2)}) async-start(bf16[8,384,128]{2,1,0:T(8,128)(2,1)} %get-tuple-element.114), calls=%async_computation.1 | async-start | bytes 1572864 | tf_op jit(solution)/shard_map/all_to_all | solution.py:875
  58.8 2.0 collective-permute-start.10
  60.8 2.0 collective-permute-start.15
  62.9 9.1 %collective-permute-done.10.a1.b1 = bf16[120,768]{1,0:T(8,128)(2,1)S(1)} collective-permute-done((bf16[120,768]{1,0:T(8,128)(2,1)S(1)}, bf16[120,768]{1,0:T(8,128)(2,1)S(1)}, u32[]{:S(2)}, u32[]{:S(2)}) %collective-permute-start.10) | collective-permute-done | bytes 184352 | tf_op jit(solution)/shard_map/ppermute | solution.py:866
  72.0 5.0 %collective-permute-done.11.a3.b3 = bf16[120,768]{1,0:T(8,128)(2,1)S(1)} collective-permute-done((bf16[120,768]{1,0:T(8,128)(2,1)S(1)}, bf16[120,768]{1,0:T(8,128)(2,1)S(1)}, u32[]{:S(2)}, u32[]{:S(2)}) %collective-permute-start.11) | collective-permute-done | bytes 184352 | tf_op jit(solution)/shard_map/ppermute | solution.py:866
  77.0 2.3 collective-permute-start.12
  79.3 1.7 collective-permute-start.13
  81.8 6.9 %attn_fwd.1 = (bf16[8,128,128]{2,1,0:T(8,128)(2,1)}, f32[8,128,128]{2,1,0:T(8,128)S(1)}, f32[8,8,256]{2,1,0:T(8,128)S(1)}) custom-call(bf16[8,384,128]{2,1,0:T(8,128)(2,1)S(1)} %all-to-all-done.1.x_ref), custom_call_target="tpu_custom_call" | custom-call | flops 1073741824 | bytes 2097152 | tf_op jit(solution)/shard_map/attn_fwd/pallas_call | solution.py:43
  89.5 5.2 %all-to-all-start.2 = ((bf16[8,128,128]{2,1,0:T(8,128)(2,1)}), bf16[8,128,128]{2,1,0:T(8,128)(2,1)S(1)}, u32[]{:S(2)}, u32[]{:S(2)}) async-start(bf16[8,128,128]{2,1,0:T(8,128)(2,1)} %get-tuple-element.124), calls=%async_computation.2 | async-start | bytes 524288 | tf_op jit(solution)/shard_map/all_to_all | solution.py:875
  95.0 1.9 collective-permute-start.17
  96.9 4.8 %collective-permute-done.17.a1 = bf16[96,768]{1,0:T(8,128)(2,1)} collective-permute-done((bf16[96,768]{1,0:T(8,128)(2,1)S(1)}, bf16[96,768]{1,0:T(8,128)(2,1)}, u32[]{:S(2)}, u32[]{:S(2)}) %collective-permute-start.17) | collective-permute-done | bytes 147488 | tf_op jit(solution)/shard_map/ppermute | solution.py:866
  101.6 1.4 all-to-all-done.2.t_ref
  104.2 1.7 collective-permute-done.18
  107.0 2.0 collective-permute-start.21
  109.1 4.6 %collective-permute-done.20.a3 = bf16[96,768]{1,0:T(8,128)(2,1)S(1)} collective-permute-done((bf16[96,768]{1,0:T(8,128)(2,1)S(1)}, bf16[96,768]{1,0:T(8,128)(2,1)S(1)}, u32[]{:S(2)}, u32[]{:S(2)}) %collective-permute-start.20) | collective-permute-done | bytes 147488 | tf_op jit(solution)/shard_map/ppermute | solution.py:866
  113.7 3.2 %collective-permute-done.21.a5 = bf16[96,768]{1,0:T(8,128)(2,1)S(1)} collective-permute-done((bf16[96,768]{1,0:T(8,128)(2,1)S(1)}, bf16[96,768]{1,0:T(8,128)(2,1)S(1)}, u32[]{:S(2)}, u32[]{:S(2)}) %collective-permute-start.21) | collective-permute-done | bytes 147488 | tf_op jit(solution)/shard_map/ppermute | solution.py:866
  116.9 2.0 collective-permute-done.22.a7
  119.1 1.7 collective-permute-done.23.got_ref
  121.6 8.9 %ff.1 = (bf16[2,2,64,768]{3,2,1,0:T(8,128)(2,1)}, bf16[2,2,64,768]{3,2,1,0:T(8,128)(2,1)}, bf16[2,2,64,768]{3,2,1,0:T(8,128)(2,1)}, bf16[2,2,64,768]{3,2,1,0:T(8...) custom-call(s32[2]{0:T(128)} %pad_add_fusion.at_ref, ...), custom_call_target="tpu_custom_call" | custom-call | flops 3623878 | bytes 9007 | tf_op jit(solution)/shard_map/ff/pallas_call | solution.py:844
  131.0 1.5 collective-permute-done.24
  132.5 1.1 add_convert_fusion.5
  133.6 1.2 collective-permute-start.25
  134.8 11.8 %collective-permute-done.26 = bf16[4,96,768]{2,1,0:T(8,128)(2,1)S(1)} collective-permute-done((bf16[4,96,768]{2,1,0:T(8,128)(2,1)}, bf16[4,96,768]{2,1,0:T(8,128)(2,1)S(1)}, u32[]{:S(2)}, u32[]{:S(2)}) %collective-permute-start.26) | collective-permute-done | bytes 589856 | tf_op jit(solution)/shard_map/ppermute | solution.py:866
  148.0 1.7 collective-permute-done.27.dgot_ref
  150.6 4.5 %middle_back.1 = (bf16[8,128,128]{2,1,0:T(8,128)(2,1)}, f32[2,64,768]{2,1,0:T(8,128)}, f32[2,1,768]{2,1,0:T(1,128)}, bf16[4,24,768]{2,1,0:T(8,128)(2,1)}, bf16[4,24,768]{2,1,0:T(8,128)(2,1)}) custom-call(s32[2]{0:T(128)} %pad_add_fusion.at_ref, bf16[4,2,2,64,768]{4,3,2,1,0:T(8,128)(2,1)} %bitcast.61, bf16[2,2,64,768]{3,2,1,0:T(8,128)(2,1)} %copy-done.18, ...), custom_call_target="tpu_custom_call" | custom-call | flops 301989 | bytes 4636 | tf_op jit(solution)/shard_map/middle_back/pallas_call | solution.py:844
  155.1 4.3 %all-to-all-start.3 = ((bf16[8,128,128]{2,1,0:T(8,128)(2,1)}), bf16[8,128,128]{2,1,0:T(8,128)(2,1)S(1)}, u32[]{:S(2)}, u32[]{:S(2)}) async-start(bf16[8,128,128]{2,1,0:T(8,128)(2,1)} %get-tuple-element.158), calls=%async_computation.3 | async-start | bytes 524288 | tf_op jit(solution)/shard_map/all_to_all | solution.py:875
  159.6 1.8 collective-permute-start.29
  161.4 1.7 collective-permute-done.28
  164.1 3.8 %collective-permute-done.29 = bf16[4,24,768]{2,1,0:T(8,128)(2,1)S(1)} collective-permute-done((bf16[4,24,768]{2,1,0:T(8,128)(2,1)}, bf16[4,24,768]{2,1,0:T(8,128)(2,1)S(1)}, u32[]{:S(2)}, u32[]{:S(2)}) %collective-permute-start.29) | collective-permute-done | bytes 147488 | tf_op jit(solution)/shard_map/ppermute | solution.py:866
  167.8 3.1 %all-to-all-done.3.d_ref = bf16[8,128,128]{2,1,0:T(8,128)(2,1)S(1)} async-done(((bf16[8,128,128]{2,1,0:T(8,128)(2,1)}), bf16[8,128,128]{2,1,0:T(8,128)(2,1)S(1)}, u32[]{:S(2)}, u32[]{:S(2)}) %all-to-all-start.3) | async-done | bytes 262176 | tf_op jit(solution)/shard_map/all_to_all | solution.py:875
  171.0 11.6 %attn_bwd.1 = bf16[8,384,128]{2,1,0:T(8,128)(2,1)} custom-call(bf16[8,384,128]{2,1,0:T(8,128)(2,1)S(1)} %all-to-all-done.1.x_ref, bf16[8,128,128]{2,1,0:T(8,128)(2,1)S(1)} %all-to-all-done.3.d_ref, f32[8,128,128]{2,1,0:T(8,128)S(1)} %get-tuple-element.165.of_ref, f32[8,8,256]{2,1,0:T(8,128)S(1)} %get-tuple-element.166.lse_ref), custom_call_target="tpu_custom_call" | custom-call | flops 268435456 | bytes 262144 | tf_op jit(solution)/shard_map/attn_bwd/pallas_call | solution.py:95
  182.5 4.5 %all-to-all-start.4 = ((bf16[8,384,128]{2,1,0:T(8,128)(2,1)}), bf16[8,384,128]{2,1,0:T(8,128)(2,1)S(1)}, u32[]{:S(2)}, u32[]{:S(2)}) async-start(bf16[8,384,128]{2,1,0:T(8,128)(2,1)} %attn_bwd.1), calls=%async_computation.5 | async-start | bytes 1572864 | tf_op jit(solution)/shard_map/all_to_all | solution.py:875
  187.2 1.6 collective-permute-done.33
  188.9 1.3 collective-permute-start.34
  190.3 5.5 %reduce-scatter.5.cloned.1.call-done = bf16[1,4,24,768]{3,2,1,0:T(8,128)(2,1)} async-done(((bf16[4,4,24,768]{3,2,1,0:T(8,128)(2,1)}), bf16[1,4,24,768]{3,2,1,0:T(8,128)(2,1)}) %reduce-scatter.5.cloned.1.call-update) | async-done | bytes 147472 | tf_op jit(solution)/shard_map/reduce_scatter | solution.py:871
  196.8 1.7 collective-permute-start.31
  199.6 1.9 collective-permute-done.31.p2
  201.5 1.2 collective-permute-done.32.p3
  202.8 6.1 %all-to-all-done.4.t_ref = bf16[8,384,128]{2,1,0:T(8,128)(2,1)S(1)} async-done(((bf16[8,384,128]{2,1,0:T(8,128)(2,1)}), bf16[8,384,128]{2,1,0:T(8,128)(2,1)S(1)}, u32[]{:S(2)}, u32[]{:S(2)}) %all-to-all-start.4) | async-done | bytes 786464 | tf_op jit(solution)/shard_map/all_to_all | solution.py:875
  209.7 5.3 %first_back.1 = (bf16[2,2,64,768]{3,2,1,0:T(8,128)(2,1)}, bf16[2,2,64,768]{3,2,1,0:T(8,128)(2,1)}, bf16[32,24,640]{2,1,0:T(8,128)(2,1)}) custom-call(s32[2]{0:T(128)} %pad_add_fusion.at_ref, bf16[8,384,128]{2,1,0:T(8,128)(2,1)} %copy-done.20, bf16[4,2,2,64,768]{4,3,2,1,0:T(8,128)(2,1)} %bitcast.62, f32[2,5376]{1,0:T(2,128)} %get-tuple-element.143.table_ref, ...), custom_call_target="tpu_custom_call" | custom-call | flops 905969 | bytes 6129 | tf_op jit(solution)/shard_map/first_back/pallas_call | solution.py:844
  215.1 4.1 %all-to-all-start.5 = ((bf16[32,24,640]{2,1,0:T(8,128)(2,1)}), bf16[32,24,640]{2,1,0:T(8,128)(2,1)S(1)}, u32[]{:S(2)}, u32[]{:S(2)}) async-start(bf16[32,24,640]{2,1,0:T(8,128)(2,1)} %get-tuple-element.185), calls=%async_computation.7 | async-start | bytes 1966080 | tf_op jit(solution)/shard_map/all_to_all | solution.py:875
  219.5 1.5 collective-permute-done.35
  221.2 1.8 collective-permute-start.36
  223.0 10.6 %collective-permute-done.36.got_ref = bf16[2,64,768]{2,1,0:T(8,128)(2,1)S(1)} collective-permute-done((bf16[2,64,768]{2,1,0:T(8,128)(2,1)S(1)}, bf16[2,64,768]{2,1,0:T(8,128)(2,1)S(1)}, u32[]{:S(2)}, u32[]{:S(2)}) %collective-permute-start.36) | collective-permute-done | bytes 196640 | tf_op jit(solution)/shard_map/ppermute | solution.py:862
  233.7 1.5 collective-permute-start.37
  235.2 3.2 %collective-permute-start.38 = (bf16[24,768]{1,0:T(8,128)(2,1)S(1)}, bf16[24,768]{1,0:T(8,128)(2,1)S(1)}, u32[]{:S(2)}, u32[]{:S(2)}) collective-permute-start(bf16[24,768]{1,0:T(8,128)(2,1)S(1)} %get-tuple-element.208), channel_id=1, source_target_pairs={{0,4},{1,5},{2,6},{3,7},{4,0},{5,1},{6,2},{7,3},{8,12},{9,13},{10,... | collective-permute-start | bytes 110600 | tf_op jit(solution)/shard_map/ppermute | solution.py:866
  239.2 1.1 input_grad.1
  240.3 6.5 %collective-permute-done.38 = bf16[24,768]{1,0:T(8,128)(2,1)S(1)} collective-permute-done((bf16[24,768]{1,0:T(8,128)(2,1)S(1)}, bf16[24,768]{1,0:T(8,128)(2,1)S(1)}, u32[]{:S(2)}, u32[]{:S(2)}) %collective-permute-start.38) | collective-permute-done | bytes 36896 | tf_op jit(solution)/shard_map/ppermute | solution.py:866
  247.5 1.6 row_grad.1
  249.1 3.3 %all-to-all-start.6 = ((f32[32,2,128]{2,1,0:T(2,128)}), f32[32,2,128]{2,1,0:T(2,128)S(1)}, u32[]{:S(2)}, u32[]{:S(2)}) async-start(f32[32,2,128]{2,1,0:T(2,128)} %get-tuple-element.190), calls=%async_computation.8 | async-start | bytes 65536 | tf_op jit(solution)/shard_map/all_to_all | solution.py:875
  252.9 6.7 %all-to-all-done.6 = f32[32,2,128]{2,1,0:T(2,128)S(1)} async-done(((f32[32,2,128]{2,1,0:T(2,128)}), f32[32,2,128]{2,1,0:T(2,128)S(1)}, u32[]{:S(2)}, u32[]{:S(2)}) %all-to-all-start.6) | async-done | bytes 32800 | tf_op jit(solution)/shard_map/all_to_all | solution.py:875
  (185 shorter events, 19.6 us)
Async XLA Ops:
  7.2 42.6 %all-gather.3.cloned.1.call-start = ((), (), s32[]{:S(2)}) async-start(), calls=%async_computation.11 | async-start | bytes 1966080 | tf_op jit(solution)/shard_map/all_gather | solution.py:938
  9.7 93.3 %copy-start.1 = (bf16[120,768]{1,0:T(8,128)(2,1)}, bf16[120,768]{1,0:T(8,128)(2,1)S(1)}, u32[]{:S(2)}) copy-start(bf16[120,768]{1,0:T(8,128)(2,1)S(1)} %constant_dynamic-update-slice_fusion.a0.b0) | copy-start | bytes 552964
  9.7 18.1 %collective-permute-start = (bf16[120,768]{1,0:T(8,128)(2,1)S(1)}, bf16[120,768]{1,0:T(8,128)(2,1)S(1)}, u32[]{:S(2)}, u32[]{:S(2)}) collective-permute-start(bf16[120,768]{1,0:T(8,128)(2,1)S(1)} %constant_dynamic-update-slice_fusion.a0.b0), channel_id=1, source_target_pairs={{0,2},{1,3},{2,0},{3,1},{4,6},{5,7},{6,4},{7,5},{8,10},{9,11},{10,... | collective-permute-start | bytes 552968 | tf_op jit(solution)/shard_map/ppermute | solution.py:866
  12.8 15.0 %collective-permute-start.1 = (bf16[120,768]{1,0:T(8,128)(2,1)S(1)}, bf16[120,768]{1,0:T(8,128)(2,1)S(1)}, u32[]{:S(2)}, u32[]{:S(2)}) collective-permute-start(bf16[120,768]{1,0:T(8,128)(2,1)S(1)} %constant_dynamic-update-slice_fusion.a0.b0), channel_id=1, source_target_pairs={{0,4},{1,5},{2,6},{3,7},{4,0},{5,1},{6,2},{7,3},{8,12},{9,13},{10,... | collective-permute-start | bytes 552968 | tf_op jit(solution)/shard_map/ppermute | solution.py:866
  15.4 12.4 %all-to-all-start = ((bf16[4,24,1408]{2,1,0:T(8,128)(2,1)}), bf16[4,24,1408]{2,1,0:T(8,128)(2,1)S(1)}, u32[]{:S(2)}, u32[]{:S(2)}) async-start(bf16[4,24,1408]{2,1,0:T(8,128)(2,1)} %get-tuple-element.104), calls=%async_computation | async-start | bytes 540672 | tf_op jit(solution)/shard_map/all_to_all | solution.py:875
  27.8 75.2 %copy-start.4 = (bf16[120,768]{1,0:T(8,128)(2,1)}, bf16[120,768]{1,0:T(8,128)(2,1)S(1)}, u32[]{:S(2)}) copy-start(bf16[120,768]{1,0:T(8,128)(2,1)S(1)} %collective-permute-done.a2.b2) | copy-start | bytes 552964
  27.8 75.2 %copy-start.5 = (bf16[120,768]{1,0:T(8,128)(2,1)}, bf16[120,768]{1,0:T(8,128)(2,1)S(1)}, u32[]{:S(2)}) copy-start(bf16[120,768]{1,0:T(8,128)(2,1)S(1)} %collective-permute-done.1.a4.b4) | copy-start | bytes 552964
  27.8 22.0 %copy-start.26 = (bf16[96,640]{1,0:T(8,128)(2,1)}, bf16[96,640]{1,0:T(8,128)(2,1)S(1)}, u32[]{:S(2)}) copy-start(bf16[96,640]{1,0:T(8,128)(2,1)S(1)} %slice.64.a0) | copy-start | bytes 368644
  27.8 6.6 %collective-permute-start.3 = (bf16[96,640]{1,0:T(8,128)(2,1)S(1)}, bf16[96,640]{1,0:T(8,128)(2,1)S(1)}, u32[]{:S(2)}, u32[]{:S(2)}) collective-permute-start(bf16[96,640]{1,0:T(8,128)(2,1)S(1)} %slice.64.a0), channel_id=1, source_target_pairs={{0,2},{1,3},{2,0},{3,1},{4,6},{5,7},{6,4},{7,5},{8,10},{9,11},{10,... | collective-permute-start | bytes 368648 | tf_op jit(solution)/shard_map/ppermute | solution.py:866
  27.9 15.5 %collective-permute-start.5 = (bf16[96,640]{1,0:T(8,128)(2,1)S(1)}, bf16[96,640]{1,0:T(8,128)(2,1)S(1)}, u32[]{:S(2)}, u32[]{:S(2)}) collective-permute-start(bf16[96,640]{1,0:T(8,128)(2,1)S(1)} %slice.64.a0), channel_id=1, source_target_pairs={{0,4},{1,5},{2,6},{3,7},{4,0},{5,1},{6,2},{7,3},{8,12},{9,13},{10,... | collective-permute-start | bytes 368648 | tf_op jit(solution)/shard_map/ppermute | solution.py:866
  28.0 17.0 %collective-permute-start.7 = (bf16[96,640]{1,0:T(8,128)(2,1)S(1)}, bf16[96,640]{1,0:T(8,128)(2,1)S(1)}, u32[]{:S(2)}, u32[]{:S(2)}) collective-permute-start(bf16[96,640]{1,0:T(8,128)(2,1)S(1)} %slice.64.a0), channel_id=1, source_target_pairs={{0,6},{1,7},{2,4},{3,5},{4,2},{5,3},{6,0},{7,1},{8,14},{9,15},{10,... | collective-permute-start | bytes 368648 | tf_op jit(solution)/shard_map/ppermute | solution.py:866
  32.3 22.6 %collective-permute-start.9 = (bf16[120,768]{1,0:T(8,128)(2,1)S(1)}, bf16[120,768]{1,0:T(8,128)(2,1)S(1)}, u32[]{:S(2)}, u32[]{:S(2)}) collective-permute-start(bf16[120,768]{1,0:T(8,128)(2,1)S(1)} %constant_dynamic-update-slice_fusion.a0.b0), channel_id=1, source_target_pairs={{0,6},{1,7},{2,4},{3,5},{4,2},{5,3},{6,0},{7,1},{8,14},{9,15},{10,... | collective-permute-start | bytes 552968 | tf_op jit(solution)/shard_map/ppermute | solution.py:866
  32.3 13.1 %collective-permute-start.2 = (bf16[96,640]{1,0:T(8,128)(2,1)S(1)}, bf16[96,640]{1,0:T(8,128)(2,1)S(1)}, u32[]{:S(2)}, u32[]{:S(2)}) collective-permute-start(bf16[96,640]{1,0:T(8,128)(2,1)S(1)} %slice.64.a0), channel_id=1, source_target_pairs={{0,1},{1,0},{2,3},{3,2},{4,5},{5,4},{6,7},{7,6},{8,9},{9,8},{10,11... | collective-permute-start | bytes 368648 | tf_op jit(solution)/shard_map/ppermute | solution.py:866
  34.4 11.1 %collective-permute-start.4 = (bf16[96,640]{1,0:T(8,128)(2,1)S(1)}, bf16[96,640]{1,0:T(8,128)(2,1)S(1)}, u32[]{:S(2)}, u32[]{:S(2)}) collective-permute-start(bf16[96,640]{1,0:T(8,128)(2,1)S(1)} %collective-permute-done.3.a2), channel_id=1, source_target_pairs={{0,1},{1,0},{2,3},{3,2},{4,5},{5,4},{6,7},{7,6},{8,9},{9,8},{10,11... | collective-permute-start | bytes 368648 | tf_op jit(solution)/shard_map/ppermute | solution.py:866
  43.4 4.9 %collective-permute-start.6 = (bf16[96,640]{1,0:T(8,128)(2,1)S(1)}, bf16[96,640]{1,0:T(8,128)(2,1)S(1)}, u32[]{:S(2)}, u32[]{:S(2)}) collective-permute-start(bf16[96,640]{1,0:T(8,128)(2,1)S(1)} %collective-permute-done.5.a4), channel_id=1, source_target_pairs={{0,1},{1,0},{2,3},{3,2},{4,5},{5,4},{6,7},{7,6},{8,9},{9,8},{10,11... | collective-permute-start | bytes 368648 | tf_op jit(solution)/shard_map/ppermute | solution.py:866
  44.9 4.9 %collective-permute-start.8 = (bf16[96,640]{1,0:T(8,128)(2,1)S(1)}, bf16[96,640]{1,0:T(8,128)(2,1)S(1)}, u32[]{:S(2)}, u32[]{:S(2)}) collective-permute-start(bf16[96,640]{1,0:T(8,128)(2,1)S(1)} %collective-permute-done.7.a6), channel_id=1, source_target_pairs={{0,1},{1,0},{2,3},{3,2},{4,5},{5,4},{6,7},{7,6},{8,9},{9,8},{10,11... | collective-permute-start | bytes 368648 | tf_op jit(solution)/shard_map/ppermute | solution.py:866
  54.8 48.1 %copy-start.6 = (bf16[120,768]{1,0:T(8,128)(2,1)}, bf16[120,768]{1,0:T(8,128)(2,1)S(1)}, u32[]{:S(2)}) copy-start(bf16[120,768]{1,0:T(8,128)(2,1)S(1)} %collective-permute-done.9.a6.b6) | copy-start | bytes 552964
  54.9 22.1 %all-to-all-start.1 = ((bf16[8,384,128]{2,1,0:T(8,128)(2,1)}), bf16[8,384,128]{2,1,0:T(8,128)(2,1)S(1)}, u32[]{:S(2)}, u32[]{:S(2)}) async-start(bf16[8,384,128]{2,1,0:T(8,128)(2,1)} %get-tuple-element.114), calls=%async_computation.1 | async-start | bytes 1572864 | tf_op jit(solution)/shard_map/all_to_all | solution.py:875
  58.8 13.2 %collective-permute-start.10 = (bf16[120,768]{1,0:T(8,128)(2,1)S(1)}, bf16[120,768]{1,0:T(8,128)(2,1)S(1)}, u32[]{:S(2)}, u32[]{:S(2)}) collective-permute-start(bf16[120,768]{1,0:T(8,128)(2,1)S(1)} %constant_dynamic-update-slice_fusion.a0.b0), channel_id=1, source_target_pairs={{0,1},{1,0},{2,3},{3,2},{4,5},{5,4},{6,7},{7,6},{8,9},{9,8},{10,11... | collective-permute-start | bytes 552968 | tf_op jit(solution)/shard_map/ppermute | solution.py:866
  60.8 16.2 %collective-permute-start.11 = (bf16[120,768]{1,0:T(8,128)(2,1)S(1)}, bf16[120,768]{1,0:T(8,128)(2,1)S(1)}, u32[]{:S(2)}, u32[]{:S(2)}) collective-permute-start(bf16[120,768]{1,0:T(8,128)(2,1)S(1)} %collective-permute-done.a2.b2), channel_id=1, source_target_pairs={{0,1},{1,0},{2,3},{3,2},{4,5},{5,4},{6,7},{7,6},{8,9},{9,8},{10,11... | collective-permute-start | bytes 552968 | tf_op jit(solution)/shard_map/ppermute | solution.py:866
  60.8 27.9 %collective-permute-start.15 = (bf16[120,768]{1,0:T(8,128)(2,1)S(1)}, bf16[120,768]{1,0:T(8,128)(2,1)S(1)}, u32[]{:S(2)}, u32[]{:S(2)}) collective-permute-start(bf16[120,768]{1,0:T(8,128)(2,1)S(1)} %collective-permute-done.1.a4.b4), channel_id=1, source_target_pairs={{0,1},{1,0},{2,3},{3,2},{4,5},{5,4},{6,7},{7,6},{8,9},{9,8},{10,11... | collective-permute-start | bytes 552968 | tf_op jit(solution)/shard_map/ppermute | solution.py:866
  62.8 25.9 %collective-permute-start.16 = (bf16[120,768]{1,0:T(8,128)(2,1)S(1)}, bf16[120,768]{1,0:T(8,128)(2,1)S(1)}, u32[]{:S(2)}, u32[]{:S(2)}) collective-permute-start(bf16[120,768]{1,0:T(8,128)(2,1)S(1)} %collective-permute-done.9.a6.b6), channel_id=1, source_target_pairs={{0,1},{1,0},{2,3},{3,2},{4,5},{5,4},{6,7},{7,6},{8,9},{9,8},{10,11... | collective-permute-start | bytes 552968 | tf_op jit(solution)/shard_map/ppermute | solution.py:866
  62.9 32.1 %copy-start.23 = (bf16[96,768]{1,0:T(8,128)(2,1)}, bf16[96,768]{1,0:T(8,128)(2,1)S(1)}, u32[]{:S(2)}) copy-start(bf16[96,768]{1,0:T(8,128)(2,1)S(1)} %slice.83.a0) | copy-start | bytes 442372
  62.9 40.1 %copy-start.15 = (s32[2]{0:T(128)S(1)}, s32[2]{0:T(128)}, u32[]{:S(2)}) copy-start(s32[2]{0:T(128)} %pad_add_fusion.at_ref) | copy-start | bytes 28
  72.0 31.0 %copy-start.7 = (bf16[120,768]{1,0:T(8,128)(2,1)}, bf16[120,768]{1,0:T(8,128)(2,1)S(1)}, u32[]{:S(2)}) copy-start(bf16[120,768]{1,0:T(8,128)(2,1)S(1)} %collective-permute-done.10.a1.b1) | copy-start | bytes 552964
  77.0 26.0 %copy-start.8 = (bf16[120,768]{1,0:T(8,128)(2,1)}, bf16[120,768]{1,0:T(8,128)(2,1)S(1)}, u32[]{:S(2)}) copy-start(bf16[120,768]{1,0:T(8,128)(2,1)S(1)} %collective-permute-done.11.a3.b3) | copy-start | bytes 552964
  77.0 11.7 %collective-permute-start.12 = (bf16[96,768]{1,0:T(8,128)(2,1)S(1)}, bf16[96,768]{1,0:T(8,128)(2,1)S(1)}, u32[]{:S(2)}, u32[]{:S(2)}) collective-permute-start(bf16[96,768]{1,0:T(8,128)(2,1)S(1)} %slice.83.a0), channel_id=1, source_target_pairs={{0,2},{1,3},{2,0},{3,1},{4,6},{5,7},{6,4},{7,5},{8,10},{9,11},{10,... | collective-permute-start | bytes 442376 | tf_op jit(solution)/shard_map/ppermute | solution.py:866
  79.3 9.4 %collective-permute-start.13 = (bf16[96,768]{1,0:T(8,128)(2,1)S(1)}, bf16[96,768]{1,0:T(8,128)(2,1)S(1)}, u32[]{:S(2)}, u32[]{:S(2)}) collective-permute-start(bf16[96,768]{1,0:T(8,128)(2,1)S(1)} %slice.83.a0), channel_id=1, source_target_pairs={{0,4},{1,5},{2,6},{3,7},{4,0},{5,1},{6,2},{7,3},{8,12},{9,13},{10,... | collective-permute-start | bytes 442376 | tf_op jit(solution)/shard_map/ppermute | solution.py:866
  81.0 7.7 %collective-permute-start.14 = (bf16[96,768]{1,0:T(8,128)(2,1)S(1)}, bf16[96,768]{1,0:T(8,128)(2,1)S(1)}, u32[]{:S(2)}, u32[]{:S(2)}) collective-permute-start(bf16[96,768]{1,0:T(8,128)(2,1)S(1)} %slice.83.a0), channel_id=1, source_target_pairs={{0,6},{1,7},{2,4},{3,5},{4,2},{5,3},{6,0},{7,1},{8,14},{9,15},{10,... | collective-permute-start | bytes 442376 | tf_op jit(solution)/shard_map/ppermute | solution.py:866
  88.7 17.3 %copy-start.10 = (bf16[120,768]{1,0:T(8,128)(2,1)}, bf16[120,768]{1,0:T(8,128)(2,1)S(1)}, u32[]{:S(2)}) copy-start(bf16[120,768]{1,0:T(8,128)(2,1)S(1)} %collective-permute-done.16.a7.b7) | copy-start | bytes 552964
  88.7 18.2 %copy-start.30 = (bf16[96,768]{1,0:T(8,128)(2,1)}, bf16[96,768]{1,0:T(8,128)(2,1)S(1)}, u32[]{:S(2)}) copy-start(bf16[96,768]{1,0:T(8,128)(2,1)S(1)} %collective-permute-done.12.a2) | copy-start | bytes 442372
  89.5 13.4 %all-to-all-start.2 = ((bf16[8,128,128]{2,1,0:T(8,128)(2,1)}), bf16[8,128,128]{2,1,0:T(8,128)(2,1)S(1)}, u32[]{:S(2)}, u32[]{:S(2)}) async-start(bf16[8,128,128]{2,1,0:T(8,128)(2,1)} %get-tuple-element.124), calls=%async_computation.2 | async-start | bytes 524288 | tf_op jit(solution)/shard_map/all_to_all | solution.py:875
  94.8 76.2 %reduce-scatter.3.cloned.1.call-start = ((), (), s32[]{:S(2)}) async-start(), calls=%async_computation.9 | async-start | bytes 737280 | tf_op jit(solution)/shard_map/reduce_scatter | solution.py:871
  95.0 6.6 %collective-permute-start.17 = (bf16[96,768]{1,0:T(8,128)(2,1)S(1)}, bf16[96,768]{1,0:T(8,128)(2,1)}, u32[]{:S(2)}, u32[]{:S(2)}) collective-permute-start(bf16[96,768]{1,0:T(8,128)(2,1)S(1)} %slice.83.a0), channel_id=1, source_target_pairs={{0,1},{1,0},{2,3},{3,2},{4,5},{5,4},{6,7},{7,6},{8,9},{9,8},{10,11... | collective-permute-start | bytes 442376 | tf_op jit(solution)/shard_map/ppermute | solution.py:866
  104.1 1.8 collective-permute-start.18
  106.0 12.9 %collective-permute-start.19 = (bf16[2,2,64,768]{3,2,1,0:T(8,128)(2,1)S(1)}, bf16[2,2,64,768]{3,2,1,0:T(8,128)(2,1)S(1)}, u32[]{:S(2)}, u32[]{:S(2)}) collective-permute-start(bf16[2,2,64,768]{3,2,1,0:T(8,128)(2,1)S(1)} %add_convert_fusion.7), channel_id=1, source_target_pairs={{0,16},{8,24},{16,0},{24,8},{1,17},{9,25},{17,1},{25,9},{2,18},{10... | collective-permute-start | bytes 1179656 | tf_op jit(solution)/shard_map/ppermute | solution.py:862
  107.0 6.7 %collective-permute-start.20 = (bf16[96,768]{1,0:T(8,128)(2,1)S(1)}, bf16[96,768]{1,0:T(8,128)(2,1)S(1)}, u32[]{:S(2)}, u32[]{:S(2)}) collective-permute-start(bf16[96,768]{1,0:T(8,128)(2,1)S(1)} %collective-permute-done.12.a2), channel_id=1, source_target_pairs={{0,1},{1,0},{2,3},{3,2},{4,5},{5,4},{6,7},{7,6},{8,9},{9,8},{10,11... | collective-permute-start | bytes 442376 | tf_op jit(solution)/shard_map/ppermute | solution.py:866
  107.0 9.9 %collective-permute-start.21 = (bf16[96,768]{1,0:T(8,128)(2,1)S(1)}, bf16[96,768]{1,0:T(8,128)(2,1)S(1)}, u32[]{:S(2)}, u32[]{:S(2)}) collective-permute-start(bf16[96,768]{1,0:T(8,128)(2,1)S(1)} %copy-done.32), channel_id=1, source_target_pairs={{0,1},{1,0},{2,3},{3,2},{4,5},{5,4},{6,7},{7,6},{8,9},{9,8},{10,11... | collective-permute-start | bytes 442376 | tf_op jit(solution)/shard_map/ppermute | solution.py:866
  109.0 9.9 %collective-permute-start.22 = (bf16[96,768]{1,0:T(8,128)(2,1)S(1)}, bf16[96,768]{1,0:T(8,128)(2,1)S(1)}, u32[]{:S(2)}, u32[]{:S(2)}) collective-permute-start(bf16[96,768]{1,0:T(8,128)(2,1)S(1)} %copy-done.34), channel_id=1, source_target_pairs={{0,1},{1,0},{2,3},{3,2},{4,5},{5,4},{6,7},{7,6},{8,9},{9,8},{10,11... | collective-permute-start | bytes 442376 | tf_op jit(solution)/shard_map/ppermute | solution.py:866
  119.1 1.8 collective-permute-start.23
  130.5 2.0 collective-permute-start.24
  130.7 15.8 %collective-permute-start.26 = (bf16[4,96,768]{2,1,0:T(8,128)(2,1)}, bf16[4,96,768]{2,1,0:T(8,128)(2,1)S(1)}, u32[]{:S(2)}, u32[]{:S(2)}) collective-permute-start(bf16[4,96,768]{2,1,0:T(8,128)(2,1)} %get-tuple-element.154), channel_id=1, source_target_pairs={{0,1},{1,0},{2,3},{3,2},{4,5},{5,4},{6,7},{7,6},{8,9},{9,8},{10,11... | collective-permute-start | bytes 1769480 | tf_op jit(solution)/shard_map/ppermute | solution.py:866
  133.6 12.9 %collective-permute-start.25 = (bf16[2,2,64,768]{3,2,1,0:T(8,128)(2,1)S(1)}, bf16[2,2,64,768]{3,2,1,0:T(8,128)(2,1)S(1)}, u32[]{:S(2)}, u32[]{:S(2)}) collective-permute-start(bf16[2,2,64,768]{3,2,1,0:T(8,128)(2,1)S(1)} %add_convert_fusion.5), channel_id=1, source_target_pairs={{0,16},{8,24},{16,0},{24,8},{1,17},{9,25},{17,1},{25,9},{2,18},{10... | collective-permute-start | bytes 1179656 | tf_op jit(solution)/shard_map/ppermute | solution.py:862
  147.5 15.6 %collective-permute-start.28 = (bf16[4,4,24,768]{3,2,1,0:T(8,128)(2,1)}, bf16[4,4,24,768]{3,2,1,0:T(8,128)(2,1)S(1)}, u32[]{:S(2)}, u32[]{:S(2)}) collective-permute-start(bf16[4,4,24,768]{3,2,1,0:T(8,128)(2,1)} %get-tuple-element.160), channel_id=1, source_target_pairs={{0,1},{1,0},{2,3},{3,2},{4,5},{5,4},{6,7},{7,6},{8,9},{9,8},{10,11... | collective-permute-start | bytes 1769480 | tf_op jit(solution)/shard_map/ppermute | solution.py:866
  148.0 1.8 collective-permute-start.27
  155.1 15.9 %all-to-all-start.3 = ((bf16[8,128,128]{2,1,0:T(8,128)(2,1)}), bf16[8,128,128]{2,1,0:T(8,128)(2,1)S(1)}, u32[]{:S(2)}, u32[]{:S(2)}) async-start(bf16[8,128,128]{2,1,0:T(8,128)(2,1)} %get-tuple-element.158), calls=%async_computation.3 | async-start | bytes 524288 | tf_op jit(solution)/shard_map/all_to_all | solution.py:875
  159.3 36.5 %reduce-scatter.5.cloned.1.call-start = ((), (), s32[]{:S(2)}) async-start(), calls=%async_computation.10 | async-start | bytes 737280 | tf_op jit(solution)/shard_map/reduce_scatter | solution.py:871
  159.6 8.2 %collective-permute-start.29 = (bf16[4,24,768]{2,1,0:T(8,128)(2,1)}, bf16[4,24,768]{2,1,0:T(8,128)(2,1)S(1)}, u32[]{:S(2)}, u32[]{:S(2)}) collective-permute-start(bf16[4,24,768]{2,1,0:T(8,128)(2,1)} %get-tuple-element.161), channel_id=1, source_target_pairs={{0,1},{1,0},{2,3},{3,2},{4,5},{5,4},{6,7},{7,6},{8,9},{9,8},{10,11... | collective-permute-start | bytes 442376 | tf_op jit(solution)/shard_map/ppermute | solution.py:866
  182.5 26.3 %all-to-all-start.4 = ((bf16[8,384,128]{2,1,0:T(8,128)(2,1)}), bf16[8,384,128]{2,1,0:T(8,128)(2,1)S(1)}, u32[]{:S(2)}, u32[]{:S(2)}) async-start(bf16[8,384,128]{2,1,0:T(8,128)(2,1)} %attn_bwd.1), calls=%async_computation.5 | async-start | bytes 1572864 | tf_op jit(solution)/shard_map/all_to_all | solution.py:875
  187.0 1.8 collective-permute-start.33
  188.9 9.8 %collective-permute-start.34 = (bf16[2,64,768]{2,1,0:T(8,128)(2,1)S(1)}, bf16[2,64,768]{2,1,0:T(8,128)(2,1)S(1)}, u32[]{:S(2)}, u32[]{:S(2)}) collective-permute-start(bf16[2,64,768]{2,1,0:T(8,128)(2,1)S(1)} %slice_bitcast_fusion.2), channel_id=1, source_target_pairs={{0,16},{8,24},{16,0},{24,8},{1,17},{9,25},{17,1},{25,9},{2,18},{10... | collective-permute-start | bytes 589832 | tf_op jit(solution)/shard_map/ppermute | solution.py:862
  196.8 2.8 %collective-permute-start.30 = (f32[24,768]{1,0:T(8,128)S(1)}, f32[24,768]{1,0:T(8,128)S(1)}, u32[]{:S(2)}, u32[]{:S(2)}) collective-permute-start(f32[24,768]{1,0:T(8,128)S(1)} %get-tuple-element.204), channel_id=1, source_target_pairs={{0,8},{8,0},{16,24},{24,16},{1,9},{9,1},{17,25},{25,17},{2,10},{10... | collective-permute-start | bytes 221192 | tf_op jit(solution)/shard_map/ppermute | solution.py:862
  196.8 4.7 %collective-permute-start.31 = (f32[24,768]{1,0:T(8,128)S(1)}, f32[24,768]{1,0:T(8,128)S(1)}, u32[]{:S(2)}, u32[]{:S(2)}) collective-permute-start(f32[24,768]{1,0:T(8,128)S(1)} %get-tuple-element.203), channel_id=1, source_target_pairs={{0,16},{8,24},{16,0},{24,8},{1,17},{9,25},{17,1},{25,9},{2,18},{10... | collective-permute-start | bytes 221192 | tf_op jit(solution)/shard_map/ppermute | solution.py:862
  198.5 4.2 %collective-permute-start.32 = (f32[24,768]{1,0:T(8,128)S(1)}, f32[24,768]{1,0:T(8,128)S(1)}, u32[]{:S(2)}, u32[]{:S(2)}) collective-permute-start(f32[24,768]{1,0:T(8,128)S(1)} %get-tuple-element.202), channel_id=1, source_target_pairs={{0,24},{8,16},{16,8},{24,0},{1,25},{9,17},{17,9},{25,1},{2,26},{10... | collective-permute-start | bytes 221192 | tf_op jit(solution)/shard_map/ppermute | solution.py:862
  215.1 32.4 %all-to-all-start.5 = ((bf16[32,24,640]{2,1,0:T(8,128)(2,1)}), bf16[32,24,640]{2,1,0:T(8,128)(2,1)S(1)}, u32[]{:S(2)}, u32[]{:S(2)}) async-start(bf16[32,24,640]{2,1,0:T(8,128)(2,1)} %get-tuple-element.185), calls=%async_computation.7 | async-start | bytes 1966080 | tf_op jit(solution)/shard_map/all_to_all | solution.py:875
  219.2 1.8 collective-permute-start.35
  221.0 17.5 %copy-start.38 = (bf16[1,96,768]{2,1,0:T(8,128)(2,1)S(1)}, bf16[1,96,768]{2,1,0:T(8,128)(2,1)}, u32[]{:S(2)}) copy-start(bf16[1,96,768]{2,1,0:T(8,128)(2,1)} %reduce-scatter.3.cloned.1.call-done) | copy-start | bytes 442372
  221.1 18.1 %copy-start.3 = (f32[2,5376]{1,0:T(2,128)S(1)}, f32[2,5376]{1,0:T(2,128)}, u32[]{:S(2)}) copy-start(f32[2,5376]{1,0:T(2,128)} %get-tuple-element.143.table_ref) | copy-start | bytes 129028
  221.1 18.1 %copy-start.11 = (f32[2,64,768]{2,1,0:T(8,128)S(1)}, f32[2,64,768]{2,1,0:T(8,128)}, u32[]{:S(2)}) copy-start(f32[2,64,768]{2,1,0:T(8,128)} %get-tuple-element.184.dmid_ref) | copy-start | bytes 1179652
  221.2 12.4 %collective-permute-start.36 = (bf16[2,64,768]{2,1,0:T(8,128)(2,1)S(1)}, bf16[2,64,768]{2,1,0:T(8,128)(2,1)S(1)}, u32[]{:S(2)}, u32[]{:S(2)}) collective-permute-start(bf16[2,64,768]{2,1,0:T(8,128)(2,1)S(1)} %get-tuple-element.198), channel_id=1, source_target_pairs={{0,16},{8,24},{16,0},{24,8},{1,17},{9,25},{17,1},{25,9},{2,18},{10... | collective-permute-start | bytes 589832 | tf_op jit(solution)/shard_map/ppermute | solution.py:862
  233.7 6.6 %collective-permute-start.37 = (bf16[24,768]{1,0:T(8,128)(2,1)S(1)}, bf16[24,768]{1,0:T(8,128)(2,1)S(1)}, u32[]{:S(2)}, u32[]{:S(2)}) collective-permute-start(bf16[24,768]{1,0:T(8,128)(2,1)S(1)} %get-tuple-element.206), channel_id=1, source_target_pairs={{0,2},{1,3},{2,0},{3,1},{4,6},{5,7},{6,4},{7,5},{8,10},{9,11},{10,... | collective-permute-start | bytes 110600 | tf_op jit(solution)/shard_map/ppermute | solution.py:866
  235.2 11.6 %collective-permute-start.38 = (bf16[24,768]{1,0:T(8,128)(2,1)S(1)}, bf16[24,768]{1,0:T(8,128)(2,1)S(1)}, u32[]{:S(2)}, u32[]{:S(2)}) collective-permute-start(bf16[24,768]{1,0:T(8,128)(2,1)S(1)} %get-tuple-element.208), channel_id=1, source_target_pairs={{0,4},{1,5},{2,6},{3,7},{4,0},{5,1},{6,2},{7,3},{8,12},{9,13},{10,... | collective-permute-start | bytes 110600 | tf_op jit(solution)/shard_map/ppermute | solution.py:866
  238.5 8.3 %collective-permute-start.39 = (bf16[24,768]{1,0:T(8,128)(2,1)S(1)}, bf16[24,768]{1,0:T(8,128)(2,1)S(1)}, u32[]{:S(2)}, u32[]{:S(2)}) collective-permute-start(bf16[24,768]{1,0:T(8,128)(2,1)S(1)} %get-tuple-element.207), channel_id=1, source_target_pairs={{0,6},{1,7},{2,4},{3,5},{4,2},{5,3},{6,0},{7,1},{8,14},{9,15},{10,... | collective-permute-start | bytes 110600 | tf_op jit(solution)/shard_map/ppermute | solution.py:866
  249.1 10.5 %all-to-all-start.6 = ((f32[32,2,128]{2,1,0:T(2,128)}), f32[32,2,128]{2,1,0:T(2,128)S(1)}, u32[]{:S(2)}, u32[]{:S(2)}) async-start(f32[32,2,128]{2,1,0:T(2,128)} %get-tuple-element.190), calls=%async_computation.8 | async-start | bytes 65536 | tf_op jit(solution)/shard_map/all_to_all | solution.py:875
  (37 other events, 254.8 us)
Sparse Core Ops, SparseCore 0:
  10.2 24.6 all-gather.2
  147.6 22.2 reduce-scatter.2
  172.2 23.5 reduce-scatter.4

commit v4 on v3

--- a/solution.py
+++ b/solution.py
@@ -706,7 +706,7 @@
     outs_ref[...] = dot_tn(att_ref[...], branch_ref[...])
     for y, out_ref in enumerate((okeep_ref, osend_ref)):
         for z in range(n_z):
-            start = pl.multiple_of((at_ref[1] ^ (2 * z + y)) * block, 8)
+            start = pl.multiple_of((2 * z + ((at_ref[1] % 2) ^ y)) * block, 8)
             out_ref[z] = outs_ref[pl.ds(start, block), :].astype(bf16)
 
 
@@ -1005,7 +1005,8 @@
     d_attn = exchange(d_chunks, "blk")
     out_other = swap_b(out_send, 1)
     up_low = pair_sum(up_keep, up_other)
-    d_attn, up_low, out_other, down_grad = lax.optimization_barrier((d_attn, up_low, out_other, down_grad))
+    d_attn, out_other, down_grad = lax.optimization_barrier((d_attn, out_other, down_grad))
+    up_low = jnp.concatenate([up_low, pair_sum(out_keep, out_other)[:, None]], axis=1)
     up_sum = scatter_z(up_low)
     d_owned = attn_bwd(owned, d_attn, attn_full, log_total)
     d_owned, lsend, lkeep = lax.optimization_barrier((d_owned, lsend, lkeep))
@@ -1029,8 +1030,6 @@
     )
     half = half_sum(send, keep)
     far = swap_u(half[1], 2)
-    far, out_other = lax.optimization_barrier((far, out_other))
-    out_grad = sum_z(out_keep.astype(f32) + out_other.astype(f32))
     inputs_grad, = call(
         input_grad_kernel, "input_grad",
         [((seqs, rows, width), f32)], [], 0,
@@ -1051,7 +1050,7 @@
         conditioning_grad,
         ada_grad.T,
         qkv_grad,
-        out_grad,
+        up_sum[n_u],
         up_grad,
         down_grad.astype(f32),
         gain_grads[0],

time: 267 us -> 266 us (level)
  starting transfers between devices: 72.5 us -> 66.4 us
  waiting for transfers between devices: 118 us -> 121 us
    all_to_all x7, waiting for transfers between devices: 23.9 us -> 39.1 us  [exchange(): return lax.all_to_all(blocks, axis, split_axis=0, concat_axis=0, tiled=True)]
    ppermute x27 -> x24, waiting for transfers between devices: 64.9 us -> 59 us  [swap_b(): return lax.ppermute(values, 'blk', [(i, i ^ mask) for i in range(8)])]
    ppermute x27 -> x24, starting transfers between devices: 35.2 us -> 30.4 us  [swap_b(): return lax.ppermute(values, 'blk', [(i, i ^ mask) for i in range(8)])]
    ppermute x13, waiting for transfers between devices: 23.5 us -> 19.5 us  [swap_u(): return lax.ppermute(values, 'ulysses', [(i, i ^ mask) for i in range(4)])]
  transfers between devices with their start and end apart: 50 -> 47, of which waited for: 29 -> 27; matrix products, arithmetic and copies ran while one was open for 3% -> 3% of each run, Pallas kernels for 11% -> 11%
where the time goes in v4:
time: 266 us; the launch traced here: 265 us
  waiting for transfers between devices  121 us (45%)
  starting transfers between devices  66.4 us (25%)
  Pallas kernels  47.7 us (18%)
  between operations  14.5 us (5%)
  other arithmetic  10 us (4%)
  local copies, waits for them, and re-layouts  5.41 us (2%)
    ppermute x24, waiting for transfers between devices, swap_b(): return lax.ppermute(values, 'blk', [(i, i ^ mask) for i in range(8)])  59 us
    all_to_all x7, waiting for transfers between devices, exchange(): return lax.all_to_all(blocks, axis, split_axis=0, concat_axis=0, tiled=True)  39.1 us
    ppermute x24, starting transfers between devices, swap_b(): return lax.ppermute(values, 'blk', [(i, i ^ mask) for i in range(8)])  30.4 us
    pallas_call x8, Pallas kernels, call(): pl.pallas_call(body, out_shape=tuple((jax.ShapeDtypeStruct(shape, dtype)...  29.2 us
    all_to_all x7, starting transfers between devices, exchange(): return lax.all_to_all(blocks, axis, split_axis=0, concat_axis=0, tiled=True)  27.5 us
    ppermute x13, waiting for transfers between devices, swap_u(): return lax.ppermute(values, 'ulysses', [(i, i ^ mask) for i in range(4)])  19.5 us
    pallas_call x1, Pallas kernels, attn_bwd(): pl.pallas_call(attn_bwd_kernel, out_shape=jax.ShapeDtypeStruct((nb, rows3...  11.6 us
    ppermute x13, starting transfers between devices, swap_u(): return lax.ppermute(values, 'ulysses', [(i, i ^ mask) for i in range(4)])  8.02 us
  transfers between devices with their start and end apart: 47, of which 27 were waited for; matrix products, arithmetic and copies ran while one was open for 3% of the time, Pallas kernels for 11%

profile of v4, /device:TPU:0, one launch (start us, length us, event | category | flops | bytes accessed | tf_op | source)
XLA Modules:
  0.0 265.4 jit_solution(3767714121645137077)
XLA Ops:
  7.2 2.3 pack.1
  9.7 3.1 %collective-permute-start = (bf16[120,768]{1,0:T(8,128)(2,1)S(1)}, bf16[120,768]{1,0:T(8,128)(2,1)S(1)}, u32[]{:S(2)}, u32[]{:S(2)}) collective-permute-start(bf16[120,768]{1,0:T(8,128)(2,1)S(1)} %constant_dynamic-update-slice_fusion.a0.b0), channel_id=1, source_target_pairs={{0,2},{1,3},{2,0},{3,1},{4,6},{5,7},{6,4},{7,5},{8,10},{9,11},{10,... | collective-permute-start | bytes 552968 | tf_op jit(solution)/shard_map/ppermute | solution.py:866
  12.8 2.6 collective-permute-start.1
  15.4 3.4 %all-to-all-start = ((bf16[4,24,1408]{2,1,0:T(8,128)(2,1)}), bf16[4,24,1408]{2,1,0:T(8,128)(2,1)S(1)}, u32[]{:S(2)}, u32[]{:S(2)}) async-start(bf16[4,24,1408]{2,1,0:T(8,128)(2,1)} %get-tuple-element.101), calls=%async_computation | async-start | bytes 540672 | tf_op jit(solution)/shard_map/all_to_all | solution.py:875
  20.1 1.0 pad_maximum_fusion.1
  21.1 6.7 %all-to-all-done = bf16[4,24,1408]{2,1,0:T(8,128)(2,1)S(1)} async-done(((bf16[4,24,1408]{2,1,0:T(8,128)(2,1)}), bf16[4,24,1408]{2,1,0:T(8,128)(2,1)S(1)}, u32[]{:S(2)}, u32[]{:S(2)}) %all-to-all-start) | async-done | bytes 270368 | tf_op jit(solution)/shard_map/all_to_all | solution.py:875
  28.0 4.3 %collective-permute-start.7 = (bf16[96,640]{1,0:T(8,128)(2,1)S(1)}, bf16[96,640]{1,0:T(8,128)(2,1)S(1)}, u32[]{:S(2)}, u32[]{:S(2)}) collective-permute-start(bf16[96,640]{1,0:T(8,128)(2,1)S(1)} %slice.53.a0), channel_id=1, source_target_pairs={{0,6},{1,7},{2,4},{3,5},{4,2},{5,3},{6,0},{7,1},{8,14},{9,15},{10,... | collective-permute-start | bytes 368648 | tf_op jit(solution)/shard_map/ppermute | solution.py:866
  32.3 1.5 collective-permute-start.2
  34.4 1.5 collective-permute-start.4
  35.9 7.5 %collective-permute-done.5.a4 = bf16[96,640]{1,0:T(8,128)(2,1)S(1)} collective-permute-done((bf16[96,640]{1,0:T(8,128)(2,1)S(1)}, bf16[96,640]{1,0:T(8,128)(2,1)S(1)}, u32[]{:S(2)}, u32[]{:S(2)}) %collective-permute-start.5) | collective-permute-done | bytes 122912 | tf_op jit(solution)/shard_map/ppermute | solution.py:866
  43.4 1.5 collective-permute-start.6
  45.5 2.8 %collective-permute-done.6.a5 = bf16[96,640]{1,0:T(8,128)(2,1)S(1)} collective-permute-done((bf16[96,640]{1,0:T(8,128)(2,1)S(1)}, bf16[96,640]{1,0:T(8,128)(2,1)S(1)}, u32[]{:S(2)}, u32[]{:S(2)}) %collective-permute-start.6) | collective-permute-done | bytes 122912 | tf_op jit(solution)/shard_map/ppermute | solution.py:866
  48.3 1.5 collective-permute-done.8.a7
  50.5 4.4 %first.1 = (bf16[8,384,128]{2,1,0:T(8,128)(2,1)}, bf16[512,768]{1,0:T(8,128)(2,1)}, f32[2,5376]{1,0:T(2,128)}, bf16[768,576]{1,0:T(8,128)(2,1)}) custom-call(s32[2]{0:T(128)} %pad_add_fusion.at_ref, bf16[4,2,2,64,768]{4,3,2,1,0:T(8,128)(2,1)} %bitcast.49, f32[256,128]{1,0:T(8,128)} %get-tuple-element.104.cos_ref, f32[256,128]{1,0:T(8,128)} %get-tuple-element.105.sin_ref, ...), custom_call_target="tpu_custom_call" | custom-call | flops 452984 | bytes 5318 | tf_op jit(solution)/shard_map/first/pallas_call | solution.py:844
  54.9 3.9 %all-to-all-start.1 = ((bf16[8,384,128]{2,1,0:T(8,128)(2,1)}), bf16[8,384,128]{2,1,0:T(8,128)(2,1)S(1)}, u32[]{:S(2)}, u32[]{:S(2)}) async-start(bf16[8,384,128]{2,1,0:T(8,128)(2,1)} %get-tuple-element.111), calls=%async_computation.1 | async-start | bytes 1572864 | tf_op jit(solution)/shard_map/all_to_all | solution.py:875
  58.8 2.0 collective-permute-start.10
  60.8 2.0 collective-permute-start.15
  62.9 9.1 %collective-permute-done.10.a1.b1 = bf16[120,768]{1,0:T(8,128)(2,1)S(1)} collective-permute-done((bf16[120,768]{1,0:T(8,128)(2,1)S(1)}, bf16[120,768]{1,0:T(8,128)(2,1)S(1)}, u32[]{:S(2)}, u32[]{:S(2)}) %collective-permute-start.10) | collective-permute-done | bytes 184352 | tf_op jit(solution)/shard_map/ppermute | solution.py:866
  72.0 5.0 %collective-permute-done.11.a3.b3 = bf16[120,768]{1,0:T(8,128)(2,1)S(1)} collective-permute-done((bf16[120,768]{1,0:T(8,128)(2,1)S(1)}, bf16[120,768]{1,0:T(8,128)(2,1)S(1)}, u32[]{:S(2)}, u32[]{:S(2)}) %collective-permute-start.11) | collective-permute-done | bytes 184352 | tf_op jit(solution)/shard_map/ppermute | solution.py:866
  77.0 2.3 collective-permute-start.12
  79.3 1.7 collective-permute-start.13
  81.8 6.9 %attn_fwd.1 = (bf16[8,128,128]{2,1,0:T(8,128)(2,1)}, f32[8,128,128]{2,1,0:T(8,128)S(1)}, f32[8,8,256]{2,1,0:T(8,128)S(1)}) custom-call(bf16[8,384,128]{2,1,0:T(8,128)(2,1)S(1)} %all-to-all-done.1.x_ref), custom_call_target="tpu_custom_call" | custom-call | flops 1073741824 | bytes 2097152 | tf_op jit(solution)/shard_map/attn_fwd/pallas_call | solution.py:43
  89.6 5.2 %all-to-all-start.2 = ((bf16[8,128,128]{2,1,0:T(8,128)(2,1)}), bf16[8,128,128]{2,1,0:T(8,128)(2,1)S(1)}, u32[]{:S(2)}, u32[]{:S(2)}) async-start(bf16[8,128,128]{2,1,0:T(8,128)(2,1)} %get-tuple-element.121), calls=%async_computation.2 | async-start | bytes 524288 | tf_op jit(solution)/shard_map/all_to_all | solution.py:875
  95.0 1.9 collective-permute-start.17
  96.9 4.8 %collective-permute-done.17.a1 = bf16[96,768]{1,0:T(8,128)(2,1)} collective-permute-done((bf16[96,768]{1,0:T(8,128)(2,1)S(1)}, bf16[96,768]{1,0:T(8,128)(2,1)}, u32[]{:S(2)}, u32[]{:S(2)}) %collective-permute-start.17) | collective-permute-done | bytes 147488 | tf_op jit(solution)/shard_map/ppermute | solution.py:866
  101.6 1.4 all-to-all-done.2.t_ref
  103.0 1.0 out.1
  104.2 1.7 collective-permute-done.18
  106.0 1.0 collective-permute-start.19
  107.0 2.0 collective-permute-start.21
  109.1 4.6 %collective-permute-done.20.a3 = bf16[96,768]{1,0:T(8,128)(2,1)S(1)} collective-permute-done((bf16[96,768]{1,0:T(8,128)(2,1)S(1)}, bf16[96,768]{1,0:T(8,128)(2,1)S(1)}, u32[]{:S(2)}, u32[]{:S(2)}) %collective-permute-start.20) | collective-permute-done | bytes 147488 | tf_op jit(solution)/shard_map/ppermute | solution.py:866
  113.7 3.2 %collective-permute-done.21.a5 = bf16[96,768]{1,0:T(8,128)(2,1)S(1)} collective-permute-done((bf16[96,768]{1,0:T(8,128)(2,1)S(1)}, bf16[96,768]{1,0:T(8,128)(2,1)S(1)}, u32[]{:S(2)}, u32[]{:S(2)}) %collective-permute-start.21) | collective-permute-done | bytes 147488 | tf_op jit(solution)/shard_map/ppermute | solution.py:866
  116.9 2.0 collective-permute-done.22.a7
  119.1 1.7 collective-permute-done.23.got_ref
  121.6 8.9 %ff.1 = (bf16[2,2,64,768]{3,2,1,0:T(8,128)(2,1)}, bf16[2,2,64,768]{3,2,1,0:T(8,128)(2,1)}, bf16[2,2,64,768]{3,2,1,0:T(8,128)(2,1)}, bf16[2,2,64,768]{3,2,1,0:T(8...) custom-call(s32[2]{0:T(128)} %pad_add_fusion.at_ref, ...), custom_call_target="tpu_custom_call" | custom-call | flops 3623878 | bytes 9007 | tf_op jit(solution)/shard_map/ff/pallas_call | solution.py:844
  131.0 1.5 collective-permute-done.24
  132.5 1.1 add_convert_fusion.5
  133.6 1.2 collective-permute-start.25
  134.8 11.7 %collective-permute-done.26 = bf16[4,96,768]{2,1,0:T(8,128)(2,1)S(1)} collective-permute-done((bf16[4,96,768]{2,1,0:T(8,128)(2,1)}, bf16[4,96,768]{2,1,0:T(8,128)(2,1)S(1)}, u32[]{:S(2)}, u32[]{:S(2)}) %collective-permute-start.26) | collective-permute-done | bytes 589856 | tf_op jit(solution)/shard_map/ppermute | solution.py:866
  148.1 1.7 collective-permute-done.27.dgot_ref
  150.6 4.5 %middle_back.1 = (bf16[8,128,128]{2,1,0:T(8,128)(2,1)}, f32[2,64,768]{2,1,0:T(8,128)}, f32[2,1,768]{2,1,0:T(1,128)}, bf16[4,24,768]{2,1,0:T(8,128)(2,1)}, bf16[4,24,768]{2,1,0:T(8,128)(2,1)}) custom-call(s32[2]{0:T(128)} %pad_add_fusion.at_ref, bf16[4,2,2,64,768]{4,3,2,1,0:T(8,128)(2,1)} %bitcast.51, bf16[2,2,64,768]{3,2,1,0:T(8,128)(2,1)} %copy-done.18, ...), custom_call_target="tpu_custom_call" | custom-call | flops 301989 | bytes 4636 | tf_op jit(solution)/shard_map/middle_back/pallas_call | solution.py:844
  155.1 4.3 %all-to-all-start.3 = ((bf16[8,128,128]{2,1,0:T(8,128)(2,1)}), bf16[8,128,128]{2,1,0:T(8,128)(2,1)S(1)}, u32[]{:S(2)}, u32[]{:S(2)}) async-start(bf16[8,128,128]{2,1,0:T(8,128)(2,1)} %get-tuple-element.155), calls=%async_computation.3 | async-start | bytes 524288 | tf_op jit(solution)/shard_map/all_to_all | solution.py:875
  159.7 1.8 collective-permute-start.28
  161.4 1.3 collective-permute-done.29
  162.9 4.8 %collective-permute-done.28 = bf16[4,24,768]{2,1,0:T(8,128)(2,1)} collective-permute-done((bf16[4,24,768]{2,1,0:T(8,128)(2,1)}, bf16[4,24,768]{2,1,0:T(8,128)(2,1)}, u32[]{:S(2)}, u32[]{:S(2)}) %collective-permute-start.28) | collective-permute-done | bytes 147488 | tf_op jit(solution)/shard_map/ppermute | solution.py:866
  167.7 3.3 %all-to-all-done.3.d_ref = bf16[8,128,128]{2,1,0:T(8,128)(2,1)S(1)} async-done(((bf16[8,128,128]{2,1,0:T(8,128)(2,1)}), bf16[8,128,128]{2,1,0:T(8,128)(2,1)S(1)}, u32[]{:S(2)}, u32[]{:S(2)}) %all-to-all-start.3) | async-done | bytes 262176 | tf_op jit(solution)/shard_map/all_to_all | solution.py:875
  171.0 1.0 fusion.3
  173.0 11.6 %attn_bwd.1 = bf16[8,384,128]{2,1,0:T(8,128)(2,1)} custom-call(bf16[8,384,128]{2,1,0:T(8,128)(2,1)S(1)} %all-to-all-done.1.x_ref, bf16[8,128,128]{2,1,0:T(8,128)(2,1)S(1)} %all-to-all-done.3.d_ref, f32[8,128,128]{2,1,0:T(8,128)S(1)} %get-tuple-element.160.of_ref, f32[8,8,256]{2,1,0:T(8,128)S(1)} %get-tuple-element.161.lse_ref), custom_call_target="tpu_custom_call" | custom-call | flops 268435456 | bytes 262144 | tf_op jit(solution)/shard_map/attn_bwd/pallas_call | solution.py:95
  184.6 4.4 %all-to-all-start.4 = ((bf16[8,384,128]{2,1,0:T(8,128)(2,1)}), bf16[8,384,128]{2,1,0:T(8,128)(2,1)S(1)}, u32[]{:S(2)}, u32[]{:S(2)}) async-start(bf16[8,384,128]{2,1,0:T(8,128)(2,1)} %attn_bwd.1), calls=%async_computation.5 | async-start | bytes 1572864 | tf_op jit(solution)/shard_map/all_to_all | solution.py:875
  189.2 1.6 collective-permute-done.33
  190.9 1.3 collective-permute-start.34
  192.2 3.7 %reduce-scatter.5.cloned.1.call-done = bf16[1,5,24,768]{3,2,1,0:T(8,128)(2,1)} async-done(((bf16[4,5,24,768]{3,2,1,0:T(8,128)(2,1)}), bf16[1,5,24,768]{3,2,1,0:T(8,128)(2,1)}) %reduce-scatter.5.cloned.1.call-update) | async-done | bytes 184336 | tf_op jit(solution)/shard_map/reduce_scatter | solution.py:871
  197.6 1.7 collective-permute-start.31
  200.3 10.5 %all-to-all-done.4.t_ref = bf16[8,384,128]{2,1,0:T(8,128)(2,1)S(1)} async-done(((bf16[8,384,128]{2,1,0:T(8,128)(2,1)}), bf16[8,384,128]{2,1,0:T(8,128)(2,1)S(1)}, u32[]{:S(2)}, u32[]{:S(2)}) %all-to-all-start.4) | async-done | bytes 786464 | tf_op jit(solution)/shard_map/all_to_all | solution.py:875
  211.7 5.3 %first_back.1 = (bf16[2,2,64,768]{3,2,1,0:T(8,128)(2,1)}, bf16[2,2,64,768]{3,2,1,0:T(8,128)(2,1)}, bf16[32,24,640]{2,1,0:T(8,128)(2,1)}) custom-call(s32[2]{0:T(128)} %pad_add_fusion.at_ref, bf16[8,384,128]{2,1,0:T(8,128)(2,1)} %copy-done.20, bf16[4,2,2,64,768]{4,3,2,1,0:T(8,128)(2,1)} %bitcast.52, f32[2,5376]{1,0:T(2,128)} %get-tuple-element.140.table_ref, ...), custom_call_target="tpu_custom_call" | custom-call | flops 905969 | bytes 6129 | tf_op jit(solution)/shard_map/first_back/pallas_call | solution.py:844
  217.0 3.7 %all-to-all-start.5 = ((bf16[32,24,640]{2,1,0:T(8,128)(2,1)}), bf16[32,24,640]{2,1,0:T(8,128)(2,1)S(1)}, u32[]{:S(2)}, u32[]{:S(2)}) async-start(bf16[32,24,640]{2,1,0:T(8,128)(2,1)} %get-tuple-element.181), calls=%async_computation.7 | async-start | bytes 1966080 | tf_op jit(solution)/shard_map/all_to_all | solution.py:875
  221.0 1.5 collective-permute-done.35
  222.7 1.8 collective-permute-start.36
  225.2 9.8 %collective-permute-done.36.got_ref = bf16[2,64,768]{2,1,0:T(8,128)(2,1)S(1)} collective-permute-done((bf16[2,64,768]{2,1,0:T(8,128)(2,1)S(1)}, bf16[2,64,768]{2,1,0:T(8,128)(2,1)S(1)}, u32[]{:S(2)}, u32[]{:S(2)}) %collective-permute-start.36) | collective-permute-done | bytes 196640 | tf_op jit(solution)/shard_map/ppermute | solution.py:862
  235.1 1.1 input_grad.1
  236.2 10.7 %all-to-all-done.5.raw_ref = bf16[32,24,640]{2,1,0:T(8,128)(2,1)S(1)} async-done(((bf16[32,24,640]{2,1,0:T(8,128)(2,1)}), bf16[32,24,640]{2,1,0:T(8,128)(2,1)S(1)}, u32[]{:S(2)}, u32[]{:S(2)}) %all-to-all-start.5) | async-done | bytes 983072 | tf_op jit(solution)/shard_map/all_to_all | solution.py:875
  246.9 1.6 row_grad.1
  248.5 2.6 all-to-all-start.6
  251.6 6.7 %all-to-all-done.6 = f32[32,2,128]{2,1,0:T(2,128)S(1)} async-done(((f32[32,2,128]{2,1,0:T(2,128)}), f32[32,2,128]{2,1,0:T(2,128)S(1)}, u32[]{:S(2)}, u32[]{:S(2)}) %all-to-all-start.6) | async-done | bytes 32800 | tf_op jit(solution)/shard_map/all_to_all | solution.py:875
  (178 shorter events, 16.6 us)
Async XLA Ops:
  7.2 42.6 %all-gather.3.cloned.1.call-start = ((), (), s32[]{:S(2)}) async-start(), calls=%async_computation.11 | async-start | bytes 1966080 | tf_op jit(solution)/shard_map/all_gather | solution.py:938
  9.7 93.3 %copy-start.1 = (bf16[120,768]{1,0:T(8,128)(2,1)}, bf16[120,768]{1,0:T(8,128)(2,1)S(1)}, u32[]{:S(2)}) copy-start(bf16[120,768]{1,0:T(8,128)(2,1)S(1)} %constant_dynamic-update-slice_fusion.a0.b0) | copy-start | bytes 552964
  9.7 18.1 %collective-permute-start = (bf16[120,768]{1,0:T(8,128)(2,1)S(1)}, bf16[120,768]{1,0:T(8,128)(2,1)S(1)}, u32[]{:S(2)}, u32[]{:S(2)}) collective-permute-start(bf16[120,768]{1,0:T(8,128)(2,1)S(1)} %constant_dynamic-update-slice_fusion.a0.b0), channel_id=1, source_target_pairs={{0,2},{1,3},{2,0},{3,1},{4,6},{5,7},{6,4},{7,5},{8,10},{9,11},{10,... | collective-permute-start | bytes 552968 | tf_op jit(solution)/shard_map/ppermute | solution.py:866
  12.8 15.0 %collective-permute-start.1 = (bf16[120,768]{1,0:T(8,128)(2,1)S(1)}, bf16[120,768]{1,0:T(8,128)(2,1)S(1)}, u32[]{:S(2)}, u32[]{:S(2)}) collective-permute-start(bf16[120,768]{1,0:T(8,128)(2,1)S(1)} %constant_dynamic-update-slice_fusion.a0.b0), channel_id=1, source_target_pairs={{0,4},{1,5},{2,6},{3,7},{4,0},{5,1},{6,2},{7,3},{8,12},{9,13},{10,... | collective-permute-start | bytes 552968 | tf_op jit(solution)/shard_map/ppermute | solution.py:866
  15.4 12.4 %all-to-all-start = ((bf16[4,24,1408]{2,1,0:T(8,128)(2,1)}), bf16[4,24,1408]{2,1,0:T(8,128)(2,1)S(1)}, u32[]{:S(2)}, u32[]{:S(2)}) async-start(bf16[4,24,1408]{2,1,0:T(8,128)(2,1)} %get-tuple-element.101), calls=%async_computation | async-start | bytes 540672 | tf_op jit(solution)/shard_map/all_to_all | solution.py:875
  27.8 75.2 %copy-start.4 = (bf16[120,768]{1,0:T(8,128)(2,1)}, bf16[120,768]{1,0:T(8,128)(2,1)S(1)}, u32[]{:S(2)}) copy-start(bf16[120,768]{1,0:T(8,128)(2,1)S(1)} %collective-permute-done.a2.b2) | copy-start | bytes 552964
  27.8 75.2 %copy-start.5 = (bf16[120,768]{1,0:T(8,128)(2,1)}, bf16[120,768]{1,0:T(8,128)(2,1)S(1)}, u32[]{:S(2)}) copy-start(bf16[120,768]{1,0:T(8,128)(2,1)S(1)} %collective-permute-done.1.a4.b4) | copy-start | bytes 552964
  27.8 22.0 %copy-start.26 = (bf16[96,640]{1,0:T(8,128)(2,1)}, bf16[96,640]{1,0:T(8,128)(2,1)S(1)}, u32[]{:S(2)}) copy-start(bf16[96,640]{1,0:T(8,128)(2,1)S(1)} %slice.53.a0) | copy-start | bytes 368644
  27.8 6.6 %collective-permute-start.3 = (bf16[96,640]{1,0:T(8,128)(2,1)S(1)}, bf16[96,640]{1,0:T(8,128)(2,1)S(1)}, u32[]{:S(2)}, u32[]{:S(2)}) collective-permute-start(bf16[96,640]{1,0:T(8,128)(2,1)S(1)} %slice.53.a0), channel_id=1, source_target_pairs={{0,2},{1,3},{2,0},{3,1},{4,6},{5,7},{6,4},{7,5},{8,10},{9,11},{10,... | collective-permute-start | bytes 368648 | tf_op jit(solution)/shard_map/ppermute | solution.py:866
  27.9 15.5 %collective-permute-start.5 = (bf16[96,640]{1,0:T(8,128)(2,1)S(1)}, bf16[96,640]{1,0:T(8,128)(2,1)S(1)}, u32[]{:S(2)}, u32[]{:S(2)}) collective-permute-start(bf16[96,640]{1,0:T(8,128)(2,1)S(1)} %slice.53.a0), channel_id=1, source_target_pairs={{0,4},{1,5},{2,6},{3,7},{4,0},{5,1},{6,2},{7,3},{8,12},{9,13},{10,... | collective-permute-start | bytes 368648 | tf_op jit(solution)/shard_map/ppermute | solution.py:866
  28.0 17.0 %collective-permute-start.7 = (bf16[96,640]{1,0:T(8,128)(2,1)S(1)}, bf16[96,640]{1,0:T(8,128)(2,1)S(1)}, u32[]{:S(2)}, u32[]{:S(2)}) collective-permute-start(bf16[96,640]{1,0:T(8,128)(2,1)S(1)} %slice.53.a0), channel_id=1, source_target_pairs={{0,6},{1,7},{2,4},{3,5},{4,2},{5,3},{6,0},{7,1},{8,14},{9,15},{10,... | collective-permute-start | bytes 368648 | tf_op jit(solution)/shard_map/ppermute | solution.py:866
  32.3 22.6 %collective-permute-start.9 = (bf16[120,768]{1,0:T(8,128)(2,1)S(1)}, bf16[120,768]{1,0:T(8,128)(2,1)S(1)}, u32[]{:S(2)}, u32[]{:S(2)}) collective-permute-start(bf16[120,768]{1,0:T(8,128)(2,1)S(1)} %constant_dynamic-update-slice_fusion.a0.b0), channel_id=1, source_target_pairs={{0,6},{1,7},{2,4},{3,5},{4,2},{5,3},{6,0},{7,1},{8,14},{9,15},{10,... | collective-permute-start | bytes 552968 | tf_op jit(solution)/shard_map/ppermute | solution.py:866
  32.3 13.1 %collective-permute-start.2 = (bf16[96,640]{1,0:T(8,128)(2,1)S(1)}, bf16[96,640]{1,0:T(8,128)(2,1)S(1)}, u32[]{:S(2)}, u32[]{:S(2)}) collective-permute-start(bf16[96,640]{1,0:T(8,128)(2,1)S(1)} %slice.53.a0), channel_id=1, source_target_pairs={{0,1},{1,0},{2,3},{3,2},{4,5},{5,4},{6,7},{7,6},{8,9},{9,8},{10,11... | collective-permute-start | bytes 368648 | tf_op jit(solution)/shard_map/ppermute | solution.py:866
  34.4 15.5 %copy-start.40 = (bf16[96,640]{1,0:T(8,128)(2,1)}, bf16[96,640]{1,0:T(8,128)(2,1)S(1)}, u32[]{:S(2)}) copy-start(bf16[96,640]{1,0:T(8,128)(2,1)S(1)} %collective-permute-done.3.a2) | copy-start | bytes 368644
  34.4 11.1 %collective-permute-start.4 = (bf16[96,640]{1,0:T(8,128)(2,1)S(1)}, bf16[96,640]{1,0:T(8,128)(2,1)S(1)}, u32[]{:S(2)}, u32[]{:S(2)}) collective-permute-start(bf16[96,640]{1,0:T(8,128)(2,1)S(1)} %collective-permute-done.3.a2), channel_id=1, source_target_pairs={{0,1},{1,0},{2,3},{3,2},{4,5},{5,4},{6,7},{7,6},{8,9},{9,8},{10,11... | collective-permute-start | bytes 368648 | tf_op jit(solution)/shard_map/ppermute | solution.py:866
  43.4 4.9 %collective-permute-start.6 = (bf16[96,640]{1,0:T(8,128)(2,1)S(1)}, bf16[96,640]{1,0:T(8,128)(2,1)S(1)}, u32[]{:S(2)}, u32[]{:S(2)}) collective-permute-start(bf16[96,640]{1,0:T(8,128)(2,1)S(1)} %collective-permute-done.5.a4), channel_id=1, source_target_pairs={{0,1},{1,0},{2,3},{3,2},{4,5},{5,4},{6,7},{7,6},{8,9},{9,8},{10,11... | collective-permute-start | bytes 368648 | tf_op jit(solution)/shard_map/ppermute | solution.py:866
  44.9 4.9 %collective-permute-start.8 = (bf16[96,640]{1,0:T(8,128)(2,1)S(1)}, bf16[96,640]{1,0:T(8,128)(2,1)S(1)}, u32[]{:S(2)}, u32[]{:S(2)}) collective-permute-start(bf16[96,640]{1,0:T(8,128)(2,1)S(1)} %collective-permute-done.7.a6), channel_id=1, source_target_pairs={{0,1},{1,0},{2,3},{3,2},{4,5},{5,4},{6,7},{7,6},{8,9},{9,8},{10,11... | collective-permute-start | bytes 368648 | tf_op jit(solution)/shard_map/ppermute | solution.py:866
  54.8 48.1 %copy-start.6 = (bf16[120,768]{1,0:T(8,128)(2,1)}, bf16[120,768]{1,0:T(8,128)(2,1)S(1)}, u32[]{:S(2)}) copy-start(bf16[120,768]{1,0:T(8,128)(2,1)S(1)} %collective-permute-done.9.a6.b6) | copy-start | bytes 552964
  54.9 22.1 %all-to-all-start.1 = ((bf16[8,384,128]{2,1,0:T(8,128)(2,1)}), bf16[8,384,128]{2,1,0:T(8,128)(2,1)S(1)}, u32[]{:S(2)}, u32[]{:S(2)}) async-start(bf16[8,384,128]{2,1,0:T(8,128)(2,1)} %get-tuple-element.111), calls=%async_computation.1 | async-start | bytes 1572864 | tf_op jit(solution)/shard_map/all_to_all | solution.py:875
  58.8 13.2 %collective-permute-start.10 = (bf16[120,768]{1,0:T(8,128)(2,1)S(1)}, bf16[120,768]{1,0:T(8,128)(2,1)S(1)}, u32[]{:S(2)}, u32[]{:S(2)}) collective-permute-start(bf16[120,768]{1,0:T(8,128)(2,1)S(1)} %constant_dynamic-update-slice_fusion.a0.b0), channel_id=1, source_target_pairs={{0,1},{1,0},{2,3},{3,2},{4,5},{5,4},{6,7},{7,6},{8,9},{9,8},{10,11... | collective-permute-start | bytes 552968 | tf_op jit(solution)/shard_map/ppermute | solution.py:866
  60.8 16.2 %collective-permute-start.11 = (bf16[120,768]{1,0:T(8,128)(2,1)S(1)}, bf16[120,768]{1,0:T(8,128)(2,1)S(1)}, u32[]{:S(2)}, u32[]{:S(2)}) collective-permute-start(bf16[120,768]{1,0:T(8,128)(2,1)S(1)} %collective-permute-done.a2.b2), channel_id=1, source_target_pairs={{0,1},{1,0},{2,3},{3,2},{4,5},{5,4},{6,7},{7,6},{8,9},{9,8},{10,11... | collective-permute-start | bytes 552968 | tf_op jit(solution)/shard_map/ppermute | solution.py:866
  60.8 27.9 %collective-permute-start.15 = (bf16[120,768]{1,0:T(8,128)(2,1)S(1)}, bf16[120,768]{1,0:T(8,128)(2,1)S(1)}, u32[]{:S(2)}, u32[]{:S(2)}) collective-permute-start(bf16[120,768]{1,0:T(8,128)(2,1)S(1)} %collective-permute-done.1.a4.b4), channel_id=1, source_target_pairs={{0,1},{1,0},{2,3},{3,2},{4,5},{5,4},{6,7},{7,6},{8,9},{9,8},{10,11... | collective-permute-start | bytes 552968 | tf_op jit(solution)/shard_map/ppermute | solution.py:866
  62.8 25.9 %collective-permute-start.16 = (bf16[120,768]{1,0:T(8,128)(2,1)S(1)}, bf16[120,768]{1,0:T(8,128)(2,1)S(1)}, u32[]{:S(2)}, u32[]{:S(2)}) collective-permute-start(bf16[120,768]{1,0:T(8,128)(2,1)S(1)} %collective-permute-done.9.a6.b6), channel_id=1, source_target_pairs={{0,1},{1,0},{2,3},{3,2},{4,5},{5,4},{6,7},{7,6},{8,9},{9,8},{10,11... | collective-permute-start | bytes 552968 | tf_op jit(solution)/shard_map/ppermute | solution.py:866
  62.9 32.1 %copy-start.23 = (bf16[96,768]{1,0:T(8,128)(2,1)}, bf16[96,768]{1,0:T(8,128)(2,1)S(1)}, u32[]{:S(2)}) copy-start(bf16[96,768]{1,0:T(8,128)(2,1)S(1)} %slice.69.a0) | copy-start | bytes 442372
  62.9 40.1 %copy-start.15 = (s32[2]{0:T(128)S(1)}, s32[2]{0:T(128)}, u32[]{:S(2)}) copy-start(s32[2]{0:T(128)} %pad_add_fusion.at_ref) | copy-start | bytes 28
  72.0 31.0 %copy-start.7 = (bf16[120,768]{1,0:T(8,128)(2,1)}, bf16[120,768]{1,0:T(8,128)(2,1)S(1)}, u32[]{:S(2)}) copy-start(bf16[120,768]{1,0:T(8,128)(2,1)S(1)} %collective-permute-done.10.a1.b1) | copy-start | bytes 552964
  77.0 26.0 %copy-start.8 = (bf16[120,768]{1,0:T(8,128)(2,1)}, bf16[120,768]{1,0:T(8,128)(2,1)S(1)}, u32[]{:S(2)}) copy-start(bf16[120,768]{1,0:T(8,128)(2,1)S(1)} %collective-permute-done.11.a3.b3) | copy-start | bytes 552964
  77.0 11.7 %collective-permute-start.12 = (bf16[96,768]{1,0:T(8,128)(2,1)S(1)}, bf16[96,768]{1,0:T(8,128)(2,1)S(1)}, u32[]{:S(2)}, u32[]{:S(2)}) collective-permute-start(bf16[96,768]{1,0:T(8,128)(2,1)S(1)} %slice.69.a0), channel_id=1, source_target_pairs={{0,2},{1,3},{2,0},{3,1},{4,6},{5,7},{6,4},{7,5},{8,10},{9,11},{10,... | collective-permute-start | bytes 442376 | tf_op jit(solution)/shard_map/ppermute | solution.py:866
  79.3 9.4 %collective-permute-start.13 = (bf16[96,768]{1,0:T(8,128)(2,1)S(1)}, bf16[96,768]{1,0:T(8,128)(2,1)S(1)}, u32[]{:S(2)}, u32[]{:S(2)}) collective-permute-start(bf16[96,768]{1,0:T(8,128)(2,1)S(1)} %slice.69.a0), channel_id=1, source_target_pairs={{0,4},{1,5},{2,6},{3,7},{4,0},{5,1},{6,2},{7,3},{8,12},{9,13},{10,... | collective-permute-start | bytes 442376 | tf_op jit(solution)/shard_map/ppermute | solution.py:866
  81.0 7.7 %collective-permute-start.14 = (bf16[96,768]{1,0:T(8,128)(2,1)S(1)}, bf16[96,768]{1,0:T(8,128)(2,1)S(1)}, u32[]{:S(2)}, u32[]{:S(2)}) collective-permute-start(bf16[96,768]{1,0:T(8,128)(2,1)S(1)} %slice.69.a0), channel_id=1, source_target_pairs={{0,6},{1,7},{2,4},{3,5},{4,2},{5,3},{6,0},{7,1},{8,14},{9,15},{10,... | collective-permute-start | bytes 442376 | tf_op jit(solution)/shard_map/ppermute | solution.py:866
  88.7 17.3 %copy-start.9 = (bf16[120,768]{1,0:T(8,128)(2,1)}, bf16[120,768]{1,0:T(8,128)(2,1)S(1)}, u32[]{:S(2)}) copy-start(bf16[120,768]{1,0:T(8,128)(2,1)S(1)} %collective-permute-done.15.a5.b5) | copy-start | bytes 552964
  88.7 17.3 %copy-start.10 = (bf16[120,768]{1,0:T(8,128)(2,1)}, bf16[120,768]{1,0:T(8,128)(2,1)S(1)}, u32[]{:S(2)}) copy-start(bf16[120,768]{1,0:T(8,128)(2,1)S(1)} %collective-permute-done.16.a7.b7) | copy-start | bytes 552964
  88.7 18.2 %copy-start.30 = (bf16[96,768]{1,0:T(8,128)(2,1)}, bf16[96,768]{1,0:T(8,128)(2,1)S(1)}, u32[]{:S(2)}) copy-start(bf16[96,768]{1,0:T(8,128)(2,1)S(1)} %collective-permute-done.12.a2) | copy-start | bytes 442372
  89.6 13.4 %all-to-all-start.2 = ((bf16[8,128,128]{2,1,0:T(8,128)(2,1)}), bf16[8,128,128]{2,1,0:T(8,128)(2,1)S(1)}, u32[]{:S(2)}, u32[]{:S(2)}) async-start(bf16[8,128,128]{2,1,0:T(8,128)(2,1)} %get-tuple-element.121), calls=%async_computation.2 | async-start | bytes 524288 | tf_op jit(solution)/shard_map/all_to_all | solution.py:875
  94.8 76.2 %reduce-scatter.3.cloned.1.call-start = ((), (), s32[]{:S(2)}) async-start(), calls=%async_computation.9 | async-start | bytes 737280 | tf_op jit(solution)/shard_map/reduce_scatter | solution.py:871
  95.0 6.6 %collective-permute-start.17 = (bf16[96,768]{1,0:T(8,128)(2,1)S(1)}, bf16[96,768]{1,0:T(8,128)(2,1)}, u32[]{:S(2)}, u32[]{:S(2)}) collective-permute-start(bf16[96,768]{1,0:T(8,128)(2,1)S(1)} %slice.69.a0), channel_id=1, source_target_pairs={{0,1},{1,0},{2,3},{3,2},{4,5},{5,4},{6,7},{7,6},{8,9},{9,8},{10,11... | collective-permute-start | bytes 442376 | tf_op jit(solution)/shard_map/ppermute | solution.py:866
  104.1 1.8 collective-permute-start.18
  106.0 12.9 %collective-permute-start.19 = (bf16[2,2,64,768]{3,2,1,0:T(8,128)(2,1)S(1)}, bf16[2,2,64,768]{3,2,1,0:T(8,128)(2,1)S(1)}, u32[]{:S(2)}, u32[]{:S(2)}) collective-permute-start(bf16[2,2,64,768]{3,2,1,0:T(8,128)(2,1)S(1)} %add_convert_fusion.7), channel_id=1, source_target_pairs={{0,16},{8,24},{16,0},{24,8},{1,17},{9,25},{17,1},{25,9},{2,18},{10... | collective-permute-start | bytes 1179656 | tf_op jit(solution)/shard_map/ppermute | solution.py:862
  107.0 6.7 %collective-permute-start.20 = (bf16[96,768]{1,0:T(8,128)(2,1)S(1)}, bf16[96,768]{1,0:T(8,128)(2,1)S(1)}, u32[]{:S(2)}, u32[]{:S(2)}) collective-permute-start(bf16[96,768]{1,0:T(8,128)(2,1)S(1)} %collective-permute-done.12.a2), channel_id=1, source_target_pairs={{0,1},{1,0},{2,3},{3,2},{4,5},{5,4},{6,7},{7,6},{8,9},{9,8},{10,11... | collective-permute-start | bytes 442376 | tf_op jit(solution)/shard_map/ppermute | solution.py:866
  107.0 9.9 %collective-permute-start.21 = (bf16[96,768]{1,0:T(8,128)(2,1)S(1)}, bf16[96,768]{1,0:T(8,128)(2,1)S(1)}, u32[]{:S(2)}, u32[]{:S(2)}) collective-permute-start(bf16[96,768]{1,0:T(8,128)(2,1)S(1)} %copy-done.32), channel_id=1, source_target_pairs={{0,1},{1,0},{2,3},{3,2},{4,5},{5,4},{6,7},{7,6},{8,9},{9,8},{10,11... | collective-permute-start | bytes 442376 | tf_op jit(solution)/shard_map/ppermute | solution.py:866
  109.0 9.9 %collective-permute-start.22 = (bf16[96,768]{1,0:T(8,128)(2,1)S(1)}, bf16[96,768]{1,0:T(8,128)(2,1)S(1)}, u32[]{:S(2)}, u32[]{:S(2)}) collective-permute-start(bf16[96,768]{1,0:T(8,128)(2,1)S(1)} %copy-done.34), channel_id=1, source_target_pairs={{0,1},{1,0},{2,3},{3,2},{4,5},{5,4},{6,7},{7,6},{8,9},{9,8},{10,11... | collective-permute-start | bytes 442376 | tf_op jit(solution)/shard_map/ppermute | solution.py:866
  119.1 1.8 collective-permute-start.23
  130.5 16.0 %copy-start.25 = (bf16[4,96,768]{2,1,0:T(8,128)(2,1)S(1)}, bf16[4,96,768]{2,1,0:T(8,128)(2,1)}, u32[]{:S(2)}) copy-start(bf16[4,96,768]{2,1,0:T(8,128)(2,1)} %get-tuple-element.157) | copy-start | bytes 1769476
  130.5 2.0 collective-permute-start.24
  130.7 15.8 %collective-permute-start.26 = (bf16[4,96,768]{2,1,0:T(8,128)(2,1)}, bf16[4,96,768]{2,1,0:T(8,128)(2,1)S(1)}, u32[]{:S(2)}, u32[]{:S(2)}) collective-permute-start(bf16[4,96,768]{2,1,0:T(8,128)(2,1)} %get-tuple-element.151), channel_id=1, source_target_pairs={{0,1},{1,0},{2,3},{3,2},{4,5},{5,4},{6,7},{7,6},{8,9},{9,8},{10,11... | collective-permute-start | bytes 1769480 | tf_op jit(solution)/shard_map/ppermute | solution.py:866
  133.6 12.9 %collective-permute-start.25 = (bf16[2,2,64,768]{3,2,1,0:T(8,128)(2,1)S(1)}, bf16[2,2,64,768]{3,2,1,0:T(8,128)(2,1)S(1)}, u32[]{:S(2)}, u32[]{:S(2)}) collective-permute-start(bf16[2,2,64,768]{3,2,1,0:T(8,128)(2,1)S(1)} %add_convert_fusion.5), channel_id=1, source_target_pairs={{0,16},{8,24},{16,0},{24,8},{1,17},{9,25},{17,1},{25,9},{2,18},{10... | collective-permute-start | bytes 1179656 | tf_op jit(solution)/shard_map/ppermute | solution.py:862
  147.6 15.1 %collective-permute-start.29 = (bf16[4,4,24,768]{3,2,1,0:T(8,128)(2,1)S(1)}, bf16[4,4,24,768]{3,2,1,0:T(8,128)(2,1)S(1)}, u32[]{:S(2)}, u32[]{:S(2)}) collective-permute-start(bf16[4,4,24,768]{3,2,1,0:T(8,128)(2,1)S(1)} %copy-done.48), channel_id=1, source_target_pairs={{0,1},{1,0},{2,3},{3,2},{4,5},{5,4},{6,7},{7,6},{8,9},{9,8},{10,11... | collective-permute-start | bytes 1769480 | tf_op jit(solution)/shard_map/ppermute | solution.py:866
  148.0 1.8 collective-permute-start.27
  155.1 15.9 %all-to-all-start.3 = ((bf16[8,128,128]{2,1,0:T(8,128)(2,1)}), bf16[8,128,128]{2,1,0:T(8,128)(2,1)S(1)}, u32[]{:S(2)}, u32[]{:S(2)}) async-start(bf16[8,128,128]{2,1,0:T(8,128)(2,1)} %get-tuple-element.155), calls=%async_computation.3 | async-start | bytes 524288 | tf_op jit(solution)/shard_map/all_to_all | solution.py:875
  159.4 36.6 %reduce-scatter.5.cloned.1.call-start = ((), (), s32[]{:S(2)}) async-start(), calls=%async_computation.10 | async-start | bytes 921600 | tf_op jit(solution)/shard_map/reduce_scatter | solution.py:871
  159.7 8.0 %collective-permute-start.28 = (bf16[4,24,768]{2,1,0:T(8,128)(2,1)}, bf16[4,24,768]{2,1,0:T(8,128)(2,1)}, u32[]{:S(2)}, u32[]{:S(2)}) collective-permute-start(bf16[4,24,768]{2,1,0:T(8,128)(2,1)} %get-tuple-element.156), channel_id=1, source_target_pairs={{0,1},{1,0},{2,3},{3,2},{4,5},{5,4},{6,7},{7,6},{8,9},{9,8},{10,11... | collective-permute-start | bytes 442376 | tf_op jit(solution)/shard_map/ppermute | solution.py:866
  184.6 26.2 %all-to-all-start.4 = ((bf16[8,384,128]{2,1,0:T(8,128)(2,1)}), bf16[8,384,128]{2,1,0:T(8,128)(2,1)S(1)}, u32[]{:S(2)}, u32[]{:S(2)}) async-start(bf16[8,384,128]{2,1,0:T(8,128)(2,1)} %attn_bwd.1), calls=%async_computation.5 | async-start | bytes 1572864 | tf_op jit(solution)/shard_map/all_to_all | solution.py:875
  189.0 1.8 collective-permute-start.33
  190.9 8.5 %collective-permute-start.34 = (bf16[2,64,768]{2,1,0:T(8,128)(2,1)S(1)}, bf16[2,64,768]{2,1,0:T(8,128)(2,1)S(1)}, u32[]{:S(2)}, u32[]{:S(2)}) collective-permute-start(bf16[2,64,768]{2,1,0:T(8,128)(2,1)S(1)} %slice_bitcast_fusion.2), channel_id=1, source_target_pairs={{0,16},{8,24},{16,0},{24,8},{1,17},{9,25},{17,1},{25,9},{2,18},{10... | collective-permute-start | bytes 589832 | tf_op jit(solution)/shard_map/ppermute | solution.py:862
  197.6 13.2 %collective-permute-start.30 = (f32[24,768]{1,0:T(8,128)S(1)}, f32[24,768]{1,0:T(8,128)S(1)}, u32[]{:S(2)}, u32[]{:S(2)}) collective-permute-start(f32[24,768]{1,0:T(8,128)S(1)} %get-tuple-element.197), channel_id=1, source_target_pairs={{0,8},{8,0},{16,24},{24,16},{1,9},{9,1},{17,25},{25,17},{2,10},{10... | collective-permute-start | bytes 221192 | tf_op jit(solution)/shard_map/ppermute | solution.py:862
  197.6 13.2 %collective-permute-start.31 = (f32[24,768]{1,0:T(8,128)S(1)}, f32[24,768]{1,0:T(8,128)S(1)}, u32[]{:S(2)}, u32[]{:S(2)}) collective-permute-start(f32[24,768]{1,0:T(8,128)S(1)} %get-tuple-element.196), channel_id=1, source_target_pairs={{0,16},{8,24},{16,0},{24,8},{1,17},{9,25},{17,1},{25,9},{2,18},{10... | collective-permute-start | bytes 221192 | tf_op jit(solution)/shard_map/ppermute | solution.py:862
  199.3 11.5 %collective-permute-start.32 = (f32[24,768]{1,0:T(8,128)S(1)}, f32[24,768]{1,0:T(8,128)S(1)}, u32[]{:S(2)}, u32[]{:S(2)}) collective-permute-start(f32[24,768]{1,0:T(8,128)S(1)} %get-tuple-element.195), channel_id=1, source_target_pairs={{0,24},{8,16},{16,8},{24,0},{1,25},{9,17},{17,9},{25,1},{2,26},{10... | collective-permute-start | bytes 221192 | tf_op jit(solution)/shard_map/ppermute | solution.py:862
  217.0 29.9 %all-to-all-start.5 = ((bf16[32,24,640]{2,1,0:T(8,128)(2,1)}), bf16[32,24,640]{2,1,0:T(8,128)(2,1)S(1)}, u32[]{:S(2)}, u32[]{:S(2)}) async-start(bf16[32,24,640]{2,1,0:T(8,128)(2,1)} %get-tuple-element.181), calls=%async_computation.7 | async-start | bytes 1966080 | tf_op jit(solution)/shard_map/all_to_all | solution.py:875
  220.7 1.8 collective-permute-start.35
  222.6 24.3 %copy-start.14 = (bf16[128,144]{0,1:T(8,128)(2,1)S(1)}, bf16[128,144]{0,1:T(8,128)(2,1)}, u32[]{:S(2)}) copy-start(bf16[128,144]{0,1:T(8,128)(2,1)} %param.12) | copy-start | bytes 110596
  222.6 24.3 %copy-start.16 = (s32[2]{0:T(128)S(1)}, s32[2]{0:T(128)}, u32[]{:S(2)}) copy-start(s32[2]{0:T(128)} %pad_add_fusion.at_ref) | copy-start | bytes 28
  222.6 24.2 %copy-start.17 = (bf16[2,128]{1,0:T(2,128)(2,1)S(1)}, bf16[2,128]{1,0:T(2,128)(2,1)}, u32[]{:S(2)}) copy-start(bf16[2,128]{1,0:T(2,128)(2,1)} %cond_ref.3) | copy-start | bytes 1540
  222.7 12.4 %collective-permute-start.36 = (bf16[2,64,768]{2,1,0:T(8,128)(2,1)S(1)}, bf16[2,64,768]{2,1,0:T(8,128)(2,1)S(1)}, u32[]{:S(2)}, u32[]{:S(2)}) collective-permute-start(bf16[2,64,768]{2,1,0:T(8,128)(2,1)S(1)} %get-tuple-element.192), channel_id=1, source_target_pairs={{0,16},{8,24},{16,0},{24,8},{1,17},{9,25},{17,1},{25,9},{2,18},{10... | collective-permute-start | bytes 589832 | tf_op jit(solution)/shard_map/ppermute | solution.py:862
  248.5 9.7 %all-to-all-start.6 = ((f32[32,2,128]{2,1,0:T(2,128)}), f32[32,2,128]{2,1,0:T(2,128)S(1)}, u32[]{:S(2)}, u32[]{:S(2)}) async-start(f32[32,2,128]{2,1,0:T(2,128)} %get-tuple-element.186), calls=%async_computation.8 | async-start | bytes 65536 | tf_op jit(solution)/shard_map/all_to_all | solution.py:875
  (34 other events, 176.5 us)
Sparse Core Ops, SparseCore 0:
  10.2 24.6 all-gather.2
  147.6 22.2 reduce-scatter.2
  173.1 22.8 reduce-scatter.4

commit v5 on v4

--- a/solution.py
+++ b/solution.py
@@ -954,7 +954,7 @@
     chunks, down_z = lax.optimization_barrier((chunks, down_z))
     owned = exchange(chunks, "blk")
     down_zy = along_y(down_z)
-    owned, up_near, down_zy[1], down_zy[3] = lax.optimization_barrier((owned, up_near, down_zy[1], down_zy[3]))
+    up_near, down_zy[1], down_zy[3] = lax.optimization_barrier((up_near, down_zy[1], down_zy[3]))
     up_z = along_z(up_near)
     attn_low, attn_full, log_total = attn_fwd(owned)
     part_shape = (2, seqs, rows, width)

time: 266 us -> 265 us (level)
  no operation moved by 1% of the time
where the time goes in v5:
time: 265 us; the launch traced here: 264 us
  waiting for transfers between devices  120 us (45%)
  starting transfers between devices  67.3 us (25%)
  Pallas kernels  47.7 us (18%)
  between operations  14.4 us (5%)
  other arithmetic  10 us (4%)
  local copies, waits for them, and re-layouts  5.4 us (2%)
    ppermute x24, waiting for transfers between devices, swap_b(): return lax.ppermute(values, 'blk', [(i, i ^ mask) for i in range(8)])  57.8 us
    all_to_all x7, waiting for transfers between devices, exchange(): return lax.all_to_all(blocks, axis, split_axis=0, concat_axis=0, tiled=True)  39.1 us
    ppermute x24, starting transfers between devices, swap_b(): return lax.ppermute(values, 'blk', [(i, i ^ mask) for i in range(8)])  32.6 us
    pallas_call x8, Pallas kernels, call(): pl.pallas_call(body, out_shape=tuple((jax.ShapeDtypeStruct(shape, dtype)...  29.1 us
    all_to_all x7, starting transfers between devices, exchange(): return lax.all_to_all(blocks, axis, split_axis=0, concat_axis=0, tiled=True)  26.2 us
    ppermute x13, waiting for transfers between devices, swap_u(): return lax.ppermute(values, 'ulysses', [(i, i ^ mask) for i in range(4)])  18.9 us
    pallas_call x1, Pallas kernels, attn_bwd(): pl.pallas_call(attn_bwd_kernel, out_shape=jax.ShapeDtypeStruct((nb, rows3...  11.6 us
    ppermute x13, starting transfers between devices, swap_u(): return lax.ppermute(values, 'ulysses', [(i, i ^ mask) for i in range(4)])  7.98 us
  transfers between devices with their start and end apart: 47, of which 27 were waited for; matrix products, arithmetic and copies ran while one was open for 3% of the time, Pallas kernels for 11%

profile of v5, /device:TPU:0, one launch (start us, length us, event | category | flops | bytes accessed | tf_op | source)
XLA Modules:
  0.0 264.5 jit_solution(2990366692375001812)
XLA Ops:
  7.2 2.3 pack.1
  9.7 3.1 %collective-permute-start = (bf16[120,768]{1,0:T(8,128)(2,1)S(1)}, bf16[120,768]{1,0:T(8,128)(2,1)S(1)}, u32[]{:S(2)}, u32[]{:S(2)}) collective-permute-start(bf16[120,768]{1,0:T(8,128)(2,1)S(1)} %constant_dynamic-update-slice_fusion.a0.b0), channel_id=1, source_target_pairs={{0,2},{1,3},{2,0},{3,1},{4,6},{5,7},{6,4},{7,5},{8,10},{9,11},{10,... | collective-permute-start | bytes 552968 | tf_op jit(solution)/shard_map/ppermute | solution.py:866
  12.8 2.6 collective-permute-start.1
  15.4 3.4 %all-to-all-start = ((bf16[4,24,1408]{2,1,0:T(8,128)(2,1)}), bf16[4,24,1408]{2,1,0:T(8,128)(2,1)S(1)}, u32[]{:S(2)}, u32[]{:S(2)}) async-start(bf16[4,24,1408]{2,1,0:T(8,128)(2,1)} %get-tuple-element.100), calls=%async_computation | async-start | bytes 540672 | tf_op jit(solution)/shard_map/all_to_all | solution.py:875
  20.1 1.0 pad_maximum_fusion.1
  21.1 6.7 %all-to-all-done = bf16[4,24,1408]{2,1,0:T(8,128)(2,1)S(1)} async-done(((bf16[4,24,1408]{2,1,0:T(8,128)(2,1)}), bf16[4,24,1408]{2,1,0:T(8,128)(2,1)S(1)}, u32[]{:S(2)}, u32[]{:S(2)}) %all-to-all-start) | async-done | bytes 270368 | tf_op jit(solution)/shard_map/all_to_all | solution.py:875
  28.0 4.3 %collective-permute-start.7 = (bf16[96,640]{1,0:T(8,128)(2,1)S(1)}, bf16[96,640]{1,0:T(8,128)(2,1)S(1)}, u32[]{:S(2)}, u32[]{:S(2)}) collective-permute-start(bf16[96,640]{1,0:T(8,128)(2,1)S(1)} %slice.53.a0), channel_id=1, source_target_pairs={{0,6},{1,7},{2,4},{3,5},{4,2},{5,3},{6,0},{7,1},{8,14},{9,15},{10,... | collective-permute-start | bytes 368648 | tf_op jit(solution)/shard_map/ppermute | solution.py:866
  32.3 1.5 collective-permute-start.2
  34.4 1.5 collective-permute-start.4
  35.9 7.5 %collective-permute-done.5.a4 = bf16[96,640]{1,0:T(8,128)(2,1)S(1)} collective-permute-done((bf16[96,640]{1,0:T(8,128)(2,1)S(1)}, bf16[96,640]{1,0:T(8,128)(2,1)S(1)}, u32[]{:S(2)}, u32[]{:S(2)}) %collective-permute-start.5) | collective-permute-done | bytes 122912 | tf_op jit(solution)/shard_map/ppermute | solution.py:866
  43.4 1.5 collective-permute-start.6
  45.5 2.8 %collective-permute-done.6.a5 = bf16[96,640]{1,0:T(8,128)(2,1)S(1)} collective-permute-done((bf16[96,640]{1,0:T(8,128)(2,1)S(1)}, bf16[96,640]{1,0:T(8,128)(2,1)S(1)}, u32[]{:S(2)}, u32[]{:S(2)}) %collective-permute-start.6) | collective-permute-done | bytes 122912 | tf_op jit(solution)/shard_map/ppermute | solution.py:866
  48.3 1.5 collective-permute-done.8.a7
  50.5 4.4 %first.1 = (bf16[8,384,128]{2,1,0:T(8,128)(2,1)}, bf16[512,768]{1,0:T(8,128)(2,1)}, f32[2,5376]{1,0:T(2,128)}, bf16[768,576]{1,0:T(8,128)(2,1)}) custom-call(s32[2]{0:T(128)} %pad_add_fusion.at_ref, bf16[4,2,2,64,768]{4,3,2,1,0:T(8,128)(2,1)} %bitcast.49, f32[256,128]{1,0:T(8,128)} %get-tuple-element.103.cos_ref, f32[256,128]{1,0:T(8,128)} %get-tuple-element.104.sin_ref, ...), custom_call_target="tpu_custom_call" | custom-call | flops 452984 | bytes 5318 | tf_op jit(solution)/shard_map/first/pallas_call | solution.py:844
  54.9 3.9 %all-to-all-start.1 = ((bf16[8,384,128]{2,1,0:T(8,128)(2,1)}), bf16[8,384,128]{2,1,0:T(8,128)(2,1)S(1)}, u32[]{:S(2)}, u32[]{:S(2)}) async-start(bf16[8,384,128]{2,1,0:T(8,128)(2,1)} %get-tuple-element.110), calls=%async_computation.1 | async-start | bytes 1572864 | tf_op jit(solution)/shard_map/all_to_all | solution.py:875
  58.8 2.0 collective-permute-start.10
  60.8 2.0 collective-permute-start.15
  62.9 9.1 %collective-permute-done.10.a1.b1 = bf16[120,768]{1,0:T(8,128)(2,1)S(1)} collective-permute-done((bf16[120,768]{1,0:T(8,128)(2,1)S(1)}, bf16[120,768]{1,0:T(8,128)(2,1)S(1)}, u32[]{:S(2)}, u32[]{:S(2)}) %collective-permute-start.10) | collective-permute-done | bytes 184352 | tf_op jit(solution)/shard_map/ppermute | solution.py:866
  72.0 5.0 %collective-permute-done.11.a3.b3 = bf16[120,768]{1,0:T(8,128)(2,1)S(1)} collective-permute-done((bf16[120,768]{1,0:T(8,128)(2,1)S(1)}, bf16[120,768]{1,0:T(8,128)(2,1)S(1)}, u32[]{:S(2)}, u32[]{:S(2)}) %collective-permute-start.11) | collective-permute-done | bytes 184352 | tf_op jit(solution)/shard_map/ppermute | solution.py:866
  77.0 2.3 collective-permute-start.12
  79.3 1.7 collective-permute-start.13
  81.7 6.9 %attn_fwd.1 = (bf16[8,128,128]{2,1,0:T(8,128)(2,1)}, f32[8,128,128]{2,1,0:T(8,128)S(1)}, f32[8,8,256]{2,1,0:T(8,128)S(1)}) custom-call(bf16[8,384,128]{2,1,0:T(8,128)(2,1)S(1)} %all-to-all-done.1.x_ref), custom_call_target="tpu_custom_call" | custom-call | flops 1073741824 | bytes 2097152 | tf_op jit(solution)/shard_map/attn_fwd/pallas_call | solution.py:43
  89.5 4.4 %all-to-all-start.2 = ((bf16[8,128,128]{2,1,0:T(8,128)(2,1)}), bf16[8,128,128]{2,1,0:T(8,128)(2,1)S(1)}, u32[]{:S(2)}, u32[]{:S(2)}) async-start(bf16[8,128,128]{2,1,0:T(8,128)(2,1)} %get-tuple-element.119), calls=%async_computation.2 | async-start | bytes 524288 | tf_op jit(solution)/shard_map/all_to_all | solution.py:875
  94.1 1.9 collective-permute-start.17
  96.0 4.8 %collective-permute-done.17.a1 = bf16[96,768]{1,0:T(8,128)(2,1)} collective-permute-done((bf16[96,768]{1,0:T(8,128)(2,1)S(1)}, bf16[96,768]{1,0:T(8,128)(2,1)}, u32[]{:S(2)}, u32[]{:S(2)}) %collective-permute-start.17) | collective-permute-done | bytes 147488 | tf_op jit(solution)/shard_map/ppermute | solution.py:866
  100.7 1.4 all-to-all-done.2.t_ref
  102.2 1.0 out.1
  103.3 1.7 collective-permute-done.18
  105.1 1.0 collective-permute-start.19
  107.1 1.1 collective-permute-start.21
  108.1 1.0 collective-permute-start.22
  109.1 3.7 %collective-permute-done.20.a3 = bf16[96,768]{1,0:T(8,128)(2,1)S(1)} collective-permute-done((bf16[96,768]{1,0:T(8,128)(2,1)S(1)}, bf16[96,768]{1,0:T(8,128)(2,1)S(1)}, u32[]{:S(2)}, u32[]{:S(2)}) %collective-permute-start.20) | collective-permute-done | bytes 147488 | tf_op jit(solution)/shard_map/ppermute | solution.py:866
  112.9 3.2 %collective-permute-done.21.a5 = bf16[96,768]{1,0:T(8,128)(2,1)S(1)} collective-permute-done((bf16[96,768]{1,0:T(8,128)(2,1)S(1)}, bf16[96,768]{1,0:T(8,128)(2,1)S(1)}, u32[]{:S(2)}, u32[]{:S(2)}) %collective-permute-start.21) | collective-permute-done | bytes 147488 | tf_op jit(solution)/shard_map/ppermute | solution.py:866
  116.0 2.0 collective-permute-done.22.a7
  118.3 1.7 collective-permute-done.23.got_ref
  120.7 8.9 %ff.1 = (bf16[2,2,64,768]{3,2,1,0:T(8,128)(2,1)}, bf16[2,2,64,768]{3,2,1,0:T(8,128)(2,1)}, bf16[2,2,64,768]{3,2,1,0:T(8,128)(2,1)}, bf16[2,2,64,768]{3,2,1,0:T(8...) custom-call(s32[2]{0:T(128)} %pad_add_fusion.at_ref, ...), custom_call_target="tpu_custom_call" | custom-call | flops 3623878 | bytes 9007 | tf_op jit(solution)/shard_map/ff/pallas_call | solution.py:844
  129.8 1.0 collective-permute-start.26
  131.6 1.1 add_convert_fusion.5
  132.7 1.2 collective-permute-start.25
  133.9 11.8 %collective-permute-done.26 = bf16[4,96,768]{2,1,0:T(8,128)(2,1)S(1)} collective-permute-done((bf16[4,96,768]{2,1,0:T(8,128)(2,1)}, bf16[4,96,768]{2,1,0:T(8,128)(2,1)S(1)}, u32[]{:S(2)}, u32[]{:S(2)}) %collective-permute-start.26) | collective-permute-done | bytes 589856 | tf_op jit(solution)/shard_map/ppermute | solution.py:866
  147.9 1.7 collective-permute-done.27.dgot_ref
  150.4 4.5 %middle_back.1 = (bf16[8,128,128]{2,1,0:T(8,128)(2,1)}, f32[2,64,768]{2,1,0:T(8,128)}, f32[2,1,768]{2,1,0:T(1,128)}, bf16[4,24,768]{2,1,0:T(8,128)(2,1)}, bf16[4,24,768]{2,1,0:T(8,128)(2,1)}) custom-call(s32[2]{0:T(128)} %pad_add_fusion.at_ref, bf16[4,2,2,64,768]{4,3,2,1,0:T(8,128)(2,1)} %bitcast.51, bf16[2,2,64,768]{3,2,1,0:T(8,128)(2,1)} %copy-done.18, ...), custom_call_target="tpu_custom_call" | custom-call | flops 301989 | bytes 4636 | tf_op jit(solution)/shard_map/middle_back/pallas_call | solution.py:844
  154.9 3.8 %all-to-all-start.3 = ((bf16[8,128,128]{2,1,0:T(8,128)(2,1)}), bf16[8,128,128]{2,1,0:T(8,128)(2,1)S(1)}, u32[]{:S(2)}, u32[]{:S(2)}) async-start(bf16[8,128,128]{2,1,0:T(8,128)(2,1)} %get-tuple-element.153), calls=%async_computation.3 | async-start | bytes 524288 | tf_op jit(solution)/shard_map/all_to_all | solution.py:875
  159.0 1.8 collective-permute-start.28
  161.8 5.0 %collective-permute-done.28 = bf16[4,24,768]{2,1,0:T(8,128)(2,1)} collective-permute-done((bf16[4,24,768]{2,1,0:T(8,128)(2,1)}, bf16[4,24,768]{2,1,0:T(8,128)(2,1)}, u32[]{:S(2)}, u32[]{:S(2)}) %collective-permute-start.28) | collective-permute-done | bytes 147488 | tf_op jit(solution)/shard_map/ppermute | solution.py:866
  166.8 3.4 %all-to-all-done.3.d_ref = bf16[8,128,128]{2,1,0:T(8,128)(2,1)S(1)} async-done(((bf16[8,128,128]{2,1,0:T(8,128)(2,1)}), bf16[8,128,128]{2,1,0:T(8,128)(2,1)S(1)}, u32[]{:S(2)}, u32[]{:S(2)}) %all-to-all-start.3) | async-done | bytes 262176 | tf_op jit(solution)/shard_map/all_to_all | solution.py:875
  170.2 1.0 fusion.3
  172.2 11.6 %attn_bwd.1 = bf16[8,384,128]{2,1,0:T(8,128)(2,1)} custom-call(bf16[8,384,128]{2,1,0:T(8,128)(2,1)S(1)} %all-to-all-done.1.x_ref, bf16[8,128,128]{2,1,0:T(8,128)(2,1)S(1)} %all-to-all-done.3.d_ref, f32[8,128,128]{2,1,0:T(8,128)S(1)} %get-tuple-element.158.of_ref, f32[8,8,256]{2,1,0:T(8,128)S(1)} %get-tuple-element.159.lse_ref), custom_call_target="tpu_custom_call" | custom-call | flops 268435456 | bytes 262144 | tf_op jit(solution)/shard_map/attn_bwd/pallas_call | solution.py:95
  183.8 4.3 %all-to-all-start.4 = ((bf16[8,384,128]{2,1,0:T(8,128)(2,1)}), bf16[8,384,128]{2,1,0:T(8,128)(2,1)S(1)}, u32[]{:S(2)}, u32[]{:S(2)}) async-start(bf16[8,384,128]{2,1,0:T(8,128)(2,1)} %attn_bwd.1), calls=%async_computation.5 | async-start | bytes 1572864 | tf_op jit(solution)/shard_map/all_to_all | solution.py:875
  188.3 1.6 collective-permute-done.33
  190.0 1.3 collective-permute-start.34
  191.4 3.9 %reduce-scatter.5.cloned.1.call-done = bf16[1,5,24,768]{3,2,1,0:T(8,128)(2,1)} async-done(((bf16[4,5,24,768]{3,2,1,0:T(8,128)(2,1)}), bf16[1,5,24,768]{3,2,1,0:T(8,128)(2,1)}) %reduce-scatter.5.cloned.1.call-update) | async-done | bytes 184336 | tf_op jit(solution)/shard_map/reduce_scatter | solution.py:871
  196.9 1.5 collective-permute-start.31
  199.6 10.3 %all-to-all-done.4.t_ref = bf16[8,384,128]{2,1,0:T(8,128)(2,1)S(1)} async-done(((bf16[8,384,128]{2,1,0:T(8,128)(2,1)}), bf16[8,384,128]{2,1,0:T(8,128)(2,1)S(1)}, u32[]{:S(2)}, u32[]{:S(2)}) %all-to-all-start.4) | async-done | bytes 786464 | tf_op jit(solution)/shard_map/all_to_all | solution.py:875
  210.8 5.3 %first_back.1 = (bf16[2,2,64,768]{3,2,1,0:T(8,128)(2,1)}, bf16[2,2,64,768]{3,2,1,0:T(8,128)(2,1)}, bf16[32,24,640]{2,1,0:T(8,128)(2,1)}) custom-call(s32[2]{0:T(128)} %pad_add_fusion.at_ref, bf16[8,384,128]{2,1,0:T(8,128)(2,1)} %copy-done.20, bf16[4,2,2,64,768]{4,3,2,1,0:T(8,128)(2,1)} %bitcast.52, f32[2,5376]{1,0:T(2,128)} %get-tuple-element.138.table_ref, ...), custom_call_target="tpu_custom_call" | custom-call | flops 905969 | bytes 6129 | tf_op jit(solution)/shard_map/first_back/pallas_call | solution.py:844
  216.1 3.7 %all-to-all-start.5 = ((bf16[32,24,640]{2,1,0:T(8,128)(2,1)}), bf16[32,24,640]{2,1,0:T(8,128)(2,1)S(1)}, u32[]{:S(2)}, u32[]{:S(2)}) async-start(bf16[32,24,640]{2,1,0:T(8,128)(2,1)} %get-tuple-element.179), calls=%async_computation.7 | async-start | bytes 1966080 | tf_op jit(solution)/shard_map/all_to_all | solution.py:875
  220.2 1.5 collective-permute-done.35
  221.8 1.8 collective-permute-start.36
  224.4 9.8 %collective-permute-done.36.got_ref = bf16[2,64,768]{2,1,0:T(8,128)(2,1)S(1)} collective-permute-done((bf16[2,64,768]{2,1,0:T(8,128)(2,1)S(1)}, bf16[2,64,768]{2,1,0:T(8,128)(2,1)S(1)}, u32[]{:S(2)}, u32[]{:S(2)}) %collective-permute-start.36) | collective-permute-done | bytes 196640 | tf_op jit(solution)/shard_map/ppermute | solution.py:862
  234.2 1.1 input_grad.1
  235.3 10.7 %all-to-all-done.5.raw_ref = bf16[32,24,640]{2,1,0:T(8,128)(2,1)S(1)} async-done(((bf16[32,24,640]{2,1,0:T(8,128)(2,1)}), bf16[32,24,640]{2,1,0:T(8,128)(2,1)S(1)}, u32[]{:S(2)}, u32[]{:S(2)}) %all-to-all-start.5) | async-done | bytes 983072 | tf_op jit(solution)/shard_map/all_to_all | solution.py:875
  246.0 1.6 row_grad.1
  247.6 2.5 all-to-all-start.6
  250.7 6.7 %all-to-all-done.6 = f32[32,2,128]{2,1,0:T(2,128)S(1)} async-done(((f32[32,2,128]{2,1,0:T(2,128)}), f32[32,2,128]{2,1,0:T(2,128)S(1)}, u32[]{:S(2)}, u32[]{:S(2)}) %all-to-all-start.6) | async-done | bytes 32800 | tf_op jit(solution)/shard_map/all_to_all | solution.py:875
  (174 shorter events, 19.7 us)
Async XLA Ops:
  7.2 42.6 %all-gather.3.cloned.1.call-start = ((), (), s32[]{:S(2)}) async-start(), calls=%async_computation.11 | async-start | bytes 1966080 | tf_op jit(solution)/shard_map/all_gather | solution.py:938
  9.7 92.4 %copy-start.1 = (bf16[120,768]{1,0:T(8,128)(2,1)}, bf16[120,768]{1,0:T(8,128)(2,1)S(1)}, u32[]{:S(2)}) copy-start(bf16[120,768]{1,0:T(8,128)(2,1)S(1)} %constant_dynamic-update-slice_fusion.a0.b0) | copy-start | bytes 552964
  9.7 18.1 %collective-permute-start = (bf16[120,768]{1,0:T(8,128)(2,1)S(1)}, bf16[120,768]{1,0:T(8,128)(2,1)S(1)}, u32[]{:S(2)}, u32[]{:S(2)}) collective-permute-start(bf16[120,768]{1,0:T(8,128)(2,1)S(1)} %constant_dynamic-update-slice_fusion.a0.b0), channel_id=1, source_target_pairs={{0,2},{1,3},{2,0},{3,1},{4,6},{5,7},{6,4},{7,5},{8,10},{9,11},{10,... | collective-permute-start | bytes 552968 | tf_op jit(solution)/shard_map/ppermute | solution.py:866
  12.8 15.0 %collective-permute-start.1 = (bf16[120,768]{1,0:T(8,128)(2,1)S(1)}, bf16[120,768]{1,0:T(8,128)(2,1)S(1)}, u32[]{:S(2)}, u32[]{:S(2)}) collective-permute-start(bf16[120,768]{1,0:T(8,128)(2,1)S(1)} %constant_dynamic-update-slice_fusion.a0.b0), channel_id=1, source_target_pairs={{0,4},{1,5},{2,6},{3,7},{4,0},{5,1},{6,2},{7,3},{8,12},{9,13},{10,... | collective-permute-start | bytes 552968 | tf_op jit(solution)/shard_map/ppermute | solution.py:866
  15.4 12.4 %all-to-all-start = ((bf16[4,24,1408]{2,1,0:T(8,128)(2,1)}), bf16[4,24,1408]{2,1,0:T(8,128)(2,1)S(1)}, u32[]{:S(2)}, u32[]{:S(2)}) async-start(bf16[4,24,1408]{2,1,0:T(8,128)(2,1)} %get-tuple-element.100), calls=%async_computation | async-start | bytes 540672 | tf_op jit(solution)/shard_map/all_to_all | solution.py:875
  27.8 74.3 %copy-start.4 = (bf16[120,768]{1,0:T(8,128)(2,1)}, bf16[120,768]{1,0:T(8,128)(2,1)S(1)}, u32[]{:S(2)}) copy-start(bf16[120,768]{1,0:T(8,128)(2,1)S(1)} %collective-permute-done.a2.b2) | copy-start | bytes 552964
  27.8 74.3 %copy-start.5 = (bf16[120,768]{1,0:T(8,128)(2,1)}, bf16[120,768]{1,0:T(8,128)(2,1)S(1)}, u32[]{:S(2)}) copy-start(bf16[120,768]{1,0:T(8,128)(2,1)S(1)} %collective-permute-done.1.a4.b4) | copy-start | bytes 552964
  27.8 22.0 %copy-start.26 = (bf16[96,640]{1,0:T(8,128)(2,1)}, bf16[96,640]{1,0:T(8,128)(2,1)S(1)}, u32[]{:S(2)}) copy-start(bf16[96,640]{1,0:T(8,128)(2,1)S(1)} %slice.53.a0) | copy-start | bytes 368644
  27.8 6.6 %collective-permute-start.3 = (bf16[96,640]{1,0:T(8,128)(2,1)S(1)}, bf16[96,640]{1,0:T(8,128)(2,1)S(1)}, u32[]{:S(2)}, u32[]{:S(2)}) collective-permute-start(bf16[96,640]{1,0:T(8,128)(2,1)S(1)} %slice.53.a0), channel_id=1, source_target_pairs={{0,2},{1,3},{2,0},{3,1},{4,6},{5,7},{6,4},{7,5},{8,10},{9,11},{10,... | collective-permute-start | bytes 368648 | tf_op jit(solution)/shard_map/ppermute | solution.py:866
  27.9 15.5 %collective-permute-start.5 = (bf16[96,640]{1,0:T(8,128)(2,1)S(1)}, bf16[96,640]{1,0:T(8,128)(2,1)S(1)}, u32[]{:S(2)}, u32[]{:S(2)}) collective-permute-start(bf16[96,640]{1,0:T(8,128)(2,1)S(1)} %slice.53.a0), channel_id=1, source_target_pairs={{0,4},{1,5},{2,6},{3,7},{4,0},{5,1},{6,2},{7,3},{8,12},{9,13},{10,... | collective-permute-start | bytes 368648 | tf_op jit(solution)/shard_map/ppermute | solution.py:866
  28.0 17.0 %collective-permute-start.7 = (bf16[96,640]{1,0:T(8,128)(2,1)S(1)}, bf16[96,640]{1,0:T(8,128)(2,1)S(1)}, u32[]{:S(2)}, u32[]{:S(2)}) collective-permute-start(bf16[96,640]{1,0:T(8,128)(2,1)S(1)} %slice.53.a0), channel_id=1, source_target_pairs={{0,6},{1,7},{2,4},{3,5},{4,2},{5,3},{6,0},{7,1},{8,14},{9,15},{10,... | collective-permute-start | bytes 368648 | tf_op jit(solution)/shard_map/ppermute | solution.py:866
  32.3 22.6 %collective-permute-start.9 = (bf16[120,768]{1,0:T(8,128)(2,1)S(1)}, bf16[120,768]{1,0:T(8,128)(2,1)S(1)}, u32[]{:S(2)}, u32[]{:S(2)}) collective-permute-start(bf16[120,768]{1,0:T(8,128)(2,1)S(1)} %constant_dynamic-update-slice_fusion.a0.b0), channel_id=1, source_target_pairs={{0,6},{1,7},{2,4},{3,5},{4,2},{5,3},{6,0},{7,1},{8,14},{9,15},{10,... | collective-permute-start | bytes 552968 | tf_op jit(solution)/shard_map/ppermute | solution.py:866
  32.3 13.1 %collective-permute-start.2 = (bf16[96,640]{1,0:T(8,128)(2,1)S(1)}, bf16[96,640]{1,0:T(8,128)(2,1)S(1)}, u32[]{:S(2)}, u32[]{:S(2)}) collective-permute-start(bf16[96,640]{1,0:T(8,128)(2,1)S(1)} %slice.53.a0), channel_id=1, source_target_pairs={{0,1},{1,0},{2,3},{3,2},{4,5},{5,4},{6,7},{7,6},{8,9},{9,8},{10,11... | collective-permute-start | bytes 368648 | tf_op jit(solution)/shard_map/ppermute | solution.py:866
  34.4 15.5 %copy-start.38 = (bf16[96,640]{1,0:T(8,128)(2,1)}, bf16[96,640]{1,0:T(8,128)(2,1)S(1)}, u32[]{:S(2)}) copy-start(bf16[96,640]{1,0:T(8,128)(2,1)S(1)} %collective-permute-done.3.a2) | copy-start | bytes 368644
  34.4 11.1 %collective-permute-start.4 = (bf16[96,640]{1,0:T(8,128)(2,1)S(1)}, bf16[96,640]{1,0:T(8,128)(2,1)S(1)}, u32[]{:S(2)}, u32[]{:S(2)}) collective-permute-start(bf16[96,640]{1,0:T(8,128)(2,1)S(1)} %collective-permute-done.3.a2), channel_id=1, source_target_pairs={{0,1},{1,0},{2,3},{3,2},{4,5},{5,4},{6,7},{7,6},{8,9},{9,8},{10,11... | collective-permute-start | bytes 368648 | tf_op jit(solution)/shard_map/ppermute | solution.py:866
  43.4 4.9 %collective-permute-start.6 = (bf16[96,640]{1,0:T(8,128)(2,1)S(1)}, bf16[96,640]{1,0:T(8,128)(2,1)S(1)}, u32[]{:S(2)}, u32[]{:S(2)}) collective-permute-start(bf16[96,640]{1,0:T(8,128)(2,1)S(1)} %collective-permute-done.5.a4), channel_id=1, source_target_pairs={{0,1},{1,0},{2,3},{3,2},{4,5},{5,4},{6,7},{7,6},{8,9},{9,8},{10,11... | collective-permute-start | bytes 368648 | tf_op jit(solution)/shard_map/ppermute | solution.py:866
  44.9 4.9 %collective-permute-start.8 = (bf16[96,640]{1,0:T(8,128)(2,1)S(1)}, bf16[96,640]{1,0:T(8,128)(2,1)S(1)}, u32[]{:S(2)}, u32[]{:S(2)}) collective-permute-start(bf16[96,640]{1,0:T(8,128)(2,1)S(1)} %collective-permute-done.7.a6), channel_id=1, source_target_pairs={{0,1},{1,0},{2,3},{3,2},{4,5},{5,4},{6,7},{7,6},{8,9},{9,8},{10,11... | collective-permute-start | bytes 368648 | tf_op jit(solution)/shard_map/ppermute | solution.py:866
  54.9 47.3 %copy-start.6 = (bf16[120,768]{1,0:T(8,128)(2,1)}, bf16[120,768]{1,0:T(8,128)(2,1)S(1)}, u32[]{:S(2)}) copy-start(bf16[120,768]{1,0:T(8,128)(2,1)S(1)} %collective-permute-done.9.a6.b6) | copy-start | bytes 552964
  54.9 26.9 %all-to-all-start.1 = ((bf16[8,384,128]{2,1,0:T(8,128)(2,1)}), bf16[8,384,128]{2,1,0:T(8,128)(2,1)S(1)}, u32[]{:S(2)}, u32[]{:S(2)}) async-start(bf16[8,384,128]{2,1,0:T(8,128)(2,1)} %get-tuple-element.110), calls=%async_computation.1 | async-start | bytes 1572864 | tf_op jit(solution)/shard_map/all_to_all | solution.py:875
  58.8 13.2 %collective-permute-start.10 = (bf16[120,768]{1,0:T(8,128)(2,1)S(1)}, bf16[120,768]{1,0:T(8,128)(2,1)S(1)}, u32[]{:S(2)}, u32[]{:S(2)}) collective-permute-start(bf16[120,768]{1,0:T(8,128)(2,1)S(1)} %constant_dynamic-update-slice_fusion.a0.b0), channel_id=1, source_target_pairs={{0,1},{1,0},{2,3},{3,2},{4,5},{5,4},{6,7},{7,6},{8,9},{9,8},{10,11... | collective-permute-start | bytes 552968 | tf_op jit(solution)/shard_map/ppermute | solution.py:866
  60.8 16.2 %collective-permute-start.11 = (bf16[120,768]{1,0:T(8,128)(2,1)S(1)}, bf16[120,768]{1,0:T(8,128)(2,1)S(1)}, u32[]{:S(2)}, u32[]{:S(2)}) collective-permute-start(bf16[120,768]{1,0:T(8,128)(2,1)S(1)} %collective-permute-done.a2.b2), channel_id=1, source_target_pairs={{0,1},{1,0},{2,3},{3,2},{4,5},{5,4},{6,7},{7,6},{8,9},{9,8},{10,11... | collective-permute-start | bytes 552968 | tf_op jit(solution)/shard_map/ppermute | solution.py:866
  60.8 27.8 %collective-permute-start.15 = (bf16[120,768]{1,0:T(8,128)(2,1)S(1)}, bf16[120,768]{1,0:T(8,128)(2,1)S(1)}, u32[]{:S(2)}, u32[]{:S(2)}) collective-permute-start(bf16[120,768]{1,0:T(8,128)(2,1)S(1)} %collective-permute-done.1.a4.b4), channel_id=1, source_target_pairs={{0,1},{1,0},{2,3},{3,2},{4,5},{5,4},{6,7},{7,6},{8,9},{9,8},{10,11... | collective-permute-start | bytes 552968 | tf_op jit(solution)/shard_map/ppermute | solution.py:866
  62.8 25.8 %collective-permute-start.16 = (bf16[120,768]{1,0:T(8,128)(2,1)S(1)}, bf16[120,768]{1,0:T(8,128)(2,1)S(1)}, u32[]{:S(2)}, u32[]{:S(2)}) collective-permute-start(bf16[120,768]{1,0:T(8,128)(2,1)S(1)} %collective-permute-done.9.a6.b6), channel_id=1, source_target_pairs={{0,1},{1,0},{2,3},{3,2},{4,5},{5,4},{6,7},{7,6},{8,9},{9,8},{10,11... | collective-permute-start | bytes 552968 | tf_op jit(solution)/shard_map/ppermute | solution.py:866
  62.9 31.2 %copy-start.23 = (bf16[96,768]{1,0:T(8,128)(2,1)}, bf16[96,768]{1,0:T(8,128)(2,1)S(1)}, u32[]{:S(2)}) copy-start(bf16[96,768]{1,0:T(8,128)(2,1)S(1)} %slice.69.a0) | copy-start | bytes 442372
  62.9 39.3 %copy-start.15 = (s32[2]{0:T(128)S(1)}, s32[2]{0:T(128)}, u32[]{:S(2)}) copy-start(s32[2]{0:T(128)} %pad_add_fusion.at_ref) | copy-start | bytes 28
  72.0 30.1 %copy-start.7 = (bf16[120,768]{1,0:T(8,128)(2,1)}, bf16[120,768]{1,0:T(8,128)(2,1)S(1)}, u32[]{:S(2)}) copy-start(bf16[120,768]{1,0:T(8,128)(2,1)S(1)} %collective-permute-done.10.a1.b1) | copy-start | bytes 552964
  77.0 25.1 %copy-start.8 = (bf16[120,768]{1,0:T(8,128)(2,1)}, bf16[120,768]{1,0:T(8,128)(2,1)S(1)}, u32[]{:S(2)}) copy-start(bf16[120,768]{1,0:T(8,128)(2,1)S(1)} %collective-permute-done.11.a3.b3) | copy-start | bytes 552964
  77.0 11.7 %collective-permute-start.12 = (bf16[96,768]{1,0:T(8,128)(2,1)S(1)}, bf16[96,768]{1,0:T(8,128)(2,1)S(1)}, u32[]{:S(2)}, u32[]{:S(2)}) collective-permute-start(bf16[96,768]{1,0:T(8,128)(2,1)S(1)} %slice.69.a0), channel_id=1, source_target_pairs={{0,2},{1,3},{2,0},{3,1},{4,6},{5,7},{6,4},{7,5},{8,10},{9,11},{10,... | collective-permute-start | bytes 442376 | tf_op jit(solution)/shard_map/ppermute | solution.py:866
  79.3 9.4 %collective-permute-start.13 = (bf16[96,768]{1,0:T(8,128)(2,1)S(1)}, bf16[96,768]{1,0:T(8,128)(2,1)S(1)}, u32[]{:S(2)}, u32[]{:S(2)}) collective-permute-start(bf16[96,768]{1,0:T(8,128)(2,1)S(1)} %slice.69.a0), channel_id=1, source_target_pairs={{0,4},{1,5},{2,6},{3,7},{4,0},{5,1},{6,2},{7,3},{8,12},{9,13},{10,... | collective-permute-start | bytes 442376 | tf_op jit(solution)/shard_map/ppermute | solution.py:866
  81.0 7.7 %collective-permute-start.14 = (bf16[96,768]{1,0:T(8,128)(2,1)S(1)}, bf16[96,768]{1,0:T(8,128)(2,1)}, u32[]{:S(2)}, u32[]{:S(2)}) collective-permute-start(bf16[96,768]{1,0:T(8,128)(2,1)S(1)} %slice.69.a0), channel_id=1, source_target_pairs={{0,6},{1,7},{2,4},{3,5},{4,2},{5,3},{6,0},{7,1},{8,14},{9,15},{10,... | collective-permute-start | bytes 442376 | tf_op jit(solution)/shard_map/ppermute | solution.py:866
  88.7 16.4 %copy-start.9 = (bf16[120,768]{1,0:T(8,128)(2,1)}, bf16[120,768]{1,0:T(8,128)(2,1)S(1)}, u32[]{:S(2)}) copy-start(bf16[120,768]{1,0:T(8,128)(2,1)S(1)} %collective-permute-done.15.a5.b5) | copy-start | bytes 552964
  88.7 16.4 %copy-start.10 = (bf16[120,768]{1,0:T(8,128)(2,1)}, bf16[120,768]{1,0:T(8,128)(2,1)S(1)}, u32[]{:S(2)}) copy-start(bf16[120,768]{1,0:T(8,128)(2,1)S(1)} %collective-permute-done.16.a7.b7) | copy-start | bytes 552964
  88.7 17.4 %copy-start.30 = (bf16[96,768]{1,0:T(8,128)(2,1)}, bf16[96,768]{1,0:T(8,128)(2,1)S(1)}, u32[]{:S(2)}) copy-start(bf16[96,768]{1,0:T(8,128)(2,1)S(1)} %collective-permute-done.12.a2) | copy-start | bytes 442372
  89.5 12.6 %all-to-all-start.2 = ((bf16[8,128,128]{2,1,0:T(8,128)(2,1)}), bf16[8,128,128]{2,1,0:T(8,128)(2,1)S(1)}, u32[]{:S(2)}, u32[]{:S(2)}) async-start(bf16[8,128,128]{2,1,0:T(8,128)(2,1)} %get-tuple-element.119), calls=%async_computation.2 | async-start | bytes 524288 | tf_op jit(solution)/shard_map/all_to_all | solution.py:875
  93.9 76.3 %reduce-scatter.3.cloned.1.call-start = ((), (), s32[]{:S(2)}) async-start(), calls=%async_computation.9 | async-start | bytes 737280 | tf_op jit(solution)/shard_map/reduce_scatter | solution.py:871
  94.1 6.6 %collective-permute-start.17 = (bf16[96,768]{1,0:T(8,128)(2,1)S(1)}, bf16[96,768]{1,0:T(8,128)(2,1)}, u32[]{:S(2)}, u32[]{:S(2)}) collective-permute-start(bf16[96,768]{1,0:T(8,128)(2,1)S(1)} %slice.69.a0), channel_id=1, source_target_pairs={{0,1},{1,0},{2,3},{3,2},{4,5},{5,4},{6,7},{7,6},{8,9},{9,8},{10,11... | collective-permute-start | bytes 442376 | tf_op jit(solution)/shard_map/ppermute | solution.py:866
  103.2 1.8 collective-permute-start.18
  105.1 12.9 %collective-permute-start.19 = (bf16[2,2,64,768]{3,2,1,0:T(8,128)(2,1)S(1)}, bf16[2,2,64,768]{3,2,1,0:T(8,128)(2,1)S(1)}, u32[]{:S(2)}, u32[]{:S(2)}) collective-permute-start(bf16[2,2,64,768]{3,2,1,0:T(8,128)(2,1)S(1)} %add_convert_fusion.7), channel_id=1, source_target_pairs={{0,16},{8,24},{16,0},{24,8},{1,17},{9,25},{17,1},{25,9},{2,18},{10... | collective-permute-start | bytes 1179656 | tf_op jit(solution)/shard_map/ppermute | solution.py:862
  106.1 6.7 %collective-permute-start.20 = (bf16[96,768]{1,0:T(8,128)(2,1)S(1)}, bf16[96,768]{1,0:T(8,128)(2,1)S(1)}, u32[]{:S(2)}, u32[]{:S(2)}) collective-permute-start(bf16[96,768]{1,0:T(8,128)(2,1)S(1)} %collective-permute-done.12.a2), channel_id=1, source_target_pairs={{0,1},{1,0},{2,3},{3,2},{4,5},{5,4},{6,7},{7,6},{8,9},{9,8},{10,11... | collective-permute-start | bytes 442376 | tf_op jit(solution)/shard_map/ppermute | solution.py:866
  107.1 8.9 %collective-permute-start.21 = (bf16[96,768]{1,0:T(8,128)(2,1)S(1)}, bf16[96,768]{1,0:T(8,128)(2,1)S(1)}, u32[]{:S(2)}, u32[]{:S(2)}) collective-permute-start(bf16[96,768]{1,0:T(8,128)(2,1)S(1)} %copy-done.32), channel_id=1, source_target_pairs={{0,1},{1,0},{2,3},{3,2},{4,5},{5,4},{6,7},{7,6},{8,9},{9,8},{10,11... | collective-permute-start | bytes 442376 | tf_op jit(solution)/shard_map/ppermute | solution.py:866
  108.1 9.9 %collective-permute-start.22 = (bf16[96,768]{1,0:T(8,128)(2,1)}, bf16[96,768]{1,0:T(8,128)(2,1)S(1)}, u32[]{:S(2)}, u32[]{:S(2)}) collective-permute-start(bf16[96,768]{1,0:T(8,128)(2,1)} %collective-permute-done.14.a6), channel_id=1, source_target_pairs={{0,1},{1,0},{2,3},{3,2},{4,5},{5,4},{6,7},{7,6},{8,9},{9,8},{10,11... | collective-permute-start | bytes 442376 | tf_op jit(solution)/shard_map/ppermute | solution.py:866
  118.2 1.8 collective-permute-start.23
  129.6 16.0 %copy-start.25 = (bf16[4,96,768]{2,1,0:T(8,128)(2,1)S(1)}, bf16[4,96,768]{2,1,0:T(8,128)(2,1)}, u32[]{:S(2)}) copy-start(bf16[4,96,768]{2,1,0:T(8,128)(2,1)} %get-tuple-element.155) | copy-start | bytes 1769476
  129.6 2.0 collective-permute-start.24
  129.8 15.8 %collective-permute-start.26 = (bf16[4,96,768]{2,1,0:T(8,128)(2,1)}, bf16[4,96,768]{2,1,0:T(8,128)(2,1)S(1)}, u32[]{:S(2)}, u32[]{:S(2)}) collective-permute-start(bf16[4,96,768]{2,1,0:T(8,128)(2,1)} %get-tuple-element.149), channel_id=1, source_target_pairs={{0,1},{1,0},{2,3},{3,2},{4,5},{5,4},{6,7},{7,6},{8,9},{9,8},{10,11... | collective-permute-start | bytes 1769480 | tf_op jit(solution)/shard_map/ppermute | solution.py:866
  132.7 12.9 %collective-permute-start.25 = (bf16[2,2,64,768]{3,2,1,0:T(8,128)(2,1)S(1)}, bf16[2,2,64,768]{3,2,1,0:T(8,128)(2,1)S(1)}, u32[]{:S(2)}, u32[]{:S(2)}) collective-permute-start(bf16[2,2,64,768]{3,2,1,0:T(8,128)(2,1)S(1)} %add_convert_fusion.5), channel_id=1, source_target_pairs={{0,16},{8,24},{16,0},{24,8},{1,17},{9,25},{17,1},{25,9},{2,18},{10... | collective-permute-start | bytes 1179656 | tf_op jit(solution)/shard_map/ppermute | solution.py:862
  146.8 14.9 %collective-permute-start.29 = (bf16[4,4,24,768]{3,2,1,0:T(8,128)(2,1)S(1)}, bf16[4,4,24,768]{3,2,1,0:T(8,128)(2,1)S(1)}, u32[]{:S(2)}, u32[]{:S(2)}) collective-permute-start(bf16[4,4,24,768]{3,2,1,0:T(8,128)(2,1)S(1)} %copy-done.46), channel_id=1, source_target_pairs={{0,1},{1,0},{2,3},{3,2},{4,5},{5,4},{6,7},{7,6},{8,9},{9,8},{10,11... | collective-permute-start | bytes 1769480 | tf_op jit(solution)/shard_map/ppermute | solution.py:866
  147.8 1.8 collective-permute-start.27
  154.9 15.3 %all-to-all-start.3 = ((bf16[8,128,128]{2,1,0:T(8,128)(2,1)}), bf16[8,128,128]{2,1,0:T(8,128)(2,1)S(1)}, u32[]{:S(2)}, u32[]{:S(2)}) async-start(bf16[8,128,128]{2,1,0:T(8,128)(2,1)} %get-tuple-element.153), calls=%async_computation.3 | async-start | bytes 524288 | tf_op jit(solution)/shard_map/all_to_all | solution.py:875
  158.7 36.5 %reduce-scatter.5.cloned.1.call-start = ((), (), s32[]{:S(2)}) async-start(), calls=%async_computation.10 | async-start | bytes 921600 | tf_op jit(solution)/shard_map/reduce_scatter | solution.py:871
  159.0 7.8 %collective-permute-start.28 = (bf16[4,24,768]{2,1,0:T(8,128)(2,1)}, bf16[4,24,768]{2,1,0:T(8,128)(2,1)}, u32[]{:S(2)}, u32[]{:S(2)}) collective-permute-start(bf16[4,24,768]{2,1,0:T(8,128)(2,1)} %get-tuple-element.154), channel_id=1, source_target_pairs={{0,1},{1,0},{2,3},{3,2},{4,5},{5,4},{6,7},{7,6},{8,9},{9,8},{10,11... | collective-permute-start | bytes 442376 | tf_op jit(solution)/shard_map/ppermute | solution.py:866
  183.8 26.1 %all-to-all-start.4 = ((bf16[8,384,128]{2,1,0:T(8,128)(2,1)}), bf16[8,384,128]{2,1,0:T(8,128)(2,1)S(1)}, u32[]{:S(2)}, u32[]{:S(2)}) async-start(bf16[8,384,128]{2,1,0:T(8,128)(2,1)} %attn_bwd.1), calls=%async_computation.5 | async-start | bytes 1572864 | tf_op jit(solution)/shard_map/all_to_all | solution.py:875
  188.1 1.8 collective-permute-start.33
  190.0 8.7 %collective-permute-start.34 = (bf16[2,64,768]{2,1,0:T(8,128)(2,1)S(1)}, bf16[2,64,768]{2,1,0:T(8,128)(2,1)S(1)}, u32[]{:S(2)}, u32[]{:S(2)}) collective-permute-start(bf16[2,64,768]{2,1,0:T(8,128)(2,1)S(1)} %slice_bitcast_fusion.2), channel_id=1, source_target_pairs={{0,16},{8,24},{16,0},{24,8},{1,17},{9,25},{17,1},{25,9},{2,18},{10... | collective-permute-start | bytes 589832 | tf_op jit(solution)/shard_map/ppermute | solution.py:862
  196.9 13.0 %collective-permute-start.30 = (f32[24,768]{1,0:T(8,128)S(1)}, f32[24,768]{1,0:T(8,128)S(1)}, u32[]{:S(2)}, u32[]{:S(2)}) collective-permute-start(f32[24,768]{1,0:T(8,128)S(1)} %get-tuple-element.195), channel_id=1, source_target_pairs={{0,8},{8,0},{16,24},{24,16},{1,9},{9,1},{17,25},{25,17},{2,10},{10... | collective-permute-start | bytes 221192 | tf_op jit(solution)/shard_map/ppermute | solution.py:862
  196.9 13.0 %collective-permute-start.31 = (f32[24,768]{1,0:T(8,128)S(1)}, f32[24,768]{1,0:T(8,128)S(1)}, u32[]{:S(2)}, u32[]{:S(2)}) collective-permute-start(f32[24,768]{1,0:T(8,128)S(1)} %get-tuple-element.194), channel_id=1, source_target_pairs={{0,16},{8,24},{16,0},{24,8},{1,17},{9,25},{17,1},{25,9},{2,18},{10... | collective-permute-start | bytes 221192 | tf_op jit(solution)/shard_map/ppermute | solution.py:862
  198.4 11.5 %collective-permute-start.32 = (f32[24,768]{1,0:T(8,128)S(1)}, f32[24,768]{1,0:T(8,128)S(1)}, u32[]{:S(2)}, u32[]{:S(2)}) collective-permute-start(f32[24,768]{1,0:T(8,128)S(1)} %get-tuple-element.193), channel_id=1, source_target_pairs={{0,24},{8,16},{16,8},{24,0},{1,25},{9,17},{17,9},{25,1},{2,26},{10... | collective-permute-start | bytes 221192 | tf_op jit(solution)/shard_map/ppermute | solution.py:862
  216.1 29.9 %all-to-all-start.5 = ((bf16[32,24,640]{2,1,0:T(8,128)(2,1)}), bf16[32,24,640]{2,1,0:T(8,128)(2,1)S(1)}, u32[]{:S(2)}, u32[]{:S(2)}) async-start(bf16[32,24,640]{2,1,0:T(8,128)(2,1)} %get-tuple-element.179), calls=%async_computation.7 | async-start | bytes 1966080 | tf_op jit(solution)/shard_map/all_to_all | solution.py:875
  219.8 1.8 collective-permute-start.35
  221.7 24.3 %copy-start.14 = (bf16[128,144]{0,1:T(8,128)(2,1)S(1)}, bf16[128,144]{0,1:T(8,128)(2,1)}, u32[]{:S(2)}) copy-start(bf16[128,144]{0,1:T(8,128)(2,1)} %param.12) | copy-start | bytes 110596
  221.8 24.3 %copy-start.16 = (s32[2]{0:T(128)S(1)}, s32[2]{0:T(128)}, u32[]{:S(2)}) copy-start(s32[2]{0:T(128)} %pad_add_fusion.at_ref) | copy-start | bytes 28
  221.8 24.2 %copy-start.17 = (bf16[2,128]{1,0:T(2,128)(2,1)S(1)}, bf16[2,128]{1,0:T(2,128)(2,1)}, u32[]{:S(2)}) copy-start(bf16[2,128]{1,0:T(2,128)(2,1)} %cond_ref.3) | copy-start | bytes 1540
  221.8 12.4 %collective-permute-start.36 = (bf16[2,64,768]{2,1,0:T(8,128)(2,1)S(1)}, bf16[2,64,768]{2,1,0:T(8,128)(2,1)S(1)}, u32[]{:S(2)}, u32[]{:S(2)}) collective-permute-start(bf16[2,64,768]{2,1,0:T(8,128)(2,1)S(1)} %get-tuple-element.190), channel_id=1, source_target_pairs={{0,16},{8,24},{16,0},{24,8},{1,17},{9,25},{17,1},{25,9},{2,18},{10... | collective-permute-start | bytes 589832 | tf_op jit(solution)/shard_map/ppermute | solution.py:862
  247.6 9.7 %all-to-all-start.6 = ((f32[32,2,128]{2,1,0:T(2,128)}), f32[32,2,128]{2,1,0:T(2,128)S(1)}, u32[]{:S(2)}, u32[]{:S(2)}) async-start(f32[32,2,128]{2,1,0:T(2,128)} %get-tuple-element.184), calls=%async_computation.8 | async-start | bytes 65536 | tf_op jit(solution)/shard_map/all_to_all | solution.py:875
  (32 other events, 169.8 us)
Sparse Core Ops, SparseCore 0:
  10.2 24.6 all-gather.2
  146.8 22.1 reduce-scatter.2
  172.3 22.9 reduce-scatter.4

commit v6 on v5

--- a/solution.py
+++ b/solution.py
@@ -949,7 +949,7 @@
         [((width, cols + HEAD_DIM), f32)],
         2 * tokens * width * cols,
         at, xg, cos_table, sin_table, *rows_zy,
-        limit=60,
+        limit=48,
     )
     chunks, down_z = lax.optimization_barrier((chunks, down_z))
     owned = exchange(chunks, "blk")

time: 265 us -> 267 us (level)
  local copies, waits for them, and re-layouts: 5.4 us -> 8.67 us
    unnamed x101 -> x97, local copies, waits for them, and re-layouts: 4.01 us -> 7.28 us
  transfers between devices with their start and end apart: 47 -> 47, of which waited for: 27 -> 27; matrix products, arithmetic and copies ran while one was open for 3% -> 2% of each run, Pallas kernels for 11% -> 10%
where the time goes in v6:
time: 267 us; the launch traced here: 266 us
  waiting for transfers between devices  121 us (45%)
  starting transfers between devices  67.4 us (25%)
  Pallas kernels  46.2 us (17%)
  between operations  14.4 us (5%)
  other arithmetic  8.78 us (3%)
  local copies, waits for them, and re-layouts  8.67 us (3%)
    ppermute x24, waiting for transfers between devices, swap_b(): return lax.ppermute(values, 'blk', [(i, i ^ mask) for i in range(8)])  57.9 us
    all_to_all x7, waiting for transfers between devices, exchange(): return lax.all_to_all(blocks, axis, split_axis=0, concat_axis=0, tiled=True)  40.4 us
    ppermute x24, starting transfers between devices, swap_b(): return lax.ppermute(values, 'blk', [(i, i ^ mask) for i in range(8)])  32.7 us
    pallas_call x8, Pallas kernels, call(): pl.pallas_call(body, out_shape=tuple((jax.ShapeDtypeStruct(shape, dtype)...  27.7 us
    all_to_all x7, starting transfers between devices, exchange(): return lax.all_to_all(blocks, axis, split_axis=0, concat_axis=0, tiled=True)  26.2 us
    ppermute x13, waiting for transfers between devices, swap_u(): return lax.ppermute(values, 'ulysses', [(i, i ^ mask) for i in range(4)])  18.8 us
    pallas_call x1, Pallas kernels, attn_bwd(): pl.pallas_call(attn_bwd_kernel, out_shape=jax.ShapeDtypeStruct((nb, rows3...  11.6 us
    ppermute x13, starting transfers between devices, swap_u(): return lax.ppermute(values, 'ulysses', [(i, i ^ mask) for i in range(4)])  8 us
  transfers between devices with their start and end apart: 47, of which 27 were waited for; matrix products, arithmetic and copies ran while one was open for 2% of the time, Pallas kernels for 10%

profile of v6, /device:TPU:0, one launch (start us, length us, event | category | flops | bytes accessed | tf_op | source)
XLA Modules:
  0.0 266.3 jit_solution(6374285551259063683)
XLA Ops:
  7.2 2.3 pack.1
  9.7 3.1 %collective-permute-start = (bf16[120,768]{1,0:T(8,128)(2,1)S(1)}, bf16[120,768]{1,0:T(8,128)(2,1)S(1)}, u32[]{:S(2)}, u32[]{:S(2)}) collective-permute-start(bf16[120,768]{1,0:T(8,128)(2,1)S(1)} %constant_dynamic-update-slice_fusion.a0.b0), channel_id=1, source_target_pairs={{0,2},{1,3},{2,0},{3,1},{4,6},{5,7},{6,4},{7,5},{8,10},{9,11},{10,... | collective-permute-start | bytes 552968 | tf_op jit(solution)/shard_map/ppermute | solution.py:866
  12.8 2.6 collective-permute-start.1
  15.4 3.4 %all-to-all-start = ((bf16[4,24,1408]{2,1,0:T(8,128)(2,1)}), bf16[4,24,1408]{2,1,0:T(8,128)(2,1)S(1)}, u32[]{:S(2)}, u32[]{:S(2)}) async-start(bf16[4,24,1408]{2,1,0:T(8,128)(2,1)} %get-tuple-element.100), calls=%async_computation | async-start | bytes 540672 | tf_op jit(solution)/shard_map/all_to_all | solution.py:875
  19.9 7.8 %all-to-all-done = bf16[4,24,1408]{2,1,0:T(8,128)(2,1)S(1)} async-done(((bf16[4,24,1408]{2,1,0:T(8,128)(2,1)}), bf16[4,24,1408]{2,1,0:T(8,128)(2,1)S(1)}, u32[]{:S(2)}, u32[]{:S(2)}) %all-to-all-start) | async-done | bytes 270368 | tf_op jit(solution)/shard_map/all_to_all | solution.py:875
  28.0 4.3 %collective-permute-start.7 = (bf16[96,640]{1,0:T(8,128)(2,1)S(1)}, bf16[96,640]{1,0:T(8,128)(2,1)S(1)}, u32[]{:S(2)}, u32[]{:S(2)}) collective-permute-start(bf16[96,640]{1,0:T(8,128)(2,1)S(1)} %slice.53.a0), channel_id=1, source_target_pairs={{0,6},{1,7},{2,4},{3,5},{4,2},{5,3},{6,0},{7,1},{8,14},{9,15},{10,... | collective-permute-start | bytes 368648 | tf_op jit(solution)/shard_map/ppermute | solution.py:866
  32.3 1.5 collective-permute-start.2
  34.4 1.5 collective-permute-start.4
  35.9 7.5 %collective-permute-done.5.a4 = bf16[96,640]{1,0:T(8,128)(2,1)S(1)} collective-permute-done((bf16[96,640]{1,0:T(8,128)(2,1)S(1)}, bf16[96,640]{1,0:T(8,128)(2,1)S(1)}, u32[]{:S(2)}, u32[]{:S(2)}) %collective-permute-start.5) | collective-permute-done | bytes 122912 | tf_op jit(solution)/shard_map/ppermute | solution.py:866
  43.4 1.5 collective-permute-start.6
  45.4 2.8 %collective-permute-done.6.a5 = bf16[96,640]{1,0:T(8,128)(2,1)S(1)} collective-permute-done((bf16[96,640]{1,0:T(8,128)(2,1)S(1)}, bf16[96,640]{1,0:T(8,128)(2,1)S(1)}, u32[]{:S(2)}, u32[]{:S(2)}) %collective-permute-start.6) | collective-permute-done | bytes 122912 | tf_op jit(solution)/shard_map/ppermute | solution.py:866
  48.3 1.5 collective-permute-done.8.a7
  49.8 1.4 copy-done
  51.2 2.9 %first.1 = (bf16[8,384,128]{2,1,0:T(8,128)(2,1)}, bf16[512,768]{1,0:T(8,128)(2,1)S(1)}, f32[2,5376]{1,0:T(2,128)S(1)}, bf16[768,576]{1,0:T(8,128)(2,1)S(1)}) custom-call(s32[2]{0:T(128)S(1)} %pad_add_fusion.at_ref, bf16[4,2,2,64,768]{4,3,2,1,0:T(8,128)(2,1)S(1)} %bitcast.50, f32[256,128]{1,0:T(8,128)S(1)} %get-tuple-element.103.cos_ref, ...), custom_call_target="tpu_custom_call" | custom-call | flops 452984 | bytes 5318 | tf_op jit(solution)/shard_map/first/pallas_call | solution.py:844
  56.6 3.9 %all-to-all-start.1 = ((bf16[8,384,128]{2,1,0:T(8,128)(2,1)}), bf16[8,384,128]{2,1,0:T(8,128)(2,1)S(1)}, u32[]{:S(2)}, u32[]{:S(2)}) async-start(bf16[8,384,128]{2,1,0:T(8,128)(2,1)} %get-tuple-element.110), calls=%async_computation.1 | async-start | bytes 1572864 | tf_op jit(solution)/shard_map/all_to_all | solution.py:875
  60.6 2.0 collective-permute-start.10
  62.6 2.0 collective-permute-start.15
  64.7 9.1 %collective-permute-done.10.a1.b1 = bf16[120,768]{1,0:T(8,128)(2,1)S(1)} collective-permute-done((bf16[120,768]{1,0:T(8,128)(2,1)S(1)}, bf16[120,768]{1,0:T(8,128)(2,1)S(1)}, u32[]{:S(2)}, u32[]{:S(2)}) %collective-permute-start.10) | collective-permute-done | bytes 184352 | tf_op jit(solution)/shard_map/ppermute | solution.py:866
  73.8 5.0 %collective-permute-done.11.a3.b3 = bf16[120,768]{1,0:T(8,128)(2,1)S(1)} collective-permute-done((bf16[120,768]{1,0:T(8,128)(2,1)S(1)}, bf16[120,768]{1,0:T(8,128)(2,1)S(1)}, u32[]{:S(2)}, u32[]{:S(2)}) %collective-permute-start.11) | collective-permute-done | bytes 184352 | tf_op jit(solution)/shard_map/ppermute | solution.py:866
  78.8 2.3 collective-permute-start.12
  81.1 1.7 collective-permute-start.13
  83.5 6.9 %attn_fwd.1 = (bf16[8,128,128]{2,1,0:T(8,128)(2,1)}, f32[8,128,128]{2,1,0:T(8,128)S(1)}, f32[8,8,256]{2,1,0:T(8,128)S(1)}) custom-call(bf16[8,384,128]{2,1,0:T(8,128)(2,1)S(1)} %all-to-all-done.1.x_ref), custom_call_target="tpu_custom_call" | custom-call | flops 1073741824 | bytes 2097152 | tf_op jit(solution)/shard_map/attn_fwd/pallas_call | solution.py:43
  91.2 4.4 %all-to-all-start.2 = ((bf16[8,128,128]{2,1,0:T(8,128)(2,1)}), bf16[8,128,128]{2,1,0:T(8,128)(2,1)S(1)}, u32[]{:S(2)}, u32[]{:S(2)}) async-start(bf16[8,128,128]{2,1,0:T(8,128)(2,1)} %get-tuple-element.119), calls=%async_computation.2 | async-start | bytes 524288 | tf_op jit(solution)/shard_map/all_to_all | solution.py:875
  95.9 1.9 collective-permute-start.17
  97.7 4.8 %collective-permute-done.17.a1 = bf16[96,768]{1,0:T(8,128)(2,1)} collective-permute-done((bf16[96,768]{1,0:T(8,128)(2,1)S(1)}, bf16[96,768]{1,0:T(8,128)(2,1)}, u32[]{:S(2)}, u32[]{:S(2)}) %collective-permute-start.17) | collective-permute-done | bytes 147488 | tf_op jit(solution)/shard_map/ppermute | solution.py:866
  102.5 1.4 all-to-all-done.2.t_ref
  103.9 1.0 out.1
  105.0 1.7 collective-permute-done.18
  107.9 1.0 collective-permute-start.20
  108.9 1.0 collective-permute-start.21
  109.9 1.0 collective-permute-start.22
  110.9 3.7 %collective-permute-done.20.a3 = bf16[96,768]{1,0:T(8,128)(2,1)S(1)} collective-permute-done((bf16[96,768]{1,0:T(8,128)(2,1)S(1)}, bf16[96,768]{1,0:T(8,128)(2,1)S(1)}, u32[]{:S(2)}, u32[]{:S(2)}) %collective-permute-start.20) | collective-permute-done | bytes 147488 | tf_op jit(solution)/shard_map/ppermute | solution.py:866
  114.6 3.2 %collective-permute-done.21.a5 = bf16[96,768]{1,0:T(8,128)(2,1)S(1)} collective-permute-done((bf16[96,768]{1,0:T(8,128)(2,1)S(1)}, bf16[96,768]{1,0:T(8,128)(2,1)S(1)}, u32[]{:S(2)}, u32[]{:S(2)}) %collective-permute-start.21) | collective-permute-done | bytes 147488 | tf_op jit(solution)/shard_map/ppermute | solution.py:866
  117.8 2.0 collective-permute-done.22.a7
  120.0 1.7 collective-permute-done.23.got_ref
  122.5 8.9 %ff.1 = (bf16[2,2,64,768]{3,2,1,0:T(8,128)(2,1)}, bf16[2,2,64,768]{3,2,1,0:T(8,128)(2,1)}, bf16[2,2,64,768]{3,2,1,0:T(8,128)(2,1)}, bf16[2,2,64,768]{3,2,1,0:T(8...) custom-call(s32[2]{0:T(128)} %copy-done.21, ...), custom_call_target="tpu_custom_call" | custom-call | flops 3623878 | bytes 9007 | tf_op jit(solution)/shard_map/ff/pallas_call | solution.py:844
  131.6 1.0 collective-permute-start.26
  133.4 1.1 add_convert_fusion.5
  134.5 1.2 collective-permute-start.25
  135.7 11.8 %collective-permute-done.26 = bf16[4,96,768]{2,1,0:T(8,128)(2,1)S(1)} collective-permute-done((bf16[4,96,768]{2,1,0:T(8,128)(2,1)}, bf16[4,96,768]{2,1,0:T(8,128)(2,1)S(1)}, u32[]{:S(2)}, u32[]{:S(2)}) %collective-permute-start.26) | collective-permute-done | bytes 589856 | tf_op jit(solution)/shard_map/ppermute | solution.py:866
  149.7 1.7 collective-permute-done.27.dgot_ref
  152.2 4.5 %middle_back.1 = (bf16[8,128,128]{2,1,0:T(8,128)(2,1)}, f32[2,64,768]{2,1,0:T(8,128)}, f32[2,1,768]{2,1,0:T(1,128)}, bf16[4,24,768]{2,1,0:T(8,128)(2,1)}, bf16[4,24,768]{2,1,0:T(8,128)(2,1)}) custom-call(s32[2]{0:T(128)} %copy-done.21, bf16[4,2,2,64,768]{4,3,2,1,0:T(8,128)(2,1)} %bitcast.48, bf16[2,2,64,768]{3,2,1,0:T(8,128)(2,1)} %copy-done.24, ...), custom_call_target="tpu_custom_call" | custom-call | flops 301989 | bytes 4636 | tf_op jit(solution)/shard_map/middle_back/pallas_call | solution.py:844
  156.7 3.8 %all-to-all-start.3 = ((bf16[8,128,128]{2,1,0:T(8,128)(2,1)}), bf16[8,128,128]{2,1,0:T(8,128)(2,1)S(1)}, u32[]{:S(2)}, u32[]{:S(2)}) async-start(bf16[8,128,128]{2,1,0:T(8,128)(2,1)} %get-tuple-element.153), calls=%async_computation.3 | async-start | bytes 524288 | tf_op jit(solution)/shard_map/all_to_all | solution.py:875
  160.8 1.8 collective-permute-start.28
  163.6 5.1 %collective-permute-done.28 = bf16[4,24,768]{2,1,0:T(8,128)(2,1)} collective-permute-done((bf16[4,24,768]{2,1,0:T(8,128)(2,1)}, bf16[4,24,768]{2,1,0:T(8,128)(2,1)}, u32[]{:S(2)}, u32[]{:S(2)}) %collective-permute-start.28) | collective-permute-done | bytes 147488 | tf_op jit(solution)/shard_map/ppermute | solution.py:866
  168.6 3.4 %all-to-all-done.3.d_ref = bf16[8,128,128]{2,1,0:T(8,128)(2,1)S(1)} async-done(((bf16[8,128,128]{2,1,0:T(8,128)(2,1)}), bf16[8,128,128]{2,1,0:T(8,128)(2,1)S(1)}, u32[]{:S(2)}, u32[]{:S(2)}) %all-to-all-start.3) | async-done | bytes 262176 | tf_op jit(solution)/shard_map/all_to_all | solution.py:875
  172.0 1.0 fusion.3
  174.0 11.6 %attn_bwd.1 = bf16[8,384,128]{2,1,0:T(8,128)(2,1)} custom-call(bf16[8,384,128]{2,1,0:T(8,128)(2,1)S(1)} %all-to-all-done.1.x_ref, bf16[8,128,128]{2,1,0:T(8,128)(2,1)S(1)} %all-to-all-done.3.d_ref, f32[8,128,128]{2,1,0:T(8,128)S(1)} %get-tuple-element.158.of_ref, f32[8,8,256]{2,1,0:T(8,128)S(1)} %get-tuple-element.159.lse_ref), custom_call_target="tpu_custom_call" | custom-call | flops 268435456 | bytes 262144 | tf_op jit(solution)/shard_map/attn_bwd/pallas_call | solution.py:95
  185.6 4.3 %all-to-all-start.4 = ((bf16[8,384,128]{2,1,0:T(8,128)(2,1)}), bf16[8,384,128]{2,1,0:T(8,128)(2,1)S(1)}, u32[]{:S(2)}, u32[]{:S(2)}) async-start(bf16[8,384,128]{2,1,0:T(8,128)(2,1)} %attn_bwd.1), calls=%async_computation.5 | async-start | bytes 1572864 | tf_op jit(solution)/shard_map/all_to_all | solution.py:875
  190.1 1.6 collective-permute-done.33
  191.8 1.3 collective-permute-start.34
  193.1 3.7 %reduce-scatter.5.cloned.1.call-done = bf16[1,5,24,768]{3,2,1,0:T(8,128)(2,1)} async-done(((bf16[4,5,24,768]{3,2,1,0:T(8,128)(2,1)}), bf16[1,5,24,768]{3,2,1,0:T(8,128)(2,1)}) %reduce-scatter.5.cloned.1.call-update) | async-done | bytes 184336 | tf_op jit(solution)/shard_map/reduce_scatter | solution.py:871
  198.5 1.7 collective-permute-start.31
  201.2 10.4 %all-to-all-done.4.t_ref = bf16[8,384,128]{2,1,0:T(8,128)(2,1)S(1)} async-done(((bf16[8,384,128]{2,1,0:T(8,128)(2,1)}), bf16[8,384,128]{2,1,0:T(8,128)(2,1)S(1)}, u32[]{:S(2)}, u32[]{:S(2)}) %all-to-all-start.4) | async-done | bytes 786464 | tf_op jit(solution)/shard_map/all_to_all | solution.py:875
  212.6 5.3 %first_back.1 = (bf16[2,2,64,768]{3,2,1,0:T(8,128)(2,1)}, bf16[2,2,64,768]{3,2,1,0:T(8,128)(2,1)}, bf16[32,24,640]{2,1,0:T(8,128)(2,1)}) custom-call(s32[2]{0:T(128)} %copy-done.21, bf16[8,384,128]{2,1,0:T(8,128)(2,1)} %copy-done.26, bf16[4,2,2,64,768]{4,3,2,1,0:T(8,128)(2,1)} %bitcast.49, f32[2,5376]{1,0:T(2,128)} %copy-done.5, f32[256,128]{1,0:T(8,128)} %copy-done.3, ...), custom_call_target="tpu_custom_call" | custom-call | flops 905969 | bytes 6129 | tf_op jit(solution)/shard_map/first_back/pallas_call | solution.py:844
  217.9 3.7 %all-to-all-start.5 = ((bf16[32,24,640]{2,1,0:T(8,128)(2,1)}), bf16[32,24,640]{2,1,0:T(8,128)(2,1)S(1)}, u32[]{:S(2)}, u32[]{:S(2)}) async-start(bf16[32,24,640]{2,1,0:T(8,128)(2,1)} %get-tuple-element.179), calls=%async_computation.7 | async-start | bytes 1966080 | tf_op jit(solution)/shard_map/all_to_all | solution.py:875
  222.0 1.5 collective-permute-done.35
  223.6 1.8 collective-permute-start.36
  226.2 9.8 %collective-permute-done.36.got_ref = bf16[2,64,768]{2,1,0:T(8,128)(2,1)S(1)} collective-permute-done((bf16[2,64,768]{2,1,0:T(8,128)(2,1)S(1)}, bf16[2,64,768]{2,1,0:T(8,128)(2,1)S(1)}, u32[]{:S(2)}, u32[]{:S(2)}) %collective-permute-start.36) | collective-permute-done | bytes 196640 | tf_op jit(solution)/shard_map/ppermute | solution.py:862
  236.0 1.1 input_grad.1
  237.1 10.7 %all-to-all-done.5.raw_ref = bf16[32,24,640]{2,1,0:T(8,128)(2,1)S(1)} async-done(((bf16[32,24,640]{2,1,0:T(8,128)(2,1)}), bf16[32,24,640]{2,1,0:T(8,128)(2,1)S(1)}, u32[]{:S(2)}, u32[]{:S(2)}) %all-to-all-start.5) | async-done | bytes 983072 | tf_op jit(solution)/shard_map/all_to_all | solution.py:875
  247.8 1.6 row_grad.1
  249.4 2.6 all-to-all-start.6
  252.5 6.7 %all-to-all-done.6 = f32[32,2,128]{2,1,0:T(2,128)S(1)} async-done(((f32[32,2,128]{2,1,0:T(2,128)}), f32[32,2,128]{2,1,0:T(2,128)S(1)}, u32[]{:S(2)}, u32[]{:S(2)}) %all-to-all-start.6) | async-done | bytes 32800 | tf_op jit(solution)/shard_map/all_to_all | solution.py:875
  (170 shorter events, 21.1 us)
Async XLA Ops:
  7.2 42.6 %all-gather.3.cloned.1.call-start = ((), (), s32[]{:S(2)}) async-start(), calls=%async_computation.11 | async-start | bytes 1966080 | tf_op jit(solution)/shard_map/all_gather | solution.py:938
  9.7 94.2 %copy-start.2 = (bf16[120,768]{1,0:T(8,128)(2,1)}, bf16[120,768]{1,0:T(8,128)(2,1)S(1)}, u32[]{:S(2)}) copy-start(bf16[120,768]{1,0:T(8,128)(2,1)S(1)} %constant_dynamic-update-slice_fusion.a0.b0) | copy-start | bytes 552964
  9.7 18.1 %collective-permute-start = (bf16[120,768]{1,0:T(8,128)(2,1)S(1)}, bf16[120,768]{1,0:T(8,128)(2,1)S(1)}, u32[]{:S(2)}, u32[]{:S(2)}) collective-permute-start(bf16[120,768]{1,0:T(8,128)(2,1)S(1)} %constant_dynamic-update-slice_fusion.a0.b0), channel_id=1, source_target_pairs={{0,2},{1,3},{2,0},{3,1},{4,6},{5,7},{6,4},{7,5},{8,10},{9,11},{10,... | collective-permute-start | bytes 552968 | tf_op jit(solution)/shard_map/ppermute | solution.py:866
  12.8 15.0 %collective-permute-start.1 = (bf16[120,768]{1,0:T(8,128)(2,1)S(1)}, bf16[120,768]{1,0:T(8,128)(2,1)S(1)}, u32[]{:S(2)}, u32[]{:S(2)}) collective-permute-start(bf16[120,768]{1,0:T(8,128)(2,1)S(1)} %constant_dynamic-update-slice_fusion.a0.b0), channel_id=1, source_target_pairs={{0,4},{1,5},{2,6},{3,7},{4,0},{5,1},{6,2},{7,3},{8,12},{9,13},{10,... | collective-permute-start | bytes 552968 | tf_op jit(solution)/shard_map/ppermute | solution.py:866
  15.4 12.4 %all-to-all-start = ((bf16[4,24,1408]{2,1,0:T(8,128)(2,1)}), bf16[4,24,1408]{2,1,0:T(8,128)(2,1)S(1)}, u32[]{:S(2)}, u32[]{:S(2)}) async-start(bf16[4,24,1408]{2,1,0:T(8,128)(2,1)} %get-tuple-element.100), calls=%async_computation | async-start | bytes 540672 | tf_op jit(solution)/shard_map/all_to_all | solution.py:875
  19.6 84.2 %copy-start.21 = (s32[2]{0:T(128)}, s32[2]{0:T(128)S(1)}, u32[]{:S(2)}) copy-start(s32[2]{0:T(128)S(1)} %pad_add_fusion.at_ref) | copy-start | bytes 28
  19.9 34.2 %copy-start.3 = (f32[256,128]{1,0:T(8,128)}, f32[256,128]{1,0:T(8,128)S(1)}, u32[]{:S(2)}) copy-start(f32[256,128]{1,0:T(8,128)S(1)} %get-tuple-element.103.cos_ref) | copy-start | bytes 393220
  19.9 34.2 %copy-start.4 = (f32[256,128]{1,0:T(8,128)}, f32[256,128]{1,0:T(8,128)S(1)}, u32[]{:S(2)}) copy-start(f32[256,128]{1,0:T(8,128)S(1)} %get-tuple-element.104.sin_ref) | copy-start | bytes 393220
  27.8 76.1 %copy-start.10 = (bf16[120,768]{1,0:T(8,128)(2,1)}, bf16[120,768]{1,0:T(8,128)(2,1)S(1)}, u32[]{:S(2)}) copy-start(bf16[120,768]{1,0:T(8,128)(2,1)S(1)} %collective-permute-done.a2.b2) | copy-start | bytes 552964
  27.8 76.1 %copy-start.11 = (bf16[120,768]{1,0:T(8,128)(2,1)}, bf16[120,768]{1,0:T(8,128)(2,1)S(1)}, u32[]{:S(2)}) copy-start(bf16[120,768]{1,0:T(8,128)(2,1)S(1)} %collective-permute-done.1.a4.b4) | copy-start | bytes 552964
  27.8 6.6 %collective-permute-start.3 = (bf16[96,640]{1,0:T(8,128)(2,1)S(1)}, bf16[96,640]{1,0:T(8,128)(2,1)S(1)}, u32[]{:S(2)}, u32[]{:S(2)}) collective-permute-start(bf16[96,640]{1,0:T(8,128)(2,1)S(1)} %slice.53.a0), channel_id=1, source_target_pairs={{0,2},{1,3},{2,0},{3,1},{4,6},{5,7},{6,4},{7,5},{8,10},{9,11},{10,... | collective-permute-start | bytes 368648 | tf_op jit(solution)/shard_map/ppermute | solution.py:866
  27.9 15.5 %collective-permute-start.5 = (bf16[96,640]{1,0:T(8,128)(2,1)S(1)}, bf16[96,640]{1,0:T(8,128)(2,1)S(1)}, u32[]{:S(2)}, u32[]{:S(2)}) collective-permute-start(bf16[96,640]{1,0:T(8,128)(2,1)S(1)} %slice.53.a0), channel_id=1, source_target_pairs={{0,4},{1,5},{2,6},{3,7},{4,0},{5,1},{6,2},{7,3},{8,12},{9,13},{10,... | collective-permute-start | bytes 368648 | tf_op jit(solution)/shard_map/ppermute | solution.py:866
  28.0 17.0 %collective-permute-start.7 = (bf16[96,640]{1,0:T(8,128)(2,1)S(1)}, bf16[96,640]{1,0:T(8,128)(2,1)S(1)}, u32[]{:S(2)}, u32[]{:S(2)}) collective-permute-start(bf16[96,640]{1,0:T(8,128)(2,1)S(1)} %slice.53.a0), channel_id=1, source_target_pairs={{0,6},{1,7},{2,4},{3,5},{4,2},{5,3},{6,0},{7,1},{8,14},{9,15},{10,... | collective-permute-start | bytes 368648 | tf_op jit(solution)/shard_map/ppermute | solution.py:866
  32.3 24.4 %collective-permute-start.9 = (bf16[120,768]{1,0:T(8,128)(2,1)S(1)}, bf16[120,768]{1,0:T(8,128)(2,1)S(1)}, u32[]{:S(2)}, u32[]{:S(2)}) collective-permute-start(bf16[120,768]{1,0:T(8,128)(2,1)S(1)} %constant_dynamic-update-slice_fusion.a0.b0), channel_id=1, source_target_pairs={{0,6},{1,7},{2,4},{3,5},{4,2},{5,3},{6,0},{7,1},{8,14},{9,15},{10,... | collective-permute-start | bytes 552968 | tf_op jit(solution)/shard_map/ppermute | solution.py:866
  32.3 13.1 %collective-permute-start.2 = (bf16[96,640]{1,0:T(8,128)(2,1)S(1)}, bf16[96,640]{1,0:T(8,128)(2,1)S(1)}, u32[]{:S(2)}, u32[]{:S(2)}) collective-permute-start(bf16[96,640]{1,0:T(8,128)(2,1)S(1)} %slice.53.a0), channel_id=1, source_target_pairs={{0,1},{1,0},{2,3},{3,2},{4,5},{5,4},{6,7},{7,6},{8,9},{9,8},{10,11... | collective-permute-start | bytes 368648 | tf_op jit(solution)/shard_map/ppermute | solution.py:866
  34.4 11.1 %collective-permute-start.4 = (bf16[96,640]{1,0:T(8,128)(2,1)S(1)}, bf16[96,640]{1,0:T(8,128)(2,1)S(1)}, u32[]{:S(2)}, u32[]{:S(2)}) collective-permute-start(bf16[96,640]{1,0:T(8,128)(2,1)S(1)} %collective-permute-done.3.a2), channel_id=1, source_target_pairs={{0,1},{1,0},{2,3},{3,2},{4,5},{5,4},{6,7},{7,6},{8,9},{9,8},{10,11... | collective-permute-start | bytes 368648 | tf_op jit(solution)/shard_map/ppermute | solution.py:866
  43.4 4.9 %collective-permute-start.6 = (bf16[96,640]{1,0:T(8,128)(2,1)S(1)}, bf16[96,640]{1,0:T(8,128)(2,1)S(1)}, u32[]{:S(2)}, u32[]{:S(2)}) collective-permute-start(bf16[96,640]{1,0:T(8,128)(2,1)S(1)} %collective-permute-done.5.a4), channel_id=1, source_target_pairs={{0,1},{1,0},{2,3},{3,2},{4,5},{5,4},{6,7},{7,6},{8,9},{9,8},{10,11... | collective-permute-start | bytes 368648 | tf_op jit(solution)/shard_map/ppermute | solution.py:866
  44.9 4.9 %collective-permute-start.8 = (bf16[96,640]{1,0:T(8,128)(2,1)S(1)}, bf16[96,640]{1,0:T(8,128)(2,1)S(1)}, u32[]{:S(2)}, u32[]{:S(2)}) collective-permute-start(bf16[96,640]{1,0:T(8,128)(2,1)S(1)} %collective-permute-done.7.a6), channel_id=1, source_target_pairs={{0,1},{1,0},{2,3},{3,2},{4,5},{5,4},{6,7},{7,6},{8,9},{9,8},{10,11... | collective-permute-start | bytes 368648 | tf_op jit(solution)/shard_map/ppermute | solution.py:866
  56.6 47.2 %copy-start.12 = (bf16[120,768]{1,0:T(8,128)(2,1)}, bf16[120,768]{1,0:T(8,128)(2,1)S(1)}, u32[]{:S(2)}) copy-start(bf16[120,768]{1,0:T(8,128)(2,1)S(1)} %collective-permute-done.9.a6.b6) | copy-start | bytes 552964
  56.6 26.8 %all-to-all-start.1 = ((bf16[8,384,128]{2,1,0:T(8,128)(2,1)}), bf16[8,384,128]{2,1,0:T(8,128)(2,1)S(1)}, u32[]{:S(2)}, u32[]{:S(2)}) async-start(bf16[8,384,128]{2,1,0:T(8,128)(2,1)} %get-tuple-element.110), calls=%async_computation.1 | async-start | bytes 1572864 | tf_op jit(solution)/shard_map/all_to_all | solution.py:875
  60.6 13.2 %collective-permute-start.10 = (bf16[120,768]{1,0:T(8,128)(2,1)S(1)}, bf16[120,768]{1,0:T(8,128)(2,1)S(1)}, u32[]{:S(2)}, u32[]{:S(2)}) collective-permute-start(bf16[120,768]{1,0:T(8,128)(2,1)S(1)} %constant_dynamic-update-slice_fusion.a0.b0), channel_id=1, source_target_pairs={{0,1},{1,0},{2,3},{3,2},{4,5},{5,4},{6,7},{7,6},{8,9},{9,8},{10,11... | collective-permute-start | bytes 552968 | tf_op jit(solution)/shard_map/ppermute | solution.py:866
  62.6 16.2 %collective-permute-start.11 = (bf16[120,768]{1,0:T(8,128)(2,1)S(1)}, bf16[120,768]{1,0:T(8,128)(2,1)S(1)}, u32[]{:S(2)}, u32[]{:S(2)}) collective-permute-start(bf16[120,768]{1,0:T(8,128)(2,1)S(1)} %collective-permute-done.a2.b2), channel_id=1, source_target_pairs={{0,1},{1,0},{2,3},{3,2},{4,5},{5,4},{6,7},{7,6},{8,9},{9,8},{10,11... | collective-permute-start | bytes 552968 | tf_op jit(solution)/shard_map/ppermute | solution.py:866
  62.6 27.8 %collective-permute-start.15 = (bf16[120,768]{1,0:T(8,128)(2,1)S(1)}, bf16[120,768]{1,0:T(8,128)(2,1)S(1)}, u32[]{:S(2)}, u32[]{:S(2)}) collective-permute-start(bf16[120,768]{1,0:T(8,128)(2,1)S(1)} %collective-permute-done.1.a4.b4), channel_id=1, source_target_pairs={{0,1},{1,0},{2,3},{3,2},{4,5},{5,4},{6,7},{7,6},{8,9},{9,8},{10,11... | collective-permute-start | bytes 552968 | tf_op jit(solution)/shard_map/ppermute | solution.py:866
  64.6 25.8 %collective-permute-start.16 = (bf16[120,768]{1,0:T(8,128)(2,1)S(1)}, bf16[120,768]{1,0:T(8,128)(2,1)S(1)}, u32[]{:S(2)}, u32[]{:S(2)}) collective-permute-start(bf16[120,768]{1,0:T(8,128)(2,1)S(1)} %collective-permute-done.9.a6.b6), channel_id=1, source_target_pairs={{0,1},{1,0},{2,3},{3,2},{4,5},{5,4},{6,7},{7,6},{8,9},{9,8},{10,11... | collective-permute-start | bytes 552968 | tf_op jit(solution)/shard_map/ppermute | solution.py:866
  64.7 31.2 %copy-start.29 = (bf16[96,768]{1,0:T(8,128)(2,1)}, bf16[96,768]{1,0:T(8,128)(2,1)S(1)}, u32[]{:S(2)}) copy-start(bf16[96,768]{1,0:T(8,128)(2,1)S(1)} %slice.69.a0) | copy-start | bytes 442372
  73.8 30.1 %copy-start.13 = (bf16[120,768]{1,0:T(8,128)(2,1)}, bf16[120,768]{1,0:T(8,128)(2,1)S(1)}, u32[]{:S(2)}) copy-start(bf16[120,768]{1,0:T(8,128)(2,1)S(1)} %collective-permute-done.10.a1.b1) | copy-start | bytes 552964
  78.8 25.1 %copy-start.14 = (bf16[120,768]{1,0:T(8,128)(2,1)}, bf16[120,768]{1,0:T(8,128)(2,1)S(1)}, u32[]{:S(2)}) copy-start(bf16[120,768]{1,0:T(8,128)(2,1)S(1)} %collective-permute-done.11.a3.b3) | copy-start | bytes 552964
  78.8 11.7 %collective-permute-start.12 = (bf16[96,768]{1,0:T(8,128)(2,1)S(1)}, bf16[96,768]{1,0:T(8,128)(2,1)S(1)}, u32[]{:S(2)}, u32[]{:S(2)}) collective-permute-start(bf16[96,768]{1,0:T(8,128)(2,1)S(1)} %slice.69.a0), channel_id=1, source_target_pairs={{0,2},{1,3},{2,0},{3,1},{4,6},{5,7},{6,4},{7,5},{8,10},{9,11},{10,... | collective-permute-start | bytes 442376 | tf_op jit(solution)/shard_map/ppermute | solution.py:866
  81.1 9.4 %collective-permute-start.13 = (bf16[96,768]{1,0:T(8,128)(2,1)S(1)}, bf16[96,768]{1,0:T(8,128)(2,1)S(1)}, u32[]{:S(2)}, u32[]{:S(2)}) collective-permute-start(bf16[96,768]{1,0:T(8,128)(2,1)S(1)} %slice.69.a0), channel_id=1, source_target_pairs={{0,4},{1,5},{2,6},{3,7},{4,0},{5,1},{6,2},{7,3},{8,12},{9,13},{10,... | collective-permute-start | bytes 442376 | tf_op jit(solution)/shard_map/ppermute | solution.py:866
  82.8 7.7 %collective-permute-start.14 = (bf16[96,768]{1,0:T(8,128)(2,1)S(1)}, bf16[96,768]{1,0:T(8,128)(2,1)}, u32[]{:S(2)}, u32[]{:S(2)}) collective-permute-start(bf16[96,768]{1,0:T(8,128)(2,1)S(1)} %slice.69.a0), channel_id=1, source_target_pairs={{0,6},{1,7},{2,4},{3,5},{4,2},{5,3},{6,0},{7,1},{8,14},{9,15},{10,... | collective-permute-start | bytes 442376 | tf_op jit(solution)/shard_map/ppermute | solution.py:866
  90.4 16.4 %copy-start.15 = (bf16[120,768]{1,0:T(8,128)(2,1)}, bf16[120,768]{1,0:T(8,128)(2,1)S(1)}, u32[]{:S(2)}) copy-start(bf16[120,768]{1,0:T(8,128)(2,1)S(1)} %collective-permute-done.15.a5.b5) | copy-start | bytes 552964
  90.4 16.4 %copy-start.16 = (bf16[120,768]{1,0:T(8,128)(2,1)}, bf16[120,768]{1,0:T(8,128)(2,1)S(1)}, u32[]{:S(2)}) copy-start(bf16[120,768]{1,0:T(8,128)(2,1)S(1)} %collective-permute-done.16.a7.b7) | copy-start | bytes 552964
  90.5 17.4 %copy-start.35 = (bf16[96,768]{1,0:T(8,128)(2,1)}, bf16[96,768]{1,0:T(8,128)(2,1)S(1)}, u32[]{:S(2)}) copy-start(bf16[96,768]{1,0:T(8,128)(2,1)S(1)} %collective-permute-done.12.a2) | copy-start | bytes 442372
  91.2 12.6 %all-to-all-start.2 = ((bf16[8,128,128]{2,1,0:T(8,128)(2,1)}), bf16[8,128,128]{2,1,0:T(8,128)(2,1)S(1)}, u32[]{:S(2)}, u32[]{:S(2)}) async-start(bf16[8,128,128]{2,1,0:T(8,128)(2,1)} %get-tuple-element.119), calls=%async_computation.2 | async-start | bytes 524288 | tf_op jit(solution)/shard_map/all_to_all | solution.py:875
  95.6 76.4 %reduce-scatter.3.cloned.1.call-start = ((), (), s32[]{:S(2)}) async-start(), calls=%async_computation.9 | async-start | bytes 737280 | tf_op jit(solution)/shard_map/reduce_scatter | solution.py:871
  95.9 6.6 %collective-permute-start.17 = (bf16[96,768]{1,0:T(8,128)(2,1)S(1)}, bf16[96,768]{1,0:T(8,128)(2,1)}, u32[]{:S(2)}, u32[]{:S(2)}) collective-permute-start(bf16[96,768]{1,0:T(8,128)(2,1)S(1)} %slice.69.a0), channel_id=1, source_target_pairs={{0,1},{1,0},{2,3},{3,2},{4,5},{5,4},{6,7},{7,6},{8,9},{9,8},{10,11... | collective-permute-start | bytes 442376 | tf_op jit(solution)/shard_map/ppermute | solution.py:866
  105.0 1.8 collective-permute-start.18
  106.9 12.9 %collective-permute-start.19 = (bf16[2,2,64,768]{3,2,1,0:T(8,128)(2,1)S(1)}, bf16[2,2,64,768]{3,2,1,0:T(8,128)(2,1)S(1)}, u32[]{:S(2)}, u32[]{:S(2)}) collective-permute-start(bf16[2,2,64,768]{3,2,1,0:T(8,128)(2,1)S(1)} %add_convert_fusion.7), channel_id=1, source_target_pairs={{0,16},{8,24},{16,0},{24,8},{1,17},{9,25},{17,1},{25,9},{2,18},{10... | collective-permute-start | bytes 1179656 | tf_op jit(solution)/shard_map/ppermute | solution.py:862
  107.9 6.7 %collective-permute-start.20 = (bf16[96,768]{1,0:T(8,128)(2,1)S(1)}, bf16[96,768]{1,0:T(8,128)(2,1)S(1)}, u32[]{:S(2)}, u32[]{:S(2)}) collective-permute-start(bf16[96,768]{1,0:T(8,128)(2,1)S(1)} %collective-permute-done.12.a2), channel_id=1, source_target_pairs={{0,1},{1,0},{2,3},{3,2},{4,5},{5,4},{6,7},{7,6},{8,9},{9,8},{10,11... | collective-permute-start | bytes 442376 | tf_op jit(solution)/shard_map/ppermute | solution.py:866
  108.9 8.9 %collective-permute-start.21 = (bf16[96,768]{1,0:T(8,128)(2,1)S(1)}, bf16[96,768]{1,0:T(8,128)(2,1)S(1)}, u32[]{:S(2)}, u32[]{:S(2)}) collective-permute-start(bf16[96,768]{1,0:T(8,128)(2,1)S(1)} %copy-done.37), channel_id=1, source_target_pairs={{0,1},{1,0},{2,3},{3,2},{4,5},{5,4},{6,7},{7,6},{8,9},{9,8},{10,11... | collective-permute-start | bytes 442376 | tf_op jit(solution)/shard_map/ppermute | solution.py:866
  109.9 9.9 %collective-permute-start.22 = (bf16[96,768]{1,0:T(8,128)(2,1)}, bf16[96,768]{1,0:T(8,128)(2,1)S(1)}, u32[]{:S(2)}, u32[]{:S(2)}) collective-permute-start(bf16[96,768]{1,0:T(8,128)(2,1)} %collective-permute-done.14.a6), channel_id=1, source_target_pairs={{0,1},{1,0},{2,3},{3,2},{4,5},{5,4},{6,7},{7,6},{8,9},{9,8},{10,11... | collective-permute-start | bytes 442376 | tf_op jit(solution)/shard_map/ppermute | solution.py:866
  119.9 1.8 collective-permute-start.23
  131.4 16.0 %copy-start.31 = (bf16[4,96,768]{2,1,0:T(8,128)(2,1)S(1)}, bf16[4,96,768]{2,1,0:T(8,128)(2,1)}, u32[]{:S(2)}) copy-start(bf16[4,96,768]{2,1,0:T(8,128)(2,1)} %get-tuple-element.155) | copy-start | bytes 1769476
  131.4 2.0 collective-permute-start.24
  131.6 15.8 %collective-permute-start.26 = (bf16[4,96,768]{2,1,0:T(8,128)(2,1)}, bf16[4,96,768]{2,1,0:T(8,128)(2,1)S(1)}, u32[]{:S(2)}, u32[]{:S(2)}) collective-permute-start(bf16[4,96,768]{2,1,0:T(8,128)(2,1)} %get-tuple-element.149), channel_id=1, source_target_pairs={{0,1},{1,0},{2,3},{3,2},{4,5},{5,4},{6,7},{7,6},{8,9},{9,8},{10,11... | collective-permute-start | bytes 1769480 | tf_op jit(solution)/shard_map/ppermute | solution.py:866
  134.5 12.9 %collective-permute-start.25 = (bf16[2,2,64,768]{3,2,1,0:T(8,128)(2,1)S(1)}, bf16[2,2,64,768]{3,2,1,0:T(8,128)(2,1)S(1)}, u32[]{:S(2)}, u32[]{:S(2)}) collective-permute-start(bf16[2,2,64,768]{3,2,1,0:T(8,128)(2,1)S(1)} %add_convert_fusion.5), channel_id=1, source_target_pairs={{0,16},{8,24},{16,0},{24,8},{1,17},{9,25},{17,1},{25,9},{2,18},{10... | collective-permute-start | bytes 1179656 | tf_op jit(solution)/shard_map/ppermute | solution.py:862
  148.5 14.9 %collective-permute-start.29 = (bf16[4,4,24,768]{3,2,1,0:T(8,128)(2,1)S(1)}, bf16[4,4,24,768]{3,2,1,0:T(8,128)(2,1)S(1)}, u32[]{:S(2)}, u32[]{:S(2)}) collective-permute-start(bf16[4,4,24,768]{3,2,1,0:T(8,128)(2,1)S(1)} %copy-done.44), channel_id=1, source_target_pairs={{0,1},{1,0},{2,3},{3,2},{4,5},{5,4},{6,7},{7,6},{8,9},{9,8},{10,11... | collective-permute-start | bytes 1769480 | tf_op jit(solution)/shard_map/ppermute | solution.py:866
  149.6 1.8 collective-permute-start.27
  156.7 15.3 %all-to-all-start.3 = ((bf16[8,128,128]{2,1,0:T(8,128)(2,1)}), bf16[8,128,128]{2,1,0:T(8,128)(2,1)S(1)}, u32[]{:S(2)}, u32[]{:S(2)}) async-start(bf16[8,128,128]{2,1,0:T(8,128)(2,1)} %get-tuple-element.153), calls=%async_computation.3 | async-start | bytes 524288 | tf_op jit(solution)/shard_map/all_to_all | solution.py:875
  160.5 36.4 %reduce-scatter.5.cloned.1.call-start = ((), (), s32[]{:S(2)}) async-start(), calls=%async_computation.10 | async-start | bytes 921600 | tf_op jit(solution)/shard_map/reduce_scatter | solution.py:871
  160.8 7.8 %collective-permute-start.28 = (bf16[4,24,768]{2,1,0:T(8,128)(2,1)}, bf16[4,24,768]{2,1,0:T(8,128)(2,1)}, u32[]{:S(2)}, u32[]{:S(2)}) collective-permute-start(bf16[4,24,768]{2,1,0:T(8,128)(2,1)} %get-tuple-element.154), channel_id=1, source_target_pairs={{0,1},{1,0},{2,3},{3,2},{4,5},{5,4},{6,7},{7,6},{8,9},{9,8},{10,11... | collective-permute-start | bytes 442376 | tf_op jit(solution)/shard_map/ppermute | solution.py:866
  185.6 26.1 %all-to-all-start.4 = ((bf16[8,384,128]{2,1,0:T(8,128)(2,1)}), bf16[8,384,128]{2,1,0:T(8,128)(2,1)S(1)}, u32[]{:S(2)}, u32[]{:S(2)}) async-start(bf16[8,384,128]{2,1,0:T(8,128)(2,1)} %attn_bwd.1), calls=%async_computation.5 | async-start | bytes 1572864 | tf_op jit(solution)/shard_map/all_to_all | solution.py:875
  189.9 1.8 collective-permute-start.33
  191.8 8.6 %collective-permute-start.34 = (bf16[2,64,768]{2,1,0:T(8,128)(2,1)S(1)}, bf16[2,64,768]{2,1,0:T(8,128)(2,1)S(1)}, u32[]{:S(2)}, u32[]{:S(2)}) collective-permute-start(bf16[2,64,768]{2,1,0:T(8,128)(2,1)S(1)} %slice_bitcast_fusion.2), channel_id=1, source_target_pairs={{0,16},{8,24},{16,0},{24,8},{1,17},{9,25},{17,1},{25,9},{2,18},{10... | collective-permute-start | bytes 589832 | tf_op jit(solution)/shard_map/ppermute | solution.py:862
  198.5 13.2 %collective-permute-start.30 = (f32[24,768]{1,0:T(8,128)S(1)}, f32[24,768]{1,0:T(8,128)S(1)}, u32[]{:S(2)}, u32[]{:S(2)}) collective-permute-start(f32[24,768]{1,0:T(8,128)S(1)} %get-tuple-element.195), channel_id=1, source_target_pairs={{0,8},{8,0},{16,24},{24,16},{1,9},{9,1},{17,25},{25,17},{2,10},{10... | collective-permute-start | bytes 221192 | tf_op jit(solution)/shard_map/ppermute | solution.py:862
  198.5 13.2 %collective-permute-start.31 = (f32[24,768]{1,0:T(8,128)S(1)}, f32[24,768]{1,0:T(8,128)S(1)}, u32[]{:S(2)}, u32[]{:S(2)}) collective-permute-start(f32[24,768]{1,0:T(8,128)S(1)} %get-tuple-element.194), channel_id=1, source_target_pairs={{0,16},{8,24},{16,0},{24,8},{1,17},{9,25},{17,1},{25,9},{2,18},{10... | collective-permute-start | bytes 221192 | tf_op jit(solution)/shard_map/ppermute | solution.py:862
  200.2 11.5 %collective-permute-start.32 = (f32[24,768]{1,0:T(8,128)S(1)}, f32[24,768]{1,0:T(8,128)S(1)}, u32[]{:S(2)}, u32[]{:S(2)}) collective-permute-start(f32[24,768]{1,0:T(8,128)S(1)} %get-tuple-element.193), channel_id=1, source_target_pairs={{0,24},{8,16},{16,8},{24,0},{1,25},{9,17},{17,9},{25,1},{2,26},{10... | collective-permute-start | bytes 221192 | tf_op jit(solution)/shard_map/ppermute | solution.py:862
  217.9 29.9 %all-to-all-start.5 = ((bf16[32,24,640]{2,1,0:T(8,128)(2,1)}), bf16[32,24,640]{2,1,0:T(8,128)(2,1)S(1)}, u32[]{:S(2)}, u32[]{:S(2)}) async-start(bf16[32,24,640]{2,1,0:T(8,128)(2,1)} %get-tuple-element.179), calls=%async_computation.7 | async-start | bytes 1966080 | tf_op jit(solution)/shard_map/all_to_all | solution.py:875
  221.6 1.8 collective-permute-start.35
  223.5 24.3 %copy-start.20 = (bf16[128,144]{0,1:T(8,128)(2,1)S(1)}, bf16[128,144]{0,1:T(8,128)(2,1)}, u32[]{:S(2)}) copy-start(bf16[128,144]{0,1:T(8,128)(2,1)} %param.12) | copy-start | bytes 110596
  223.6 24.3 %copy-start.22 = (s32[2]{0:T(128)S(1)}, s32[2]{0:T(128)}, u32[]{:S(2)}) copy-start(s32[2]{0:T(128)} %copy-done.21) | copy-start | bytes 28
  223.6 24.2 %copy-start.23 = (bf16[2,128]{1,0:T(2,128)(2,1)S(1)}, bf16[2,128]{1,0:T(2,128)(2,1)}, u32[]{:S(2)}) copy-start(bf16[2,128]{1,0:T(2,128)(2,1)} %cond_ref.3) | copy-start | bytes 1540
  223.6 12.4 %collective-permute-start.36 = (bf16[2,64,768]{2,1,0:T(8,128)(2,1)S(1)}, bf16[2,64,768]{2,1,0:T(8,128)(2,1)S(1)}, u32[]{:S(2)}, u32[]{:S(2)}) collective-permute-start(bf16[2,64,768]{2,1,0:T(8,128)(2,1)S(1)} %get-tuple-element.190), channel_id=1, source_target_pairs={{0,16},{8,24},{16,0},{24,8},{1,17},{9,25},{17,1},{25,9},{2,18},{10... | collective-permute-start | bytes 589832 | tf_op jit(solution)/shard_map/ppermute | solution.py:862
  249.4 9.7 %all-to-all-start.6 = ((f32[32,2,128]{2,1,0:T(2,128)}), f32[32,2,128]{2,1,0:T(2,128)S(1)}, u32[]{:S(2)}, u32[]{:S(2)}) async-start(f32[32,2,128]{2,1,0:T(2,128)} %get-tuple-element.184), calls=%async_computation.8 | async-start | bytes 65536 | tf_op jit(solution)/shard_map/all_to_all | solution.py:875
  (30 other events, 151.0 us)
Sparse Core Ops, SparseCore 0:
  10.2 24.6 all-gather.2
  148.5 22.0 reduce-scatter.2
  174.1 22.7 reduce-scatter.4
